TPU v7x, 32 devices: a whole 2x2x4 slice. The times are simulated.
32 devices in a mesh: dp: 8 (over z, y), tensor: 4 (over x, core).
Axes of the slice: x: 2, y: 2, z: 4, core: 2. Of those that a mesh axis runs over, the one named last changes fastest.
Arguments:
- tokens_long: bfloat16 [8, 1024, 1152], P('dp'), may hold values from -6 to 6
- tokens_short: bfloat16 [8, 256, 1152], P('dp'), may hold values from -6 to 6
- cond_long: bfloat16 [8, 1152], P('dp'), may hold values from -6 to 6
- cond_short: bfloat16 [8, 1152], P('dp'), may hold values from -6 to 6
- perm_long: int32 [8, 1024], P('dp'), may hold values from 0 to 1023, each once within a row
- perm_short: int32 [8, 256], P('dp'), may hold values from 0 to 255, each once within a row
- ada_weight: bfloat16 [2, 1152, 6912], P(None, None, 'dp'), may hold values from -0.09375 to 0.09375
- ada_bias: bfloat16 [2, 6912], P(None, 'dp'), may hold values from -1.5 to 1.5
- qkv_weight: bfloat16 [2, 1152, 3, 1152], P(None, None, None, 'tensor'), may hold values from -0.1875 to 0.1875
- qv_bias: bfloat16 [2, 2, 1152], P(None, None, 'tensor'), may hold values from -0.59765625 to 0.59765625
- proj_weight: bfloat16 [2, 1152, 1152], P(None, 'tensor'), may hold values from -0.375 to 0.375
- proj_bias: bfloat16 [2, 1152], replicated, may hold values from -1.796875 to 1.796875
- up_weight: bfloat16 [2, 1152, 4608], P(None, None, 'tensor'), may hold values from -0.1875 to 0.1875
- up_bias: bfloat16 [2, 4608], P(None, 'tensor'), may hold values from -3 to 3
- down_weight: bfloat16 [2, 4608, 1152], P(None, 'tensor'), may hold values from -0.09375 to 0.09375
- down_bias: bfloat16 [2, 1152], replicated, may hold values from -1.796875 to 1.796875
- mask_token: bfloat16 [1152], replicated, may hold values from -6 to 6
- cot_long: bfloat16 [8, 1024, 1152], P('dp'), may hold values from -6 to 6
- cot_short: bfloat16 [8, 256, 1152], P('dp'), may hold values from -6 to 6
Outputs:
- result_long: bfloat16 [8, 1024, 1152], P('dp')
- result_short: bfloat16 [8, 256, 1152], P('dp')
- dtok_long: bfloat16 [8, 1024, 1152], P('dp')
- dtok_short: bfloat16 [8, 256, 1152], P('dp')
- dcond_long: bfloat16 [8, 1152], P('dp')
- dcond_short: bfloat16 [8, 1152], P('dp')
- grad_ada_weight: float32 [2, 1152, 6912], P(None, None, 'dp')
- grad_ada_bias: float32 [2, 6912], P(None, 'dp')
- grad_qkv_weight: float32 [2, 1152, 3, 1152], P(None, 'dp', None, 'tensor')
- grad_qv_bias: float32 [2, 2, 1152], P(None, None, 'tensor')
- grad_proj_weight: float32 [2, 1152, 1152], P(None, 'tensor', 'dp')
- grad_proj_bias: float32 [2, 1152], replicated
- grad_up_weight: float32 [2, 1152, 4608], P(None, 'dp', 'tensor')
- grad_up_bias: float32 [2, 4608], P(None, 'tensor')
- grad_down_weight: float32 [2, 4608, 1152], P(None, 'tensor', 'dp')
- grad_down_bias: float32 [2, 1152], replicated
- grad_mask_token: float32 [1152], replicated
Inputs may be any that keep to these rules, and one draw needn't show every extreme that they name: `perm_long`: each row lists every position of its latent once; its first 512 entries are the kept positions. `perm_short`: each row lists every position of its latent once; its first 128 entries are the kept positions.
All inputs are finite; a program needn't handle non-finite values.
Results may differ from a plain program's by a relative error of at most 0.029.
Values may be sent and summed in bfloat16 or wider, within the bound.
No kernel may reach another device: no remote copies, remote signals or barrier semaphores. Data moves between devices by JAX's collectives and lax.ppermute only.
A program may use at most 320 MiB of HBM per device.

v0:
```python
from functools import partial
import math

import jax
import jax.numpy as jnp
from jax import lax
from jax.sharding import PartitionSpec as P

HEAD_DIM = 72


EPSILON = 1e-06


def layer_norm(values):
    center = values - jnp.mean(values, axis=-1, keepdims=True)
    spread = jnp.mean(center * center, axis=-1, keepdims=True)
    return center * lax.rsqrt(spread + EPSILON)


def sincos_table(grid_side, features):
    quarter = features // 4
    frequency = 1.0 / 10000.0 ** (jnp.arange(quarter, dtype=jnp.float32) / quarter)
    places = jnp.arange(grid_side * grid_side, dtype=jnp.int32)
    row_angle = (places // grid_side).astype(jnp.float32)[:, None] * frequency[None, :]
    col_angle = (places % grid_side).astype(jnp.float32)[:, None] * frequency[None, :]
    return jnp.concatenate(
        [jnp.sin(row_angle), jnp.cos(row_angle), jnp.sin(col_angle), jnp.cos(col_angle)], axis=1
    )


def split_latents(residual_stream, layout):
    portions = []
    offset = 0
    for latent_count, length in layout:
        portions.append(
            residual_stream[offset : offset + latent_count * length].reshape(
                (latent_count, length) + residual_stream.shape[1:]
            )
        )
        offset += latent_count * length
    return portions


def join_latents(portions):
    return jnp.concatenate(
        [portion.reshape((-1,) + portion.shape[2:]) for portion in portions], axis=0
    )


def mod_part(modulation_vector, position, features):
    return [
        mod_rows[:, position * features : (position + 1) * features]
        for mod_rows in modulation_vector
    ]


def plus_one(factors):
    return [1.0 + factor for factor in factors]


def modulated(values, layout, factors, offsets):
    return join_latents(
        [
            portion * (1.0 + factor[:, None, :]) + offset[:, None, :]
            for portion, factor, offset in zip(split_latents(values, layout), factors, offsets)
        ]
    )


def scaled(values, layout, factors):
    return join_latents(
        [
            portion * factor[:, None, :]
            for portion, factor in zip(split_latents(values, layout), factors)
        ]
    )


def latent_sums(values, layout):
    return [jnp.sum(portion, axis=1) for portion in split_latents(values, layout)]


def inverse_order(token_ordering):
    latent_count, length = token_ordering.shape
    places = jnp.arange(length, dtype=jnp.int32)[None, :]
    latents = jnp.broadcast_to(
        jnp.arange(latent_count, dtype=jnp.int32)[:, None], (latent_count, length)
    )
    return jnp.zeros((latent_count, length), jnp.int32).at[latents, token_ordering].set(places)


def tensor_total(partial_sum):
    return lax.psum(partial_sum.astype(jnp.bfloat16), "tensor").astype(jnp.float32)


def tensor_grad(partial_sum):
    return lax.psum(partial_sum.astype(jnp.bfloat16), "tensor").astype(jnp.float32)


def head_split(portion, latent_count, length):
    local_width = portion.shape[-1]
    shaped = portion.reshape(latent_count, length, 3, local_width // HEAD_DIM, HEAD_DIM)
    return (shaped[:, :, 0], shaped[:, :, 1], shaped[:, :, 2])


def attend_rows(queries, keys_all, values_all):
    scores = jnp.einsum(
        "nqhe,nkhe->nhqk", queries, keys_all, preferred_element_type=jnp.float32
    ) * HEAD_DIM ** (-0.5)
    highest = jnp.max(scores, axis=-1, keepdims=True)
    normer = highest + jnp.log(jnp.sum(jnp.exp(scores - highest), axis=-1, keepdims=True))
    weight_tree = jnp.exp(scores - normer).astype(jnp.bfloat16)
    attended = jnp.einsum(
        "nhqk,nkhe->nqhe", weight_tree, values_all, preferred_element_type=jnp.float32
    )
    return (attended, normer)


def attend_back(queries, keys_all, values_all, normer, d_attended):
    scaling = HEAD_DIM ** (-0.5)
    scores = (
        jnp.einsum("nqhe,nkhe->nhqk", queries, keys_all, preferred_element_type=jnp.float32)
        * scaling
    )
    softmax_rows = jnp.exp(scores - normer)
    d_probs = jnp.einsum(
        "nqhe,nkhe->nhqk", d_attended, values_all, preferred_element_type=jnp.float32
    )
    d_scores = (
        softmax_rows * (d_probs - jnp.sum(softmax_rows * d_probs, axis=-1, keepdims=True))
    ).astype(jnp.bfloat16)
    d_values = jnp.einsum(
        "nhqk,nqhe->nkhe",
        softmax_rows.astype(jnp.bfloat16),
        d_attended,
        preferred_element_type=jnp.float32,
    )
    d_queries = (
        jnp.einsum("nhqk,nkhe->nqhe", d_scores, keys_all, preferred_element_type=jnp.float32)
        * scaling
    )
    d_keys = (
        jnp.einsum("nhqk,nqhe->nkhe", d_scores, queries, preferred_element_type=jnp.float32)
        * scaling
    )
    return (d_queries, d_keys, d_values)


def attend_forward(merged, layout):
    local_width = merged.shape[2]
    attended_parts = []
    normers = []
    for portion, (latent_count, length) in zip(split_latents(merged, layout), layout):
        queries, keys_all, values_all = head_split(portion, latent_count, length)
        block_rows = min(length, 512)
        results = [
            attend_rows(queries[:, first_row : first_row + block_rows], keys_all, values_all)
            for first_row in range(0, length, block_rows)
        ]
        attended_parts.append(
            jnp.concatenate([result[0] for result in results], axis=1).reshape(
                latent_count * length, local_width
            )
        )
        normers.append(jnp.concatenate([result[1] for result in results], axis=2))
    return (jnp.concatenate(attended_parts, axis=0).astype(jnp.bfloat16), normers)


def attend_backward(merged, normers, d_attended, layout):
    local_width = merged.shape[2]
    d_parts = []
    for portion, d_portion, normer, (latent_count, length) in zip(
        split_latents(merged, layout), split_latents(d_attended, layout), normers, layout
    ):
        queries, keys_all, values_all = head_split(portion, latent_count, length)
        d_heads = d_portion.reshape(latent_count, length, local_width // HEAD_DIM, HEAD_DIM)
        block_rows = min(length, 512)
        d_keys = jnp.zeros(keys_all.shape, jnp.float32)
        d_values = jnp.zeros(values_all.shape, jnp.float32)
        d_query_parts = []
        for first_row in range(0, length, block_rows):
            rows_end = first_row + block_rows
            d_queries, d_keys_part, d_values_part = attend_back(
                queries[:, first_row:rows_end],
                keys_all,
                values_all,
                normer[:, :, first_row:rows_end],
                d_heads[:, first_row:rows_end],
            )
            d_query_parts.append(d_queries)
            d_keys = d_keys + d_keys_part
            d_values = d_values + d_values_part
        stacked = jnp.stack([jnp.concatenate(d_query_parts, axis=1), d_keys, d_values], axis=2)
        d_parts.append(stacked.reshape(latent_count * length, 3, local_width))
    return jnp.concatenate(d_parts, axis=0)


def block_forward(residual_stream, layout, modulation_vector, weight_tree):
    qkv_weight, qv_bias, proj_weight, proj_bias, up_weight, up_bias, down_weight, down_bias = (
        weight_tree
    )
    token_count, features = residual_stream.shape
    local_width = qkv_weight.shape[2]
    shift_attn, scale_attn, gate_attn, shift_mlp, scale_mlp, gate_mlp = [
        mod_part(modulation_vector, position, features) for position in range(6)
    ]
    normed_attn = modulated(layer_norm(residual_stream), layout, scale_attn, shift_attn).astype(
        jnp.bfloat16
    )
    bias_rows = jnp.stack([qv_bias[0], jnp.zeros_like(qv_bias[0]), qv_bias[1]]).astype(jnp.float32)
    merged = jnp.dot(
        normed_attn,
        qkv_weight.reshape(features, 3 * local_width),
        preferred_element_type=jnp.float32,
    )
    merged = (merged.reshape(token_count, 3, local_width) + bias_rows).astype(jnp.bfloat16)
    attended, normers = attend_forward(merged, layout)
    branch_attn = tensor_total(
        jnp.dot(attended, proj_weight, preferred_element_type=jnp.float32)
    ) + proj_bias.astype(jnp.float32)
    middle = residual_stream + scaled(branch_attn, layout, gate_attn)
    normed_mlp = modulated(layer_norm(middle), layout, scale_mlp, shift_mlp).astype(jnp.bfloat16)
    hidden = jnp.dot(normed_mlp, up_weight, preferred_element_type=jnp.float32) + up_bias.astype(
        jnp.float32
    )
    active = jax.nn.gelu(hidden, approximate=True).astype(jnp.bfloat16)
    branch_mlp = tensor_total(
        jnp.dot(active, down_weight, preferred_element_type=jnp.float32)
    ) + down_bias.astype(jnp.float32)
    output = middle + scaled(branch_mlp, layout, gate_mlp)
    saved = (
        residual_stream,
        normed_attn,
        merged,
        normers,
        attended,
        branch_attn,
        middle,
        normed_mlp,
        hidden,
        active,
        branch_mlp,
    )
    return (output, saved)


def block_backward(saved, d_output, layout, modulation_vector, weight_tree):
    qkv_weight, qv_bias, proj_weight, proj_bias, up_weight, up_bias, down_weight, down_bias = (
        weight_tree
    )
    (
        residual_stream,
        normed_attn,
        merged,
        normers,
        attended,
        branch_attn,
        middle,
        normed_mlp,
        hidden,
        active,
        branch_mlp,
    ) = saved
    token_count, features = residual_stream.shape
    shift_attn, scale_attn, gate_attn, shift_mlp, scale_mlp, gate_mlp = [
        mod_part(modulation_vector, position, features) for position in range(6)
    ]
    d_gate_mlp = latent_sums(d_output * branch_mlp, layout)
    d_branch_mlp = scaled(d_output, layout, gate_mlp).astype(jnp.bfloat16)
    grad_down = jnp.einsum("pi,po->io", active, d_branch_mlp, preferred_element_type=jnp.float32)
    grad_down_bias = jnp.sum(d_branch_mlp.astype(jnp.float32), axis=0)
    d_active = jnp.einsum(
        "po,io->pi", d_branch_mlp, down_weight, preferred_element_type=jnp.float32
    )
    unused, gelu_back = jax.vjp(partial(jax.nn.gelu, approximate=True), hidden)
    d_hidden = gelu_back(d_active)[0].astype(jnp.bfloat16)
    grad_up = jnp.einsum("pd,pi->di", normed_mlp, d_hidden, preferred_element_type=jnp.float32)
    grad_up_bias = jnp.sum(d_hidden.astype(jnp.float32), axis=0)
    d_normed_mlp = tensor_grad(
        jnp.einsum("pi,di->pd", d_hidden, up_weight, preferred_element_type=jnp.float32)
    )
    normed_values, norm_back = jax.vjp(layer_norm, middle)
    d_scale_mlp = latent_sums(d_normed_mlp * normed_values, layout)
    d_shift_mlp = latent_sums(d_normed_mlp, layout)
    d_middle = d_output + norm_back(scaled(d_normed_mlp, layout, plus_one(scale_mlp)))[0]
    d_gate_attn = latent_sums(d_middle * branch_attn, layout)
    d_branch_attn = scaled(d_middle, layout, gate_attn).astype(jnp.bfloat16)
    grad_proj = jnp.einsum("pi,po->io", attended, d_branch_attn, preferred_element_type=jnp.float32)
    grad_proj_bias = jnp.sum(d_branch_attn.astype(jnp.float32), axis=0)
    d_attended = jnp.einsum(
        "po,io->pi", d_branch_attn, proj_weight, preferred_element_type=jnp.float32
    ).astype(jnp.bfloat16)
    d_merged = attend_backward(merged, normers, d_attended, layout).astype(jnp.bfloat16)
    grad_qkv = jnp.einsum("pd,pte->dte", normed_attn, d_merged, preferred_element_type=jnp.float32)
    grad_qv_bias = jnp.stack(
        [
            jnp.sum(d_merged[:, 0].astype(jnp.float32), axis=0),
            jnp.sum(d_merged[:, 2].astype(jnp.float32), axis=0),
        ]
    )
    d_normed_attn = tensor_grad(
        jnp.einsum("pte,dte->pd", d_merged, qkv_weight, preferred_element_type=jnp.float32)
    )
    normed_values, norm_back = jax.vjp(layer_norm, residual_stream)
    d_scale_attn = latent_sums(d_normed_attn * normed_values, layout)
    d_shift_attn = latent_sums(d_normed_attn, layout)
    d_stream = d_middle + norm_back(scaled(d_normed_attn, layout, plus_one(scale_attn)))[0]
    d_modulation = [
        jnp.concatenate(list(members), axis=1)
        for members in zip(
            d_shift_attn, d_scale_attn, d_gate_attn, d_shift_mlp, d_scale_mlp, d_gate_mlp
        )
    ]
    grads = (
        grad_qkv,
        grad_qv_bias,
        grad_proj,
        grad_proj_bias,
        grad_up,
        grad_up_bias,
        grad_down,
        grad_down_bias,
    )
    return (d_stream, d_modulation, grads)


def on_device(
    tokens_long,
    tokens_short,
    cond_long,
    cond_short,
    perm_long,
    perm_short,
    ada_weight,
    ada_bias,
    qkv_weight,
    qv_bias,
    proj_weight,
    proj_bias,
    up_weight,
    up_bias,
    down_weight,
    down_bias,
    mask_token,
    cot_long,
    cot_short,
):
    long_count, long_length, features = tokens_long.shape
    short_count, short_length, unused = tokens_short.shape
    long_kept = long_length // 2
    short_kept = short_length // 2
    enc_layout = ((long_count, long_kept), (short_count, short_kept))
    dec_layout = ((long_count, long_length), (short_count, short_length))
    act_long = jax.nn.silu(cond_long.astype(jnp.float32)).astype(jnp.bfloat16)
    act_short = jax.nn.silu(cond_short.astype(jnp.float32)).astype(jnp.bfloat16)
    all_long, all_short = (
        lax.all_gather(act_long, "dp", axis=0, tiled=True),
        lax.all_gather(act_short, "dp", axis=0, tiled=True),
    )
    bias_float = ada_bias.astype(jnp.float32)[:, None, :]
    cols_long = (
        jnp.einsum("nd,ldm->lnm", all_long, ada_weight, preferred_element_type=jnp.float32)
        + bias_float
    )
    cols_short = (
        jnp.einsum("nd,ldm->lnm", all_short, ada_weight, preferred_element_type=jnp.float32)
        + bias_float
    )
    mod_long, mod_short = (
        lax.all_to_all(
            cols_long.astype(jnp.bfloat16), "dp", split_axis=1, concat_axis=2, tiled=True
        ).astype(cols_long.dtype),
        lax.all_to_all(
            cols_short.astype(jnp.bfloat16), "dp", split_axis=1, concat_axis=2, tiled=True
        ).astype(cols_short.dtype),
    )
    stacks = (
        qkv_weight,
        qv_bias,
        proj_weight,
        proj_bias,
        up_weight,
        up_bias,
        down_weight,
        down_bias,
    )
    enc_weights = tuple((stacked[0] for stacked in stacks))
    dec_weights = tuple((stacked[1] for stacked in stacks))
    enc_mod = [mod_long[0], mod_short[0]]
    dec_mod = [mod_long[1], mod_short[1]]
    gather_rows = jax.vmap(partial(jnp.take, axis=0))
    enc_in = join_latents(
        [
            gather_rows(tokens_long, perm_long[:, :long_kept]),
            gather_rows(tokens_short, perm_short[:, :short_kept]),
        ]
    ).astype(jnp.float32)
    encoder_result, enc_first = block_forward(enc_in, enc_layout, enc_mod, enc_weights)
    inv_long = inverse_order(perm_long)
    inv_short = inverse_order(perm_short)
    filler = mask_token.astype(jnp.float32)

    def decoder_input(encoded_part, inverse, visible_count):
        latent_count, length = inverse.shape
        pooled = jnp.concatenate(
            [
                encoded_part,
                jnp.broadcast_to(filler, (latent_count, length - visible_count, features)),
            ],
            axis=1,
        )
        return gather_rows(pooled, inverse) + sincos_table(math.isqrt(length), features)[None]

    enc_parts = split_latents(encoder_result, enc_layout)
    dec_in = join_latents(
        [
            decoder_input(enc_parts[0], inv_long, long_kept),
            decoder_input(enc_parts[1], inv_short, short_kept),
        ]
    )
    decoded, dec_saved = block_forward(dec_in, dec_layout, dec_mod, dec_weights)
    dec_parts = split_latents(decoded, dec_layout)
    d_decoded = join_latents([cot_long, cot_short]).astype(jnp.float32)
    d_dec_in, d_mod_dec, dec_grads = block_backward(
        dec_saved, d_decoded, dec_layout, dec_mod, dec_weights
    )
    d_pools = [
        gather_rows(portion, token_ordering)
        for portion, token_ordering in zip(
            split_latents(d_dec_in, dec_layout), (perm_long, perm_short)
        )
    ]
    grad_mask = jnp.sum(d_pools[0][:, long_kept:], axis=(0, 1)) + jnp.sum(
        d_pools[1][:, short_kept:], axis=(0, 1)
    )
    d_encoded = join_latents([d_pools[0][:, :long_kept], d_pools[1][:, :short_kept]])
    d_enc_in, d_mod_enc, enc_grads = block_backward(
        enc_first, d_encoded, enc_layout, enc_mod, enc_weights
    )
    d_tokens = []
    for portion, inverse, visible_count in zip(
        split_latents(d_enc_in, enc_layout), (inv_long, inv_short), (long_kept, short_kept)
    ):
        latent_count, length = inverse.shape
        pooled = jnp.concatenate(
            [portion, jnp.zeros((latent_count, length - visible_count, features), jnp.float32)],
            axis=1,
        )
        d_tokens.append(gather_rows(pooled, inverse).astype(jnp.bfloat16))
    dmod_long = jnp.stack([d_mod_enc[0], d_mod_dec[0]]).astype(jnp.bfloat16)
    dmod_short = jnp.stack([d_mod_enc[1], d_mod_dec[1]]).astype(jnp.bfloat16)
    grads = [jnp.stack([enc_part, dec_part]) for enc_part, dec_part in zip(enc_grads, dec_grads)]
    (
        grad_qkv,
        grad_qv_bias,
        grad_proj,
        grad_proj_bias,
        grad_up,
        grad_up_bias,
        grad_down,
        grad_down_bias,
    ) = grads
    mine_long, mine_short = (
        lax.all_to_all(dmod_long, "dp", split_axis=2, concat_axis=1, tiled=True),
        lax.all_to_all(dmod_short, "dp", split_axis=2, concat_axis=1, tiled=True),
    )
    col_weight = jnp.einsum(
        "nd,lnm->ldm", all_long, mine_long, preferred_element_type=jnp.float32
    ) + jnp.einsum("nd,lnm->ldm", all_short, mine_short, preferred_element_type=jnp.float32)
    row_bias = jnp.sum(mine_long.astype(jnp.float32), axis=1) + jnp.sum(
        mine_short.astype(jnp.float32), axis=1
    )
    part_long = jnp.einsum("lnm,ldm->nd", mine_long, ada_weight, preferred_element_type=jnp.float32)
    part_short = jnp.einsum(
        "lnm,ldm->nd", mine_short, ada_weight, preferred_element_type=jnp.float32
    )
    d_act_long, d_act_short = (
        lax.psum_scatter(
            part_long.astype(jnp.bfloat16), "dp", scatter_dimension=0, tiled=True
        ).astype(jnp.float32),
        lax.psum_scatter(
            part_short.astype(jnp.bfloat16), "dp", scatter_dimension=0, tiled=True
        ).astype(jnp.float32),
    )
    row_qkv, row_up = (
        lax.psum_scatter(
            grad_qkv.astype(jnp.bfloat16), "dp", scatter_dimension=1, tiled=True
        ).astype(jnp.float32),
        lax.psum_scatter(
            grad_up.astype(jnp.bfloat16), "dp", scatter_dimension=1, tiled=True
        ).astype(jnp.float32),
    )
    col_proj, col_down = (
        lax.psum_scatter(
            grad_proj.astype(jnp.bfloat16), "dp", scatter_dimension=2, tiled=True
        ).astype(jnp.float32),
        lax.psum_scatter(
            grad_down.astype(jnp.bfloat16), "dp", scatter_dimension=2, tiled=True
        ).astype(jnp.float32),
    )
    unused_long, silu_long_back = jax.vjp(jax.nn.silu, cond_long.astype(jnp.float32))
    unused_short, silu_short_back = jax.vjp(jax.nn.silu, cond_short.astype(jnp.float32))
    dcond_long = silu_long_back(d_act_long)[0].astype(jnp.bfloat16)
    dcond_short = silu_short_back(d_act_short)[0].astype(jnp.bfloat16)
    sum_qv, sum_proj, sum_up, sum_down, sum_mask = (
        lax.psum(grad_qv_bias.astype(jnp.bfloat16), "dp").astype(jnp.float32),
        lax.psum(grad_proj_bias.astype(jnp.bfloat16), "dp").astype(jnp.float32),
        lax.psum(grad_up_bias.astype(jnp.bfloat16), "dp").astype(jnp.float32),
        lax.psum(grad_down_bias.astype(jnp.bfloat16), "dp").astype(jnp.float32),
        lax.psum(grad_mask.astype(jnp.bfloat16), "dp").astype(jnp.float32),
    )
    return (
        dec_parts[0].astype(jnp.bfloat16),
        dec_parts[1].astype(jnp.bfloat16),
        d_tokens[0],
        d_tokens[1],
        dcond_long,
        dcond_short,
        col_weight,
        row_bias,
        row_qkv,
        sum_qv,
        col_proj,
        sum_proj,
        row_up,
        sum_up,
        col_down,
        sum_down,
        sum_mask,
    )


def solution(mesh):
    in_specs = (
        P("dp", None, None),
        P("dp", None, None),
        P("dp", None),
        P("dp", None),
        P("dp", None),
        P("dp", None),
        P(None, None, "dp"),
        P(None, "dp"),
        P(None, None, None, "tensor"),
        P(None, None, "tensor"),
        P(None, "tensor", None),
        P(),
        P(None, None, "tensor"),
        P(None, "tensor"),
        P(None, "tensor", None),
        P(),
        P(),
        P("dp", None, None),
        P("dp", None, None),
    )
    out_specs = (
        P("dp", None, None),
        P("dp", None, None),
        P("dp", None, None),
        P("dp", None, None),
        P("dp", None),
        P("dp", None),
        P(None, None, "dp"),
        P(None, "dp"),
        P(None, "dp", None, "tensor"),
        P(None, None, "tensor"),
        P(None, "tensor", "dp"),
        P(),
        P(None, "dp", "tensor"),
        P(None, "tensor"),
        P(None, "tensor", "dp"),
        P(),
        P(),
    )
    return jax.shard_map(
        on_device, mesh=mesh, in_specs=in_specs, out_specs=out_specs, check_vma=False
    )
```

profile of v0, /device:TPU:0, one launch (start us, length us, event | category | flops | bytes accessed | tf_op | source)
XLA Modules:
  0.0 1362.9 jit_solution(14781711525921647473)
XLA Ops:
  9.4 32.4 %all-gather.1 = bf16[8,1,1152]{2,1,0:T(2,128)(2,1)S(1)} all-gather(bf16[1,1,1152]{2,1,0:T(2,128)(2,1)S(1)} %get-tuple-element.165), channel_id=1, replica_groups=mesh['dp'=8,'tensor'=4] {'dp'}, dimensions={0}, use_global_device_ids=true | all-gather | bytes 20736 | tf_op jit(solution)/shard_map/all_gather | solution.py:359
  46.4 5.4 all-to-all-start.1
  56.6 31.1 %all-gather = bf16[8,1,1152]{2,1,0:T(2,128)(2,1)S(1)} all-gather(bf16[1,1,1152]{2,1,0:T(2,128)(2,1)S(1)} %get-tuple-element.163), channel_id=1, replica_groups=mesh['dp'=8,'tensor'=4] {'dp'}, dimensions={0}, use_global_device_ids=true | all-gather | bytes 20736 | tf_op jit(solution)/shard_map/all_gather | solution.py:358
  93.4 7.9 gather_fusion
  108.5 13.5 multiply_cosine_fusion
  124.5 4.8 scatter_custom_fusion.1
  130.7 6.8 concatenate.174
  137.5 5.3 all-to-all-start
  143.3 6.2 all-to-all-done
  162.2 38.1 %all-reduce.21.cloned.1.call-done = bf16[640,1152]{1,0:T(8,128)(2,1)} async-done(((bf16[640,1152]{1,0:T(8,128)(2,1)}), bf16[640,1152]{1,0:T(8,128)(2,1)}) %all-reduce.21.cloned.1.call-update) | async-done | bytes 1474576 | tf_op jit(solution)/shard_map/psum | solution.py:94
  215.5 40.3 %all-reduce.23.cloned.1.call-done = bf16[640,1152]{1,0:T(8,128)(2,1)} async-done(((bf16[640,1152]{1,0:T(8,128)(2,1)}), bf16[640,1152]{1,0:T(8,128)(2,1)}) %all-reduce.23.cloned.1.call-update) | async-done | bytes 1474576 | tf_op jit(solution)/shard_map/psum | solution.py:94
  262.8 21.4 %gather_fusion.2 = f32[1024,1152]{1,0:T(8,128)} fusion(f32[1,1024,1152]{2,1,0:T(8,128)} %pad_maximum_fusion.5, s32[1024]{0:T(1024)S(1)} %bitcast.482), kind=kCustom, calls=%fused_computation.clone | custom fusion | bytes 9445376 | tf_op jit(solution)/shard_map/vmap(jit(_take))/gather | solution.py:413
  327.9 58.8 %all-reduce.25.cloned.1.call-done = bf16[1280,1152]{1,0:T(8,128)(2,1)} async-done(((bf16[1280,1152]{1,0:T(8,128)(2,1)}), bf16[1280,1152]{1,0:T(8,128)(2,1)}) %all-reduce.25.cloned.1.call-update) | async-done | bytes 2949136 | tf_op jit(solution)/shard_map/psum | solution.py:94
  392.5 7.3 fusion.255
  410.4 6.4 fusion.2
  416.8 7.4 fusion.259
  425.8 5.7 convolution_convert_fusion.2
  431.5 8.3 fusion.1
  439.8 10.3 convolution_convert_fusion.3
  450.2 46.8 %all-reduce.27.cloned.1.call-done = bf16[1280,1152]{1,0:T(8,128)(2,1)} async-done(((bf16[1280,1152]{1,0:T(8,128)(2,1)}), bf16[1280,1152]{1,0:T(8,128)(2,1)}) %all-reduce.27.cloned.1.call-update) | async-done | bytes 2949136 | tf_op jit(solution)/shard_map/psum | solution.py:98
  508.2 7.1 fusion.106
  526.4 4.6 multiply_reduce_fusion
  531.0 4.5 multiply_reduce_fusion.1
  535.5 4.9 multiply_convert_fusion.1
  552.1 5.2 fusion
  558.0 5.9 convert_multiply_fusion.1
  564.0 58.9 %all-reduce.29.cloned.1.call-done = bf16[1280,1152]{1,0:T(8,128)(2,1)} async-done(((bf16[1280,1152]{1,0:T(8,128)(2,1)}), bf16[1280,1152]{1,0:T(8,128)(2,1)}) %all-reduce.29.cloned.1.call-update) | async-done | bytes 2949136 | tf_op jit(solution)/shard_map/psum | solution.py:98
  637.6 4.8 slice_bitcast_fusion
  648.3 21.5 %gather_fusion.4 = f32[1024,1152]{1,0:T(8,128)} fusion(f32[1,1024,1152]{2,1,0:T(8,128)} %slice_bitcast_fusion, s32[1024]{0:T(1024)S(1)} %bitcast.486), kind=kCustom, calls=%fused_computation.2.clone | custom fusion | bytes 9445376 | tf_op jit(solution)/shard_map/vmap(jit(_take))/gather | solution.py:429
  676.5 5.8 fusion.260
  697.5 30.9 %all-reduce.31.cloned.1.call-done = bf16[640,1152]{1,0:T(8,128)(2,1)} async-done(((bf16[640,1152]{1,0:T(8,128)(2,1)}), bf16[640,1152]{1,0:T(8,128)(2,1)}) %all-reduce.31.cloned.1.call-update) | async-done | bytes 1474576 | tf_op jit(solution)/shard_map/psum | solution.py:98
  775.7 16.8 %copy.108 = bf16[2,1152,1152]{1,0,2:T(2,128)(2,1)} copy(bf16[2,1152,1152]{2,1,0:T(8,128)(2,1)} %pad_maximum_fusion.4) | data formatting | bytes 10616832 | tf_op jit(solution)/shard_map/stack | solution.py:453
  811.9 17.5 %copy.106 = bf16[2,1152,3,288]{3,0,2,1:T(2,128)(2,1)} copy(bf16[2,1152,3,288]{1,3,2,0:T(8,128)(2,1)} %pad_maximum_fusion.6) | data formatting | bytes 7962624 | tf_op jit(solution)/shard_map/stack | solution.py:453
  835.6 5.8 all-reduce.35.cloned.1.call-done
  867.3 21.4 %gather_fusion.6 = bf16[1024,1152]{1,0:T(8,128)(2,1)} fusion(bf16[1,1024,1152]{2,1,0:T(8,128)(2,1)} %concatenate.198, s32[1024]{0:T(1024)S(1)} %bitcast.483), kind=kCustom, calls=%fused_computation.3.clone | custom fusion | bytes 4726784 | tf_op jit(solution)/shard_map/vmap(jit(_take))/gather | solution.py:450
  888.6 5.8 copy.104
  895.0 38.9 %reduce.201 = bf16[6912,2]{1,0:T(8,128)(2,1)S(1)} reduce(bf16[6912,1,2]{2,1,0:T(2,128)(2,1)} %bitcast.509, bf16[]{:T(256)} %broadcast.1016), dimensions={1}, to_apply=%bitcast.404.reduce_sub_computation | reduce | bytes 55298
  936.0 5.1 all-to-all-start.3
  945.4 5.0 slice_multiply_fusion.2
  959.8 5.8 copy.102
  965.7 38.5 %reduce.200 = bf16[6912,2]{1,0:T(8,128)(2,1)S(1)} reduce(bf16[6912,1,2]{2,1,0:T(2,128)(2,1)} %bitcast.510, bf16[]{:T(256)} %broadcast.1016), dimensions={1}, to_apply=%bitcast.402.reduce_sub_computation | reduce | bytes 55298
  1006.2 6.2 all-to-all-start.2
  1014.4 5.4 reshape.1567
  1019.8 6.9 copy.105
  1026.8 5.4 reshape.1565
  1032.3 6.9 copy.103
  1043.4 40.5 %all-reduce.9 = (bf16[8,1152]{1,0:T(8,128)(2,1)S(1)}, bf16[8,1152]{1,0:T(8,128)(2,1)S(1)}, bf16[2,2,288]{2,1,0:T(2,128)(2,1)S(1)}, bf16[2,1152]{1,0:T(2,128)(2,1...) all-reduce(bf16[8,1152]{1,0:T(8,128)(2,1)S(1)} %fusion.70, ...), channel_id=2, replica_groups=mesh['dp'=8,'tensor'=4] {'dp'}, use_global_device_ids=true, to_apply=%region_53.56.clone | all-reduce | flops 27648 | bytes 110592
  1098.1 250.7 %all-reduce.33.cloned.1.call-done = (bf16[2,1152,3,288]{3,0,2,1:T(2,128)(2,1)}, bf16[2,288,1152]{1,0,2:T(2,128)(2,1)}, bf16[2,1152,1152]{1,0,2:T(2,128)(2,1)}) async-done(((bf16[2,1152,3,288]{3,0,2,1:T(2,128)(2,1)}, bf16[2,288,1152]{1,0,2:T(2,128)(2,1)}, bf16[2,1152,1152]{1,0,2:T(2,128)(2,1)}), (bf16[2,1152,3,288]{3,0,2,1:T(2,128)(2,1)}, bf16[2,288,1152]{1,0,2:T(2,128)(2,1)}, ...) | async-done | bytes 10616848
  (914 shorter events, 343.6 us)
Async XLA Ops:
  7.2 86.2 %copy-start = (bf16[1,1024,1152]{2,1,0:T(8,128)(2,1)S(1)}, bf16[1,1024,1152]{2,1,0:T(8,128)(2,1)}, u32[]{:S(2)}) copy-start(bf16[1,1024,1152]{2,1,0:T(8,128)(2,1)} %param.23) | copy-start | bytes 7077892
  7.2 47.3 %copy-start.232 = (s32[2]{0:T(128)S(1)}, s32[2]{0:T(128)}, u32[]{:S(2)}) copy-start(s32[2]{0:T(128)} %constant.207) | copy-start | bytes 28
  7.2 47.4 %copy-start.231 = (s32[2]{0:T(128)S(1)}, s32[2]{0:T(128)}, u32[]{:S(2)}) copy-start(s32[2]{0:T(128)} %constant.204) | copy-start | bytes 28
  7.2 45.1 %copy-start.189 = (s32[1,1024]{1,0:T(1,128)S(1)}, s32[1,1024]{1,0:T(1,128)}, u32[]{:S(2)}) copy-start(s32[1,1024]{1,0:T(1,128)} %param.27) | copy-start | bytes 12292
  7.3 47.2 %copy-start.218 = (bf16[2,2,288]{2,1,0:T(2,128)(2,1)S(1)}, bf16[2,2,288]{2,1,0:T(2,128)(2,1)}, u32[]{:S(2)}) copy-start(bf16[2,2,288]{2,1,0:T(2,128)(2,1)} %param.32) | copy-start | bytes 6916
  7.3 47.4 %copy-start.199 = (bf16[1,1152]{1,0:T(2,128)(2,1)S(1)}, bf16[1,1152]{1,0:T(2,128)(2,1)}, u32[]{:S(2)}) copy-start(bf16[1,1152]{1,0:T(2,128)(2,1)} %param.25) | copy-start | bytes 6916
  7.3 48.0 %copy-start.192 = (bf16[2,1152]{1,0:T(2,128)(2,1)S(1)}, bf16[2,1152]{1,0:T(2,128)(2,1)}, u32[]{:S(2)}) copy-start(bf16[2,1152]{1,0:T(2,128)(2,1)} %param.34) | copy-start | bytes 13828
  7.3 48.0 %copy-start.193 = (bf16[2,1152]{1,0:T(2,128)(2,1)S(1)}, bf16[2,1152]{1,0:T(2,128)(2,1)}, u32[]{:S(2)}) copy-start(bf16[2,1152]{1,0:T(2,128)(2,1)} %param.36) | copy-start | bytes 13828
  7.3 48.7 %copy-start.194 = (bf16[2,1152]{1,0:T(2,128)(2,1)S(1)}, bf16[2,1152]{1,0:T(2,128)(2,1)}, u32[]{:S(2)}) copy-start(bf16[2,1152]{1,0:T(2,128)(2,1)} %param.38) | copy-start | bytes 13828
  45.7 45.9 %copy-start.37 = (bf16[1,256,1152]{2,1,0:T(8,128)(2,1)S(1)}, bf16[1,256,1152]{2,1,0:T(8,128)(2,1)}, u32[]{:S(2)}) copy-start(bf16[1,256,1152]{2,1,0:T(8,128)(2,1)} %param.24) | copy-start | bytes 1769476
  46.4 91.1 %all-to-all-start.1 = ((bf16[2,8,864]{2,0,1:T(2,128)(2,1)}), bf16[2,8,864]{2,0,1:T(2,128)(2,1)S(1)}, u32[]{:S(2)}, u32[]{:S(2)}) async-start(bf16[2,8,864]{2,0,1:T(2,128)(2,1)} %copy.89), calls=%async_computation.1 | async-start | bytes 57344 | tf_op jit(solution)/shard_map/all_to_all | solution.py:374
  55.3 145.0 %copy-start.148 = (f32[1152]{0:T(1024)}, f32[1152]{0:T(1024)S(1)}, u32[]{:S(2)}) copy-start(f32[1152]{0:T(1024)S(1)} %get-tuple-element.124) | copy-start | bytes 13828
  55.4 331.3 %copy-start.140 = (f32[1152]{0:T(1024)}, f32[1152]{0:T(1024)S(1)}, u32[]{:S(2)}) copy-start(f32[1152]{0:T(1024)S(1)} %get-tuple-element.123) | copy-start | bytes 13828
  56.6 199.2 %copy-start.150 = (f32[1152]{0:T(1024)}, f32[1152]{0:T(1024)S(1)}, u32[]{:S(2)}) copy-start(f32[1152]{0:T(1024)S(1)} %get-tuple-element.120) | copy-start | bytes 13828
  93.4 108.7 %copy-start.29 = (bf16[128,1152]{1,0:T(8,128)(2,1)}, bf16[128,1152]{1,0:T(8,128)(2,1)S(1)}, u32[]{:S(2)}) copy-start(bf16[128,1152]{1,0:T(8,128)(2,1)S(1)} %broadcast_select_fusion.1) | copy-start | bytes 884740
  102.8 99.3 %copy-start.13 = (bf16[512,1152]{1,0:T(8,128)(2,1)}, bf16[512,1152]{1,0:T(8,128)(2,1)S(1)}, u32[]{:S(2)}) copy-start(bf16[512,1152]{1,0:T(8,128)(2,1)S(1)} %broadcast_select_fusion) | copy-start | bytes 3538948
  137.5 12.0 all-to-all-start
  142.8 57.5 %all-reduce.21.cloned.1.call-start = ((), (), s32[]{:S(2)}) async-start(), calls=%async_computation.5 | async-start | bytes 2949120 | tf_op jit(solution)/shard_map/psum | solution.py:94
  143.2 58.7 %copy-start.152 = (f32[1152]{0:T(1024)}, f32[1152]{0:T(1024)S(1)}, u32[]{:S(2)}) copy-start(f32[1152]{0:T(1024)S(1)} %get-tuple-element.116) | copy-start | bytes 13828
  143.2 60.9 %copy-start.156 = (f32[1152]{0:T(1024)}, f32[1152]{0:T(1024)S(1)}, u32[]{:S(2)}) copy-start(f32[1152]{0:T(1024)S(1)} %get-tuple-element.115) | copy-start | bytes 13828
  143.2 114.1 %copy-start.133 = (f32[1152]{0:T(1024)}, f32[1152]{0:T(1024)S(1)}, u32[]{:S(2)}) copy-start(f32[1152]{0:T(1024)S(1)} %get-tuple-element.113) | copy-start | bytes 13828
  149.8 52.1 %copy-start.154 = (f32[1152]{0:T(1024)}, f32[1152]{0:T(1024)S(1)}, u32[]{:S(2)}) copy-start(f32[1152]{0:T(1024)S(1)} %get-tuple-element.110) | copy-start | bytes 13828
  149.9 54.3 %copy-start.158 = (f32[1152]{0:T(1024)}, f32[1152]{0:T(1024)S(1)}, u32[]{:S(2)}) copy-start(f32[1152]{0:T(1024)S(1)} %get-tuple-element.109) | copy-start | bytes 13828
  149.9 107.6 %copy-start.135 = (f32[1152]{0:T(1024)}, f32[1152]{0:T(1024)S(1)}, u32[]{:S(2)}) copy-start(f32[1152]{0:T(1024)S(1)} %get-tuple-element.107) | copy-start | bytes 13828
  161.5 94.3 %all-reduce.23.cloned.1.call-start = ((), (), s32[]{:S(2)}) async-start(), calls=%async_computation.6 | async-start | bytes 2949120 | tf_op jit(solution)/shard_map/psum | solution.py:94
  162.2 126.7 %copy-start.219 = (pred[1024]{0:T(1024)(128)(4,1)}, pred[1024]{0:T(1024)(128)(4,1)S(1)}, u32[]{:S(2)}) copy-start(pred[1024]{0:T(1024)(128)(4,1)S(1)} %and_reduce_fusion.1) | copy-start | bytes 3076
  162.2 122.2 %copy-start.16 = (s32[256,1]{0,1:T(1,128)}, s32[256,1]{0,1:T(1,128)S(1)}, u32[]{:S(2)}) copy-start(s32[256,1]{0,1:T(1,128)S(1)} %fusion.206) | copy-start | bytes 3076
  214.4 172.3 %all-reduce.25.cloned.1.call-start = ((), (), s32[]{:S(2)}) async-start(), calls=%async_computation.7 | async-start | bytes 5898240 | tf_op jit(solution)/shard_map/psum | solution.py:94
  215.0 47.8 %copy-start.5 = (s32[1024,1]{0,1:T(1,128)}, s32[1024,1]{0,1:T(1,128)S(1)}, u32[]{:S(2)}) copy-start(s32[1024,1]{0,1:T(1,128)S(1)} %fusion.192) | copy-start | bytes 12292
  215.3 81.5 %copy-start.160 = (f32[1152]{0:T(1024)}, f32[1152]{0:T(1024)S(1)}, u32[]{:S(2)}) copy-start(f32[1152]{0:T(1024)S(1)} %get-tuple-element.106) | copy-start | bytes 13828
  215.4 109.0 %copy-start.144 = (f32[1152]{0:T(1024)}, f32[1152]{0:T(1024)S(1)}, u32[]{:S(2)}) copy-start(f32[1152]{0:T(1024)S(1)} %get-tuple-element.101) | copy-start | bytes 13828
  215.4 81.5 %copy-start.162 = (f32[1152]{0:T(1024)}, f32[1152]{0:T(1024)S(1)}, u32[]{:S(2)}) copy-start(f32[1152]{0:T(1024)S(1)} %get-tuple-element.100) | copy-start | bytes 13828
  215.5 109.8 %copy-start.170 = (f32[1152]{0:T(1024)}, f32[1152]{0:T(1024)S(1)}, u32[]{:S(2)}) copy-start(f32[1152]{0:T(1024)S(1)} %get-tuple-element.95) | copy-start | bytes 13828
  321.2 175.7 %all-reduce.27.cloned.1.call-start = ((), (), s32[]{:S(2)}) async-start(), calls=%async_computation.8 | async-start | bytes 5898240 | tf_op jit(solution)/shard_map/psum | solution.py:98
  404.2 99.9 %copy-start.138 = (f32[1280]{0:T(1024)}, f32[1280]{0:T(1024)S(1)}, u32[]{:S(2)}) copy-start(f32[1280]{0:T(1024)S(1)} %fusion.164) | copy-start | bytes 15364
  431.5 191.4 %all-reduce.29.cloned.1.call-start = ((), (), s32[]{:S(2)}) async-start(), calls=%async_computation.9 | async-start | bytes 5898240 | tf_op jit(solution)/shard_map/psum | solution.py:98
  557.4 171.1 %all-reduce.31.cloned.1.call-start = ((), (), s32[]{:S(2)}) async-start(), calls=%async_computation.10 | async-start | bytes 2949120 | tf_op jit(solution)/shard_map/psum | solution.py:98
  564.0 61.1 %copy-start.161 = (f32[1152]{0:T(1024)S(1)}, f32[1152]{0:T(1024)}, u32[]{:S(2)}) copy-start(f32[1152]{0:T(1024)} %copy-done.160) | copy-start | bytes 13828
  564.0 61.9 %copy-start.163 = (f32[1152]{0:T(1024)S(1)}, f32[1152]{0:T(1024)}, u32[]{:S(2)}) copy-start(f32[1152]{0:T(1024)} %copy-done.162) | copy-start | bytes 13828
  686.9 154.5 %all-reduce.35.cloned.1.call-start = ((), (), s32[]{:S(2)}) async-start(), calls=%async_computation.13 | async-start | bytes 8847360 | tf_op jit(solution)/shard_map/psum | solution.py:94
  751.8 344.0 %reduce-scatter.2.cloned.1.call-start = ((), (), s32[]{:S(2)}) async-start(), calls=%async_computation.11 | async-start | bytes 5971968 | tf_op jit(solution)/shard_map/reduce_scatter | solution.py:490
  767.2 581.5 %all-reduce.33.cloned.1.call-start = ((), (), s32[]{:S(2)}) async-start(), calls=%async_computation.12 | async-start | bytes 24772608
  895.0 46.1 %copy-start.178 = (bf16[1,6912]{1,0:T(2,128)(2,1)S(1)}, bf16[1,6912]{1,0:T(2,128)(2,1)}, u32[]{:S(2)}) copy-start(bf16[1,6912]{1,0:T(2,128)(2,1)} %constant_dynamic-update-slice_fusion.5) | copy-start | bytes 41476
  895.0 46.1 %copy-start.213 = (bf16[1152]{0:T(1024)(128)(2,1)S(1)}, bf16[1152]{0:T(1024)(128)(2,1)}, u32[]{:S(2)}) copy-start(bf16[1152]{0:T(1024)(128)(2,1)} %slice_reduce_fusion.9) | copy-start | bytes 6916
  895.0 46.1 %copy-start.215 = (bf16[1152]{0:T(1024)(128)(2,1)S(1)}, bf16[1152]{0:T(1024)(128)(2,1)}, u32[]{:S(2)}) copy-start(bf16[1152]{0:T(1024)(128)(2,1)} %get-tuple-element.187) | copy-start | bytes 6916
  936.0 70.2 %all-to-all-start.3 = ((bf16[8,2,864]{2,1,0:T(2,128)(2,1)}), bf16[8,2,864]{2,1,0:T(2,128)(2,1)S(1)}, u32[]{:S(2)}, u32[]{:S(2)}) async-start(bf16[8,2,864]{2,1,0:T(2,128)(2,1)} %reshape.1566), calls=%async_computation.3 | async-start | bytes 57344 | tf_op jit(solution)/shard_map/all_to_all | solution.py:466
  1006.2 20.6 %all-to-all-start.2 = ((bf16[8,2,864]{2,1,0:T(2,128)(2,1)}), bf16[8,2,864]{2,1,0:T(2,128)(2,1)S(1)}, u32[]{:S(2)}, u32[]{:S(2)}) async-start(bf16[8,2,864]{2,1,0:T(2,128)(2,1)} %reshape.1564), calls=%async_computation.2 | async-start | bytes 57344 | tf_op jit(solution)/shard_map/all_to_all | solution.py:465
  1042.7 44.9 %copy-start.128 = (bf16[8,1,1152]{2,1,0:T(2,128)(2,1)S(1)}, bf16[8,1,1152]{2,1,0:T(2,128)(2,1)}, u32[]{:S(2)}) copy-start(bf16[8,1,1152]{2,1,0:T(2,128)(2,1)} %copy-done.127) | copy-start | bytes 55300
  (238 other events, 963.8 us)
Sparse Core Ops, SparseCore 0:
  161.7 38.5 all-reduce.20
  214.5 41.2 all-reduce.22
  321.4 65.2 all-reduce.24
  431.6 65.3 all-reduce.26
  557.5 65.3 all-reduce.28
  687.1 41.3 all-reduce.30
  751.9 89.4 all-reduce.34
  845.6 104.7 reduce-scatter.1
  955.9 392.8 all-reduce.32
where the time goes:
time: 1380 us; the launch traced here: 1360 us
  waiting for transfers between devices  537 us (39%)
  other arithmetic  289 us (21%)
  local copies, waits for them, and re-layouts  244 us (18%)
  matrix products  147 us (11%)
  blocking collectives  104 us (8%)
  starting transfers between devices  23.5 us (2%)
  between operations  18.3 us (1%)
    unnamed x10, waiting for transfers between devices  251 us
    psum x4, waiting for transfers between devices, tensor_total(): lax.psum(partial_sum.astype(jnp.bfloat16), 'tensor').astype(jnp.float32)  143 us
    psum x3, waiting for transfers between devices, tensor_grad(): lax.psum(partial_sum.astype(jnp.bfloat16), 'tensor').astype(jnp.float32)  137 us
    unnamed x18, other arithmetic  79.3 us
    unnamed x576, local copies, waits for them, and re-layouts  67.8 us
    another operation x9, local copies, waits for them, and re-layouts, on_device(): jnp.stack([enc_part, dec_part])  41.1 us
    unnamed x1, blocking collectives  40.5 us
    all_gather x1, blocking collectives, on_device(): lax.all_gather(act_short, 'dp', axis=0, tiled=True)  32.4 us
  transfers between devices with their start and end apart: 13, of which 9 were waited for; matrix products, arithmetic and copies ran while one was open for 28% of the time, Pallas kernels for 0%

commit v1 on v0

v1 whole, which is shorter than its diff:
```python
import math

import jax
import jax.numpy as jnp
from jax import lax
from jax.sharding import PartitionSpec as P

HEAD_DIM = 72
EPSILON = 1e-06
BF16 = jnp.bfloat16
F32 = jnp.float32


def dot(left, right, dims, out=F32):
    result = lax.dot_general(left, right, (dims, ((), ())), preferred_element_type=F32)
    return result.astype(out)


def rows_by(left, right, out=F32):
    return dot(left, right, ((1,), (0,)), out)


def rows_by_t(left, right, out=F32):
    return dot(left, right, ((1,), (1,)), out)


def rows_summed(left, right, out=F32):
    return dot(left, right, ((0,), (0,)), out)


def partners(size, bit):
    return [(index, index ^ bit) for index in range(size)]


def bits_of(size):
    bits = []
    while (1 << len(bits)) < size:
        bits.append(1 << len(bits))
    assert (1 << len(bits)) == size
    return bits


class Links:
    def __init__(self, dp_size, tensor_size):
        self.dp_size = dp_size
        self.tensor_size = tensor_size
        self.dp_bits = bits_of(dp_size)
        self.me = lax.axis_index("dp")
        self.core = lax.rem(lax.axis_index("tensor"), 2)

    def swap(self, value):
        return lax.ppermute(value, "tensor", partners(self.tensor_size, 1))

    def cross(self, value):
        return lax.ppermute(value, "tensor", partners(self.tensor_size, 2))

    def dp_move(self, value, bit):
        return lax.ppermute(value, "dp", partners(self.dp_size, bit))

    def my_bit(self, bit):
        return lax.rem(self.me // bit, 2)

    def gather_relative(self, value):
        held = value[None]
        for bit in self.dp_bits:
            held = jnp.concatenate([held, self.dp_move(held, bit)], axis=0)
        return held

    def exchange_relative(self, value):
        held = value
        for bit in self.dp_bits:
            shaped = held.reshape((self.dp_size // (2 * bit), 2, bit) + held.shape[1:])
            moved = self.dp_move(shaped[:, 1], bit)
            held = jnp.stack([shaped[:, 0], moved], axis=1).reshape(held.shape)
        return held

    def sum_relative(self, value):
        held = value
        for bit in reversed(self.dp_bits):
            moved = self.dp_move(held[bit:].astype(BF16), bit)
            held = held[:bit].astype(F32) + moved.astype(F32)
        return held[0]

    def reorder(self, value):
        held = value
        for bit in self.dp_bits:
            shaped = held.reshape((self.dp_size // (2 * bit), 2, bit) + held.shape[1:])
            flipped = jnp.where(self.my_bit(bit) == 1, shaped[:, ::-1], shaped)
            held = flipped.reshape(held.shape)
        return held

    def scatter_sum(self, value, axis):
        lead, rest = value.shape[:axis], value.shape[axis + 1 :]
        held = value.reshape(lead + (2,) * len(self.dp_bits) + rest)
        for done, bit in enumerate(self.dp_bits):
            place = axis + len(self.dp_bits) - 1 - done
            mine = self.my_bit(bit)
            away = lax.dynamic_index_in_dim(held, 1 - mine, place, keepdims=False)
            kept = lax.dynamic_index_in_dim(held, mine, place, keepdims=False)
            moved = self.dp_move(away, bit)
            held = (kept.astype(F32) + moved.astype(F32)).astype(BF16)
        return held

    def sum_all(self, value):
        held = value
        for bit in self.dp_bits:
            held = held + self.dp_move(held, bit)
        return held


def norm_of(values):
    center = values - jnp.mean(values, axis=-1, keepdims=True)
    spread = jnp.mean(center * center, axis=-1, keepdims=True)
    scale = lax.rsqrt(spread + EPSILON)
    return center * scale, scale


def norm_back(normed, scale, grad):
    return scale * (
        grad
        - jnp.mean(grad, axis=-1, keepdims=True)
        - normed * jnp.mean(grad * normed, axis=-1, keepdims=True)
    )


GELU_A = math.sqrt(2.0 / math.pi)
GELU_B = 0.044715


def gelu(hidden):
    return 0.5 * hidden * (1.0 + jnp.tanh(GELU_A * (hidden + GELU_B * hidden * hidden * hidden)))


def gelu_slope(hidden):
    squared = hidden * hidden
    bent = jnp.tanh(GELU_A * (hidden + GELU_B * hidden * squared))
    return 0.5 * (1.0 + bent) + 0.5 * hidden * (1.0 - bent * bent) * GELU_A * (
        1.0 + 3.0 * GELU_B * squared
    )


def heads_of(part):
    return part.reshape(part.shape[0], -1, HEAD_DIM)


def attend(queries, keys_all, values_all):
    scores = jnp.einsum(
        "qhe,khe->hqk", heads_of(queries), heads_of(keys_all), preferred_element_type=F32
    ) * HEAD_DIM ** (-0.5)
    highest = jnp.max(scores, axis=-1, keepdims=True)
    normer = highest + jnp.log(jnp.sum(jnp.exp(scores - highest), axis=-1, keepdims=True))
    probs = jnp.exp(scores - normer).astype(BF16)
    attended = jnp.einsum(
        "hqk,khe->qhe", probs, heads_of(values_all), preferred_element_type=F32
    )
    return attended.reshape(queries.shape).astype(BF16), normer


def attend_back(queries, keys_all, values_all, normer, d_attended):
    scaling = HEAD_DIM ** (-0.5)
    width = queries.shape[1]
    queries, keys_all, values_all, d_attended = (
        heads_of(part) for part in (queries, keys_all, values_all, d_attended)
    )
    scores = jnp.einsum("qhe,khe->hqk", queries, keys_all, preferred_element_type=F32) * scaling
    probs = jnp.exp(scores - normer)
    d_probs = jnp.einsum("qhe,khe->hqk", d_attended, values_all, preferred_element_type=F32)
    d_scores = (
        probs * (d_probs - jnp.sum(probs * d_probs, axis=-1, keepdims=True))
    ).astype(BF16)
    d_values = jnp.einsum("hqk,qhe->khe", probs.astype(BF16), d_attended, preferred_element_type=F32)
    d_queries = (
        jnp.einsum("hqk,khe->qhe", d_scores, keys_all, preferred_element_type=F32) * scaling
    )
    d_keys = jnp.einsum("hqk,qhe->khe", d_scores, queries, preferred_element_type=F32) * scaling
    return tuple(part.reshape(-1, width) for part in (d_queries, d_keys, d_values))


SHIFT_ATTN, SCALE_ATTN, GATE_ATTN, SHIFT_MLP, SCALE_MLP, GATE_MLP = range(6)


class Block:
    def __init__(self, links, weights, mods, owners):
        self.links = links
        (
            self.qkv_weight,
            self.qv_bias,
            self.proj_weight,
            self.proj_bias,
            self.up_weight,
            self.up_bias,
            self.down_weight,
            self.down_bias,
        ) = weights
        self.mods = mods
        self.owners = owners
        self.width = self.qkv_weight.shape[2]
        bias = self.qv_bias.astype(F32)
        self.qkv_bias = jnp.concatenate([bias[0], jnp.zeros_like(bias[0]), bias[1]])

    def mod(self, chunk, part):
        return self.mods[self.owners[chunk]][part][None]

    def joined(self, part_other, own_of):
        moved = self.links.swap(part_other)
        mine = (own_of() + moved.astype(F32)).astype(BF16)
        far = self.links.cross(mine)
        return mine.astype(F32) + far.astype(F32)

    def members(self, latent):
        return [chunk for chunk, owner in enumerate(self.owners) if owner == latent]

    def qkv_of(self, normed):
        features = normed.shape[1]
        flat = self.qkv_weight.reshape(features, 3 * self.width)
        return (rows_by(normed, flat) + self.qkv_bias[None]).astype(BF16)

    def parts(self, merged):
        return [merged[:, part * self.width : (part + 1) * self.width] for part in range(3)]

    def forward(self, streams):
        swap = self.links.swap
        chunks = range(len(streams))
        saved = [dict() for _ in chunks]
        for c in chunks:
            keep = saved[c]
            keep["x"] = streams[c]
            normed, _ = norm_of(streams[c])
            own = (normed * (1.0 + self.mod(c, SCALE_ATTN)) + self.mod(c, SHIFT_ATTN)).astype(BF16)
            keep["normed_attn"] = (own, swap(own))
            keep["qkv"] = tuple(self.qkv_of(half) for half in keep["normed_attn"])
        outputs = [None] * len(streams)
        for latent in sorted(set(self.owners)):
            halves = [half for c in self.members(latent) for half in saved[c]["qkv"]]
            keys_all = jnp.concatenate([self.parts(half)[1] for half in halves])
            values_all = jnp.concatenate([self.parts(half)[2] for half in halves])
            for c in self.members(latent):
                keep = saved[c]
                keep["keys"], keep["values"] = keys_all, values_all
                other, normer_other = attend(self.parts(keep["qkv"][1])[0], keys_all, values_all)
                part_other = rows_by(other, self.proj_weight, BF16)
                own, normer_own = attend(self.parts(keep["qkv"][0])[0], keys_all, values_all)
                keep["attended"] = (own, other)
                keep["normer"] = (normer_own, normer_other)
                branch = self.joined(
                    part_other, lambda own=own: rows_by(own, self.proj_weight)
                ) + self.proj_bias.astype(F32)
                keep["branch_attn"] = branch
                middle = keep["x"] + self.mod(c, GATE_ATTN) * branch
                keep["middle"] = middle
                normed, _ = norm_of(middle)
                normed = (normed * (1.0 + self.mod(c, SCALE_MLP)) + self.mod(c, SHIFT_MLP)).astype(
                    BF16
                )
                keep["normed_mlp"] = (normed, swap(normed))
                hidden, active = [], []
                for half in keep["normed_mlp"]:
                    raw = rows_by(half, self.up_weight) + self.up_bias.astype(F32)
                    hidden.append(raw)
                    active.append(gelu(raw).astype(BF16))
                keep["hidden"], keep["active"] = tuple(hidden), tuple(active)
                branch = self.joined(
                    rows_by(active[1], self.down_weight, BF16),
                    lambda half=active[0]: rows_by(half, self.down_weight),
                ) + self.down_bias.astype(F32)
                keep["branch_mlp"] = branch
                outputs[c] = middle + self.mod(c, GATE_MLP) * branch
        self.saved = saved
        return outputs

    def backward(self, d_outputs):
        swap = self.links.swap
        saved = self.saved
        chunks = range(len(d_outputs))
        sums = [[0.0] * 6 for _ in set(self.owners)]
        proj_sum, down_sum = 0.0, 0.0

        def add(chunk, part, value):
            sums[self.owners[chunk]][part] = sums[self.owners[chunk]][part] + value

        for c in chunks:
            keep = saved[c]
            d_out = d_outputs[c]
            add(c, GATE_MLP, jnp.sum(d_out * keep["branch_mlp"], axis=0))
            own = (self.mod(c, GATE_MLP) * d_out).astype(BF16)
            down_sum = down_sum + jnp.sum(own.astype(F32), axis=0)
            keep["d_branch_mlp"] = (own, swap(own))
            d_hidden = []
            for grad, hidden in zip(keep["d_branch_mlp"], keep["hidden"]):
                d_active = rows_by_t(grad, self.down_weight)
                d_hidden.append((d_active * gelu_slope(hidden)).astype(BF16))
            keep["d_hidden"] = tuple(d_hidden)
            d_normed = self.joined(
                rows_by_t(d_hidden[1], self.up_weight, BF16),
                lambda half=d_hidden[0]: rows_by_t(half, self.up_weight),
            )
            normed, scale = norm_of(keep["middle"])
            add(c, SCALE_MLP, jnp.sum(d_normed * normed, axis=0))
            add(c, SHIFT_MLP, jnp.sum(d_normed, axis=0))
            d_middle = d_out + norm_back(
                normed, scale, d_normed * (1.0 + self.mod(c, SCALE_MLP))
            )
            keep["d_middle"] = d_middle
            add(c, GATE_ATTN, jnp.sum(d_middle * keep["branch_attn"], axis=0))
            own = (self.mod(c, GATE_ATTN) * d_middle).astype(BF16)
            proj_sum = proj_sum + jnp.sum(own.astype(F32), axis=0)
            keep["d_branch_attn"] = (own, swap(own))
            keep["d_attended"] = tuple(
                rows_by_t(half, self.proj_weight, BF16) for half in keep["d_branch_attn"]
            )
        d_inputs = [None] * len(d_outputs)
        for latent in sorted(set(self.owners)):
            members = self.members(latent)
            d_queries = {}
            d_keys, d_values = 0.0, 0.0
            for c in members:
                keep = saved[c]
                for side in (1, 0):
                    query_grad, key_grad, value_grad = attend_back(
                        self.parts(keep["qkv"][side])[0],
                        keep["keys"],
                        keep["values"],
                        keep["normer"][side],
                        keep["d_attended"][side],
                    )
                    d_queries[c, side] = query_grad.astype(BF16)
                    d_keys = d_keys + key_grad
                    d_values = d_values + value_grad
            d_keys, d_values = d_keys.astype(BF16), d_values.astype(BF16)
            first = 0
            for c in members:
                keep = saved[c]
                halves = []
                for side in (0, 1):
                    count = d_queries[c, side].shape[0]
                    halves.append(
                        jnp.concatenate(
                            [
                                d_queries[c, side],
                                d_keys[first : first + count],
                                d_values[first : first + count],
                            ],
                            axis=1,
                        )
                    )
                    first += count
                keep["d_qkv"] = tuple(halves)
                features = self.qkv_weight.shape[0]
                flat = self.qkv_weight.reshape(features, 3 * self.width)
                d_normed = self.joined(
                    rows_by_t(halves[1], flat, BF16), lambda half=halves[0]: rows_by_t(half, flat)
                )
                normed, scale = norm_of(keep["x"])
                add(c, SCALE_ATTN, jnp.sum(d_normed * normed, axis=0))
                add(c, SHIFT_ATTN, jnp.sum(d_normed, axis=0))
                d_inputs[c] = keep["d_middle"] + norm_back(
                    normed, scale, d_normed * (1.0 + self.mod(c, SCALE_ATTN))
                )
        d_mods = jnp.stack([jnp.stack(rows) for rows in sums])
        return d_inputs, d_mods, proj_sum, down_sum

    def all_rows(self, name):
        return jnp.concatenate([half for keep in self.saved for half in keep[name]])

    def weight_grads(self):
        links = self.links
        blocks = links.dp_size

        def scattered(value):
            lead = value.shape[:-2]
            shaped = value.reshape(lead + (blocks, value.shape[-2] // blocks, value.shape[-1]))
            return links.scatter_sum(shaped, len(lead)).astype(F32)

        d_hidden = self.all_rows("d_hidden")
        down = scattered(rows_summed(self.all_rows("d_branch_mlp"), self.all_rows("active"), BF16))
        up = scattered(rows_summed(self.all_rows("normed_mlp"), d_hidden, BF16))
        proj = scattered(
            rows_summed(self.all_rows("d_branch_attn"), self.all_rows("attended"), BF16)
        )
        normed = self.all_rows("normed_attn")
        d_qkv = self.all_rows("d_qkv")
        qkv = scattered(
            jnp.stack([rows_summed(normed, part, BF16) for part in self.parts(d_qkv)])
        )
        qkv_sums = jnp.sum(d_qkv.astype(F32), axis=0)
        return {
            "qkv": jnp.transpose(qkv, (1, 0, 2)),
            "proj": proj.T,
            "up": up,
            "down": down.T,
            "qv_bias": jnp.stack([qkv_sums[: self.width], qkv_sums[2 * self.width :]]),
            "up_bias": jnp.sum(d_hidden.astype(F32), axis=0),
        }


def pick_matrix(places, length):
    return (places[:, None] == jnp.arange(length, dtype=jnp.int32)[None, :]).astype(BF16)


def table_rows(places, length, features):
    side = math.isqrt(length)
    quarter = features // 4
    frequency = 1.0 / 10000.0 ** (jnp.arange(quarter, dtype=F32) / quarter)
    angle = jnp.arange(side, dtype=jnp.int32).astype(F32)[:, None] * frequency[None, :]
    small = jnp.concatenate([jnp.sin(angle), jnp.cos(angle)], axis=1)
    steps = jnp.arange(side, dtype=jnp.int32)[None, :]
    row_pick = (places[:, None] // side == steps).astype(F32)
    col_pick = (places[:, None] % side == steps).astype(F32)
    return jnp.concatenate(
        [
            jnp.dot(row_pick, small, precision=lax.Precision.HIGHEST),
            jnp.dot(col_pick, small, precision=lax.Precision.HIGHEST),
        ],
        axis=1,
    )


def on_device(dp_size, tensor_size, *arguments):
    (
        tokens_long,
        tokens_short,
        cond_long,
        cond_short,
        perm_long,
        perm_short,
        ada_weight,
        ada_bias,
        qkv_weight,
        qv_bias,
        proj_weight,
        proj_bias,
        up_weight,
        up_bias,
        down_weight,
        down_bias,
        mask_token,
        cot_long,
        cot_short,
    ) = arguments
    assert tokens_long.shape[0] == 1 and tokens_short.shape[0] == 1
    links = Links(dp_size, tensor_size)
    features = tokens_long.shape[2]
    tokens = (tokens_long[0], tokens_short[0])
    cots = (cot_long[0], cot_short[0])
    perms = (perm_long[0], perm_short[0])
    lengths = tuple(rows.shape[0] for rows in tokens)
    kept = tuple(length // 2 for length in lengths)

    cond = jnp.concatenate([cond_long, cond_short]).astype(F32)
    acts = links.gather_relative(jax.nn.silu(cond).astype(BF16))
    flat_acts = acts.reshape(-1, features)
    columns = jnp.einsum("nd,ldm->nlm", flat_acts, ada_weight, preferred_element_type=F32)
    columns = (columns + ada_bias.astype(F32)[None]).astype(BF16)
    columns = columns.reshape((dp_size, 2) + columns.shape[1:])
    mods = links.reorder(links.exchange_relative(columns)).astype(F32)
    mods = jnp.transpose(mods, (2, 1, 0, 3)).reshape(2, 2, 6, features)

    def own_places(latent, first):
        half = kept[latent] // 2
        mine = lax.dynamic_slice_in_dim(perms[latent], first + links.core * half, half)
        other = lax.dynamic_slice_in_dim(perms[latent], first + (1 - links.core) * half, half)
        return mine, other

    kept_places = [own_places(latent, 0) for latent in (0, 1)]
    masked_places = [own_places(latent, kept[latent]) for latent in (0, 1)]

    def weights_of(block):
        return tuple(
            stacked[block]
            for stacked in (
                qkv_weight,
                qv_bias,
                proj_weight,
                proj_bias,
                up_weight,
                up_bias,
                down_weight,
                down_bias,
            )
        )

    encoder = Block(links, weights_of(0), mods[0], (0, 1))
    decoder = Block(links, weights_of(1), mods[1], (0, 0, 1))
    enc_in = [
        rows_by(pick_matrix(kept_places[latent][0], lengths[latent]), tokens[latent])
        for latent in (0, 1)
    ]
    encoded = encoder.forward(enc_in)
    filler = mask_token.astype(F32)[None]
    dec_places = [
        kept_places[0],
        masked_places[0],
        tuple(jnp.concatenate(pair) for pair in zip(kept_places[1], masked_places[1])),
    ]
    chunk_latents = (0, 0, 1)
    table = [
        table_rows(places[0], lengths[latent], features)
        for places, latent in zip(dec_places, chunk_latents)
    ]
    half_short = kept[1] // 2
    dec_in = [
        encoded[0] + table[0],
        filler + table[1],
        jnp.concatenate([encoded[1], jnp.broadcast_to(filler, (half_short, features))]) + table[2],
    ]
    decoded = decoder.forward(dec_in)

    def placed(rows, places, length):
        pick = pick_matrix(jnp.concatenate(places), length)
        return dot(pick, jnp.concatenate(rows), ((0,), (0,)), BF16)

    swapped = []
    for rows in decoded:
        own = rows.astype(BF16)
        swapped.append((own, links.swap(own)))
    results = [
        placed(
            swapped[0] + swapped[1], dec_places[0] + dec_places[1], lengths[0]
        ),
        placed(swapped[2], dec_places[2], lengths[1]),
    ]

    d_decoded = [
        rows_by(pick_matrix(places[0], lengths[latent]), cots[latent])
        for places, latent in zip(dec_places, chunk_latents)
    ]
    d_dec_in, d_mods_dec, proj_dec, down_dec = decoder.backward(d_decoded)
    mask_sum = jnp.sum(d_dec_in[1], axis=0) + jnp.sum(d_dec_in[2][half_short:], axis=0)
    d_encoded = [d_dec_in[0], d_dec_in[2][:half_short]]
    d_enc_in, d_mods_enc, proj_enc, down_enc = encoder.backward(d_encoded)
    d_tokens = []
    for latent in (0, 1):
        own = d_enc_in[latent].astype(BF16)
        d_tokens.append(placed((own, links.swap(own)), kept_places[latent], lengths[latent]))

    grads_dec = decoder.weight_grads()
    grads_enc = encoder.weight_grads()

    own_sums = jnp.concatenate(
        [
            d_mods_enc.reshape(12, features),
            d_mods_dec.reshape(12, features),
            jnp.stack([proj_enc, proj_dec, down_enc, down_dec, mask_sum]),
        ]
    )
    own_sums = own_sums + links.swap(own_sums)
    d_mods = own_sums[:24].reshape(2, 2, dp_size, -1).astype(BF16)
    mine = links.exchange_relative(links.reorder(jnp.transpose(d_mods, (2, 1, 0, 3))))
    flat_mine = mine.reshape((-1,) + mine.shape[2:])
    grad_ada = jnp.einsum("nd,nlm->ldm", flat_acts, flat_mine, preferred_element_type=F32)
    grad_ada_bias = jnp.sum(flat_mine.astype(F32), axis=0)
    d_acts = jnp.einsum("nlm,ldm->nd", flat_mine, ada_weight, preferred_element_type=F32)
    d_act = links.sum_relative(d_acts.reshape(dp_size, 2, features))
    gate = jax.nn.sigmoid(cond)
    d_cond = (d_act * gate * (1.0 + cond * (1.0 - gate))).astype(BF16)

    small = jnp.concatenate(
        [
            own_sums[24:].reshape(-1),
            grads_enc["up_bias"],
            grads_dec["up_bias"],
            grads_enc["qv_bias"].reshape(-1),
            grads_dec["qv_bias"].reshape(-1),
        ]
    )
    small = links.sum_all(small)
    wide = up_bias.shape[1]
    local = qv_bias.shape[2]
    proj_out = small[: 2 * features].reshape(2, features)
    down_out = small[2 * features : 4 * features].reshape(2, features)
    mask_out = small[4 * features : 5 * features]
    first = 5 * features
    up_out = small[first : first + 2 * wide].reshape(2, wide)
    first += 2 * wide
    qv_out = small[first : first + 4 * local].reshape(2, 2, local)

    def both(name):
        return jnp.stack([grads_enc[name], grads_dec[name]])

    return (
        results[0][None],
        results[1][None],
        d_tokens[0][None],
        d_tokens[1][None],
        d_cond[:1],
        d_cond[1:],
        grad_ada,
        grad_ada_bias,
        both("qkv").reshape(2, -1, 3, local),
        qv_out,
        both("proj"),
        proj_out,
        both("up"),
        up_out,
        both("down"),
        down_out,
        mask_out,
    )


def solution(mesh):
    in_specs = (
        P("dp", None, None),
        P("dp", None, None),
        P("dp", None),
        P("dp", None),
        P("dp", None),
        P("dp", None),
        P(None, None, "dp"),
        P(None, "dp"),
        P(None, None, None, "tensor"),
        P(None, None, "tensor"),
        P(None, "tensor", None),
        P(),
        P(None, None, "tensor"),
        P(None, "tensor"),
        P(None, "tensor", None),
        P(),
        P(),
        P("dp", None, None),
        P("dp", None, None),
    )
    out_specs = (
        P("dp", None, None),
        P("dp", None, None),
        P("dp", None, None),
        P("dp", None, None),
        P("dp", None),
        P("dp", None),
        P(None, None, "dp"),
        P(None, "dp"),
        P(None, "dp", None, "tensor"),
        P(None, None, "tensor"),
        P(None, "tensor", "dp"),
        P(),
        P(None, "dp", "tensor"),
        P(None, "tensor"),
        P(None, "tensor", "dp"),
        P(),
        P(),
    )

    def step(*arguments):
        return on_device(mesh.shape["dp"], mesh.shape["tensor"], *arguments)

    return jax.shard_map(
        step, mesh=mesh, in_specs=in_specs, out_specs=out_specs, check_vma=False
    )
```

time: 1380 us -> 790 us (0.57)
  waiting for transfers between devices: 537 us -> 218 us
  other arithmetic: 289 us -> 109 us
  local copies, waits for them, and re-layouts: 244 us -> 98.4 us
  matrix products: 147 us -> 261 us
  blocking collectives: 104 us -> 0 us
  starting transfers between devices: 23.5 us -> 89 us
    psum x7 -> x0, waiting for transfers between devices: 280 us -> none  [the longest x4 143 us: tensor_total(): lax.psum(partial_sum.astype(jnp.bfloat16), 'tensor').astype(jnp.float32)]
    unnamed x10 -> x0, waiting for transfers between devices: 251 us -> none
    ppermute x0 -> x105, waiting for transfers between devices: none -> 218 us  [the longest x39 127 us: dp_move(): return lax.ppermute(value, 'dp', partners(self.dp_size, bit))]
    dot_general x60 -> x170, matrix products: 147 us -> 261 us  [the longest x101 205 us: dot(): lax.dot_general(left, right, (dims, ((), ())), preferred_element_type=F32)]
    ppermute x0 -> x105, starting transfers between devices: none -> 89 us  [the longest x39 56.9 us: dp_move(): return lax.ppermute(value, 'dp', partners(self.dp_size, bit))]
    gather x12 -> x0, local copies, waits for them, and re-layouts: 83.3 us -> none  [the longest x2 24.9 us: on_device(): d_tokens.append(gather_rows(pooled, inverse).astype(jnp.bfloat16))]
    unnamed x18 -> x24, other arithmetic: 79.3 us -> 8.81 us
    all_gather x2 -> x0, blocking collectives: 63.5 us -> none  [the longest x1 32.4 us: on_device(): lax.all_gather(act_short, 'dp', axis=0, tiled=True)]
  transfers between devices with their start and end apart: 13 -> 105, of which waited for: 9 -> 36; matrix products, arithmetic and copies ran while one was open for 28% -> 55% of each run, Pallas kernels for 0% -> 0%
where the time goes in v1:
time: 790 us; the launch traced here: 782 us
  matrix products  261 us (33%)
  waiting for transfers between devices  218 us (28%)
  other arithmetic  109 us (14%)
  local copies, waits for them, and re-layouts  98.4 us (12%)
  starting transfers between devices  89 us (11%)
    dot_general x101, matrix products, dot(): lax.dot_general(left, right, (dims, ((), ())), preferred_element_type=F32)  205 us
    ppermute x39, waiting for transfers between devices, dp_move(): return lax.ppermute(value, 'dp', partners(self.dp_size, bit))  127 us
    ppermute x20, waiting for transfers between devices, cross(): return lax.ppermute(value, 'tensor', partners(self.tensor_size, 2))  87.6 us
    ppermute x39, starting transfers between devices, dp_move(): return lax.ppermute(value, 'dp', partners(self.dp_size, bit))  56.9 us
    unnamed x712, local copies, waits for them, and re-layouts  26 us
    ppermute x20, starting transfers between devices, cross(): return lax.ppermute(value, 'tensor', partners(self.tensor_size, 2))  23.4 us
    convert_element_type x8, local copies, waits for them, and re-layouts, dot(): return result.astype(out)  17.7 us
  transfers between devices with their start and end apart: 105, of which 36 were waited for; matrix products, arithmetic and copies ran while one was open for 55% of the time, Pallas kernels for 0%

profile of v1, /device:TPU:0, one launch (start us, length us, event | category | flops | bytes accessed | tf_op | source)
XLA Modules:
  0.0 781.9 jit_solution(16323420789454904738)
XLA Ops:
  35.7 3.3 fusion.307
  40.0 3.1 collective-permute-done.3
  95.2 3.2 fusion.479
  110.8 3.2 fusion.484
  119.5 3.9 collective-permute-done.31
  123.5 11.8 %collective-permute-done.8 = bf16[256,1152]{1,0:T(8,128)(2,1)S(1)} collective-permute-done((bf16[256,1152]{1,0:T(8,128)(2,1)S(1)}, bf16[256,1152]{1,0:T(8,128)(2,1)S(1)}, u32[]{:S(2)}, u32[]{:S(2)}) %collective-permute-start.8) | collective-permute-done | bytes 589856 | tf_op jit(solution)/shard_map/ppermute | solution.py:55
  150.5 12.4 %collective-permute-done.11 = bf16[256,1152]{1,0:T(8,128)(2,1)S(1)} collective-permute-done((bf16[256,1152]{1,0:T(8,128)(2,1)S(1)}, bf16[256,1152]{1,0:T(8,128)(2,1)S(1)}, u32[]{:S(2)}, u32[]{:S(2)}) %collective-permute-start.11) | collective-permute-done | bytes 589856 | tf_op jit(solution)/shard_map/ppermute | solution.py:55
  194.9 5.1 collective-permute-done.34
  200.5 12.1 %collective-permute-done.21 = bf16[256,1152]{1,0:T(8,128)(2,1)S(1)} collective-permute-done((bf16[256,1152]{1,0:T(8,128)(2,1)S(1)}, bf16[256,1152]{1,0:T(8,128)(2,1)S(1)}, u32[]{:S(2)}, u32[]{:S(2)}) %collective-permute-start.21) | collective-permute-done | bytes 589856 | tf_op jit(solution)/shard_map/ppermute | solution.py:55
  212.7 12.1 %collective-permute-done.15 = bf16[256,1152]{1,0:T(8,128)(2,1)S(1)} collective-permute-done((bf16[256,1152]{1,0:T(8,128)(2,1)S(1)}, bf16[256,1152]{1,0:T(8,128)(2,1)S(1)}, u32[]{:S(2)}, u32[]{:S(2)}) %collective-permute-start.15) | collective-permute-done | bytes 589856 | tf_op jit(solution)/shard_map/ppermute | solution.py:55
  230.2 3.8 constant_dynamic-update-slice_fusion.13
  243.5 3.4 constant_dynamic-update-slice_fusion.12
  250.0 3.8 constant_dynamic-update-slice_fusion.11
  265.9 3.3 constant_dynamic-update-slice_fusion.10
  271.9 3.9 fusion.91
  277.5 3.4 constant_dynamic-update-slice_fusion.9
  283.4 4.4 fusion.141
  288.3 6.8 convolution_convert_fusion
  296.5 3.6 constant_dynamic-update-slice_fusion.8
  301.9 5.9 convolution_convert_fusion.1
  325.8 4.9 collective-permute-done.58
  337.6 5.7 collective-permute-done.24
  343.3 12.2 %collective-permute-done.45 = bf16[256,1152]{1,0:T(8,128)(2,1)S(1)} collective-permute-done((bf16[256,1152]{1,0:T(8,128)(2,1)S(1)}, bf16[256,1152]{1,0:T(8,128)(2,1)S(1)}, u32[]{:S(2)}, u32[]{:S(2)}) %collective-permute-start.45) | collective-permute-done | bytes 589856 | tf_op jit(solution)/shard_map/ppermute | solution.py:55
  355.5 3.3 multiply_reduce_fusion.13
  370.0 24.6 %collective-permute-done.96 = bf16[2,2,144,1152]{3,2,0,1:T(8,128)(2,1)} collective-permute-done((bf16[2,2,144,1152]{3,2,0,1:T(8,128)(2,1)S(1)}, bf16[2,2,144,1152]{3,2,0,1:T(8,128)(2,1)}, u32[]{:S(2)}, u32[]{:S(2)}) %collective-permute-start.96) | collective-permute-done | bytes 1327136 | tf_op jit(solution)/shard_map/ppermute | solution.py:58
  412.0 6.0 fusion.2
  440.9 3.8 collective-permute-done.104
  445.5 6.3 collective-permute-done.98
  464.6 3.8 convolution_convert_fusion.9
  506.1 4.4 collective-permute-done.92
  514.0 3.4 fusion.175
  519.3 3.5 add_convert_fusion.30
  527.6 3.1 convert_reduce_fusion.6
  530.8 4.0 fusion.112
  560.8 3.3 fusion.115
  567.7 3.8 convolution_convert_fusion.2
  579.9 3.2 collective-permute-start.83
  585.4 12.0 %collective-permute-done.83 = bf16[3,144,288]{2,1,0:T(8,128)(2,1)S(1)} collective-permute-done((bf16[3,144,288]{2,1,0:T(8,128)(2,1)S(1)}, bf16[3,144,288]{2,1,0:T(8,128)(2,1)S(1)}, u32[]{:S(2)}, u32[]{:S(2)}) %collective-permute-start.83) | collective-permute-done | bytes 248864 | tf_op jit(solution)/shard_map/ppermute | solution.py:58
  610.0 24.3 %collective-permute-done.93 = bf16[2,2,144,1152]{3,2,0,1:T(8,128)(2,1)S(1)} collective-permute-done((bf16[2,2,144,1152]{3,2,0,1:T(8,128)(2,1)S(1)}, bf16[2,2,144,1152]{3,2,0,1:T(8,128)(2,1)S(1)}, u32[]{:S(2)}, u32[]{:S(2)}) %collective-permute-start.93) | collective-permute-done | bytes 1327136 | tf_op jit(solution)/shard_map/ppermute | solution.py:58
  655.0 3.1 convolution_convert_fusion.6
  664.9 3.5 convolution_convert_fusion.7
  684.0 9.8 %collective-permute-done.88 = bf16[2,144,288]{2,1,0:T(8,128)(2,1)S(1)} collective-permute-done((bf16[2,144,288]{2,1,0:T(8,128)(2,1)S(1)}, bf16[2,144,288]{2,1,0:T(8,128)(2,1)S(1)}, u32[]{:S(2)}, u32[]{:S(2)}) %collective-permute-start.88) | collective-permute-done | bytes 165920 | tf_op jit(solution)/shard_map/ppermute | solution.py:58
  695.5 9.9 %collective-permute-done.101 = bf16[144,1152]{1,0:T(8,128)(2,1)S(1)} collective-permute-done((bf16[144,1152]{1,0:T(8,128)(2,1)S(1)}, bf16[144,1152]{1,0:T(8,128)(2,1)S(1)}, u32[]{:S(2)}, u32[]{:S(2)}) %collective-permute-start.101) | collective-permute-done | bytes 331808 | tf_op jit(solution)/shard_map/ppermute | solution.py:58
  708.2 4.4 collective-permute-done.95
  714.9 7.0 collective-permute-done.54
  745.8 4.5 convolution_bitcast_fusion
  765.1 10.9 %collective-permute-done.80 = bf16[3,144,288]{2,1,0:T(8,128)(2,1)S(1)} collective-permute-done((bf16[3,144,288]{2,1,0:T(8,128)(2,1)S(1)}, bf16[3,144,288]{2,1,0:T(8,128)(2,1)S(1)}, u32[]{:S(2)}, u32[]{:S(2)}) %collective-permute-start.80) | collective-permute-done | bytes 248864 | tf_op jit(solution)/shard_map/ppermute | solution.py:58
  777.3 4.4 fusion.3
  (1454 shorter events, 469.5 us)
Async XLA Ops:
  1.6 25.5 %collective-permute-start = (bf16[1,2,1152]{2,1,0:T(2,128)(2,1)S(1)}, bf16[1,2,1152]{2,1,0:T(2,128)(2,1)S(1)}, u32[]{:S(2)}, u32[]{:S(2)}) collective-permute-start(bf16[1,2,1152]{2,1,0:T(2,128)(2,1)S(1)} %fusion.567), channel_id=1, source_target_pairs={{0,4},{4,0},{8,12},{12,8},{16,20},{20,16},{24,28},{28,24},{1,5},{5... | collective-permute-start | bytes 13832 | tf_op jit(solution)/shard_map/ppermute | solution.py:58
  58.6 39.9 %collective-permute-start.6 = (bf16[256,1152]{1,0:T(8,128)(2,1)}, bf16[256,1152]{1,0:T(8,128)(2,1)}, u32[]{:S(2)}, u32[]{:S(2)}) collective-permute-start(bf16[256,1152]{1,0:T(8,128)(2,1)} %add_convert_fusion.20), channel_id=1, source_target_pairs={{0,1},{1,0},{2,3},{3,2},{4,5},{5,4},{6,7},{7,6},{8,9},{9,8},{10,11... | collective-permute-start | bytes 1769480 | tf_op jit(solution)/shard_map/ppermute | solution.py:52
  109.9 33.2 %collective-permute-start.43 = (bf16[256,1152]{1,0:T(8,128)(2,1)S(1)}, bf16[256,1152]{1,0:T(8,128)(2,1)S(1)}, u32[]{:S(2)}, u32[]{:S(2)}) collective-permute-start(bf16[256,1152]{1,0:T(8,128)(2,1)S(1)} %get-tuple-element.107), channel_id=1, source_target_pairs={{0,1},{1,0},{2,3},{3,2},{4,5},{5,4},{6,7},{7,6},{8,9},{9,8},{10,11... | collective-permute-start | bytes 1769480 | tf_op jit(solution)/shard_map/ppermute | solution.py:52
  192.2 20.5 %collective-permute-start.21 = (bf16[256,1152]{1,0:T(8,128)(2,1)S(1)}, bf16[256,1152]{1,0:T(8,128)(2,1)S(1)}, u32[]{:S(2)}, u32[]{:S(2)}) collective-permute-start(bf16[256,1152]{1,0:T(8,128)(2,1)S(1)} %add_convert_fusion.10), channel_id=1, source_target_pairs={{0,2},{1,3},{2,0},{3,1},{4,6},{5,7},{6,4},{7,5},{8,10},{9,11},{10,... | collective-permute-start | bytes 1769480 | tf_op jit(solution)/shard_map/ppermute | solution.py:55
  193.9 30.8 %collective-permute-start.15 = (bf16[256,1152]{1,0:T(8,128)(2,1)S(1)}, bf16[256,1152]{1,0:T(8,128)(2,1)S(1)}, u32[]{:S(2)}, u32[]{:S(2)}) collective-permute-start(bf16[256,1152]{1,0:T(8,128)(2,1)S(1)} %add_convert_fusion.14), channel_id=1, source_target_pairs={{0,2},{1,3},{2,0},{3,1},{4,6},{5,7},{6,4},{7,5},{8,10},{9,11},{10,... | collective-permute-start | bytes 1769480 | tf_op jit(solution)/shard_map/ppermute | solution.py:55
  249.7 26.0 %collective-permute-start.40 = (bf16[256,1152]{1,0:T(8,128)(2,1)S(1)}, bf16[256,1152]{1,0:T(8,128)(2,1)S(1)}, u32[]{:S(2)}, u32[]{:S(2)}) collective-permute-start(bf16[256,1152]{1,0:T(8,128)(2,1)S(1)} %fusion.88), channel_id=1, source_target_pairs={{0,1},{1,0},{2,3},{3,2},{4,5},{5,4},{6,7},{7,6},{8,9},{9,8},{10,11... | collective-permute-start | bytes 1769480 | tf_op jit(solution)/shard_map/ppermute | solution.py:52
  255.6 25.3 %collective-permute-start.35 = (bf16[128,1152]{1,0:T(8,128)(2,1)S(1)}, bf16[128,1152]{1,0:T(8,128)(2,1)S(1)}, u32[]{:S(2)}, u32[]{:S(2)}) collective-permute-start(bf16[128,1152]{1,0:T(8,128)(2,1)S(1)} %get-tuple-element.111), channel_id=1, source_target_pairs={{0,1},{1,0},{2,3},{3,2},{4,5},{5,4},{6,7},{7,6},{8,9},{9,8},{10,11... | collective-permute-start | bytes 884744 | tf_op jit(solution)/shard_map/ppermute | solution.py:52
  261.9 56.9 %collective-permute-start.23 = (bf16[256,1152]{1,0:T(8,128)(2,1)}, bf16[256,1152]{1,0:T(8,128)(2,1)S(1)}, u32[]{:S(2)}, u32[]{:S(2)}) collective-permute-start(bf16[256,1152]{1,0:T(8,128)(2,1)} %fusion.97), channel_id=1, source_target_pairs={{0,1},{1,0},{2,3},{3,2},{4,5},{5,4},{6,7},{7,6},{8,9},{9,8},{10,11... | collective-permute-start | bytes 1769480 | tf_op jit(solution)/shard_map/ppermute | solution.py:52
  264.4 71.7 %collective-permute-start.18 = (bf16[256,1152]{1,0:T(8,128)(2,1)S(1)}, bf16[256,1152]{1,0:T(8,128)(2,1)S(1)}, u32[]{:S(2)}, u32[]{:S(2)}) collective-permute-start(bf16[256,1152]{1,0:T(8,128)(2,1)S(1)} %add_convert_fusion.12), channel_id=1, source_target_pairs={{0,2},{1,3},{2,0},{3,1},{4,6},{5,7},{6,4},{7,5},{8,10},{9,11},{10,... | collective-permute-start | bytes 1769480 | tf_op jit(solution)/shard_map/ppermute | solution.py:55
  276.9 60.7 %collective-permute-start.41 = (bf16[256,1152]{1,0:T(8,128)(2,1)S(1)}, bf16[256,1152]{1,0:T(8,128)(2,1)S(1)}, u32[]{:S(2)}, u32[]{:S(2)}) collective-permute-start(bf16[256,1152]{1,0:T(8,128)(2,1)S(1)} %add_convert_fusion.6), channel_id=1, source_target_pairs={{0,2},{1,3},{2,0},{3,1},{4,6},{5,7},{6,4},{7,5},{8,10},{9,11},{10,... | collective-permute-start | bytes 1769480 | tf_op jit(solution)/shard_map/ppermute | solution.py:55
  277.5 43.0 %collective-permute-start.44 = (bf16[256,1152]{1,0:T(8,128)(2,1)}, bf16[256,1152]{1,0:T(8,128)(2,1)}, u32[]{:S(2)}, u32[]{:S(2)}) collective-permute-start(bf16[256,1152]{1,0:T(8,128)(2,1)} %fusion.91), channel_id=1, source_target_pairs={{0,1},{1,0},{2,3},{3,2},{4,5},{5,4},{6,7},{7,6},{8,9},{9,8},{10,11... | collective-permute-start | bytes 1769480 | tf_op jit(solution)/shard_map/ppermute | solution.py:52
  287.8 24.1 %collective-permute-start.36 = (bf16[128,1152]{1,0:T(8,128)(2,1)}, bf16[128,1152]{1,0:T(8,128)(2,1)S(1)}, u32[]{:S(2)}, u32[]{:S(2)}) collective-permute-start(bf16[128,1152]{1,0:T(8,128)(2,1)} %fusion.141), channel_id=1, source_target_pairs={{0,1},{1,0},{2,3},{3,2},{4,5},{5,4},{6,7},{7,6},{8,9},{9,8},{10,11... | collective-permute-start | bytes 884744 | tf_op jit(solution)/shard_map/ppermute | solution.py:52
  320.5 22.8 %collective-permute-start.24 = (bf16[256,1152]{1,0:T(8,128)(2,1)S(1)}, bf16[256,1152]{1,0:T(8,128)(2,1)S(1)}, u32[]{:S(2)}, u32[]{:S(2)}) collective-permute-start(bf16[256,1152]{1,0:T(8,128)(2,1)S(1)} %add_convert_fusion.8), channel_id=1, source_target_pairs={{0,2},{1,3},{2,0},{3,1},{4,6},{5,7},{6,4},{7,5},{8,10},{9,11},{10,... | collective-permute-start | bytes 1769480 | tf_op jit(solution)/shard_map/ppermute | solution.py:55
  325.0 30.5 %collective-permute-start.45 = (bf16[256,1152]{1,0:T(8,128)(2,1)S(1)}, bf16[256,1152]{1,0:T(8,128)(2,1)S(1)}, u32[]{:S(2)}, u32[]{:S(2)}) collective-permute-start(bf16[256,1152]{1,0:T(8,128)(2,1)S(1)} %add_convert_fusion.5), channel_id=1, source_target_pairs={{0,2},{1,3},{2,0},{3,1},{4,6},{5,7},{6,4},{7,5},{8,10},{9,11},{10,... | collective-permute-start | bytes 1769480 | tf_op jit(solution)/shard_map/ppermute | solution.py:55
  334.3 32.3 %collective-permute-start.102 = (bf16[2,2,144,1152]{3,2,0,1:T(8,128)(2,1)}, bf16[2,2,144,1152]{3,2,0,1:T(8,128)(2,1)}, u32[]{:S(2)}, u32[]{:S(2)}) collective-permute-start(bf16[2,2,144,1152]{3,2,0,1:T(8,128)(2,1)} %bitcast.835), channel_id=1, source_target_pairs={{0,4},{4,0},{8,12},{12,8},{16,20},{20,16},{24,28},{28,24},{1,5},{5... | collective-permute-start | bytes 3981320 | tf_op jit(solution)/shard_map/ppermute | solution.py:58
  336.1 58.5 %collective-permute-start.96 = (bf16[2,2,144,1152]{3,2,0,1:T(8,128)(2,1)S(1)}, bf16[2,2,144,1152]{3,2,0,1:T(8,128)(2,1)}, u32[]{:S(2)}, u32[]{:S(2)}) collective-permute-start(bf16[2,2,144,1152]{3,2,0,1:T(8,128)(2,1)S(1)} %bitcast.970), channel_id=1, source_target_pairs={{0,4},{4,0},{8,12},{12,8},{16,20},{20,16},{24,28},{28,24},{1,5},{5... | collective-permute-start | bytes 3981320 | tf_op jit(solution)/shard_map/ppermute | solution.py:58
  360.7 37.3 %collective-permute-start.42 = (bf16[256,1152]{1,0:T(8,128)(2,1)S(1)}, bf16[256,1152]{1,0:T(8,128)(2,1)S(1)}, u32[]{:S(2)}, u32[]{:S(2)}) collective-permute-start(bf16[256,1152]{1,0:T(8,128)(2,1)S(1)} %get-tuple-element.123), channel_id=1, source_target_pairs={{0,1},{1,0},{2,3},{3,2},{4,5},{5,4},{6,7},{7,6},{8,9},{9,8},{10,11... | collective-permute-start | bytes 1769480 | tf_op jit(solution)/shard_map/ppermute | solution.py:52
  365.2 46.8 %collective-permute-start.19 = (bf16[256,1152]{1,0:T(8,128)(2,1)}, bf16[256,1152]{1,0:T(8,128)(2,1)}, u32[]{:S(2)}, u32[]{:S(2)}) collective-permute-start(bf16[256,1152]{1,0:T(8,128)(2,1)} %get-tuple-element.174), channel_id=1, source_target_pairs={{0,1},{1,0},{2,3},{3,2},{4,5},{5,4},{6,7},{7,6},{8,9},{9,8},{10,11... | collective-permute-start | bytes 1769480 | tf_op jit(solution)/shard_map/ppermute | solution.py:52
  365.7 46.3 %collective-permute-start.25 = (bf16[256,1152]{1,0:T(8,128)(2,1)}, bf16[256,1152]{1,0:T(8,128)(2,1)}, u32[]{:S(2)}, u32[]{:S(2)}) collective-permute-start(bf16[256,1152]{1,0:T(8,128)(2,1)} %get-tuple-element.175), channel_id=1, source_target_pairs={{0,1},{1,0},{2,3},{3,2},{4,5},{5,4},{6,7},{7,6},{8,9},{9,8},{10,11... | collective-permute-start | bytes 1769480 | tf_op jit(solution)/shard_map/ppermute | solution.py:52
  368.4 49.7 %collective-permute-start.103 = (bf16[2,144,1152]{2,1,0:T(8,128)(2,1)S(1)}, bf16[2,144,1152]{2,1,0:T(8,128)(2,1)}, u32[]{:S(2)}, u32[]{:S(2)}) collective-permute-start(bf16[2,144,1152]{2,1,0:T(8,128)(2,1)S(1)} %dynamic-slice_bitcast_fusion.1), channel_id=1, source_target_pairs={{0,8},{4,12},{8,0},{12,4},{16,24},{20,28},{24,16},{28,20},{1,9},{5... | collective-permute-start | bytes 1990664 | tf_op jit(solution)/shard_map/ppermute | solution.py:58
  396.3 25.9 %collective-permute-start.97 = (bf16[2,144,1152]{2,1,0:T(8,128)(2,1)S(1)}, bf16[2,144,1152]{2,1,0:T(8,128)(2,1)S(1)}, u32[]{:S(2)}, u32[]{:S(2)}) collective-permute-start(bf16[2,144,1152]{2,1,0:T(8,128)(2,1)S(1)} %dynamic-slice_bitcast_fusion.3), channel_id=1, source_target_pairs={{0,8},{4,12},{8,0},{12,4},{16,24},{20,28},{24,16},{28,20},{1,9},{5... | collective-permute-start | bytes 1990664 | tf_op jit(solution)/shard_map/ppermute | solution.py:58
  401.0 21.8 %collective-permute-start.46 = (bf16[256,1152]{1,0:T(8,128)(2,1)S(1)}, bf16[256,1152]{1,0:T(8,128)(2,1)}, u32[]{:S(2)}, u32[]{:S(2)}) collective-permute-start(bf16[256,1152]{1,0:T(8,128)(2,1)S(1)} %get-tuple-element.120), channel_id=1, source_target_pairs={{0,1},{1,0},{2,3},{3,2},{4,5},{5,4},{6,7},{7,6},{8,9},{9,8},{10,11... | collective-permute-start | bytes 1769480 | tf_op jit(solution)/shard_map/ppermute | solution.py:52
  419.4 25.3 %collective-permute-start.104 = (bf16[144,1152]{1,0:T(8,128)(2,1)S(1)}, bf16[144,1152]{1,0:T(8,128)(2,1)S(1)}, u32[]{:S(2)}, u32[]{:S(2)}) collective-permute-start(bf16[144,1152]{1,0:T(8,128)(2,1)S(1)} %dynamic-slice_bitcast_fusion.8), channel_id=1, source_target_pairs={{0,16},{4,20},{8,24},{12,28},{16,0},{20,4},{24,8},{28,12},{1,17},{... | collective-permute-start | bytes 995336 | tf_op jit(solution)/shard_map/ppermute | solution.py:58
  422.5 29.2 %collective-permute-start.98 = (bf16[144,1152]{1,0:T(8,128)(2,1)S(1)}, bf16[144,1152]{1,0:T(8,128)(2,1)S(1)}, u32[]{:S(2)}, u32[]{:S(2)}) collective-permute-start(bf16[144,1152]{1,0:T(8,128)(2,1)S(1)} %dynamic-slice_bitcast_fusion.10), channel_id=1, source_target_pairs={{0,16},{4,20},{8,24},{12,28},{16,0},{20,4},{24,8},{28,12},{1,17},{... | collective-permute-start | bytes 995336 | tf_op jit(solution)/shard_map/ppermute | solution.py:58
  426.4 26.2 %collective-permute-start.59 = (bf16[128,1152]{1,0:T(8,128)(2,1)S(1)}, bf16[128,1152]{1,0:T(8,128)(2,1)S(1)}, u32[]{:S(2)}, u32[]{:S(2)}) collective-permute-start(bf16[128,1152]{1,0:T(8,128)(2,1)S(1)} %get-tuple-element.117), channel_id=1, source_target_pairs={{0,1},{1,0},{2,3},{3,2},{4,5},{5,4},{6,7},{7,6},{8,9},{9,8},{10,11... | collective-permute-start | bytes 884744 | tf_op jit(solution)/shard_map/ppermute | solution.py:52
  438.0 53.5 %collective-permute-start.47 = (bf16[256,1152]{1,0:T(8,128)(2,1)}, bf16[256,1152]{1,0:T(8,128)(2,1)}, u32[]{:S(2)}, u32[]{:S(2)}) collective-permute-start(bf16[256,1152]{1,0:T(8,128)(2,1)} %convolution_convert_fusion.15), channel_id=1, source_target_pairs={{0,1},{1,0},{2,3},{3,2},{4,5},{5,4},{6,7},{7,6},{8,9},{9,8},{10,11... | collective-permute-start | bytes 1769480 | tf_op jit(solution)/shard_map/ppermute | solution.py:52
  440.1 56.1 %collective-permute-start.69 = (bf16[256,1152]{1,0:T(8,128)(2,1)}, bf16[256,1152]{1,0:T(8,128)(2,1)}, u32[]{:S(2)}, u32[]{:S(2)}) collective-permute-start(bf16[256,1152]{1,0:T(8,128)(2,1)} %convolution_convert_fusion.13), channel_id=1, source_target_pairs={{0,1},{1,0},{2,3},{3,2},{4,5},{5,4},{6,7},{7,6},{8,9},{9,8},{10,11... | collective-permute-start | bytes 1769480 | tf_op jit(solution)/shard_map/ppermute | solution.py:52
  473.6 21.3 %collective-permute-start.90 = (bf16[2,2,144,288]{3,2,0,1:T(8,128)(2,1)}, bf16[2,2,144,288]{3,2,0,1:T(8,128)(2,1)}, u32[]{:S(2)}, u32[]{:S(2)}) collective-permute-start(bf16[2,2,144,288]{3,2,0,1:T(8,128)(2,1)} %bitcast.839), channel_id=1, source_target_pairs={{0,4},{4,0},{8,12},{12,8},{16,20},{20,16},{24,28},{28,24},{1,5},{5... | collective-permute-start | bytes 995336 | tf_op jit(solution)/shard_map/ppermute | solution.py:58
  486.7 65.8 %collective-permute-start.81 = (bf16[3,2,2,144,288]{4,3,0,1,2:T(8,128)(2,1)}, bf16[3,2,2,144,288]{4,3,0,1,2:T(8,128)(2,1)}, u32[]{:S(2)}, u32[]{:S(2)}) collective-permute-start(bf16[3,2,2,144,288]{4,3,0,1,2:T(8,128)(2,1)} %bitcast.834), channel_id=1, source_target_pairs={{0,4},{4,0},{8,12},{12,8},{16,20},{20,16},{24,28},{28,24},{1,5},{5... | collective-permute-start | bytes 2985992 | tf_op jit(solution)/shard_map/ppermute | solution.py:58
  494.3 29.9 %collective-permute-start.48 = (bf16[256,1152]{1,0:T(8,128)(2,1)}, bf16[256,1152]{1,0:T(8,128)(2,1)}, u32[]{:S(2)}, u32[]{:S(2)}) collective-permute-start(bf16[256,1152]{1,0:T(8,128)(2,1)} %add_convert_fusion.4), channel_id=1, source_target_pairs={{0,2},{1,3},{2,0},{3,1},{4,6},{5,7},{6,4},{7,5},{8,10},{9,11},{10,... | collective-permute-start | bytes 1769480 | tf_op jit(solution)/shard_map/ppermute | solution.py:55
  499.1 25.5 %collective-permute-start.70 = (bf16[256,1152]{1,0:T(8,128)(2,1)}, bf16[256,1152]{1,0:T(8,128)(2,1)S(1)}, u32[]{:S(2)}, u32[]{:S(2)}) collective-permute-start(bf16[256,1152]{1,0:T(8,128)(2,1)} %add_convert_fusion), channel_id=1, source_target_pairs={{0,2},{1,3},{2,0},{3,1},{4,6},{5,7},{6,4},{7,5},{8,10},{9,11},{10,... | collective-permute-start | bytes 1769480 | tf_op jit(solution)/shard_map/ppermute | solution.py:55
  530.8 30.0 %collective-permute-start.49 = (bf16[256,1152]{1,0:T(8,128)(2,1)}, bf16[256,1152]{1,0:T(8,128)(2,1)}, u32[]{:S(2)}, u32[]{:S(2)}) collective-permute-start(bf16[256,1152]{1,0:T(8,128)(2,1)} %get-tuple-element.138), channel_id=1, source_target_pairs={{0,1},{1,0},{2,3},{3,2},{4,5},{5,4},{6,7},{7,6},{8,9},{9,8},{10,11... | collective-permute-start | bytes 1769480 | tf_op jit(solution)/shard_map/ppermute | solution.py:52
  556.2 20.6 %collective-permute-start.82 = (bf16[3,2,144,288]{3,2,0,1:T(8,128)(2,1)}, bf16[3,2,144,288]{3,2,0,1:T(8,128)(2,1)}, u32[]{:S(2)}, u32[]{:S(2)}) collective-permute-start(bf16[3,2,144,288]{3,2,0,1:T(8,128)(2,1)} %dynamic-slice_bitcast_fusion.5), channel_id=1, source_target_pairs={{0,8},{4,12},{8,0},{12,4},{16,24},{20,28},{24,16},{28,20},{1,9},{5... | collective-permute-start | bytes 1493000 | tf_op jit(solution)/shard_map/ppermute | solution.py:58
  560.0 24.2 %collective-permute-start.68 = (bf16[64,1152]{1,0:T(8,128)(2,1)S(1)}, bf16[64,1152]{1,0:T(8,128)(2,1)S(1)}, u32[]{:S(2)}, u32[]{:S(2)}) collective-permute-start(bf16[64,1152]{1,0:T(8,128)(2,1)S(1)} %get-tuple-element.227), channel_id=1, source_target_pairs={{0,1},{1,0},{2,3},{3,2},{4,5},{5,4},{6,7},{7,6},{8,9},{9,8},{10,11... | collective-permute-start | bytes 442376 | tf_op jit(solution)/shard_map/ppermute | solution.py:52
  574.7 32.2 %collective-permute-start.99 = (bf16[2,2,144,1152]{3,2,0,1:T(8,128)(2,1)S(1)}, bf16[2,2,144,1152]{3,2,0,1:T(8,128)(2,1)S(1)}, u32[]{:S(2)}, u32[]{:S(2)}) collective-permute-start(bf16[2,2,144,1152]{3,2,0,1:T(8,128)(2,1)S(1)} %bitcast.972), channel_id=1, source_target_pairs={{0,4},{4,0},{8,12},{12,8},{16,20},{20,16},{24,28},{28,24},{1,5},{5... | collective-permute-start | bytes 3981320 | tf_op jit(solution)/shard_map/ppermute | solution.py:58
  575.4 59.0 %collective-permute-start.93 = (bf16[2,2,144,1152]{3,2,0,1:T(8,128)(2,1)S(1)}, bf16[2,2,144,1152]{3,2,0,1:T(8,128)(2,1)S(1)}, u32[]{:S(2)}, u32[]{:S(2)}) collective-permute-start(bf16[2,2,144,1152]{3,2,0,1:T(8,128)(2,1)S(1)} %bitcast.971), channel_id=1, source_target_pairs={{0,4},{4,0},{8,12},{12,8},{16,20},{20,16},{24,28},{28,24},{1,5},{5... | collective-permute-start | bytes 3981320 | tf_op jit(solution)/shard_map/ppermute | solution.py:58
  579.2 19.1 %collective-permute-start.51 = (bf16[256,1152]{1,0:T(8,128)(2,1)S(1)}, bf16[256,1152]{1,0:T(8,128)(2,1)S(1)}, u32[]{:S(2)}, u32[]{:S(2)}) collective-permute-start(bf16[256,1152]{1,0:T(8,128)(2,1)S(1)} %add_convert_fusion.3), channel_id=1, source_target_pairs={{0,2},{1,3},{2,0},{3,1},{4,6},{5,7},{6,4},{7,5},{8,10},{9,11},{10,... | collective-permute-start | bytes 1769480 | tf_op jit(solution)/shard_map/ppermute | solution.py:55
  604.2 33.4 %collective-permute-start.52 = (bf16[256,1152]{1,0:T(8,128)(2,1)S(1)}, bf16[256,1152]{1,0:T(8,128)(2,1)S(1)}, u32[]{:S(2)}, u32[]{:S(2)}) collective-permute-start(bf16[256,1152]{1,0:T(8,128)(2,1)S(1)} %get-tuple-element.144), channel_id=1, source_target_pairs={{0,1},{1,0},{2,3},{3,2},{4,5},{5,4},{6,7},{7,6},{8,9},{9,8},{10,11... | collective-permute-start | bytes 1769480 | tf_op jit(solution)/shard_map/ppermute | solution.py:52
  608.2 67.9 %collective-permute-start.100 = (bf16[2,144,1152]{2,1,0:T(8,128)(2,1)}, bf16[2,144,1152]{2,1,0:T(8,128)(2,1)}, u32[]{:S(2)}, u32[]{:S(2)}) collective-permute-start(bf16[2,144,1152]{2,1,0:T(8,128)(2,1)} %dynamic-slice_bitcast_fusion.2), channel_id=1, source_target_pairs={{0,8},{4,12},{8,0},{12,4},{16,24},{20,28},{24,16},{28,20},{1,9},{5... | collective-permute-start | bytes 1990664 | tf_op jit(solution)/shard_map/ppermute | solution.py:58
  635.6 44.0 %collective-permute-start.94 = (bf16[2,144,1152]{2,1,0:T(8,128)(2,1)}, bf16[2,144,1152]{2,1,0:T(8,128)(2,1)}, u32[]{:S(2)}, u32[]{:S(2)}) collective-permute-start(bf16[2,144,1152]{2,1,0:T(8,128)(2,1)} %dynamic-slice_bitcast_fusion.4), channel_id=1, source_target_pairs={{0,8},{4,12},{8,0},{12,4},{16,24},{20,28},{24,16},{28,20},{1,9},{5... | collective-permute-start | bytes 1990664 | tf_op jit(solution)/shard_map/ppermute | solution.py:58
  648.6 32.3 %collective-permute-start.87 = (bf16[2,2,144,288]{3,2,1,0:T(8,128)(2,1)}, bf16[2,2,144,288]{3,2,1,0:T(8,128)(2,1)}, u32[]{:S(2)}, u32[]{:S(2)}) collective-permute-start(bf16[2,2,144,288]{3,2,1,0:T(8,128)(2,1)} %dynamic-slice_bitcast_fusion.7), channel_id=1, source_target_pairs={{0,4},{4,0},{8,12},{12,8},{16,20},{20,16},{24,28},{28,24},{1,5},{5... | collective-permute-start | bytes 995336 | tf_op jit(solution)/shard_map/ppermute | solution.py:58
  655.0 50.5 %collective-permute-start.53 = (bf16[256,1152]{1,0:T(8,128)(2,1)}, bf16[256,1152]{1,0:T(8,128)(2,1)}, u32[]{:S(2)}, u32[]{:S(2)}) collective-permute-start(bf16[256,1152]{1,0:T(8,128)(2,1)} %convolution_convert_fusion.14), channel_id=1, source_target_pairs={{0,1},{1,0},{2,3},{3,2},{4,5},{5,4},{6,7},{7,6},{8,9},{9,8},{10,11... | collective-permute-start | bytes 1769480 | tf_op jit(solution)/shard_map/ppermute | solution.py:52
  674.7 56.8 %collective-permute-start.78 = (bf16[3,2,2,144,288]{4,3,2,1,0:T(8,128)(2,1)}, bf16[3,2,2,144,288]{4,3,2,1,0:T(8,128)(2,1)}, u32[]{:S(2)}, u32[]{:S(2)}) collective-permute-start(bf16[3,2,2,144,288]{4,3,2,1,0:T(8,128)(2,1)} %dynamic-slice_bitcast_fusion), channel_id=1, source_target_pairs={{0,4},{4,0},{8,12},{12,8},{16,20},{20,16},{24,28},{28,24},{1,5},{5... | collective-permute-start | bytes 2985992 | tf_op jit(solution)/shard_map/ppermute | solution.py:58
  677.4 28.0 %collective-permute-start.101 = (bf16[144,1152]{1,0:T(8,128)(2,1)S(1)}, bf16[144,1152]{1,0:T(8,128)(2,1)S(1)}, u32[]{:S(2)}, u32[]{:S(2)}) collective-permute-start(bf16[144,1152]{1,0:T(8,128)(2,1)S(1)} %dynamic-slice_bitcast_fusion.9), channel_id=1, source_target_pairs={{0,16},{4,20},{8,24},{12,28},{16,0},{20,4},{24,8},{28,12},{1,17},{... | collective-permute-start | bytes 995336 | tf_op jit(solution)/shard_map/ppermute | solution.py:58
  683.2 29.3 %collective-permute-start.95 = (bf16[144,1152]{1,0:T(8,128)(2,1)S(1)}, bf16[144,1152]{1,0:T(8,128)(2,1)S(1)}, u32[]{:S(2)}, u32[]{:S(2)}) collective-permute-start(bf16[144,1152]{1,0:T(8,128)(2,1)S(1)} %dynamic-slice_bitcast_fusion.11), channel_id=1, source_target_pairs={{0,16},{4,20},{8,24},{12,28},{16,0},{20,4},{24,8},{28,12},{1,17},{... | collective-permute-start | bytes 995336 | tf_op jit(solution)/shard_map/ppermute | solution.py:58
  694.6 30.4 %collective-permute-start.89 = (bf16[144,288]{1,0:T(8,128)(2,1)}, bf16[144,288]{1,0:T(8,128)(2,1)}, u32[]{:S(2)}, u32[]{:S(2)}) collective-permute-start(bf16[144,288]{1,0:T(8,128)(2,1)} %dynamic-slice_bitcast_fusion.17), channel_id=1, source_target_pairs={{0,16},{4,20},{8,24},{12,28},{16,0},{20,4},{24,8},{28,12},{1,17},{... | collective-permute-start | bytes 248840 | tf_op jit(solution)/shard_map/ppermute | solution.py:58
  737.1 24.4 %collective-permute-start.79 = (bf16[3,2,144,288]{3,2,1,0:T(8,128)(2,1)S(1)}, bf16[3,2,144,288]{3,2,1,0:T(8,128)(2,1)S(1)}, u32[]{:S(2)}, u32[]{:S(2)}) collective-permute-start(bf16[3,2,144,288]{3,2,1,0:T(8,128)(2,1)S(1)} %dynamic-slice_bitcast_fusion.6), channel_id=1, source_target_pairs={{0,8},{4,12},{8,0},{12,4},{16,24},{20,28},{24,16},{28,20},{1,9},{5... | collective-permute-start | bytes 1493000 | tf_op jit(solution)/shard_map/ppermute | solution.py:58
  739.1 38.2 %collective-permute-start.55 = (bf16[256,1152]{1,0:T(8,128)(2,1)}, bf16[256,1152]{1,0:T(8,128)(2,1)}, u32[]{:S(2)}, u32[]{:S(2)}) collective-permute-start(bf16[256,1152]{1,0:T(8,128)(2,1)} %get-tuple-element.186), channel_id=1, source_target_pairs={{0,1},{1,0},{2,3},{3,2},{4,5},{5,4},{6,7},{7,6},{8,9},{9,8},{10,11... | collective-permute-start | bytes 1769480 | tf_op jit(solution)/shard_map/ppermute | solution.py:52
  (404 other events, 3884.3 us)

commit v2 on v1

v2 whole, which is shorter than its diff:
```python
import math

import jax
import jax.numpy as jnp
from jax import lax
from jax.experimental import pallas as pl
from jax.experimental.pallas import tpu as pltpu
from jax.sharding import PartitionSpec as P

HEAD_DIM = 72
EPSILON = 1e-06
BF16 = jnp.bfloat16
F32 = jnp.float32
MIB = 1 << 20
SCALING = HEAD_DIM**-0.5
EXPONENT = SCALING * math.log2(math.e)
GELU_A = math.sqrt(2.0 / math.pi)
GELU_B = 0.044715

SHIFT_ATTN, SCALE_ATTN, GATE_ATTN, SHIFT_MLP, SCALE_MLP, GATE_MLP = range(6)
PROJ_BIAS, DOWN_BIAS, UP_BIAS, QKV_BIAS = 0, 2, 4, 6


def nn(left, right):
    return lax.dot_general(left, right, (((1,), (0,)), ((), ())), preferred_element_type=F32)


def nt(left, right):
    return lax.dot_general(left, right, (((1,), (1,)), ((), ())), preferred_element_type=F32)


def tn(left, right):
    return lax.dot_general(left, right, (((0,), (0,)), ((), ())), preferred_element_type=F32)


def shaped(shape, dtype=BF16):
    return jax.ShapeDtypeStruct(shape, dtype)


def bytes_of(value):
    return math.prod(value.shape) * value.dtype.itemsize


def call(body, operands, outs, name, scalars=(), scratch=(), flops=0, limit=16):
    fast = pl.BlockSpec(memory_space=pltpu.VMEM)
    small = pl.BlockSpec(memory_space=pltpu.SMEM)
    moved = sum(bytes_of(value) for value in operands) + sum(bytes_of(value) for value in outs)
    return pl.pallas_call(
        body,
        in_specs=[small] * len(scalars) + [fast] * len(operands),
        out_specs=[fast] * len(outs),
        out_shape=list(outs),
        scratch_shapes=list(scratch),
        cost_estimate=pl.CostEstimate(
            flops=int(flops), transcendentals=0, bytes_accessed=int(moved)
        ),
        compiler_params=pltpu.CompilerParams(vmem_limit_bytes=limit * MIB),
        name=name,
    )(
        *scalars,
        *[pltpu.with_memory_space_constraint(value, pltpu.VMEM) for value in operands],
    )


def normed_of(values):
    center = values - jnp.mean(values, axis=-1, keepdims=True)
    spread = jnp.mean(center * center, axis=-1, keepdims=True)
    scale = lax.rsqrt(spread + EPSILON)
    return center * scale, scale


def modulate(values, mods_ref, at, scale_part, shift_part):
    block, latent = at
    scale = mods_ref[block, latent, scale_part : scale_part + 1, :]
    shift = mods_ref[block, latent, shift_part : shift_part + 1, :]
    return (normed_of(values)[0] * (1.0 + scale) + shift).astype(BF16)


def ln_open(stream, mods, at):
    rows, features = stream.shape

    def body(x_ref, mods_ref, out_ref):
        out_ref[...] = modulate(x_ref[...], mods_ref, at, SCALE_ATTN, SHIFT_ATTN)

    return call(body, [stream, mods], [shaped((rows, features))], "ln_open", flops=20 * rows * features)[0]


def merge_attn(stream, near, far, small, mods, at):
    rows, features = stream.shape
    block, latent = at

    def body(x_ref, near_ref, far_ref, small_ref, mods_ref, mid_ref, out_ref):
        bias = small_ref[PROJ_BIAS + block : PROJ_BIAS + block + 1, :features]
        branch = near_ref[...].astype(F32) + far_ref[...].astype(F32) + bias
        middle = x_ref[...] + mods_ref[block, latent, GATE_ATTN : GATE_ATTN + 1, :] * branch
        mid_ref[...] = middle
        out_ref[...] = modulate(middle, mods_ref, at, SCALE_MLP, SHIFT_MLP)

    return call(
        body,
        [stream, near, far, small, mods],
        [shaped((rows, features), F32), shaped((rows, features))],
        "merge_attn",
        flops=25 * rows * features,
    )


def merge_mlp(middle, near, far, small, mods, at, table, tail):
    rows, features = middle.shape
    block, latent = at
    total = rows + (0 if tail is None else tail.shape[0])
    following = (block + 1, latent)

    def body(mid_ref, near_ref, far_ref, table_ref, small_ref, mods_ref, *rest):
        x_ref, out_ref = rest[-2:]
        bias = small_ref[DOWN_BIAS + block : DOWN_BIAS + block + 1, :features]
        branch = near_ref[...].astype(F32) + far_ref[...].astype(F32) + bias
        gate = mods_ref[block, latent, GATE_MLP : GATE_MLP + 1, :]
        stream = mid_ref[...] + gate * branch + table_ref[...]
        x_ref[:rows, :] = stream
        out_ref[:rows, :] = modulate(stream, mods_ref, following, SCALE_ATTN, SHIFT_ATTN)
        if tail is not None:
            stream = rest[0][...]
            x_ref[rows:, :] = stream
            out_ref[rows:, :] = modulate(stream, mods_ref, following, SCALE_ATTN, SHIFT_ATTN)

    return call(
        body,
        [middle, near, far, table, small, mods] + ([] if tail is None else [tail]),
        [shaped((total, features), F32), shaped((total, features))],
        "merge_mlp",
        flops=25 * total * features,
    )


def qkv_forward(own, other, weight, small, block):
    rows, features = own.shape
    width = weight.shape[1]

    def body(own_ref, other_ref, w_ref, small_ref, out_ref):
        bias = small_ref[QKV_BIAS + block : QKV_BIAS + block + 1, :width]
        both = jnp.concatenate([own_ref[...], other_ref[...]], axis=0)
        out = (nt(both, w_ref[block]) + bias).astype(BF16)
        out_ref[0] = out[:rows]
        out_ref[1] = out[rows:]

    return call(
        body,
        [own, other, weight, small],
        [shaped((2, rows, width))],
        "qkv_forward",
        flops=4 * rows * features * width,
    )[0]


def qkv_backward(grads, weight, block):
    _, rows, width = grads.shape
    features = weight.shape[2]

    def body(g_ref, w_ref, own_ref, other_ref):
        both = jnp.concatenate([g_ref[0], g_ref[1]], axis=0)
        out = nn(both, w_ref[block]).astype(BF16)
        own_ref[...] = out[:rows]
        other_ref[...] = out[rows:]

    return call(
        body,
        [grads, weight],
        [shaped((rows, features)), shaped((rows, features))],
        "qkv_backward",
        flops=4 * rows * features * width,
    )


def mlp_forward(own, other, up_weight, down_weight, small, block):
    rows, features = own.shape
    wide = up_weight.shape[2]

    def body(own_ref, other_ref, up_ref, down_ref, small_ref, own_out, other_out, act_ref, slope_ref):
        bias = small_ref[UP_BIAS + block : UP_BIAS + block + 1, :wide]
        both = jnp.concatenate([own_ref[...], other_ref[...]], axis=0)
        hidden = nn(both, up_ref[block]) + bias
        squared = hidden * hidden
        bent = jnp.tanh(GELU_A * hidden * (1.0 + GELU_B * squared))
        half = 0.5 + 0.5 * bent
        active = (hidden * half).astype(BF16)
        slope = half + 0.5 * hidden * (1.0 - bent * bent) * (
            GELU_A + 3.0 * GELU_A * GELU_B * squared
        )
        act_ref[...] = active
        slope_ref[...] = slope.astype(BF16)
        out = nn(active, down_ref[block]).astype(BF16)
        own_out[...] = out[:rows]
        other_out[...] = out[rows:]

    return call(
        body,
        [own, other, up_weight, down_weight, small],
        [
            shaped((rows, features)),
            shaped((rows, features)),
            shaped((2 * rows, wide)),
            shaped((2 * rows, wide)),
        ],
        "mlp_forward",
        flops=8 * rows * features * wide,
    )


def mlp_backward(own, other, slope, up_weight, down_weight, block):
    rows, features = own.shape
    wide = up_weight.shape[2]

    def body(own_ref, other_ref, slope_ref, up_ref, down_ref, own_out, other_out, hid_ref):
        both = jnp.concatenate([own_ref[...], other_ref[...]], axis=0)
        d_active = nt(both, down_ref[block])
        d_hidden = (d_active * slope_ref[...].astype(F32)).astype(BF16)
        hid_ref[...] = d_hidden
        out = nt(d_hidden, up_ref[block]).astype(BF16)
        own_out[...] = out[:rows]
        other_out[...] = out[rows:]

    return call(
        body,
        [own, other, slope, up_weight, down_weight],
        [shaped((rows, features)), shaped((rows, features)), shaped((2 * rows, wide))],
        "mlp_backward",
        flops=8 * rows * features * wide,
    )


def ln_back(near, far, stream, d_out, mods, at, scale_part, branch=None, cut=None, narrow=False):
    rows, features = stream.shape
    cut = rows if cut is None else cut
    operands = [near, far, stream, d_out, mods]
    outs = [shaped((rows, features), BF16 if narrow else F32), shaped((8, features), F32)]
    if branch is not None:
        branch_near, branch_far, small, bias_row, gate_at, gate_part = branch
        operands += [branch_near, branch_far, small]
        outs.append(shaped((cut, features)))

    def body(near_ref, far_ref, x_ref, d_ref, mods_ref, *rest):
        scale = mods_ref[at[0], at[1], scale_part : scale_part + 1, :]
        d_normed = near_ref[...].astype(F32) + far_ref[...].astype(F32)
        normed, spread = normed_of(x_ref[...])
        product = d_normed * normed
        grad = d_normed * (1.0 + scale)
        d_x = d_ref[...] + spread * (
            grad
            - jnp.mean(grad, axis=-1, keepdims=True)
            - normed * jnp.mean(grad * normed, axis=-1, keepdims=True)
        )
        sums = [jnp.sum(product, axis=0, keepdims=True), jnp.sum(d_normed, axis=0, keepdims=True)]
        if branch is None:
            d_ref_out, sums_ref = rest
            sums += [jnp.zeros_like(sums[0])] * 2
        else:
            b_near, b_far, small_ref, d_ref_out, sums_ref, grad_ref = rest
            value = b_near[...].astype(F32) + b_far[...].astype(F32)
            value = value + small_ref[bias_row : bias_row + 1, :features]
            kept = d_x[:cut]
            gate = mods_ref[gate_at[0], gate_at[1], gate_part : gate_part + 1, :]
            d_branch = (gate * kept).astype(BF16)
            grad_ref[...] = d_branch
            sums += [
                jnp.sum(kept * value, axis=0, keepdims=True),
                jnp.sum(d_branch.astype(F32), axis=0, keepdims=True),
            ]
        if cut < rows:
            sums.append(jnp.sum(d_x[cut:], axis=0, keepdims=True))
        else:
            sums.append(jnp.zeros_like(sums[0]))
        sums.append(jnp.zeros((3, features), F32))
        sums_ref[...] = jnp.concatenate(sums, axis=0)
        d_ref_out[...] = d_x.astype(d_ref_out.dtype)

    return call(body, operands, outs, "ln_back", flops=60 * rows * features)


def attn_forward(query, merged, proj_weight, block):
    _, rows, width = query.shape
    local = width // 3
    heads = local // HEAD_DIM
    counts = [part.shape[1] for part in merged]
    total = 2 * sum(counts)
    features = proj_weight.shape[2]
    by_keys = rows <= 128

    def body(*refs):
        q_ref, refs = refs[0], refs[1:]
        kv_refs, refs = refs[: len(merged)], refs[len(merged) :]
        proj_ref, att_ref, lse_ref, own_out, other_out, q_s, k_s, v_s, o_s, l_s = refs
        for head in range(heads):
            low = head * HEAD_DIM
            first = 0
            for part, count in zip(kv_refs, counts):
                for side in range(2):
                    at = pl.ds(first, count)
                    k_s[head, at, :] = part[side, :, local + low : local + low + HEAD_DIM]
                    v_s[head, at, :] = part[side, :, 2 * local + low : 2 * local + low + HEAD_DIM]
                    first += count
            for side in range(2):
                q_s[head, side] = q_ref[side, :, low : low + HEAD_DIM]
        for head in range(heads):
            for side in range(2):
                if by_keys:
                    scores = nt(k_s[head], q_s[head, side])
                    highest = jnp.max(scores, axis=0, keepdims=True)
                    raised = jnp.exp2((scores - highest) * EXPONENT)
                    total_row = jnp.sum(raised, axis=0, keepdims=True)
                    out = tn(v_s[head], raised.astype(BF16))
                    o_s[head, side] = (out / total_row).T.astype(BF16)
                    lse_ref[head, side] = highest * EXPONENT + jnp.log2(total_row)
                else:
                    scores = nt(q_s[head, side], k_s[head])
                    highest = jnp.max(scores, axis=1, keepdims=True)
                    raised = jnp.exp2((scores - highest) * EXPONENT)
                    total_row = jnp.sum(raised, axis=1, keepdims=True)
                    out = nn(raised.astype(BF16), v_s[head])
                    o_s[head, side] = (out / total_row).astype(BF16)
                    l_s[head, side] = jnp.broadcast_to(
                        highest * EXPONENT + jnp.log2(total_row), (rows, 128)
                    )
        if not by_keys:
            for head in range(heads):
                for side in range(2):
                    lse_ref[head, side] = l_s[head, side].T[:1]
        for side, out_ref in ((1, other_out), (0, own_out)):
            for head in range(heads):
                low = head * HEAD_DIM
                att_ref[side * rows : (side + 1) * rows, low : low + HEAD_DIM] = o_s[head, side]
            out_ref[...] = nn(
                att_ref[side * rows : (side + 1) * rows, :], proj_ref[block]
            ).astype(BF16)

    return call(
        body,
        [query, *merged, proj_weight],
        [
            shaped((2 * rows, local)),
            shaped((heads, 2, 1, rows), F32),
            shaped((rows, features)),
            shaped((rows, features)),
        ],
        "attn_forward",
        scratch=[
            pltpu.VMEM((heads, 2, rows, HEAD_DIM), BF16),
            pltpu.VMEM((heads, total, HEAD_DIM), BF16),
            pltpu.VMEM((heads, total, HEAD_DIM), BF16),
            pltpu.VMEM((heads, 2, rows, HEAD_DIM), BF16),
            pltpu.VMEM((heads, 2, 8 if by_keys else rows, 128), F32),
        ],
        flops=16 * heads * rows * total * HEAD_DIM + 4 * rows * local * features,
        limit=24,
    )


def attn_backward(merged, normers, grads, proj_weight, block):
    count = len(merged)
    width = merged[0].shape[2]
    local = width // 3
    heads = local // HEAD_DIM
    halves = [part.shape[1] for part in merged]
    total = 2 * sum(halves)
    features = proj_weight.shape[2]
    step = min(halves)
    steps = total // step
    unroll = 4 if step >= 256 else steps * heads

    def body(*refs):
        m_refs, refs = refs[:count], refs[count:]
        l_refs, refs = refs[:count], refs[count:]
        g_refs, refs = refs[: 2 * count], refs[2 * count :]
        proj_ref, refs = refs[0], refs[1:]
        out_refs, refs = refs[:count], refs[count:]
        q_s, k_s, kt_s, v_s, g_s, dq_s, dk_s, dv_s, l_s = refs
        first = 0
        for index in range(count):
            rows = halves[index]
            for side in range(2):
                at = pl.ds(first, rows)
                grad = nt(g_refs[2 * index + side][...], proj_ref[block]).astype(BF16)
                for head in range(heads):
                    low = head * HEAD_DIM
                    part = m_refs[index]
                    q_s[head, at, :] = part[side, :, low : low + HEAD_DIM]
                    keys = part[side, :, local + low : local + low + HEAD_DIM]
                    k_s[head, at, :] = keys
                    kt_s[head, :, at] = keys.T
                    v_s[head, at, :] = part[side, :, 2 * local + low : 2 * local + low + HEAD_DIM]
                    g_s[head, at, :] = grad[:, low : low + HEAD_DIM]
                    for piece in range(rows // step):
                        l_s[head, first // step + piece] = l_refs[index][
                            head, side, :, piece * step : (piece + 1) * step
                        ]
                first += rows
        dk_s[...] = jnp.zeros_like(dk_s)
        dv_s[...] = jnp.zeros_like(dv_s)

        def one(index, carry):
            head, piece = index // steps, lax.rem(index, steps)
            at = pl.ds(pl.multiple_of(piece * step, step), step)
            queries, grad = q_s[head, at, :], g_s[head, at, :]
            probs = jnp.exp2(nt(k_s[head], queries) * EXPONENT - l_s[head, piece])
            product = probs * nt(v_s[head], grad)
            delta = jnp.sum(product, axis=0, keepdims=True)
            d_scores = (product - probs * delta).astype(BF16)
            dv_s[head] += nn(probs.astype(BF16), grad)
            dk_s[head] += nn(d_scores, queries)
            dq_s[head, at, :] = (nn(kt_s[head], d_scores) * SCALING).T.astype(BF16)
            return carry

        lax.fori_loop(0, steps * heads, one, 0, unroll=unroll)
        first = 0
        for index in range(count):
            rows = halves[index]
            for side in range(2):
                at = pl.ds(first, rows)
                out = out_refs[index]
                for head in range(heads):
                    low = head * HEAD_DIM
                    out[side, :, low : low + HEAD_DIM] = dq_s[head, at, :]
                    out[side, :, local + low : local + low + HEAD_DIM] = (
                        dk_s[head, at, :] * SCALING
                    ).astype(BF16)
                    out[side, :, 2 * local + low : 2 * local + low + HEAD_DIM] = dv_s[
                        head, at, :
                    ].astype(BF16)
                first += rows

    def lanes(dtype=BF16):
        return pltpu.VMEM((heads, total, HEAD_DIM), dtype)

    return call(
        body,
        [*merged, *normers, *[half for pair in grads for half in pair], proj_weight],
        [shaped(part.shape) for part in merged],
        "attn_backward",
        scratch=[
            lanes(),
            lanes(),
            pltpu.VMEM((heads, HEAD_DIM, total), BF16),
            lanes(),
            lanes(),
            lanes(),
            lanes(F32),
            lanes(F32),
            pltpu.VMEM((heads, steps, 1, step), F32),
        ],
        flops=20 * heads * total * total * HEAD_DIM + 2 * total * local * features,
        limit=28,
    )


def weight_grads(pairs, bit, blocks):
    features = pairs[0][0][0].shape[1]
    widths = [rights[0].shape[1] for _, rights in pairs]
    each = features // blocks
    operands, spans = [], []
    for lefts, rights in pairs:
        spans.append((len(operands), len(lefts)))
        operands += list(lefts) + list(rights)
    rows = sum(part.shape[0] for part in pairs[0][0])
    out = shaped((blocks // 2, each, sum(widths)))

    def body(bit_ref, *refs):
        kept_ref, away_ref = refs[-2:]
        mine = bit_ref[0]
        low = 0
        for (first, number), width in zip(spans, widths):
            total = None
            for index in range(number):
                term = tn(refs[first + index][...], refs[first + number + index][...])
                total = term if total is None else total + term
            total = total.astype(BF16)
            columns = slice(low, low + width)
            for block in range(blocks):
                piece = total[block * each : (block + 1) * each]

                @pl.when(mine == block % 2)
                def _():
                    kept_ref[block // 2, :, columns] = piece

                @pl.when(mine != block % 2)
                def _():
                    away_ref[block // 2, :, columns] = piece

            low += width

    return call(
        body,
        operands,
        [out, out],
        "weight_grads",
        scalars=[bit],
        flops=2 * rows * features * sum(widths),
        limit=28,
    )


def halve(kept, moved, bit):
    blocks, each, width = kept.shape
    out = shaped((blocks // 2, each, width))

    def body(bit_ref, kept_ref, moved_ref, next_ref, away_ref):
        mine = bit_ref[0]
        for index in range(blocks // 2):
            for place, out_ref in ((1 - mine, away_ref), (mine, next_ref)):
                at = 2 * index + place
                out_ref[index] = (kept_ref[at].astype(F32) + moved_ref[at].astype(F32)).astype(BF16)

    return call(
        body, [kept, moved], [out, out], "halve", scalars=[bit], flops=blocks * each * width
    )


def partners(size, bit):
    return [(index, index ^ bit) for index in range(size)]


def bits_of(size):
    bits = []
    while (1 << len(bits)) < size:
        bits.append(1 << len(bits))
    assert (1 << len(bits)) == size
    return bits


class Links:
    def __init__(self, dp_size, tensor_size):
        self.dp_size = dp_size
        self.tensor_size = tensor_size
        self.dp_bits = bits_of(dp_size)
        self.me = lax.axis_index("dp")
        self.core = lax.rem(lax.axis_index("tensor"), 2)

    def swap(self, value):
        return lax.ppermute(value, "tensor", partners(self.tensor_size, 1))

    def cross(self, value):
        return lax.ppermute(value, "tensor", partners(self.tensor_size, 2))

    def dp_move(self, value, bit):
        return lax.ppermute(value, "dp", partners(self.dp_size, bit))

    def my_bit(self, bit):
        return lax.rem(self.me // bit, 2)

    def joined(self, own, other):
        moved = self.swap(other)
        near = (own.astype(F32) + moved.astype(F32)).astype(BF16)
        return near, self.cross(near)

    def gather_relative(self, value):
        held = value[None]
        for bit in self.dp_bits:
            held = jnp.concatenate([held, self.dp_move(held, bit)], axis=0)
        return held

    def exchange_relative(self, value):
        held = value
        for bit in self.dp_bits:
            split = held.reshape((self.dp_size // (2 * bit), 2, bit) + held.shape[1:])
            moved = self.dp_move(split[:, 1], bit)
            held = jnp.stack([split[:, 0], moved], axis=1).reshape(held.shape)
        return held

    def sum_relative(self, value):
        held = value
        for bit in reversed(self.dp_bits):
            moved = self.dp_move(held[bit:].astype(BF16), bit)
            held = held[:bit].astype(F32) + moved.astype(F32)
        return held[0]

    def reorder(self, value):
        held = value
        for bit in self.dp_bits:
            split = held.reshape((self.dp_size // (2 * bit), 2, bit) + held.shape[1:])
            flipped = jnp.where(self.my_bit(bit) == 1, split[:, ::-1], split)
            held = flipped.reshape(held.shape)
        return held

    def scatter_sum(self, pairs):
        bits = [self.my_bit(bit).reshape(1) for bit in self.dp_bits]
        kept, away = weight_grads(pairs, bits[0], self.dp_size)
        for bit, mine in zip(self.dp_bits[:-1], bits[1:]):
            kept, away = halve(kept, self.dp_move(away, bit), mine)
        moved = self.dp_move(away, self.dp_bits[-1])
        return kept[0].astype(F32) + moved[0].astype(F32)

    def sum_all(self, value):
        held = value
        for bit in self.dp_bits:
            held = held + self.dp_move(held, bit)
        return held


class Weights:
    def __init__(self, qkv, proj, up, down, small, mods):
        self.qkv, self.proj, self.up, self.down = qkv, proj, up, down
        self.small, self.mods = small, mods


class Block:
    def __init__(self, links, weights, index, owners):
        self.links, self.weights, self.index, self.owners = links, weights, index, owners
        self.saved = [dict() for _ in owners]

    def at(self, chunk):
        return (self.index, self.owners[chunk])

    def members(self, latent):
        return [chunk for chunk, owner in enumerate(self.owners) if owner == latent]

    def latents(self):
        return sorted(set(self.owners))

    def enter(self, chunk, stream, normed):
        keep, w = self.saved[chunk], self.weights
        keep["x"] = stream
        keep["normed_attn"] = (normed, self.links.swap(normed))
        keep["qkv"] = qkv_forward(*keep["normed_attn"], w.qkv, w.small, self.index)

    def attention(self, chunk):
        keep, w = self.saved[chunk], self.weights
        merged = [self.saved[c]["qkv"] for c in self.members(self.owners[chunk])]
        keep["attended"], keep["normer"], own, other = attn_forward(
            keep["qkv"], merged, w.proj, self.index
        )
        keep["branch_attn"] = self.links.joined(own, other)

    def mlp(self, chunk):
        keep, w = self.saved[chunk], self.weights
        keep["middle"], normed = merge_attn(
            keep["x"], *keep["branch_attn"], w.small, w.mods, self.at(chunk)
        )
        keep["normed_mlp"] = (normed, self.links.swap(normed))
        own, other, keep["active"], keep["slope"] = mlp_forward(
            *keep["normed_mlp"], w.up, w.down, w.small, self.index
        )
        keep["branch_mlp"] = self.links.joined(own, other)

    def mlp_back(self, chunk, d_out, d_branch):
        keep, w = self.saved[chunk], self.weights
        keep["d_branch_mlp"] = (d_branch, self.links.swap(d_branch))
        own, other, keep["d_hidden"] = mlp_backward(
            *keep["d_branch_mlp"], keep["slope"], w.up, w.down, self.index
        )
        near, far = self.links.joined(own, other)
        branch = (*keep["branch_attn"], w.small, PROJ_BIAS + self.index, self.at(chunk), GATE_ATTN)
        keep["d_middle"], keep["mlp_sums"], grad = ln_back(
            near, far, keep["middle"], d_out, w.mods, self.at(chunk), SCALE_MLP, branch
        )
        keep["d_branch_attn"] = (grad, self.links.swap(grad))

    def attention_back(self, latent):
        w = self.weights
        chunks = [self.saved[c] for c in self.members(latent)]
        grads = attn_backward(
            [keep["qkv"] for keep in chunks],
            [keep["normer"] for keep in chunks],
            [keep["d_branch_attn"] for keep in chunks],
            w.proj,
            self.index,
        )
        for keep, grad in zip(chunks, grads):
            keep["d_qkv"] = grad

    def leave_back(self, chunk, branch=None, cut=None, narrow=False):
        keep, w = self.saved[chunk], self.weights
        near, far = self.links.joined(*qkv_backward(keep["d_qkv"], w.qkv, self.index))
        d_x, keep["attn_sums"], *grad = ln_back(
            near,
            far,
            keep["x"],
            keep["d_middle"],
            w.mods,
            self.at(chunk),
            SCALE_ATTN,
            branch,
            cut,
            narrow,
        )
        return d_x, (grad[0] if grad else None)

    def rows(self, name):
        found = []
        for keep in self.saved:
            value = keep[name]
            if isinstance(value, tuple):
                found += list(value)
            else:
                found.append(value.reshape(-1, value.shape[-1]))
        return found

    def halves(self, name):
        found = []
        for keep in self.saved:
            value = keep[name]
            value = value.reshape(-1, value.shape[-1])
            middle = value.shape[0] // 2
            found += [value[:middle], value[middle:]]
        return found


def pick_matrix(places, length):
    return (places[:, None] == jnp.arange(length, dtype=jnp.int32)[None, :]).astype(BF16)


def table_rows(places, length, features):
    side = math.isqrt(length)
    quarter = features // 4
    frequency = 1.0 / 10000.0 ** (jnp.arange(quarter, dtype=F32) / quarter)
    angle = jnp.arange(side, dtype=jnp.int32).astype(F32)[:, None] * frequency[None, :]
    near = jnp.concatenate([jnp.sin(angle), jnp.cos(angle)], axis=1)
    steps = jnp.arange(side, dtype=jnp.int32)[None, :]
    row_pick = (places[:, None] // side == steps).astype(F32)
    col_pick = (places[:, None] % side == steps).astype(F32)
    return jnp.concatenate(
        [
            jnp.dot(row_pick, near, precision=lax.Precision.HIGHEST),
            jnp.dot(col_pick, near, precision=lax.Precision.HIGHEST),
        ],
        axis=1,
    )


def on_device(dp_size, tensor_size, *arguments):
    (
        tokens_long,
        tokens_short,
        cond_long,
        cond_short,
        perm_long,
        perm_short,
        ada_weight,
        ada_bias,
        qkv_weight,
        qv_bias,
        proj_weight,
        proj_bias,
        up_weight,
        up_bias,
        down_weight,
        down_bias,
        mask_token,
        cot_long,
        cot_short,
    ) = arguments
    assert tokens_long.shape[0] == 1 and tokens_short.shape[0] == 1
    links = Links(dp_size, tensor_size)
    features = tokens_long.shape[2]
    wide = up_weight.shape[2]
    local = qv_bias.shape[2]
    tokens = (tokens_long[0], tokens_short[0])
    cots = (cot_long[0], cot_short[0])
    perms = (perm_long[0], perm_short[0])
    lengths = tuple(rows.shape[0] for rows in tokens)
    kept = tuple(length // 2 for length in lengths)

    cond = jnp.concatenate([cond_long, cond_short]).astype(F32)
    acts = links.gather_relative(jax.nn.silu(cond).astype(BF16))
    flat_acts = acts.reshape(-1, features)
    columns = jnp.einsum("nd,ldm->nlm", flat_acts, ada_weight, preferred_element_type=F32)
    columns = (columns + ada_bias.astype(F32)[None]).astype(BF16)
    columns = columns.reshape((dp_size, 2) + columns.shape[1:])
    mods = links.reorder(links.exchange_relative(columns)).astype(F32)
    mods = jnp.transpose(mods, (2, 1, 0, 3)).reshape(2, 2, 6, features)

    table_width = max(features, wide, 3 * local)

    def padded(rows):
        return jnp.pad(rows.astype(F32), ((0, 0), (0, table_width - rows.shape[1])))

    qkv_bias = jnp.concatenate(
        [qv_bias[:, 0], jnp.zeros_like(qv_bias[:, 0]), qv_bias[:, 1]], axis=1
    )
    small = jnp.concatenate([padded(proj_bias), padded(down_bias), padded(up_bias), padded(qkv_bias)])
    weights = Weights(
        jnp.transpose(qkv_weight, (0, 2, 3, 1)).reshape(2, 3 * local, features),
        proj_weight,
        up_weight,
        down_weight,
        small,
        mods,
    )

    def places_of(latent, first):
        half = kept[latent] // 2
        mine = lax.dynamic_slice_in_dim(perms[latent], first + links.core * half, half)
        other = lax.dynamic_slice_in_dim(perms[latent], first + (1 - links.core) * half, half)
        return mine, other

    kept_places = [places_of(latent, 0) for latent in (0, 1)]
    masked_places = [places_of(latent, kept[latent]) for latent in (0, 1)]
    half_short = kept[1] // 2
    encoder = Block(links, weights, 0, (0, 1))
    decoder = Block(links, weights, 1, (0, 0, 1))
    dec_places = [
        kept_places[0],
        masked_places[0],
        tuple(jnp.concatenate(pair) for pair in zip(kept_places[1], masked_places[1])),
    ]
    dec_lengths = (lengths[0], lengths[0], lengths[1])

    filler = mask_token.astype(F32)[None]
    kept_tables = [
        table_rows(kept_places[latent][0], lengths[latent], features) for latent in (0, 1)
    ]
    masked_rows = [
        filler + table_rows(masked_places[latent][0], lengths[latent], features)
        for latent in (0, 1)
    ]
    for latent in (0, 1):
        stream = nn(pick_matrix(kept_places[latent][0], lengths[latent]), tokens[latent])
        encoder.enter(latent, stream, ln_open(stream, mods, (0, latent)))
    for chunk in (0, 1):
        encoder.attention(chunk)
    decoder.enter(1, masked_rows[0], ln_open(masked_rows[0], mods, (1, 0)))
    for chunk in (0, 1):
        encoder.mlp(chunk)
    for latent, chunk, tail in ((0, 0, None), (1, 2, masked_rows[1])):
        keep = encoder.saved[latent]
        stream, normed = merge_mlp(
            keep["middle"],
            *keep["branch_mlp"],
            small,
            mods,
            (0, latent),
            kept_tables[latent],
            tail,
        )
        decoder.enter(chunk, stream, normed)
    for chunk in (0, 1, 2):
        decoder.attention(chunk)
    for chunk in (0, 1, 2):
        decoder.mlp(chunk)

    decoded, d_decoded, gate_sums, bias_sums, grads_in = [], [], [], [], []
    for chunk in (0, 1, 2):
        keep = decoder.saved[chunk]
        latent = decoder.owners[chunk]
        gate = mods[1, latent, GATE_MLP][None]
        near, far = keep["branch_mlp"]
        branch = near.astype(F32) + far.astype(F32) + down_bias[1].astype(F32)[None]
        own = (keep["middle"] + gate * branch).astype(BF16)
        decoded.append((own, links.swap(own)))
        pick = pick_matrix(dec_places[chunk][0], dec_lengths[chunk])
        d_out = nn(pick, cots[latent])
        grad = (gate * d_out).astype(BF16)
        d_decoded.append(d_out)
        grads_in.append(grad)
        gate_sums.append(jnp.sum(d_out * branch, axis=0))
        bias_sums.append(jnp.sum(grad.astype(F32), axis=0))

    def placed(pairs, places, length):
        pick = pick_matrix(jnp.concatenate([part for pair in places for part in pair]), length)
        return tn(pick, jnp.concatenate([part for pair in pairs for part in pair])).astype(BF16)

    results = (
        placed(decoded[:2], dec_places[:2], lengths[0]),
        placed(decoded[2:], dec_places[2:], lengths[1]),
    )

    for chunk in (0, 1, 2):
        decoder.mlp_back(chunk, d_decoded[chunk], grads_in[chunk])
    dec_wide = links.scatter_sum(
        [
            (decoder.rows("normed_mlp"), decoder.halves("d_hidden")),
            (decoder.rows("d_branch_mlp"), decoder.halves("active")),
            (decoder.rows("d_branch_attn"), decoder.halves("attended")),
        ]
    )
    for latent in (0, 1):
        decoder.attention_back(latent)
    enc_branch = [
        (*encoder.saved[latent]["branch_mlp"], small, DOWN_BIAS, (0, latent), GATE_MLP)
        for latent in (0, 1)
    ]
    d_long, grad_long = decoder.leave_back(0, enc_branch[0])
    d_masked, _ = decoder.leave_back(1, None, 0)
    d_short, grad_short = decoder.leave_back(2, enc_branch[1], half_short)
    dec_qkv = links.scatter_sum([(decoder.rows("normed_attn"), decoder.halves("d_qkv"))])
    encoder.mlp_back(0, d_long, grad_long)
    encoder.mlp_back(1, d_short[:half_short], grad_short)
    enc_wide = links.scatter_sum(
        [
            (encoder.rows("normed_mlp"), encoder.halves("d_hidden")),
            (encoder.rows("d_branch_mlp"), encoder.halves("active")),
            (encoder.rows("d_branch_attn"), encoder.halves("attended")),
        ]
    )
    d_tokens = []
    for latent in (0, 1):
        encoder.attention_back(latent)
    for latent in (0, 1):
        own, _ = encoder.leave_back(latent, narrow=True)
        d_tokens.append(
            placed([(own, links.swap(own))], [kept_places[latent]], lengths[latent])
        )
    enc_qkv = links.scatter_sum([(encoder.rows("normed_attn"), encoder.halves("d_qkv"))])

    def gathered(block, gates):
        sums = []
        for latent in block.latents():
            chunks = block.members(latent)
            attn = sum(block.saved[c]["attn_sums"] for c in chunks)
            mlp = sum(block.saved[c]["mlp_sums"] for c in chunks)
            sums.append(jnp.stack([attn[1], attn[0], mlp[2], mlp[1], mlp[0], gates[latent]]))
        return jnp.stack(sums)

    dec_attn = [keep["attn_sums"] for keep in decoder.saved]
    d_mods = jnp.stack(
        [
            gathered(encoder, [dec_attn[0][2], dec_attn[2][2]]),
            gathered(decoder, [gate_sums[0] + gate_sums[1], gate_sums[2]]),
        ]
    )
    own_sums = jnp.concatenate(
        [
            d_mods.reshape(24, features),
            jnp.stack(
                [
                    sum(keep["mlp_sums"][3] for keep in encoder.saved),
                    sum(keep["mlp_sums"][3] for keep in decoder.saved),
                    dec_attn[0][3] + dec_attn[2][3],
                    sum(bias_sums),
                    dec_attn[1][4] + dec_attn[2][4],
                ]
            ),
        ]
    )
    own_sums = own_sums + links.swap(own_sums)
    d_mods = own_sums[:24].reshape(2, 2, dp_size, -1).astype(BF16)
    mine = links.exchange_relative(links.reorder(jnp.transpose(d_mods, (2, 1, 0, 3))))
    flat_mine = mine.reshape((-1,) + mine.shape[2:])
    grad_ada = jnp.einsum("nd,nlm->ldm", flat_acts, flat_mine, preferred_element_type=F32)
    grad_ada_bias = jnp.sum(flat_mine.astype(F32), axis=0)
    d_acts = jnp.einsum("nlm,ldm->nd", flat_mine, ada_weight, preferred_element_type=F32)
    d_act = links.sum_relative(d_acts.reshape(dp_size, 2, features))
    gate = jax.nn.sigmoid(cond)
    d_cond = (d_act * gate * (1.0 + cond * (1.0 - gate))).astype(BF16)

    def column_sums(block, name):
        return sum(jnp.sum(part.astype(F32), axis=0) for part in block.rows(name))

    qkv_sums = [column_sums(block, "d_qkv") for block in (encoder, decoder)]
    totals = jnp.concatenate(
        [own_sums[24:].reshape(-1)]
        + [column_sums(block, "d_hidden") for block in (encoder, decoder)]
        + [part for sums in qkv_sums for part in (sums[:local], sums[2 * local :])]
    )
    totals = links.sum_all(totals)
    proj_out = totals[: 2 * features].reshape(2, features)
    down_out = totals[2 * features : 4 * features].reshape(2, features)
    mask_out = totals[4 * features : 5 * features]
    first = 5 * features
    up_out = totals[first : first + 2 * wide].reshape(2, wide)
    first += 2 * wide
    qv_out = totals[first : first + 4 * local].reshape(2, 2, local)

    up_grad = jnp.stack([enc_wide[:, :wide], dec_wide[:, :wide]])
    down_grad = jnp.stack([enc_wide[:, wide : 2 * wide], dec_wide[:, wide : 2 * wide]])
    proj_grad = jnp.stack([enc_wide[:, 2 * wide :], dec_wide[:, 2 * wide :]])
    qkv_grad = jnp.stack([enc_qkv, dec_qkv]).reshape(2, -1, 3, local)

    return (
        results[0][None],
        results[1][None],
        d_tokens[0][None],
        d_tokens[1][None],
        d_cond[:1],
        d_cond[1:],
        grad_ada,
        grad_ada_bias,
        qkv_grad,
        qv_out,
        jnp.transpose(proj_grad, (0, 2, 1)),
        proj_out,
        up_grad,
        up_out,
        jnp.transpose(down_grad, (0, 2, 1)),
        down_out,
        mask_out,
    )


def solution(mesh):
    in_specs = (
        P("dp", None, None),
        P("dp", None, None),
        P("dp", None),
        P("dp", None),
        P("dp", None),
        P("dp", None),
        P(None, None, "dp"),
        P(None, "dp"),
        P(None, None, None, "tensor"),
        P(None, None, "tensor"),
        P(None, "tensor", None),
        P(),
        P(None, None, "tensor"),
        P(None, "tensor"),
        P(None, "tensor", None),
        P(),
        P(),
        P("dp", None, None),
        P("dp", None, None),
    )
    out_specs = (
        P("dp", None, None),
        P("dp", None, None),
        P("dp", None, None),
        P("dp", None, None),
        P("dp", None),
        P("dp", None),
        P(None, None, "dp"),
        P(None, "dp"),
        P(None, "dp", None, "tensor"),
        P(None, None, "tensor"),
        P(None, "tensor", "dp"),
        P(),
        P(None, "dp", "tensor"),
        P(None, "tensor"),
        P(None, "tensor", "dp"),
        P(),
        P(),
    )

    def step(*arguments):
        return on_device(mesh.shape["dp"], mesh.shape["tensor"], *arguments)

    return jax.shard_map(
        step, mesh=mesh, in_specs=in_specs, out_specs=out_specs, check_vma=False
    )
```

time: 790 us -> 752 us (0.952)
  matrix products: 261 us -> 33.5 us
  Pallas kernels: 0 us -> 171 us
  waiting for transfers between devices: 218 us -> 338 us
  other arithmetic: 109 us -> 34.5 us
  starting transfers between devices: 89 us -> 74.5 us
  local copies, waits for them, and re-layouts: 98.4 us -> 89.8 us
    dot_general x167 -> x17, matrix products: 251 us -> 23 us  [the longest x4 12.9 us: tn(): lax.dot_general(left, right, (((0,), (0,)), ((), ())), preferred_element_...]
    pallas_call x0 -> x61, Pallas kernels: none -> 171 us  [call(): pl.pallas_call(body, in_specs=[small] * len(scalars) + [fast] * len(opera...]
    ppermute x39 -> x27, waiting for transfers between devices: 127 us -> 190 us  [dp_move(): return lax.ppermute(value, 'dp', partners(self.dp_size, bit))]
    ppermute x20, waiting for transfers between devices: 87.6 us -> 138 us  [cross(): return lax.ppermute(value, 'tensor', partners(self.tensor_size, 2))]
    reduce_sum x53 -> x12, other arithmetic: 39.2 us -> 6.02 us  [the longest x2 3.37 us: on_device(): gate_sums.append(jnp.sum(d_out * branch, axis=0))]
    unnamed x712 -> x454, local copies, waits for them, and re-layouts: 26 us -> 51.8 us
    convert_element_type x18 -> x0, local copies, waits for them, and re-layouts: 24.2 us -> none  [the longest x8 17.7 us: dot(): return result.astype(out)]
    convert_element_type x31 -> x20, other arithmetic: 27.1 us -> 4.09 us  [joined(): near = (own.astype(F32) + moved.astype(F32)).astype(BF16)]
  transfers between devices with their start and end apart: 105 -> 93, of which waited for: 36 -> 47; matrix products, arithmetic and copies ran while one was open for 55% -> 12% of each run, Pallas kernels for 0% -> 22%
where the time goes in v2:
time: 752 us; the launch traced here: 745 us
  waiting for transfers between devices  338 us (45%)
  Pallas kernels  171 us (23%)
  local copies, waits for them, and re-layouts  89.8 us (12%)
  starting transfers between devices  74.5 us (10%)
  other arithmetic  34.5 us (5%)
  matrix products  33.5 us (4%)
    ppermute x27, waiting for transfers between devices, dp_move(): return lax.ppermute(value, 'dp', partners(self.dp_size, bit))  190 us
    pallas_call x61, Pallas kernels, call(): pl.pallas_call(body, in_specs=[small] * len(scalars) + [fast] * len(opera...  171 us
    ppermute x20, waiting for transfers between devices, cross(): return lax.ppermute(value, 'tensor', partners(self.tensor_size, 2))  138 us
    unnamed x454, local copies, waits for them, and re-layouts  51.8 us
    ppermute x27, starting transfers between devices, dp_move(): return lax.ppermute(value, 'dp', partners(self.dp_size, bit))  44.3 us
    ppermute x20, starting transfers between devices, cross(): return lax.ppermute(value, 'tensor', partners(self.tensor_size, 2))  21.3 us
    slice x20, local copies, waits for them, and re-layouts, halves(): found += [value[:middle], value[middle:]]  16.5 us
  transfers between devices with their start and end apart: 93, of which 47 were waited for; matrix products, arithmetic and copies ran while one was open for 12% of the time, Pallas kernels for 22%

profile of v2, /device:TPU:0, one launch (start us, length us, event | category | flops | bytes accessed | tf_op | source)
XLA Modules:
  0.0 745.0 jit_solution(13823364612075048472)
XLA Ops:
  29.3 3.3 fusion.23
  33.0 3.7 collective-permute-done.3
  59.6 4.1 collective-permute-done.28.far_ref.rest_1_
  73.4 3.3 collective-permute-done.31.far_ref.rest_1_
  86.0 5.0 attn_forward.5
  103.4 12.1 %collective-permute-done.8.far_ref.rest_1_ = bf16[256,1152]{1,0:T(8,128)(2,1)S(1)} collective-permute-done((bf16[256,1152]{1,0:T(8,128)(2,1)S(1)}, bf16[256,1152]{1,0:T(8,128)(2,1)S(1)}, u32[]{:S(2)}, u32[]{:S(2)}) %collective-permute-start.8) | collective-permute-done | bytes 589856 | tf_op jit(solution)/shard_map/ppermute | solution.py:541
  116.3 4.6 collective-permute-done.37
  122.2 4.1 mlp_forward.5
  133.5 7.6 %collective-permute-done.58.far_ref = bf16[128,1152]{1,0:T(8,128)(2,1)S(1)} collective-permute-done((bf16[128,1152]{1,0:T(8,128)(2,1)S(1)}, bf16[128,1152]{1,0:T(8,128)(2,1)S(1)}, u32[]{:S(2)}, u32[]{:S(2)}) %collective-permute-start.58) | collective-permute-done | bytes 294944 | tf_op jit(solution)/shard_map/ppermute | solution.py:541
  144.5 8.4 %collective-permute-done.11.far_ref.rest_1_ = bf16[256,1152]{1,0:T(8,128)(2,1)S(1)} collective-permute-done((bf16[256,1152]{1,0:T(8,128)(2,1)S(1)}, bf16[256,1152]{1,0:T(8,128)(2,1)S(1)}, u32[]{:S(2)}, u32[]{:S(2)}) %collective-permute-start.11) | collective-permute-done | bytes 589856 | tf_op jit(solution)/shard_map/ppermute | solution.py:541
  163.1 5.5 attn_forward.6
  168.8 5.9 attn_forward.7
  181.9 4.6 collective-permute-done.64.far_ref
  193.5 10.0 %collective-permute-done.15.far_ref.rest_1_ = bf16[256,1152]{1,0:T(8,128)(2,1)S(1)} collective-permute-done((bf16[256,1152]{1,0:T(8,128)(2,1)S(1)}, bf16[256,1152]{1,0:T(8,128)(2,1)S(1)}, u32[]{:S(2)}, u32[]{:S(2)}) %collective-permute-start.15) | collective-permute-done | bytes 589856 | tf_op jit(solution)/shard_map/ppermute | solution.py:541
  204.8 11.3 %collective-permute-done.21.far_ref.rest_1_ = bf16[256,1152]{1,0:T(8,128)(2,1)S(1)} collective-permute-done((bf16[256,1152]{1,0:T(8,128)(2,1)S(1)}, bf16[256,1152]{1,0:T(8,128)(2,1)S(1)}, u32[]{:S(2)}, u32[]{:S(2)}) %collective-permute-start.21) | collective-permute-done | bytes 589856 | tf_op jit(solution)/shard_map/ppermute | solution.py:541
  219.2 4.3 mlp_forward.6
  223.7 4.1 mlp_forward.7
  233.8 11.5 %collective-permute-done.18 = bf16[256,1152]{1,0:T(8,128)(2,1)S(1)} collective-permute-done((bf16[256,1152]{1,0:T(8,128)(2,1)S(1)}, bf16[256,1152]{1,0:T(8,128)(2,1)S(1)}, u32[]{:S(2)}, u32[]{:S(2)}) %collective-permute-start.18) | collective-permute-done | bytes 589856 | tf_op jit(solution)/shard_map/ppermute | solution.py:541
  245.3 12.2 %collective-permute-done.24 = bf16[256,1152]{1,0:T(8,128)(2,1)S(1)} collective-permute-done((bf16[256,1152]{1,0:T(8,128)(2,1)S(1)}, bf16[256,1152]{1,0:T(8,128)(2,1)S(1)}, u32[]{:S(2)}, u32[]{:S(2)}) %collective-permute-start.24) | collective-permute-done | bytes 589856 | tf_op jit(solution)/shard_map/ppermute | solution.py:541
  258.4 3.1 multiply_reduce_fusion
  264.9 3.5 mlp_backward.6
  268.6 3.7 mlp_backward.5
  278.0 12.6 %collective-permute-done.45.far_ref = bf16[256,1152]{1,0:T(8,128)(2,1)S(1)} collective-permute-done((bf16[256,1152]{1,0:T(8,128)(2,1)S(1)}, bf16[256,1152]{1,0:T(8,128)(2,1)S(1)}, u32[]{:S(2)}, u32[]{:S(2)}) %collective-permute-start.45) | collective-permute-done | bytes 589856 | tf_op jit(solution)/shard_map/ppermute | solution.py:541
  292.1 10.3 %collective-permute-done.41.far_ref = bf16[256,1152]{1,0:T(8,128)(2,1)S(1)} collective-permute-done((bf16[256,1152]{1,0:T(8,128)(2,1)S(1)}, bf16[256,1152]{1,0:T(8,128)(2,1)S(1)}, u32[]{:S(2)}, u32[]{:S(2)}) %collective-permute-start.41) | collective-permute-done | bytes 589856 | tf_op jit(solution)/shard_map/ppermute | solution.py:541
  305.9 18.7 %attn_backward.4 = (bf16[2,256,864]{2,1,0:T(8,128)(2,1)S(1)}, bf16[2,256,864]{2,1,0:T(8,128)(2,1)S(1)}) custom-call(bf16[2,256,864]{2,1,0:T(8,128)(2,1)S(1)} %copy-done.46, bf16[2,256,864]{2,1,0:T(8,128)(2,1)S(1)} %qkv_forward.7.refs_2_.refs_0_.refs_1_, f32[4,2,1,256]{3,2,1,0:T(1,128)S(1)} %get-tuple-element.183.refs_2_, ...), custom_call_target="tpu_custom_call" | custom-call | flops 6719275008 | bytes 7241728 | tf_op jit(solution)/shard_map/attn_backward/pallas_call | solution.py:48
  332.9 5.2 weight_grads.5
  339.4 4.4 collective-permute-done.48.far_ref
  368.0 18.7 %weight_grads.7 = (bf16[4,144,2592]{2,1,0:T(8,128)(2,1)S(1)}, bf16[4,144,2592]{2,1,0:T(8,128)(2,1)}) custom-call(s32[1]{0:T(128)} %bitcast.59.bit_ref, bf16[256,1152]{1,0:T(8,128)(2,1)S(1)} %copy-done.83, bf16[256,1152]{1,0:T(8,128)(2,1)S(1)} %copy-done.85, bf16[256,1152]{1,0:T(8,128)(2,1)S(1)} %copy-done.87, bf16[256,1152]{1,0:T(8,128)(2,1)S(1)} %copy-done.89, ...), custom_call_target="tpu_custom_call" | custom-call | flops 7644119040 | bytes 21454848 | tf_op jit(solution)/shard_map/weight_grads/pallas_call | solution.py:48
  389.9 4.7 mlp_backward.7
  402.7 9.8 %collective-permute-done.70.far_ref = bf16[256,1152]{1,0:T(8,128)(2,1)S(1)} collective-permute-done((bf16[256,1152]{1,0:T(8,128)(2,1)S(1)}, bf16[256,1152]{1,0:T(8,128)(2,1)S(1)}, u32[]{:S(2)}, u32[]{:S(2)}) %collective-permute-start.70) | collective-permute-done | bytes 589856 | tf_op jit(solution)/shard_map/ppermute | solution.py:541
  416.3 8.4 %collective-permute-done.51.far_ref = bf16[256,1152]{1,0:T(8,128)(2,1)} collective-permute-done((bf16[256,1152]{1,0:T(8,128)(2,1)}, bf16[256,1152]{1,0:T(8,128)(2,1)}, u32[]{:S(2)}, u32[]{:S(2)}) %collective-permute-start.51) | collective-permute-done | bytes 589856 | tf_op jit(solution)/shard_map/ppermute | solution.py:541
  427.3 3.5 ln_back.13
  435.4 8.5 %attn_backward.5.g_ref = bf16[2,256,864]{2,1,0:T(8,128)(2,1)S(1)} custom-call(bf16[2,256,864]{2,1,0:T(8,128)(2,1)S(1)} %copy-done.44, f32[4,2,1,256]{3,2,1,0:T(1,128)S(1)} %get-tuple-element.182.refs_1_, bf16[256,1152]{1,0:T(8,128)(2,1)} %get-tuple-element.202.refs_2_.refs_16_, bf16[256,1152]{1,0:T(8,128)(2,1)S(1)} %collective-permute-done.52.refs_3_.refs_17_, ...), custom_call_target="tpu_custom_call" | custom-call | flops 1849688064 | bytes 4284416 | tf_op jit(solution)/shard_map/attn_backward/pallas_call | solution.py:48
  449.0 20.1 %collective-permute-done.90.moved_ref = bf16[4,144,2592]{2,1,0:T(8,128)(2,1)} collective-permute-done((bf16[4,144,2592]{2,1,0:T(8,128)(2,1)}, bf16[4,144,2592]{2,1,0:T(8,128)(2,1)}, u32[]{:S(2)}, u32[]{:S(2)}) %collective-permute-start.90) | collective-permute-done | bytes 2986016 | tf_op jit(solution)/shard_map/ppermute | solution.py:544
  471.2 3.8 halve.14
  477.6 10.2 %weight_grads.6 = (bf16[4,144,2592]{2,1,0:T(8,128)(2,1)S(1)}, bf16[4,144,2592]{2,1,0:T(8,128)(2,1)S(1)}) custom-call(s32[1]{0:T(128)} %bitcast.59.bit_ref, bf16[256,1152]{1,0:T(8,128)(2,1)S(1)} %copy-done.79, bf16[256,1152]{1,0:T(8,128)(2,1)S(1)} %copy-done.81, bf16[64,1152]{1,0:T(8,128)(2,1)S(1)} %copy-done.135, bf16[64,1152]{1,0:T(8,128)(2,1)S(1)} %copy-done.137, ...), custom_call_target="tpu_custom_call" | custom-call | flops 3822059520 | bytes 13713408 | tf_op jit(solution)/shard_map/weight_grads/pallas_call | solution.py:48
  487.8 3.4 ln_back.14
  516.8 6.0 fusion.2
  524.0 76.7 %collective-permute-done.84 = f32[9216]{0:T(1024)S(1)} collective-permute-done((f32[9216]{0:T(1024)S(1)}, f32[9216]{0:T(1024)S(1)}, u32[]{:S(2)}, u32[]{:S(2)}) %collective-permute-start.84) | collective-permute-done | bytes 36896 | tf_op jit(solution)/shard_map/ppermute | solution.py:544
  608.7 3.8 collective-permute-done.83
  627.3 4.5 convolution_bitcast_fusion
  631.8 17.1 %collective-permute-done.76 = bf16[2,2,1152]{2,1,0:T(2,128)(2,1)S(1)} collective-permute-done((bf16[2,2,1152]{2,1,0:T(2,128)(2,1)S(1)}, bf16[2,2,1152]{2,1,0:T(2,128)(2,1)S(1)}, u32[]{:S(2)}, u32[]{:S(2)}) %collective-permute-start.76) | collective-permute-done | bytes 9248 | tf_op jit(solution)/shard_map/ppermute | solution.py:544
  648.9 5.1 collective-permute-start.86
  665.5 3.4 collective-permute-start.80
  671.3 31.2 %collective-permute-done.88.moved_ref = bf16[2,144,2592]{2,1,0:T(8,128)(2,1)S(1)} collective-permute-done((bf16[2,144,2592]{2,1,0:T(8,128)(2,1)S(1)}, bf16[2,144,2592]{2,1,0:T(8,128)(2,1)S(1)}, u32[]{:S(2)}, u32[]{:S(2)}) %collective-permute-start.88) | collective-permute-done | bytes 1493024 | tf_op jit(solution)/shard_map/ppermute | solution.py:544
  702.9 3.1 collective-permute-start.89
  710.1 4.3 fusion.3
  714.4 24.6 %collective-permute-done.89 = bf16[1,144,2592]{2,1,0:T(8,128)(2,1)} collective-permute-done((bf16[1,144,2592]{2,1,0:T(8,128)(2,1)S(1)}, bf16[1,144,2592]{2,1,0:T(8,128)(2,1)}, u32[]{:S(2)}, u32[]{:S(2)}) %collective-permute-start.89) | collective-permute-done | bytes 746528 | tf_op jit(solution)/shard_map/ppermute | solution.py:544
  (857 shorter events, 282.9 us)
Async XLA Ops:
  1.6 19.1 %collective-permute-start = (bf16[1,2,1152]{2,1,0:T(2,128)(2,1)S(1)}, bf16[1,2,1152]{2,1,0:T(2,128)(2,1)S(1)}, u32[]{:S(2)}, u32[]{:S(2)}) collective-permute-start(bf16[1,2,1152]{2,1,0:T(2,128)(2,1)S(1)} %fusion.69), channel_id=1, source_target_pairs={{0,4},{4,0},{8,12},{12,8},{16,20},{20,16},{24,28},{28,24},{1,5},{5... | collective-permute-start | bytes 13832 | tf_op jit(solution)/shard_map/ppermute | solution.py:544
  82.3 11.7 %collective-permute-start.13 = (bf16[256,1152]{1,0:T(8,128)(2,1)S(1)}, bf16[256,1152]{1,0:T(8,128)(2,1)S(1)}, u32[]{:S(2)}, u32[]{:S(2)}) collective-permute-start(bf16[256,1152]{1,0:T(8,128)(2,1)S(1)} %ln_open.4.own_ref.refs_2_), channel_id=1, source_target_pairs={{0,1},{1,0},{2,3},{3,2},{4,5},{5,4},{6,7},{7,6},{8,9},{9,8},{10,11... | collective-permute-start | bytes 1769480 | tf_op jit(solution)/shard_map/ppermute | solution.py:538
  99.3 16.3 %collective-permute-start.8 = (bf16[256,1152]{1,0:T(8,128)(2,1)S(1)}, bf16[256,1152]{1,0:T(8,128)(2,1)S(1)}, u32[]{:S(2)}, u32[]{:S(2)}) collective-permute-start(bf16[256,1152]{1,0:T(8,128)(2,1)S(1)} %add_convert_fusion.13.near_ref.rest_0_), channel_id=1, source_target_pairs={{0,2},{1,3},{2,0},{3,1},{4,6},{5,7},{6,4},{7,5},{8,10},{9,11},{10,... | collective-permute-start | bytes 1769480 | tf_op jit(solution)/shard_map/ppermute | solution.py:541
  100.9 20.0 %collective-permute-start.37 = (bf16[128,1152]{1,0:T(8,128)(2,1)S(1)}, bf16[128,1152]{1,0:T(8,128)(2,1)S(1)}, u32[]{:S(2)}, u32[]{:S(2)}) collective-permute-start(bf16[128,1152]{1,0:T(8,128)(2,1)S(1)} %add_convert_fusion.17), channel_id=1, source_target_pairs={{0,2},{1,3},{2,0},{3,1},{4,6},{5,7},{6,4},{7,5},{8,10},{9,11},{10,... | collective-permute-start | bytes 884744 | tf_op jit(solution)/shard_map/ppermute | solution.py:541
  130.6 12.6 %collective-permute-start.38 = (bf16[128,1152]{1,0:T(8,128)(2,1)S(1)}, bf16[128,1152]{1,0:T(8,128)(2,1)S(1)}, u32[]{:S(2)}, u32[]{:S(2)}) collective-permute-start(bf16[128,1152]{1,0:T(8,128)(2,1)S(1)} %get-tuple-element.358), channel_id=1, source_target_pairs={{0,1},{1,0},{2,3},{3,2},{4,5},{5,4},{6,7},{7,6},{8,9},{9,8},{10,11... | collective-permute-start | bytes 884744 | tf_op jit(solution)/shard_map/ppermute | solution.py:538
  131.2 9.9 %collective-permute-start.58 = (bf16[128,1152]{1,0:T(8,128)(2,1)S(1)}, bf16[128,1152]{1,0:T(8,128)(2,1)S(1)}, u32[]{:S(2)}, u32[]{:S(2)}) collective-permute-start(bf16[128,1152]{1,0:T(8,128)(2,1)S(1)} %add_convert_fusion.15.near_ref), channel_id=1, source_target_pairs={{0,2},{1,3},{2,0},{3,1},{4,6},{5,7},{6,4},{7,5},{8,10},{9,11},{10,... | collective-permute-start | bytes 884744 | tf_op jit(solution)/shard_map/ppermute | solution.py:541
  132.9 20.0 %collective-permute-start.11 = (bf16[256,1152]{1,0:T(8,128)(2,1)S(1)}, bf16[256,1152]{1,0:T(8,128)(2,1)S(1)}, u32[]{:S(2)}, u32[]{:S(2)}) collective-permute-start(bf16[256,1152]{1,0:T(8,128)(2,1)S(1)} %add_convert_fusion.12.near_ref.rest_0_), channel_id=1, source_target_pairs={{0,2},{1,3},{2,0},{3,1},{4,6},{5,7},{6,4},{7,5},{8,10},{9,11},{10,... | collective-permute-start | bytes 1769480 | tf_op jit(solution)/shard_map/ppermute | solution.py:541
  142.1 11.4 %collective-permute-start.59 = (bf16[128,1152]{1,0:T(8,128)(2,1)S(1)}, bf16[128,1152]{1,0:T(8,128)(2,1)S(1)}, u32[]{:S(2)}, u32[]{:S(2)}) collective-permute-start(bf16[128,1152]{1,0:T(8,128)(2,1)S(1)} %get-tuple-element.212.refs_2_.refs_28_), channel_id=1, source_target_pairs={{0,1},{1,0},{2,3},{3,2},{4,5},{5,4},{6,7},{7,6},{8,9},{9,8},{10,11... | collective-permute-start | bytes 884744 | tf_op jit(solution)/shard_map/ppermute | solution.py:538
  159.2 16.0 %collective-permute-start.61 = (bf16[128,1152]{1,0:T(8,128)(2,1)S(1)}, bf16[128,1152]{1,0:T(8,128)(2,1)S(1)}, u32[]{:S(2)}, u32[]{:S(2)}) collective-permute-start(bf16[128,1152]{1,0:T(8,128)(2,1)S(1)} %add_convert_fusion.14.near_ref), channel_id=1, source_target_pairs={{0,2},{1,3},{2,0},{3,1},{4,6},{5,7},{6,4},{7,5},{8,10},{9,11},{10,... | collective-permute-start | bytes 884744 | tf_op jit(solution)/shard_map/ppermute | solution.py:541
  168.7 18.5 %collective-permute-start.14 = (bf16[256,1152]{1,0:T(8,128)(2,1)S(1)}, bf16[256,1152]{1,0:T(8,128)(2,1)S(1)}, u32[]{:S(2)}, u32[]{:S(2)}) collective-permute-start(bf16[256,1152]{1,0:T(8,128)(2,1)S(1)} %get-tuple-element.157), channel_id=1, source_target_pairs={{0,1},{1,0},{2,3},{3,2},{4,5},{5,4},{6,7},{7,6},{8,9},{9,8},{10,11... | collective-permute-start | bytes 1769480 | tf_op jit(solution)/shard_map/ppermute | solution.py:538
  174.7 16.9 %collective-permute-start.20 = (bf16[256,1152]{1,0:T(8,128)(2,1)S(1)}, bf16[256,1152]{1,0:T(8,128)(2,1)S(1)}, u32[]{:S(2)}, u32[]{:S(2)}) collective-permute-start(bf16[256,1152]{1,0:T(8,128)(2,1)S(1)} %get-tuple-element.163), channel_id=1, source_target_pairs={{0,1},{1,0},{2,3},{3,2},{4,5},{5,4},{6,7},{7,6},{8,9},{9,8},{10,11... | collective-permute-start | bytes 1769480 | tf_op jit(solution)/shard_map/ppermute | solution.py:538
  187.3 16.2 %collective-permute-start.15 = (bf16[256,1152]{1,0:T(8,128)(2,1)S(1)}, bf16[256,1152]{1,0:T(8,128)(2,1)S(1)}, u32[]{:S(2)}, u32[]{:S(2)}) collective-permute-start(bf16[256,1152]{1,0:T(8,128)(2,1)S(1)} %add_convert_fusion.11.near_ref.rest_0_), channel_id=1, source_target_pairs={{0,2},{1,3},{2,0},{3,1},{4,6},{5,7},{6,4},{7,5},{8,10},{9,11},{10,... | collective-permute-start | bytes 1769480 | tf_op jit(solution)/shard_map/ppermute | solution.py:541
  191.4 12.7 %collective-permute-start.66 = (bf16[64,1152]{1,0:T(8,128)(2,1)S(1)}, bf16[64,1152]{1,0:T(8,128)(2,1)S(1)}, u32[]{:S(2)}, u32[]{:S(2)}) collective-permute-start(bf16[64,1152]{1,0:T(8,128)(2,1)S(1)} %get-tuple-element.223), channel_id=1, source_target_pairs={{0,1},{1,0},{2,3},{3,2},{4,5},{5,4},{6,7},{7,6},{8,9},{9,8},{10,11... | collective-permute-start | bytes 442376 | tf_op jit(solution)/shard_map/ppermute | solution.py:538
  191.8 24.3 %collective-permute-start.21 = (bf16[256,1152]{1,0:T(8,128)(2,1)S(1)}, bf16[256,1152]{1,0:T(8,128)(2,1)S(1)}, u32[]{:S(2)}, u32[]{:S(2)}) collective-permute-start(bf16[256,1152]{1,0:T(8,128)(2,1)S(1)} %add_convert_fusion.8.near_ref.rest_0_), channel_id=1, source_target_pairs={{0,2},{1,3},{2,0},{3,1},{4,6},{5,7},{6,4},{7,5},{8,10},{9,11},{10,... | collective-permute-start | bytes 1769480 | tf_op jit(solution)/shard_map/ppermute | solution.py:541
  204.1 15.1 %collective-permute-start.16 = (bf16[256,1152]{1,0:T(8,128)(2,1)S(1)}, bf16[256,1152]{1,0:T(8,128)(2,1)S(1)}, u32[]{:S(2)}, u32[]{:S(2)}) collective-permute-start(bf16[256,1152]{1,0:T(8,128)(2,1)S(1)} %get-tuple-element.159.own_ref.refs_0_), channel_id=1, source_target_pairs={{0,1},{1,0},{2,3},{3,2},{4,5},{5,4},{6,7},{7,6},{8,9},{9,8},{10,11... | collective-permute-start | bytes 1769480 | tf_op jit(solution)/shard_map/ppermute | solution.py:538
  204.2 14.7 %collective-permute-start.67 = (bf16[64,1152]{1,0:T(8,128)(2,1)S(1)}, bf16[64,1152]{1,0:T(8,128)(2,1)S(1)}, u32[]{:S(2)}, u32[]{:S(2)}) collective-permute-start(bf16[64,1152]{1,0:T(8,128)(2,1)S(1)} %add_convert_fusion.19.near_ref), channel_id=1, source_target_pairs={{0,2},{1,3},{2,0},{3,1},{4,6},{5,7},{6,4},{7,5},{8,10},{9,11},{10,... | collective-permute-start | bytes 442376 | tf_op jit(solution)/shard_map/ppermute | solution.py:541
  229.1 16.2 %collective-permute-start.18 = (bf16[256,1152]{1,0:T(8,128)(2,1)S(1)}, bf16[256,1152]{1,0:T(8,128)(2,1)S(1)}, u32[]{:S(2)}, u32[]{:S(2)}) collective-permute-start(bf16[256,1152]{1,0:T(8,128)(2,1)S(1)} %add_convert_fusion.10), channel_id=1, source_target_pairs={{0,2},{1,3},{2,0},{3,1},{4,6},{5,7},{6,4},{7,5},{8,10},{9,11},{10,... | collective-permute-start | bytes 1769480 | tf_op jit(solution)/shard_map/ppermute | solution.py:541
  230.1 27.4 %collective-permute-start.24 = (bf16[256,1152]{1,0:T(8,128)(2,1)S(1)}, bf16[256,1152]{1,0:T(8,128)(2,1)S(1)}, u32[]{:S(2)}, u32[]{:S(2)}) collective-permute-start(bf16[256,1152]{1,0:T(8,128)(2,1)S(1)} %add_convert_fusion.7), channel_id=1, source_target_pairs={{0,2},{1,3},{2,0},{3,1},{4,6},{5,7},{6,4},{7,5},{8,10},{9,11},{10,... | collective-permute-start | bytes 1769480 | tf_op jit(solution)/shard_map/ppermute | solution.py:541
  264.4 247.7 %collective-permute-start.19 = (bf16[256,1152]{1,0:T(8,128)(2,1)}, bf16[256,1152]{1,0:T(8,128)(2,1)}, u32[]{:S(2)}, u32[]{:S(2)}) collective-permute-start(bf16[256,1152]{1,0:T(8,128)(2,1)} %get-tuple-element.333), channel_id=1, source_target_pairs={{0,1},{1,0},{2,3},{3,2},{4,5},{5,4},{6,7},{7,6},{8,9},{9,8},{10,11... | collective-permute-start | bytes 1769480 | tf_op jit(solution)/shard_map/ppermute | solution.py:538
  264.4 249.2 %collective-permute-start.25 = (bf16[256,1152]{1,0:T(8,128)(2,1)}, bf16[256,1152]{1,0:T(8,128)(2,1)}, u32[]{:S(2)}, u32[]{:S(2)}) collective-permute-start(bf16[256,1152]{1,0:T(8,128)(2,1)} %get-tuple-element.334), channel_id=1, source_target_pairs={{0,1},{1,0},{2,3},{3,2},{4,5},{5,4},{6,7},{7,6},{8,9},{9,8},{10,11... | collective-permute-start | bytes 1769480 | tf_op jit(solution)/shard_map/ppermute | solution.py:538
  274.4 16.2 %collective-permute-start.45 = (bf16[256,1152]{1,0:T(8,128)(2,1)S(1)}, bf16[256,1152]{1,0:T(8,128)(2,1)S(1)}, u32[]{:S(2)}, u32[]{:S(2)}) collective-permute-start(bf16[256,1152]{1,0:T(8,128)(2,1)S(1)} %add_convert_fusion.4.near_ref), channel_id=1, source_target_pairs={{0,2},{1,3},{2,0},{3,1},{4,6},{5,7},{6,4},{7,5},{8,10},{9,11},{10,... | collective-permute-start | bytes 1769480 | tf_op jit(solution)/shard_map/ppermute | solution.py:541
  275.1 27.3 %collective-permute-start.41 = (bf16[256,1152]{1,0:T(8,128)(2,1)S(1)}, bf16[256,1152]{1,0:T(8,128)(2,1)S(1)}, u32[]{:S(2)}, u32[]{:S(2)}) collective-permute-start(bf16[256,1152]{1,0:T(8,128)(2,1)S(1)} %add_convert_fusion.5.near_ref), channel_id=1, source_target_pairs={{0,2},{1,3},{2,0},{3,1},{4,6},{5,7},{6,4},{7,5},{8,10},{9,11},{10,... | collective-permute-start | bytes 1769480 | tf_op jit(solution)/shard_map/ppermute | solution.py:541
  292.0 13.2 %collective-permute-start.46 = (bf16[256,1152]{1,0:T(8,128)(2,1)S(1)}, bf16[256,1152]{1,0:T(8,128)(2,1)S(1)}, u32[]{:S(2)}, u32[]{:S(2)}) collective-permute-start(bf16[256,1152]{1,0:T(8,128)(2,1)S(1)} %get-tuple-element.192.refs_6_.refs_26_), channel_id=1, source_target_pairs={{0,1},{1,0},{2,3},{3,2},{4,5},{5,4},{6,7},{7,6},{8,9},{9,8},{10,11... | collective-permute-start | bytes 1769480 | tf_op jit(solution)/shard_map/ppermute | solution.py:538
  328.3 15.4 %collective-permute-start.48 = (bf16[256,1152]{1,0:T(8,128)(2,1)S(1)}, bf16[256,1152]{1,0:T(8,128)(2,1)S(1)}, u32[]{:S(2)}, u32[]{:S(2)}) collective-permute-start(bf16[256,1152]{1,0:T(8,128)(2,1)S(1)} %add_convert_fusion.3.near_ref), channel_id=1, source_target_pairs={{0,2},{1,3},{2,0},{3,1},{4,6},{5,7},{6,4},{7,5},{8,10},{9,11},{10,... | collective-permute-start | bytes 1769480 | tf_op jit(solution)/shard_map/ppermute | solution.py:541
  331.3 63.8 %collective-permute-start.69 = (bf16[256,1152]{1,0:T(8,128)(2,1)}, bf16[256,1152]{1,0:T(8,128)(2,1)}, u32[]{:S(2)}, u32[]{:S(2)}) collective-permute-start(bf16[256,1152]{1,0:T(8,128)(2,1)} %get-tuple-element.234), channel_id=1, source_target_pairs={{0,1},{1,0},{2,3},{3,2},{4,5},{5,4},{6,7},{7,6},{8,9},{9,8},{10,11... | collective-permute-start | bytes 1769480 | tf_op jit(solution)/shard_map/ppermute | solution.py:538
  339.1 60.9 %collective-permute-start.81 = (bf16[4,144,864]{2,1,0:T(8,128)(2,1)}, bf16[4,144,864]{2,1,0:T(8,128)(2,1)}, u32[]{:S(2)}, u32[]{:S(2)}) collective-permute-start(bf16[4,144,864]{2,1,0:T(8,128)(2,1)} %get-tuple-element.247), channel_id=1, source_target_pairs={{0,4},{4,0},{8,12},{12,8},{16,20},{20,16},{24,28},{28,24},{1,5},{5... | collective-permute-start | bytes 2985992 | tf_op jit(solution)/shard_map/ppermute | solution.py:544
  347.6 39.4 %collective-permute-start.49 = (bf16[256,1152]{1,0:T(8,128)(2,1)}, bf16[256,1152]{1,0:T(8,128)(2,1)S(1)}, u32[]{:S(2)}, u32[]{:S(2)}) collective-permute-start(bf16[256,1152]{1,0:T(8,128)(2,1)} %get-tuple-element.197.own_ref.refs_8_), channel_id=1, source_target_pairs={{0,1},{1,0},{2,3},{3,2},{4,5},{5,4},{6,7},{7,6},{8,9},{9,8},{10,11... | collective-permute-start | bytes 1769480 | tf_op jit(solution)/shard_map/ppermute | solution.py:538
  396.4 16.2 %collective-permute-start.70 = (bf16[256,1152]{1,0:T(8,128)(2,1)S(1)}, bf16[256,1152]{1,0:T(8,128)(2,1)S(1)}, u32[]{:S(2)}, u32[]{:S(2)}) collective-permute-start(bf16[256,1152]{1,0:T(8,128)(2,1)S(1)} %add_convert_fusion.near_ref), channel_id=1, source_target_pairs={{0,2},{1,3},{2,0},{3,1},{4,6},{5,7},{6,4},{7,5},{8,10},{9,11},{10,... | collective-permute-start | bytes 1769480 | tf_op jit(solution)/shard_map/ppermute | solution.py:541
  398.0 26.8 %collective-permute-start.51 = (bf16[256,1152]{1,0:T(8,128)(2,1)}, bf16[256,1152]{1,0:T(8,128)(2,1)}, u32[]{:S(2)}, u32[]{:S(2)}) collective-permute-start(bf16[256,1152]{1,0:T(8,128)(2,1)} %add_convert_fusion.2.near_ref), channel_id=1, source_target_pairs={{0,2},{1,3},{2,0},{3,1},{4,6},{5,7},{6,4},{7,5},{8,10},{9,11},{10,... | collective-permute-start | bytes 1769480 | tf_op jit(solution)/shard_map/ppermute | solution.py:541
  400.1 69.1 %collective-permute-start.90 = (bf16[4,144,2592]{2,1,0:T(8,128)(2,1)}, bf16[4,144,2592]{2,1,0:T(8,128)(2,1)}, u32[]{:S(2)}, u32[]{:S(2)}) collective-permute-start(bf16[4,144,2592]{2,1,0:T(8,128)(2,1)} %get-tuple-element.274), channel_id=1, source_target_pairs={{0,4},{4,0},{8,12},{12,8},{16,20},{20,16},{24,28},{28,24},{1,5},{5... | collective-permute-start | bytes 8957960 | tf_op jit(solution)/shard_map/ppermute | solution.py:544
  412.6 101.6 %collective-permute-start.82 = (bf16[2,144,864]{2,1,0:T(8,128)(2,1)}, bf16[2,144,864]{2,1,0:T(8,128)(2,1)}, u32[]{:S(2)}, u32[]{:S(2)}) collective-permute-start(bf16[2,144,864]{2,1,0:T(8,128)(2,1)} %get-tuple-element.249), channel_id=1, source_target_pairs={{0,8},{4,12},{8,0},{12,4},{16,24},{20,28},{24,16},{28,20},{1,9},{5... | collective-permute-start | bytes 1493000 | tf_op jit(solution)/shard_map/ppermute | solution.py:544
  447.7 40.1 %collective-permute-start.54 = (bf16[256,1152]{1,0:T(8,128)(2,1)S(1)}, bf16[256,1152]{1,0:T(8,128)(2,1)}, u32[]{:S(2)}, u32[]{:S(2)}) collective-permute-start(bf16[256,1152]{1,0:T(8,128)(2,1)S(1)} %add_convert_fusion.1.near_ref), channel_id=1, source_target_pairs={{0,2},{1,3},{2,0},{3,1},{4,6},{5,7},{6,4},{7,5},{8,10},{9,11},{10,... | collective-permute-start | bytes 1769480 | tf_op jit(solution)/shard_map/ppermute | solution.py:541
  475.0 141.7 %collective-permute-start.91 = (bf16[2,144,2592]{2,1,0:T(8,128)(2,1)}, bf16[2,144,2592]{2,1,0:T(8,128)(2,1)}, u32[]{:S(2)}, u32[]{:S(2)}) collective-permute-start(bf16[2,144,2592]{2,1,0:T(8,128)(2,1)} %get-tuple-element.276), channel_id=1, source_target_pairs={{0,8},{4,12},{8,0},{12,4},{16,24},{20,28},{24,16},{28,20},{1,9},{5... | collective-permute-start | bytes 4478984 | tf_op jit(solution)/shard_map/ppermute | solution.py:544
  499.2 11.4 %collective-permute-start.73 = (bf16[2,2,2,2,864]{4,3,2,0,1:T(2,128)(2,1)}, bf16[2,2,2,2,864]{4,3,2,0,1:T(2,128)(2,1)}, u32[]{:S(2)}, u32[]{:S(2)}) collective-permute-start(bf16[2,2,2,2,864]{4,3,2,0,1:T(2,128)(2,1)} %get-tuple-element.386), channel_id=1, source_target_pairs={{0,8},{4,12},{8,0},{12,4},{16,24},{20,28},{24,16},{28,20},{1,9},{5... | collective-permute-start | bytes 82952 | tf_op jit(solution)/shard_map/ppermute | solution.py:544
  510.6 149.6 %collective-permute-start.87 = (bf16[4,144,2592]{2,1,0:T(8,128)(2,1)}, bf16[4,144,2592]{2,1,0:T(8,128)(2,1)}, u32[]{:S(2)}, u32[]{:S(2)}) collective-permute-start(bf16[4,144,2592]{2,1,0:T(8,128)(2,1)} %copy-done.154), channel_id=1, source_target_pairs={{0,4},{4,0},{8,12},{12,8},{16,20},{20,16},{24,28},{28,24},{1,5},{5... | collective-permute-start | bytes 8957960 | tf_op jit(solution)/shard_map/ppermute | solution.py:544
  512.0 110.1 %collective-permute-start.78 = (bf16[4,144,864]{2,1,0:T(8,128)(2,1)}, bf16[4,144,864]{2,1,0:T(8,128)(2,1)}, u32[]{:S(2)}, u32[]{:S(2)}) collective-permute-start(bf16[4,144,864]{2,1,0:T(8,128)(2,1)} %copy-done.155), channel_id=1, source_target_pairs={{0,4},{4,0},{8,12},{12,8},{16,20},{20,16},{24,28},{28,24},{1,5},{5... | collective-permute-start | bytes 2985992 | tf_op jit(solution)/shard_map/ppermute | solution.py:544
  513.6 87.0 %collective-permute-start.84 = (f32[9216]{0:T(1024)S(1)}, f32[9216]{0:T(1024)S(1)}, u32[]{:S(2)}, u32[]{:S(2)}) collective-permute-start(f32[9216]{0:T(1024)S(1)} %concatenate.124), channel_id=1, source_target_pairs={{0,4},{4,0},{8,12},{12,8},{16,20},{20,16},{24,28},{28,24},{1,5},{5... | collective-permute-start | bytes 110600 | tf_op jit(solution)/shard_map/ppermute | solution.py:544
  514.1 89.2 %collective-permute-start.74 = (bf16[1,4,2,2,864]{4,2,1,3,0:T(2,128)(2,1)S(1)}, bf16[1,4,2,2,864]{4,2,1,3,0:T(2,128)(2,1)S(1)}, u32[]{:S(2)}, u32[]{:S(2)}) collective-permute-start(bf16[1,4,2,2,864]{4,2,1,3,0:T(2,128)(2,1)S(1)} %bitcast.211), channel_id=1, source_target_pairs={{0,16},{4,20},{8,24},{12,28},{16,0},{20,4},{24,8},{28,12},{1,17},{... | collective-permute-start | bytes 82952 | tf_op jit(solution)/shard_map/ppermute | solution.py:544
  600.7 11.8 %collective-permute-start.83 = (bf16[1,144,864]{2,1,0:T(8,128)(2,1)S(1)}, bf16[1,144,864]{2,1,0:T(8,128)(2,1)}, u32[]{:S(2)}, u32[]{:S(2)}) collective-permute-start(bf16[1,144,864]{2,1,0:T(8,128)(2,1)S(1)} %get-tuple-element.251), channel_id=1, source_target_pairs={{0,16},{4,20},{8,24},{12,28},{16,0},{20,4},{24,8},{28,12},{1,17},{... | collective-permute-start | bytes 746504 | tf_op jit(solution)/shard_map/ppermute | solution.py:544
  603.4 23.2 %collective-permute-start.85 = (f32[9216]{0:T(1024)S(1)}, f32[9216]{0:T(1024)S(1)}, u32[]{:S(2)}, u32[]{:S(2)}) collective-permute-start(f32[9216]{0:T(1024)S(1)} %add.463), channel_id=1, source_target_pairs={{0,8},{4,12},{8,0},{12,4},{16,24},{20,28},{24,16},{28,20},{1,9},{5... | collective-permute-start | bytes 110600 | tf_op jit(solution)/shard_map/ppermute | solution.py:544
  612.5 14.1 %collective-permute-start.75 = (bf16[4,2,1152]{2,1,0:T(2,128)(2,1)S(1)}, bf16[4,2,1152]{2,1,0:T(2,128)(2,1)S(1)}, u32[]{:S(2)}, u32[]{:S(2)}) collective-permute-start(bf16[4,2,1152]{2,1,0:T(2,128)(2,1)S(1)} %convert_element_type.506), channel_id=1, source_target_pairs={{0,16},{4,20},{8,24},{12,28},{16,0},{20,4},{24,8},{28,12},{1,17},{... | collective-permute-start | bytes 55304 | tf_op jit(solution)/shard_map/ppermute | solution.py:544
  619.2 49.6 %collective-permute-start.92 = (bf16[1,144,2592]{2,1,0:T(8,128)(2,1)}, bf16[1,144,2592]{2,1,0:T(8,128)(2,1)}, u32[]{:S(2)}, u32[]{:S(2)}) collective-permute-start(bf16[1,144,2592]{2,1,0:T(8,128)(2,1)} %get-tuple-element.278), channel_id=1, source_target_pairs={{0,16},{4,20},{8,24},{12,28},{16,0},{20,4},{24,8},{28,12},{1,17},{... | collective-permute-start | bytes 2239496 | tf_op jit(solution)/shard_map/ppermute | solution.py:544
  625.1 39.2 %collective-permute-start.79 = (bf16[2,144,864]{2,1,0:T(8,128)(2,1)}, bf16[2,144,864]{2,1,0:T(8,128)(2,1)}, u32[]{:S(2)}, u32[]{:S(2)}) collective-permute-start(bf16[2,144,864]{2,1,0:T(8,128)(2,1)} %get-tuple-element.243), channel_id=1, source_target_pairs={{0,8},{4,12},{8,0},{12,4},{16,24},{20,28},{24,16},{28,20},{1,9},{5... | collective-permute-start | bytes 1493000 | tf_op jit(solution)/shard_map/ppermute | solution.py:544
  626.6 83.5 %collective-permute-start.55 = (bf16[256,1152]{1,0:T(8,128)(2,1)}, bf16[256,1152]{1,0:T(8,128)(2,1)}, u32[]{:S(2)}, u32[]{:S(2)}) collective-permute-start(bf16[256,1152]{1,0:T(8,128)(2,1)} %get-tuple-element.206), channel_id=1, source_target_pairs={{0,1},{1,0},{2,3},{3,2},{4,5},{5,4},{6,7},{7,6},{8,9},{9,8},{10,11... | collective-permute-start | bytes 1769480 | tf_op jit(solution)/shard_map/ppermute | solution.py:538
  626.7 22.2 %collective-permute-start.76 = (bf16[2,2,1152]{2,1,0:T(2,128)(2,1)S(1)}, bf16[2,2,1152]{2,1,0:T(2,128)(2,1)S(1)}, u32[]{:S(2)}, u32[]{:S(2)}) collective-permute-start(bf16[2,2,1152]{2,1,0:T(2,128)(2,1)S(1)} %slice.664), channel_id=1, source_target_pairs={{0,8},{4,12},{8,0},{12,4},{16,24},{20,28},{24,16},{28,20},{1,9},{5... | collective-permute-start | bytes 27656 | tf_op jit(solution)/shard_map/ppermute | solution.py:544
  662.9 39.7 %collective-permute-start.88 = (bf16[2,144,2592]{2,1,0:T(8,128)(2,1)S(1)}, bf16[2,144,2592]{2,1,0:T(8,128)(2,1)S(1)}, u32[]{:S(2)}, u32[]{:S(2)}) collective-permute-start(bf16[2,144,2592]{2,1,0:T(8,128)(2,1)S(1)} %get-tuple-element.264), channel_id=1, source_target_pairs={{0,8},{4,12},{8,0},{12,4},{16,24},{20,28},{24,16},{28,20},{1,9},{5... | collective-permute-start | bytes 4478984 | tf_op jit(solution)/shard_map/ppermute | solution.py:544
  665.5 40.6 %collective-permute-start.80 = (bf16[1,144,864]{2,1,0:T(8,128)(2,1)S(1)}, bf16[1,144,864]{2,1,0:T(8,128)(2,1)S(1)}, u32[]{:S(2)}, u32[]{:S(2)}) collective-permute-start(bf16[1,144,864]{2,1,0:T(8,128)(2,1)S(1)} %get-tuple-element.245), channel_id=1, source_target_pairs={{0,16},{4,20},{8,24},{12,28},{16,0},{20,4},{24,8},{28,12},{1,17},{... | collective-permute-start | bytes 746504 | tf_op jit(solution)/shard_map/ppermute | solution.py:544
  702.9 36.1 %collective-permute-start.89 = (bf16[1,144,2592]{2,1,0:T(8,128)(2,1)S(1)}, bf16[1,144,2592]{2,1,0:T(8,128)(2,1)}, u32[]{:S(2)}, u32[]{:S(2)}) collective-permute-start(bf16[1,144,2592]{2,1,0:T(8,128)(2,1)S(1)} %get-tuple-element.266), channel_id=1, source_target_pairs={{0,16},{4,20},{8,24},{12,28},{16,0},{20,4},{24,8},{28,12},{1,17},{... | collective-permute-start | bytes 2239496 | tf_op jit(solution)/shard_map/ppermute | solution.py:544
  (271 other events, 1430.6 us)

commit v3 on v2

v3 whole, which is shorter than its diff:
```python
import math

import jax
import jax.numpy as jnp
from jax import lax
from jax.experimental import pallas as pl
from jax.experimental.pallas import tpu as pltpu
from jax.sharding import PartitionSpec as P

HEAD_DIM = 72
EPSILON = 1e-06
BF16 = jnp.bfloat16
F32 = jnp.float32
MIB = 1 << 20
SCALING = HEAD_DIM**-0.5
EXPONENT = SCALING * math.log2(math.e)
GELU_A = math.sqrt(2.0 / math.pi)
GELU_B = 0.044715

SHIFT_ATTN, SCALE_ATTN, GATE_ATTN, SHIFT_MLP, SCALE_MLP, GATE_MLP = range(6)
PROJ_BIAS, DOWN_BIAS, UP_BIAS, QKV_BIAS = 0, 2, 4, 6


def nn(left, right):
    return lax.dot_general(left, right, (((1,), (0,)), ((), ())), preferred_element_type=F32)


def nt(left, right):
    return lax.dot_general(left, right, (((1,), (1,)), ((), ())), preferred_element_type=F32)


def tn(left, right):
    return lax.dot_general(left, right, (((0,), (0,)), ((), ())), preferred_element_type=F32)


def shaped(shape, dtype=BF16):
    return jax.ShapeDtypeStruct(shape, dtype)


class Queue:
    def __init__(self):
        self.token = jnp.zeros((8, 128), F32)

    def tie(self, *values):
        *values, self.token = lax.optimization_barrier((*values, self.token))
        return values[0] if len(values) == 1 else tuple(values)

    def call(self, body, operands, outs, name, scalars=(), far=(), scratch=(), limit=16):
        fast = pl.BlockSpec(memory_space=pltpu.VMEM)
        small = pl.BlockSpec(memory_space=pltpu.SMEM)
        anywhere = pl.BlockSpec(memory_space=pl.ANY)
        inputs = len(scalars) + len(far) + len(operands)

        def whole(token_ref, *refs):
            body(*refs[: inputs + len(outs)], *refs[inputs + len(outs) + 1 :])
            refs[inputs + len(outs)][...] = token_ref[...]

        *results, self.token = pl.pallas_call(
            whole,
            in_specs=[fast] + [small] * len(scalars) + [anywhere] * len(far) + [fast] * len(operands),
            out_specs=[fast] * (len(outs) + 1),
            out_shape=[*outs, shaped((8, 128), F32)],
            scratch_shapes=list(scratch),
            cost_estimate=pl.CostEstimate(flops=1000, transcendentals=0, bytes_accessed=1000),
            compiler_params=pltpu.CompilerParams(vmem_limit_bytes=limit * MIB),
            name=name,
        )(
            pltpu.with_memory_space_constraint(self.token, pltpu.VMEM),
            *scalars,
            *far,
            *[pltpu.with_memory_space_constraint(value, pltpu.VMEM) for value in operands],
        )
        return results


def normed_of(values):
    center = values - jnp.mean(values, axis=-1, keepdims=True)
    spread = jnp.mean(center * center, axis=-1, keepdims=True)
    scale = lax.rsqrt(spread + EPSILON)
    return center * scale, scale


def modulate(values, mods_ref, at, scale_part, shift_part):
    block, latent = at
    scale = mods_ref[block, latent, scale_part : scale_part + 1, :]
    shift = mods_ref[block, latent, shift_part : shift_part + 1, :]
    return (normed_of(values)[0] * (1.0 + scale) + shift).astype(BF16)


def branch_of(near_ref, far_ref, small_ref, row, features):
    return (
        near_ref[...].astype(F32)
        + far_ref[...].astype(F32)
        + small_ref[row : row + 1, :features]
    )


class Rows:
    def __init__(self, *spans):
        self.spans = spans
        self.count = sum(span[2] for span in spans)

    def places(self, perm_ref, core, other=False):
        found = []
        for first, stride, count in self.spans:
            low = perm_ref[:, first : first + count]
            high = perm_ref[:, first + stride : first + stride + count]
            found.append(jnp.where((core == 1) != other, high, low))
        return found[0] if len(found) == 1 else jnp.concatenate(found, axis=1)


def pick_columns(places, length):
    index = lax.broadcasted_iota(jnp.int32, (length, places.shape[1]), 0)
    return (index == places).astype(F32).astype(BF16)


def gather_rows(queue, core, perm, source, rows):
    length, features = source.shape

    def body(core_ref, perm_ref, source_ref, out_ref):
        pick = pick_columns(rows.places(perm_ref, core_ref[0]), length)
        out_ref[...] = tn(pick, source_ref[...])

    outs = [shaped((rows.count, features), F32)]
    return queue.call(body, [perm, source], outs, "gather_rows", scalars=[core])[0]


def place_rows(queue, core, perm, pairs, rows):
    length = perm.shape[1]
    features = pairs[0][0].shape[1]

    def body(core_ref, perm_ref, *refs):
        out_ref = refs[-1]
        places = [
            chunk.places(perm_ref, core_ref[0], other) for chunk in rows for other in (False, True)
        ]
        values = jnp.concatenate([ref[...] for ref in refs[:-1]], axis=0)
        pick = pick_columns(jnp.concatenate(places, axis=1), length)
        out_ref[...] = nn(pick, values).astype(BF16)

    operands = [perm] + [half for pair in pairs for half in pair]
    outs = [shaped((length, features))]
    return queue.call(body, operands, outs, "place_rows", scalars=[core], limit=24)[0]


def table_rows(queue, core, perm, waves, rows, filler=None):
    side, half = waves.shape

    def body(core_ref, perm_ref, waves_ref, *refs):
        places = rows.places(perm_ref, core_ref[0])
        index = lax.broadcasted_iota(jnp.int32, (side, places.shape[1]), 0)
        row_pick = ((places >= index * side) & (places < (index + 1) * side)).astype(F32)
        row = jnp.sum(row_pick * index.astype(F32), axis=0, keepdims=True)
        col_pick = (index.astype(F32) == places.astype(F32) - row * side).astype(F32)
        for low, pick in ((0, row_pick), (half, col_pick)):
            out = lax.dot_general(
                pick,
                waves_ref[...],
                (((0,), (0,)), ((), ())),
                precision=lax.Precision.HIGHEST,
                preferred_element_type=F32,
            )
            if filler is not None:
                out = out + refs[0][:, low : low + half]
            refs[-1][:, low : low + half] = out

    operands = [perm, waves] + ([] if filler is None else [filler])
    outs = [shaped((rows.count, 2 * half), F32)]
    return queue.call(body, operands, outs, "table_rows", scalars=[core])[0]


def ln_open(queue, stream, mods, at):
    def body(x_ref, mods_ref, out_ref):
        out_ref[...] = modulate(x_ref[...], mods_ref, at, SCALE_ATTN, SHIFT_ATTN)

    return queue.call(body, [stream, mods], [shaped(stream.shape)], "ln_open")[0]


def near_sum(queue, own, moved):
    def body(own_ref, moved_ref, out_ref):
        out_ref[...] = (own_ref[...].astype(F32) + moved_ref[...].astype(F32)).astype(BF16)

    return queue.call(body, [own, moved], [shaped(own.shape)], "near_sum")[0]


def merge_attn(queue, stream, near, far, small, mods, at):
    features = stream.shape[1]
    block, latent = at

    def body(x_ref, near_ref, far_ref, small_ref, mods_ref, mid_ref, out_ref):
        branch = branch_of(near_ref, far_ref, small_ref, PROJ_BIAS + block, features)
        middle = x_ref[...] + mods_ref[block, latent, GATE_ATTN : GATE_ATTN + 1, :] * branch
        mid_ref[...] = middle
        out_ref[...] = modulate(middle, mods_ref, at, SCALE_MLP, SHIFT_MLP)

    outs = [shaped(stream.shape, F32), shaped(stream.shape)]
    return queue.call(body, [stream, near, far, small, mods], outs, "merge_attn")


def merge_mlp(queue, pieces, small, mods, at, table, tail):
    features = table.shape[1]
    counts = [piece[0].shape[0] for piece in pieces]
    block, latent = at
    total = sum(counts) + (0 if tail is None else tail.shape[0])
    following = (block + 1, latent)

    def body(table_ref, small_ref, mods_ref, *refs):
        x_ref, out_ref = refs[-2:]
        gate = mods_ref[block, latent, GATE_MLP : GATE_MLP + 1, :]
        first = 0
        for index, count in enumerate(counts):
            mid_ref, near_ref, far_ref = refs[3 * index : 3 * index + 3]
            branch = branch_of(near_ref, far_ref, small_ref, DOWN_BIAS + block, features)
            stream = mid_ref[...] + gate * branch + table_ref[first : first + count, :]
            x_ref[first : first + count, :] = stream
            out_ref[first : first + count, :] = modulate(
                stream, mods_ref, following, SCALE_ATTN, SHIFT_ATTN
            )
            first += count
        if tail is not None:
            stream = refs[3 * len(counts)][...]
            x_ref[first:, :] = stream
            out_ref[first:, :] = modulate(stream, mods_ref, following, SCALE_ATTN, SHIFT_ATTN)

    operands = [table, small, mods] + [part for piece in pieces for part in piece]
    operands += [] if tail is None else [tail]
    outs = [shaped((total, features), F32), shaped((total, features))]
    return queue.call(body, operands, outs, "merge_mlp")


def finish(queue, middle, near, far, d_out, small, mods, at):
    features = middle.shape[1]
    block, latent = at

    def body(mid_ref, near_ref, far_ref, d_ref, small_ref, mods_ref, out_ref, sums_ref):
        branch = branch_of(near_ref, far_ref, small_ref, DOWN_BIAS + block, features)
        gate = mods_ref[block, latent, GATE_MLP : GATE_MLP + 1, :]
        out_ref[...] = (mid_ref[...] + gate * branch).astype(BF16)
        total = jnp.sum(d_ref[...] * branch, axis=0, keepdims=True)
        sums_ref[...] = jnp.broadcast_to(total, (8, features))

    outs = [shaped(middle.shape), shaped((8, features), F32)]
    return queue.call(body, [middle, near, far, d_out, small, mods], outs, "finish")


def first_grad(queue, d_out, mods, at):
    features = d_out.shape[1]
    block, latent = at

    def body(d_ref, mods_ref, out_ref, sums_ref):
        gate = mods_ref[block, latent, GATE_MLP : GATE_MLP + 1, :]
        grad = (gate * d_ref[...]).astype(BF16)
        out_ref[...] = grad
        total = jnp.sum(grad.astype(F32), axis=0, keepdims=True)
        sums_ref[...] = jnp.broadcast_to(total, (8, features))

    outs = [shaped(d_out.shape), shaped((8, features), F32)]
    return queue.call(body, [d_out, mods], outs, "first_grad")


def qkv_forward(queue, own, other, weight, small, block):
    rows = own.shape[0]
    width = weight.shape[1]

    def body(own_ref, other_ref, w_ref, small_ref, out_ref):
        bias = small_ref[QKV_BIAS + block : QKV_BIAS + block + 1, :width]
        both = jnp.concatenate([own_ref[...], other_ref[...]], axis=0)
        out = (nt(both, w_ref[block]) + bias).astype(BF16)
        out_ref[0] = out[:rows]
        out_ref[1] = out[rows:]

    outs = [shaped((2, rows, width))]
    return queue.call(body, [own, other, weight, small], outs, "qkv_forward")[0]


def qkv_backward(queue, grads, weight, block):
    _, rows, _ = grads.shape
    features = weight.shape[2]

    def body(g_ref, w_ref, own_ref, other_ref):
        both = jnp.concatenate([g_ref[0], g_ref[1]], axis=0)
        out = nn(both, w_ref[block]).astype(BF16)
        own_ref[...] = out[:rows]
        other_ref[...] = out[rows:]

    outs = [shaped((rows, features)), shaped((rows, features))]
    return queue.call(body, [grads, weight], outs, "qkv_backward")


def mlp_forward(queue, own, other, up_weight, down_weight, small, block):
    rows, features = own.shape
    wide = up_weight.shape[2]

    def body(own_ref, other_ref, up_ref, down_ref, small_ref, own_out, other_out, act_ref, slope_ref):
        bias = small_ref[UP_BIAS + block : UP_BIAS + block + 1, :wide]
        both = jnp.concatenate([own_ref[...], other_ref[...]], axis=0)
        hidden = nn(both, up_ref[block]) + bias
        squared = hidden * hidden
        bent = jnp.tanh(GELU_A * hidden * (1.0 + GELU_B * squared))
        half = 0.5 + 0.5 * bent
        active = (hidden * half).astype(BF16)
        slope = half + 0.5 * hidden * (1.0 - bent * bent) * (
            GELU_A + 3.0 * GELU_A * GELU_B * squared
        )
        act_ref[...] = active
        slope_ref[...] = slope.astype(BF16)
        out = nn(active, down_ref[block]).astype(BF16)
        own_out[...] = out[:rows]
        other_out[...] = out[rows:]

    part, full = shaped((rows, features)), shaped((2 * rows, wide))
    operands = [own, other, up_weight, down_weight, small]
    return queue.call(body, operands, [part, part, full, full], "mlp_forward")


def mlp_backward(queue, own, other, slope, up_weight, down_weight, block):
    rows, features = own.shape
    wide = up_weight.shape[2]

    def body(own_ref, other_ref, slope_ref, up_ref, down_ref, own_out, other_out, hid_ref):
        both = jnp.concatenate([own_ref[...], other_ref[...]], axis=0)
        d_active = nt(both, down_ref[block])
        d_hidden = (d_active * slope_ref[...].astype(F32)).astype(BF16)
        hid_ref[...] = d_hidden
        out = nt(d_hidden, up_ref[block]).astype(BF16)
        own_out[...] = out[:rows]
        other_out[...] = out[rows:]

    part = shaped((rows, features))
    operands = [own, other, slope, up_weight, down_weight]
    return queue.call(body, operands, [part, part, shaped((2 * rows, wide))], "mlp_backward")


def ln_back(queue, near, far, stream, d_out, mods, at, scale_part, branch=None, narrow=False):
    rows, features = stream.shape
    pieces = [] if branch is None else branch[0]
    counts = [piece[0].shape[0] for piece in pieces]
    inner = sum(counts)
    operands = [near, far, stream, d_out, mods]
    outs = [shaped((8, features), F32)]
    if narrow:
        outs.append(shaped((rows, features)))
    if pieces:
        _, small, bias_row, gate_at, gate_part = branch
        operands += [small] + [half for piece in pieces for half in piece]
        outs += [shaped((count, features), F32) for count in counts]
        outs += [shaped((count, features)) for count in counts]
    inputs = len(operands)

    def body(*refs):
        near_ref, far_ref, x_ref, d_ref, mods_ref = refs[:5]
        sums_ref, *out_refs = refs[inputs:]
        scale = mods_ref[at[0], at[1], scale_part : scale_part + 1, :]
        d_normed = near_ref[...].astype(F32) + far_ref[...].astype(F32)
        normed, spread = normed_of(x_ref[...])
        product = d_normed * normed
        grad = d_normed * (1.0 + scale)
        d_x = d_ref[...] + spread * (
            grad
            - jnp.mean(grad, axis=-1, keepdims=True)
            - normed * jnp.mean(grad * normed, axis=-1, keepdims=True)
        )
        zero = jnp.zeros((1, features), F32)
        gate_sum, bias_sum, rest_sum = zero, zero, zero
        if narrow:
            out_refs[0][...] = d_x.astype(BF16)
        elif inner < rows:
            rest_sum = jnp.sum(d_x[inner:], axis=0, keepdims=True)
        first = 0
        for index, count in enumerate(counts):
            piece_near, piece_far = refs[6 + 2 * index : 8 + 2 * index]
            value = branch_of(piece_near, piece_far, refs[5], bias_row, features)
            part = d_x[first : first + count]
            gate = mods_ref[gate_at[0], gate_at[1], gate_part : gate_part + 1, :]
            d_branch = (gate * part).astype(BF16)
            out_refs[index][...] = part
            out_refs[len(counts) + index][...] = d_branch
            gate_sum = gate_sum + jnp.sum(part * value, axis=0, keepdims=True)
            bias_sum = bias_sum + jnp.sum(d_branch.astype(F32), axis=0, keepdims=True)
            first += count
        sums_ref[...] = jnp.concatenate(
            [
                jnp.sum(product, axis=0, keepdims=True),
                jnp.sum(d_normed, axis=0, keepdims=True),
                gate_sum,
                bias_sum,
                rest_sum,
                jnp.zeros((3, features), F32),
            ],
            axis=0,
        )

    return queue.call(body, operands, outs, "ln_back")


def attn_forward(queue, query, merged, proj_weight, block):
    _, rows, width = query.shape
    local = width // 3
    heads = local // HEAD_DIM
    counts = [part.shape[1] for part in merged]
    total = 2 * sum(counts)
    features = proj_weight.shape[2]
    by_keys = rows < 128

    def body(*refs):
        q_ref, refs = refs[0], refs[1:]
        kv_refs, refs = refs[: len(merged)], refs[len(merged) :]
        proj_ref, att_ref, lse_ref, own_out, other_out, q_s, k_s, v_s, o_s, l_s = refs
        for head in range(heads):
            low = head * HEAD_DIM
            first = 0
            for part, count in zip(kv_refs, counts):
                for side in range(2):
                    at = pl.ds(first, count)
                    k_s[head, at, :] = part[side, :, local + low : local + low + HEAD_DIM]
                    v_s[head, at, :] = part[side, :, 2 * local + low : 2 * local + low + HEAD_DIM]
                    first += count
            for side in range(2):
                q_s[head, side] = q_ref[side, :, low : low + HEAD_DIM]
        for head in range(heads):
            for side in range(2):
                if by_keys:
                    scores = nt(k_s[head], q_s[head, side])
                    highest = jnp.max(scores, axis=0, keepdims=True)
                    raised = jnp.exp2((scores - highest) * EXPONENT)
                    total_row = jnp.sum(raised, axis=0, keepdims=True)
                    out = tn(v_s[head], raised.astype(BF16))
                    o_s[head, side] = (out / total_row).T.astype(BF16)
                    lse_ref[head, side] = highest * EXPONENT + jnp.log2(total_row)
                else:
                    scores = nt(q_s[head, side], k_s[head])
                    highest = jnp.max(scores, axis=1, keepdims=True)
                    raised = jnp.exp2((scores - highest) * EXPONENT)
                    total_row = jnp.sum(raised, axis=1, keepdims=True)
                    out = nn(raised.astype(BF16), v_s[head])
                    o_s[head, side] = (out / total_row).astype(BF16)
                    l_s[head, side] = jnp.broadcast_to(
                        highest * EXPONENT + jnp.log2(total_row), (rows, 128)
                    )
        if not by_keys:
            for head in range(heads):
                for side in range(2):
                    lse_ref[head, side] = l_s[head, side].T[:1]
        for side, out_ref in ((1, other_out), (0, own_out)):
            for head in range(heads):
                low = head * HEAD_DIM
                att_ref[side * rows : (side + 1) * rows, low : low + HEAD_DIM] = o_s[head, side]
            out_ref[...] = nn(
                att_ref[side * rows : (side + 1) * rows, :], proj_ref[block]
            ).astype(BF16)

    return queue.call(
        body,
        [query, *merged, proj_weight],
        [
            shaped((2 * rows, local)),
            shaped((heads, 2, 1, rows), F32),
            shaped((rows, features)),
            shaped((rows, features)),
        ],
        "attn_forward",
        scratch=[
            pltpu.VMEM((heads, 2, rows, HEAD_DIM), BF16),
            pltpu.VMEM((heads, total, HEAD_DIM), BF16),
            pltpu.VMEM((heads, total, HEAD_DIM), BF16),
            pltpu.VMEM((heads, 2, rows, HEAD_DIM), BF16),
            pltpu.VMEM((heads, 2, 8 if by_keys else rows, 128), F32),
        ],
        limit=24,
    )


def attn_backward(queue, merged, normers, grads, proj_weight, block):
    count = len(merged)
    width = merged[0].shape[2]
    local = width // 3
    heads = local // HEAD_DIM
    halves = [part.shape[1] for part in merged]
    total = 2 * sum(halves)
    step = min(halves)
    steps = total // step
    unroll = 4 if step * steps > 512 else steps * heads

    def body(*refs):
        m_refs, refs = refs[:count], refs[count:]
        l_refs, refs = refs[:count], refs[count:]
        g_refs, refs = refs[: 2 * count], refs[2 * count :]
        proj_ref, refs = refs[0], refs[1:]
        out_refs, refs = refs[:count], refs[count:]
        q_s, k_s, kt_s, v_s, g_s, dq_s, dk_s, dv_s, l_s = refs
        first = 0
        for index in range(count):
            rows = halves[index]
            for side in range(2):
                at = pl.ds(first, rows)
                grad = nt(g_refs[2 * index + side][...], proj_ref[block]).astype(BF16)
                for head in range(heads):
                    low = head * HEAD_DIM
                    part = m_refs[index]
                    q_s[head, at, :] = part[side, :, low : low + HEAD_DIM]
                    keys = part[side, :, local + low : local + low + HEAD_DIM]
                    k_s[head, at, :] = keys
                    kt_s[head, :, at] = keys.T
                    v_s[head, at, :] = part[side, :, 2 * local + low : 2 * local + low + HEAD_DIM]
                    g_s[head, at, :] = grad[:, low : low + HEAD_DIM]
                    for piece in range(rows // step):
                        l_s[head, first // step + piece] = l_refs[index][
                            head, side, :, piece * step : (piece + 1) * step
                        ]
                first += rows
        dk_s[...] = jnp.zeros_like(dk_s)
        dv_s[...] = jnp.zeros_like(dv_s)

        def one(index, carry):
            head, piece = index // steps, lax.rem(index, steps)
            at = pl.ds(pl.multiple_of(piece * step, step), step)
            queries, grad = q_s[head, at, :], g_s[head, at, :]
            probs = jnp.exp2(nt(k_s[head], queries) * EXPONENT - l_s[head, piece])
            product = probs * nt(v_s[head], grad)
            delta = jnp.sum(product, axis=0, keepdims=True)
            d_scores = (product - probs * delta).astype(BF16)
            dv_s[head] += nn(probs.astype(BF16), grad)
            dk_s[head] += nn(d_scores, queries)
            dq_s[head, at, :] = (nn(kt_s[head], d_scores) * SCALING).T.astype(BF16)
            return carry

        lax.fori_loop(0, steps * heads, one, 0, unroll=unroll)
        first = 0
        for index in range(count):
            rows = halves[index]
            for side in range(2):
                at = pl.ds(first, rows)
                out = out_refs[index]
                for head in range(heads):
                    low = head * HEAD_DIM
                    out[side, :, low : low + HEAD_DIM] = dq_s[head, at, :]
                    out[side, :, local + low : local + low + HEAD_DIM] = (
                        dk_s[head, at, :] * SCALING
                    ).astype(BF16)
                    out[side, :, 2 * local + low : 2 * local + low + HEAD_DIM] = dv_s[
                        head, at, :
                    ].astype(BF16)
                first += rows

    def lanes(dtype=BF16):
        return pltpu.VMEM((heads, total, HEAD_DIM), dtype)

    return queue.call(
        body,
        [*merged, *normers, *[half for pair in grads for half in pair], proj_weight],
        [shaped(part.shape) for part in merged],
        "attn_backward",
        scratch=[
            lanes(),
            lanes(),
            pltpu.VMEM((heads, HEAD_DIM, total), BF16),
            lanes(),
            lanes(),
            lanes(),
            lanes(F32),
            lanes(F32),
            pltpu.VMEM((heads, steps, 1, step), F32),
        ],
        limit=28,
    )


def split_at(bits, bit):
    place = len(bits) - 1 - bits.index(bit)
    stride = 1 << place
    return [index for index in range(1 << len(bits)) if not index & stride], stride


def weight_grads(queue, pairs, mine, bits, bit):
    blocks = 1 << len(bits)
    features = pairs[0][0][0].shape[1]
    widths = [rights[0].shape[1] for _, rights in pairs]
    each = features // blocks
    rows = sum(part.shape[0] for part in pairs[0][0])
    far, plan, scratch = [], [], []
    for number, (lefts, rights) in enumerate(pairs):
        for place, parts in enumerate((lefts, rights)):
            first = 0
            for part in parts:
                plan.append((len(far), 2 * number + place, first, part.shape[0]))
                far.append(part)
                first += part.shape[0]
            scratch.append(pltpu.VMEM((rows, parts[0].shape[1]), BF16))
    buffers = len(scratch)
    scratch.append(pltpu.VMEM((blocks, each, sum(widths)), BF16))
    scratch.append(pltpu.SemaphoreType.DMA((len(plan),)))
    out = shaped((blocks // 2, each, sum(widths)))
    starts, stride = split_at(bits, bit)

    def body(mine_ref, *refs):
        sources, refs = refs[: len(far)], refs[len(far) :]
        kept_ref, away_ref, sums_ref, *held = refs
        full, done = held[buffers], held[buffers + 1]
        copies = [
            pltpu.make_async_copy(
                sources[source], held[buffer].at[pl.ds(first, count)], done.at[index]
            )
            for index, (source, buffer, first, count) in enumerate(plan)
        ]
        for copy in copies:
            copy.start()
        low = 0
        ones = jnp.ones((8, rows), BF16)
        for number, width in enumerate(widths):
            for copy, (_, buffer, _, _) in zip(copies, plan):
                if buffer // 2 == number:
                    copy.wait()
            left, right = held[2 * number][...], held[2 * number + 1][...]
            total = tn(left, right).astype(BF16)
            columns = slice(low, low + width)
            for block in range(blocks):
                full[block, :, columns] = total[block * each : (block + 1) * each]
            sums_ref[:, columns] = nn(ones, right)
            low += width
        at = mine_ref[0] * stride
        for index, start in enumerate(starts):
            kept_ref[index] = full[start + at]
            away_ref[index] = full[start + stride - at]

    return queue.call(
        body,
        [],
        [out, out, shaped((8, sum(widths)), F32)],
        "weight_grads",
        scalars=[mine],
        far=far,
        scratch=scratch,
        limit=32,
    )


def halve(queue, kept, moved, mine, bits, bit):
    blocks, each, width = kept.shape
    out = shaped((blocks // 2, each, width))
    starts, stride = split_at(bits, bit)

    def body(mine_ref, kept_ref, moved_ref, next_ref, away_ref):
        at = mine_ref[0] * stride
        for place, out_ref in ((stride - at, away_ref), (at, next_ref)):
            for index, start in enumerate(starts):
                total = kept_ref[start + place].astype(F32) + moved_ref[start + place].astype(F32)
                out_ref[index] = total.astype(BF16)

    return queue.call(body, [kept, moved], [out, out], "halve", scalars=[mine])


def spread_mods(queue, me, columns, features):
    size, latents, blocks, each = columns.shape

    def body(me_ref, in_ref, out_ref, flat):
        for device in range(size):
            block = in_ref[jnp.bitwise_xor(device, me_ref[0])].astype(F32)
            for latent in range(latents):
                flat[latent, :, device * each : (device + 1) * each] = block[latent]
        for latent in range(latents):
            for part in range(6):
                rows = flat[latent, :, part * features : (part + 1) * features]
                for index in range(blocks):
                    out_ref[index, latent, part : part + 1, :] = rows[index : index + 1]

    return queue.call(
        body,
        [columns],
        [shaped((blocks, latents, 6, features), F32)],
        "spread_mods",
        scalars=[me],
        scratch=[pltpu.VMEM((latents, blocks, size * each), F32)],
    )[0]


def collect_sums(queue, sources, recipe):
    features = sources[0].shape[1]
    count = -(-len(recipe) // 8) * 8

    def body(*refs):
        out_ref = refs[-1]
        for index, terms in enumerate(recipe):
            total = None
            for source, row in terms:
                term = refs[source][row : row + 1, :]
                total = term if total is None else total + term
            out_ref[index : index + 1, :] = total
        if count > len(recipe):
            out_ref[len(recipe) :, :] = jnp.zeros((count - len(recipe), features), F32)

    return queue.call(body, sources, [shaped((count, features), F32)], "collect_sums")[0]


def pack_mods(queue, me, own, moved, latents, blocks, size, features):
    each = 6 * features // size
    rows = own.shape[0]

    def body(me_ref, own_ref, moved_ref, out_ref, total_ref, flat):
        total = own_ref[...] + moved_ref[...]
        total_ref[...] = total
        for latent in range(latents):
            for index in range(blocks):
                for part in range(6):
                    row = (index * latents + latent) * 6 + part
                    flat[latent, index : index + 1, part * features : (part + 1) * features] = total[
                        row : row + 1
                    ]
        for device in range(size):
            for latent in range(latents):
                out_ref[jnp.bitwise_xor(device, me_ref[0]), latent] = flat[
                    latent, :, device * each : (device + 1) * each
                ].astype(BF16)

    return queue.call(
        body,
        [own, moved],
        [shaped((size, latents, blocks, each)), shaped((rows, features), F32)],
        "pack_mods",
        scalars=[me],
        scratch=[pltpu.VMEM((latents, blocks, 6 * features), F32)],
    )


def partners(size, bit):
    return [(index, index ^ bit) for index in range(size)]


def bits_of(size):
    bits = []
    while (1 << len(bits)) < size:
        bits.append(1 << len(bits))
    assert (1 << len(bits)) == size
    return bits


class Links:
    def __init__(self, dp_size, tensor_size):
        self.dp_size = dp_size
        self.tensor_size = tensor_size
        self.dp_bits = bits_of(dp_size)
        me = lax.axis_index("dp")
        self.me = me.reshape(1)
        self.core = lax.rem(lax.axis_index("tensor"), 2).reshape(1)
        self.mine = {bit: lax.rem(me // bit, 2).reshape(1) for bit in self.dp_bits}

    def swap(self, value):
        return lax.ppermute(value, "tensor", partners(self.tensor_size, 1))

    def cross(self, value):
        return lax.ppermute(value, "tensor", partners(self.tensor_size, 2))

    def dp_move(self, value, bit):
        return lax.ppermute(value, "dp", partners(self.dp_size, bit))

    def gather_relative(self, value):
        held = value[None]
        for bit in self.dp_bits:
            held = jnp.concatenate([held, self.dp_move(held, bit)], axis=0)
        return held

    def exchange_relative(self, value):
        held = value
        for bit in self.dp_bits:
            split = held.reshape((self.dp_size // (2 * bit), 2, bit) + held.shape[1:])
            moved = self.dp_move(split[:, 1], bit)
            held = jnp.stack([split[:, 0], moved], axis=1).reshape(held.shape)
        return held

    def sum_relative(self, value):
        held = value
        for bit in reversed(self.dp_bits):
            moved = self.dp_move(held[bit:].astype(BF16), bit)
            held = held[:bit].astype(F32) + moved.astype(F32)
        return held[0]

    def sum_all(self, value):
        held = value
        for bit in self.dp_bits:
            held = held + self.dp_move(held, bit)
        return held


class ScatterSum:
    def __init__(self, queue, links, pairs, order):
        self.queue, self.links = queue, links
        self.order = list(order)
        self.open = sorted(self.order, reverse=True)
        bit = self.order[0]
        self.kept, away, self.sums = weight_grads(
            queue, pairs, links.mine[bit], self.open, bit
        )
        self.send(away)

    def send(self, away):
        bit = self.order.pop(0)
        self.open.remove(bit)
        self.moved = self.links.dp_move(away, bit)

    def step(self):
        if self.order:
            bit = self.order[0]
            self.kept, away = halve(
                self.queue, self.kept, self.moved, self.links.mine[bit], self.open, bit
            )
            self.send(away)

    def result(self):
        while self.order:
            self.step()
        return self.kept[0].astype(F32) + self.moved[0].astype(F32)


class Weights:
    def __init__(self, qkv, proj, up, down, small, mods):
        self.qkv, self.proj, self.up, self.down = qkv, proj, up, down
        self.small, self.mods = small, mods


class Chunk:
    def __init__(self, queue, links, weights, block, latent, family):
        self.queue, self.links, self.weights = queue, links, weights
        self.block, self.latent, self.at = block, latent, (block, latent)
        self.family = family
        family.append(self)

    def enter(self, stream, normed):
        self.x = stream
        self.normed_attn = (normed, self.links.swap(normed))

    def qkv(self):
        w = self.weights
        self.merged = qkv_forward(self.queue, *self.normed_attn, w.qkv, w.small, self.block)

    def attention(self):
        merged = [chunk.merged for chunk in self.family]
        self.attended, self.normer, own, other = attn_forward(
            self.queue, self.merged, merged, self.weights.proj, self.block
        )
        self.part = (own, self.links.swap(other))

    def near(self):
        near = near_sum(self.queue, *self.part)
        self.sum = (near, self.links.cross(near))

    def merge(self):
        w = self.weights
        self.branch_attn = self.sum
        self.middle, normed = merge_attn(
            self.queue, self.x, *self.branch_attn, w.small, w.mods, self.at
        )
        self.normed_mlp = (normed, self.links.swap(normed))

    def mlp(self):
        w = self.weights
        own, other, self.active, self.slope = mlp_forward(
            self.queue, *self.normed_mlp, w.up, w.down, w.small, self.block
        )
        self.part = (own, self.links.swap(other))

    def start_back(self, d_out, d_branch):
        self.d_out = d_out
        self.d_branch_mlp = (d_branch, self.links.swap(d_branch))

    def mlp_back(self):
        w = self.weights
        own, other, self.d_hidden = mlp_backward(
            self.queue, *self.d_branch_mlp, self.slope, w.up, w.down, self.block
        )
        self.part = (own, self.links.swap(other))

    def merge_back(self):
        w = self.weights
        branch = ([self.branch_attn], w.small, PROJ_BIAS + self.block, self.at, GATE_ATTN)
        self.mlp_sums, self.d_middle, grad = ln_back(
            self.queue, *self.sum, self.middle, self.d_out, w.mods, self.at, SCALE_MLP, branch
        )
        self.d_branch_attn = (grad, self.links.swap(grad))

    def attention_back(self):
        family = self.family
        grads = attn_backward(
            self.queue,
            [chunk.merged for chunk in family],
            [chunk.normer for chunk in family],
            [chunk.d_branch_attn for chunk in family],
            self.weights.proj,
            self.block,
        )
        for chunk, grad in zip(family, grads):
            chunk.d_qkv = grad

    def qkv_back(self):
        own, other = qkv_backward(self.queue, self.d_qkv, self.weights.qkv, self.block)
        self.part = (own, self.links.swap(other))

    def leave_back(self, branch=None, narrow=False):
        w = self.weights
        self.attn_sums, *rest = ln_back(
            self.queue,
            *self.sum,
            self.x,
            self.d_middle,
            w.mods,
            self.at,
            SCALE_ATTN,
            branch,
            narrow,
        )
        return rest


def pair_rows(chunks, name):
    return [half for chunk in chunks for half in getattr(chunk, name)]


def flat_rows(chunks, name):
    return [
        getattr(chunk, name).reshape(-1, getattr(chunk, name).shape[-1]) for chunk in chunks
    ]


def on_device(dp_size, tensor_size, *arguments):
    (
        tokens_long,
        tokens_short,
        cond_long,
        cond_short,
        perm_long,
        perm_short,
        ada_weight,
        ada_bias,
        qkv_weight,
        qv_bias,
        proj_weight,
        proj_bias,
        up_weight,
        up_bias,
        down_weight,
        down_bias,
        mask_token,
        cot_long,
        cot_short,
    ) = arguments
    assert tokens_long.shape[0] == 1 and tokens_short.shape[0] == 1
    queue = Queue()
    links = Links(dp_size, tensor_size)
    core = links.core
    features = tokens_long.shape[2]
    wide = up_weight.shape[2]
    local = qv_bias.shape[2]
    tokens = (tokens_long[0], tokens_short[0])
    cots = (cot_long[0], cot_short[0])
    perms = (perm_long, perm_short)
    lengths = tuple(rows.shape[0] for rows in tokens)
    kept = tuple(length // 2 for length in lengths)

    cond = jnp.concatenate([cond_long, cond_short]).astype(F32)
    acts = links.gather_relative(jax.nn.silu(cond).astype(BF16))
    flat_acts = acts.reshape(-1, features)
    columns = jnp.einsum("nd,ldm->nlm", flat_acts, ada_weight, preferred_element_type=F32)
    columns = (columns + ada_bias.astype(F32)[None]).astype(BF16)
    columns = links.exchange_relative(columns.reshape((dp_size, 2) + columns.shape[1:]))

    table_width = max(features, wide, 3 * local)

    def padded(rows):
        return jnp.pad(rows.astype(F32), ((0, 0), (0, table_width - rows.shape[1])))

    qkv_bias = jnp.concatenate(
        [qv_bias[:, 0], jnp.zeros_like(qv_bias[:, 0]), qv_bias[:, 1]], axis=1
    )
    small = jnp.concatenate([padded(proj_bias), padded(down_bias), padded(up_bias), padded(qkv_bias)])

    long_half, short_half = kept[0] // 2, kept[1] // 2
    quarter = long_half // 2
    enc_rows = [
        Rows((0, long_half, quarter)),
        Rows((quarter, long_half, quarter)),
        Rows((0, short_half, short_half)),
    ]
    table_places = [Rows((0, long_half, long_half)), Rows((0, short_half, short_half))]
    masked_places = [
        Rows((kept[0], long_half, long_half)),
        Rows((kept[1], short_half, short_half)),
    ]
    dec_rows = [
        table_places[0],
        masked_places[0],
        Rows((0, short_half, short_half), (kept[1], short_half, short_half)),
    ]
    enc_latents, dec_latents = (0, 0, 1), (0, 0, 1)

    streams = [
        gather_rows(queue, core, perms[latent], tokens[latent], rows)
        for latent, rows in zip(enc_latents, enc_rows)
    ]
    mods = spread_mods(queue, links.me, columns, features)
    weights = Weights(
        jnp.transpose(qkv_weight, (0, 2, 3, 1)).reshape(2, 3 * local, features),
        proj_weight,
        up_weight,
        down_weight,
        small,
        mods,
    )
    families = {(block, latent): [] for block in (0, 1) for latent in (0, 1)}

    def chunks_of(block, latents):
        return [
            Chunk(queue, links, weights, block, latent, families[block, latent])
            for latent in latents
        ]

    encoder = chunks_of(0, enc_latents)
    decoder = chunks_of(1, dec_latents)
    ea, eb, es = encoder
    dk, dm, dt = decoder

    for chunk, stream in zip(encoder, streams):
        chunk.enter(stream, ln_open(queue, stream, mods, chunk.at))
    for chunk in encoder:
        chunk.qkv()
    ea.attention()
    eb.attention()
    ea.near()
    es.attention()
    eb.near()
    es.near()
    perms_later, filler, cots_later = queue.tie(perms, mask_token, cots)
    filler = filler.astype(F32)[None]
    waves = []
    for length in lengths:
        side = math.isqrt(length)
        quarter_wave = features // 4
        frequency = 1.0 / 10000.0 ** (jnp.arange(quarter_wave, dtype=F32) / quarter_wave)
        angle = jnp.arange(side, dtype=jnp.int32).astype(F32)[:, None] * frequency[None, :]
        waves.append(jnp.concatenate([jnp.sin(angle), jnp.cos(angle)], axis=1))
    masked = table_rows(queue, core, perms_later[0], waves[0], masked_places[0], filler)
    dm.enter(masked, ln_open(queue, masked, mods, dm.at))
    ea.merge()
    dm.qkv()
    ea.mlp()
    eb.merge()
    ea.near()
    es.merge()
    eb.mlp()
    es.mlp()
    eb.near()
    es.near()
    table_long = table_rows(queue, core, perms_later[0], waves[0], table_places[0])
    table_short = table_rows(queue, core, perms_later[1], waves[1], table_places[1])
    masked_short = table_rows(queue, core, perms_later[1], waves[1], masked_places[1], filler)
    d_out = [
        gather_rows(queue, core, perms_later[latent], cots_later[latent], rows)
        for latent, rows in zip(dec_latents, dec_rows)
    ]
    first_sums = []
    for chunk, grad in zip(decoder, d_out):
        d_branch, sums = first_grad(queue, grad, mods, chunk.at)
        first_sums.append(sums)
        chunk.start_back(grad, d_branch)

    pieces = [(chunk.middle, *chunk.sum) for chunk in encoder]
    for chunk in encoder:
        chunk.branch_mlp = chunk.sum
    dk.enter(*merge_mlp(queue, pieces[:2], small, mods, (0, 0), table_long, None))
    dt.enter(*merge_mlp(queue, pieces[2:], small, mods, (0, 1), table_short, masked_short))
    dk.qkv()
    dk.attention()
    dt.qkv()
    dk.near()
    dm.attention()
    dt.attention()
    dm.near()
    dt.near()
    dk.merge()
    dk.mlp()
    dm.merge()
    dk.near()
    dt.merge()
    forward_sums = [dk.sum]
    dm.mlp()
    dk.mlp_back()
    dm.near()
    forward_sums.append(dm.sum)
    dt.mlp()
    dm.mlp_back()
    dt.near()
    forward_sums.append(dt.sum)
    dt.mlp_back()

    dt.near()
    dk.near()
    dm.near()
    y_first, z_first = list(links.dp_bits), list(links.dp_bits)
    if len(z_first) > 1:
        z_first[0], z_first[1] = z_first[1], z_first[0]

    def wide_sum(chunks, left, right, order):
        return ScatterSum(queue, links, [(pair_rows(chunks, left), flat_rows(chunks, right))], order)

    dec_up = wide_sum(decoder, "normed_mlp", "d_hidden", y_first)
    decoded, gate_sums = [], []
    for chunk, grad, summed in zip(decoder, d_out, forward_sums):
        own, sums = finish(queue, chunk.middle, *summed, grad, small, mods, chunk.at)
        gate_sums.append(sums)
        decoded.append((own, links.swap(own)))
    dt.merge_back()
    dec_down = wide_sum(decoder, "d_branch_mlp", "active", z_first)
    dt.attention_back()
    dk.merge_back()
    dt.qkv_back()
    dt.near()
    dm.merge_back()
    dm.attention_back()
    dk.qkv_back()
    dm.qkv_back()
    dk.near()
    dm.near()

    enc_branch = (small, DOWN_BIAS, (0, 0), GATE_MLP)
    short_branch = (small, DOWN_BIAS, (0, 1), GATE_MLP)
    d_short, grad_short = dt.leave_back(([es.branch_mlp], *short_branch))
    es.start_back(d_short, grad_short)
    dec_proj = ScatterSum(
        queue,
        links,
        [
            (pair_rows(decoder, "d_branch_attn"), flat_rows(decoder, "attended")),
            (pair_rows(decoder, "normed_attn"), flat_rows(decoder, "d_qkv")),
        ],
        y_first,
    )
    dec_up.step()
    d_a, d_b, grad_a, grad_b = dk.leave_back(([ea.branch_mlp, eb.branch_mlp], *enc_branch))
    ea.start_back(d_a, grad_a)
    eb.start_back(d_b, grad_b)

    es.mlp_back()
    ea.mlp_back()
    eb.mlp_back()
    es.near()
    ea.near()
    eb.near()
    dm.leave_back()
    dec_down.step()
    enc_up = wide_sum(encoder, "normed_mlp", "d_hidden", y_first)
    es.merge_back()
    enc_down = wide_sum(encoder, "d_branch_mlp", "active", z_first)
    es.attention_back()
    es.qkv_back()
    ea.merge_back()
    es.near()
    eb.merge_back()
    ea.attention_back()
    ea.qkv_back()
    eb.qkv_back()
    ea.near()
    eb.near()
    enc_proj = ScatterSum(
        queue,
        links,
        [
            (pair_rows(encoder, "d_branch_attn"), flat_rows(encoder, "attended")),
            (pair_rows(encoder, "normed_attn"), flat_rows(encoder, "d_qkv")),
        ],
        y_first,
    )
    own_tokens = []
    for chunk in (es, ea, eb):
        (own,) = chunk.leave_back(narrow=True)
        own_tokens.append((own, links.swap(own)))

    sources, recipe = [], []

    def row(array, index):
        for place, source in enumerate(sources):
            if source is array:
                return place, index
        sources.append(array)
        return len(sources) - 1, index

    for block, chunks in ((0, encoder), (1, decoder)):
        for latent in (0, 1):
            members = [chunk for chunk in chunks if chunk.latent == latent]
            if block == 0:
                gates = [row((dk, dt)[latent].attn_sums, 2)]
            else:
                gates = [
                    row(gate_sums[index], 0)
                    for index, chunk in enumerate(decoder)
                    if chunk.latent == latent
                ]
            recipe += [
                [row(chunk.attn_sums, 1) for chunk in members],
                [row(chunk.attn_sums, 0) for chunk in members],
                [row(chunk.mlp_sums, 2) for chunk in members],
                [row(chunk.mlp_sums, 1) for chunk in members],
                [row(chunk.mlp_sums, 0) for chunk in members],
                gates,
            ]
    recipe += [
        [row(chunk.mlp_sums, 3) for chunk in encoder],
        [row(chunk.mlp_sums, 3) for chunk in decoder],
        [row(chunk.attn_sums, 3) for chunk in (dk, dt)],
        [row(sums, 0) for sums in first_sums],
        [row(chunk.attn_sums, 4) for chunk in (dm, dt)],
    ]
    own_sums = collect_sums(queue, sources, recipe)
    packed, all_sums = pack_mods(
        queue, links.me, own_sums, links.swap(own_sums), 2, 2, dp_size, features
    )
    mine = links.exchange_relative(packed)
    flat_mine = mine.reshape((-1,) + mine.shape[2:])
    grad_ada = jnp.einsum("nd,nlm->ldm", flat_acts, flat_mine, preferred_element_type=F32)
    grad_ada_bias = jnp.sum(flat_mine.astype(F32), axis=0)
    d_acts = jnp.einsum("nlm,ldm->nd", flat_mine, ada_weight, preferred_element_type=F32)
    d_act = links.sum_relative(d_acts.reshape(dp_size, 2, features))
    gate = jax.nn.sigmoid(cond)
    d_cond = (d_act * gate * (1.0 + cond * (1.0 - gate))).astype(BF16)

    qkv_sums = [part.sums[0, local:] for part in (enc_proj, dec_proj)]
    totals = jnp.concatenate(
        [all_sums[24:29].reshape(-1), enc_up.sums[0], dec_up.sums[0]]
        + [part for sums in qkv_sums for part in (sums[:local], sums[2 * local :])]
    )
    totals = links.sum_all(totals)
    proj_out = totals[: 2 * features].reshape(2, features)
    down_out = totals[2 * features : 4 * features].reshape(2, features)
    mask_out = totals[4 * features : 5 * features]
    first = 5 * features
    up_out = totals[first : first + 2 * wide].reshape(2, wide)
    first += 2 * wide
    qv_out = totals[first : first + 4 * local].reshape(2, 2, local)

    for part in (enc_up, dec_proj, enc_down, dec_up, dec_down):
        part.step()
    results = (
        place_rows(queue, core, perms_later[0], decoded[:2], dec_rows[:2]),
        place_rows(queue, core, perms_later[1], decoded[2:], dec_rows[2:]),
    )
    for part in (enc_up, dec_proj, enc_down, enc_proj):
        part.step()
    d_tokens = (
        place_rows(queue, core, perms_later[0], own_tokens[1:], enc_rows[:2]),
        place_rows(queue, core, perms_later[1], own_tokens[:1], enc_rows[2:]),
    )
    enc_att, dec_att = enc_proj.result(), dec_proj.result()
    up_grad = jnp.stack([enc_up.result(), dec_up.result()])
    down_grad = jnp.stack([enc_down.result(), dec_down.result()])
    proj_grad = jnp.stack([enc_att[:, :local], dec_att[:, :local]])
    qkv_grad = jnp.stack([enc_att[:, local:], dec_att[:, local:]]).reshape(2, -1, 3, local)

    return (
        results[0][None],
        results[1][None],
        d_tokens[0][None],
        d_tokens[1][None],
        d_cond[:1],
        d_cond[1:],
        grad_ada,
        grad_ada_bias,
        qkv_grad,
        qv_out,
        jnp.transpose(proj_grad, (0, 2, 1)),
        proj_out,
        up_grad,
        up_out,
        jnp.transpose(down_grad, (0, 2, 1)),
        down_out,
        mask_out,
    )


def solution(mesh):
    in_specs = (
        P("dp", None, None),
        P("dp", None, None),
        P("dp", None),
        P("dp", None),
        P("dp", None),
        P("dp", None),
        P(None, None, "dp"),
        P(None, "dp"),
        P(None, None, None, "tensor"),
        P(None, None, "tensor"),
        P(None, "tensor", None),
        P(),
        P(None, None, "tensor"),
        P(None, "tensor"),
        P(None, "tensor", None),
        P(),
        P(),
        P("dp", None, None),
        P("dp", None, None),
    )
    out_specs = (
        P("dp", None, None),
        P("dp", None, None),
        P("dp", None, None),
        P("dp", None, None),
        P("dp", None),
        P("dp", None),
        P(None, None, "dp"),
        P(None, "dp"),
        P(None, "dp", None, "tensor"),
        P(None, None, "tensor"),
        P(None, "tensor", "dp"),
        P(),
        P(None, "dp", "tensor"),
        P(None, "tensor"),
        P(None, "tensor", "dp"),
        P(),
        P(),
    )

    def step(*arguments):
        return on_device(mesh.shape["dp"], mesh.shape["tensor"], *arguments)

    return jax.shard_map(
        step, mesh=mesh, in_specs=in_specs, out_specs=out_specs, check_vma=False
    )
```

time: 752 us -> 656 us (0.87)
  waiting for transfers between devices: 338 us -> 254 us
  Pallas kernels: 171 us -> 214 us
  local copies, waits for them, and re-layouts: 89.8 us -> 62.6 us
  matrix products: 33.5 us -> 10.9 us
  other arithmetic: 34.5 us -> 13.8 us
  starting transfers between devices: 74.5 us -> 85.9 us
    ppermute x20 -> x24, waiting for transfers between devices: 138 us -> 86 us  [cross(): return lax.ppermute(value, 'tensor', partners(self.tensor_size, 2))]
    pallas_call x61 -> x123, Pallas kernels: 171 us -> 214 us  [call(): pl.pallas_call(whole, in_specs=[fast] + [small] * len(scalars) + [anywher...]
    ppermute x27 -> x33, waiting for transfers between devices: 190 us -> 156 us  [dp_move(): return lax.ppermute(value, 'dp', partners(self.dp_size, bit))]
    dot_general x17 -> x0, matrix products: 23 us -> none  [the longest x4 12.9 us: tn(): lax.dot_general(left, right, (((0,), (0,)), ((), ())), preferred_element_...]
    slice x29 -> x5, local copies, waits for them, and re-layouts: 17.8 us -> 1.21 us  [the longest x1 0.79 us: on_device(): dec_up.sums[0]]
    ppermute x20 -> x24, starting transfers between devices: 21.3 us -> 29.7 us  [cross(): return lax.ppermute(value, 'tensor', partners(self.tensor_size, 2))]
    unnamed x454 -> x564, local copies, waits for them, and re-layouts: 51.8 us -> 54.1 us
    ppermute x27 -> x33, starting transfers between devices: 44.3 us -> 45.2 us  [dp_move(): return lax.ppermute(value, 'dp', partners(self.dp_size, bit))]
  transfers between devices with their start and end apart: 93 -> 112, of which waited for: 47 -> 43; matrix products, arithmetic and copies ran while one was open for 12% -> 4% of each run, Pallas kernels for 22% -> 28%
where the time goes in v3:
time: 656 us; the launch traced here: 645 us
  waiting for transfers between devices  254 us (39%)
  Pallas kernels  214 us (33%)
  starting transfers between devices  85.9 us (13%)
  local copies, waits for them, and re-layouts  62.6 us (10%)
  other arithmetic  13.8 us (2%)
  matrix products  10.9 us (2%)
    pallas_call x123, Pallas kernels, call(): pl.pallas_call(whole, in_specs=[fast] + [small] * len(scalars) + [anywher...  214 us
    ppermute x33, waiting for transfers between devices, dp_move(): return lax.ppermute(value, 'dp', partners(self.dp_size, bit))  156 us
    ppermute x24, waiting for transfers between devices, cross(): return lax.ppermute(value, 'tensor', partners(self.tensor_size, 2))  86 us
    unnamed x564, local copies, waits for them, and re-layouts  54.1 us
    ppermute x33, starting transfers between devices, dp_move(): return lax.ppermute(value, 'dp', partners(self.dp_size, bit))  45.2 us
    ppermute x24, starting transfers between devices, cross(): return lax.ppermute(value, 'tensor', partners(self.tensor_size, 2))  29.7 us
  transfers between devices with their start and end apart: 112, of which 43 were waited for; matrix products, arithmetic and copies ran while one was open for 4% of the time, Pallas kernels for 28%

profile of v3, /device:TPU:0, one launch (start us, length us, event | category | flops | bytes accessed | tf_op | source)
XLA Modules:
  0.0 645.1 jit_solution(3062985082923400950)
XLA Ops:
  1.4 3.0 collective-permute-start
  9.9 3.1 collective-permute-start.2
  14.8 3.4 fusion
  26.5 3.0 collective-permute-start.5
  42.1 3.3 attn_forward.6
  46.4 3.3 attn_forward.7
  56.4 5.2 collective-permute-done.12.refs_2_.refs_7_
  67.7 3.7 collective-permute-done.15.refs_2_.refs_7_
  73.5 4.6 collective-permute-done.17.refs_2_.refs_7_
  94.2 4.0 collective-permute-done.23.refs_8_.refs_9_
  100.5 4.7 collective-permute-done.24.refs_5_.refs_7_
  107.1 5.5 attn_forward.9
  116.3 6.0 attn_forward.10
  128.9 9.8 %collective-permute-done.30.refs_2_.refs_7_ = bf16[256,1152]{1,0:T(8,128)(2,1)S(1)} collective-permute-done((bf16[256,1152]{1,0:T(8,128)(2,1)S(1)}, bf16[256,1152]{1,0:T(8,128)(2,1)S(1)}, u32[]{:S(2)}, u32[]{:S(2)}) %collective-permute-start.30) | collective-permute-done | bytes 589856 | tf_op jit(solution)/shard_map/ppermute | solution.py:750
  141.5 4.1 mlp_forward.9
  145.8 9.4 %collective-permute-done.32.refs_2_.refs_7_ = bf16[256,1152]{1,0:T(8,128)(2,1)S(1)} collective-permute-done((bf16[256,1152]{1,0:T(8,128)(2,1)S(1)}, bf16[256,1152]{1,0:T(8,128)(2,1)S(1)}, u32[]{:S(2)}, u32[]{:S(2)}) %collective-permute-start.32) | collective-permute-done | bytes 589856 | tf_op jit(solution)/shard_map/ppermute | solution.py:750
  158.8 6.7 %collective-permute-done.34.refs_2_.refs_7_ = bf16[128,1152]{1,0:T(8,128)(2,1)S(1)} collective-permute-done((bf16[128,1152]{1,0:T(8,128)(2,1)S(1)}, bf16[128,1152]{1,0:T(8,128)(2,1)S(1)}, u32[]{:S(2)}, u32[]{:S(2)}) %collective-permute-start.34) | collective-permute-done | bytes 294944 | tf_op jit(solution)/shard_map/ppermute | solution.py:750
  166.3 4.3 mlp_forward.10
  171.3 3.5 mlp_backward.6
  180.0 3.5 mlp_backward.7
  208.4 7.0 %weight_grads.6 = (bf16[4,144,1152]{2,1,0:T(8,128)(2,1)S(1)}, bf16[4,144,1152]{2,1,0:T(8,128)(2,1)}, f32[8,1152]{1,0:T(8,128)S(1)}, f32[8,128]{1,0:T(8,128)S(1)}) custom-call(f32[8,128]{1,0:T(8,128)S(1)} %get-tuple-element.528.token_ref, s32[1]{0:T(128)} %bitcast.22.refs_0_, bf16[256,1152]{1,0:T(8,128)(2,1)S(1)} %copy-done.67, ...), custom_call_target="tpu_custom_call" | custom-call | flops 1000 | bytes 1000 | tf_op jit(solution)/shard_map/weight_grads/pallas_call | solution.py:58
  242.0 7.4 %weight_grads.7 = (bf16[4,144,1152]{2,1,0:T(8,128)(2,1)S(1)}, bf16[4,144,1152]{2,1,0:T(8,128)(2,1)}, f32[8,1152]{1,0:T(8,128)}, f32[8,128]{1,0:T(8,128)S(1)}) custom-call(f32[8,128]{1,0:T(8,128)S(1)} %copy-done.256, s32[1]{0:T(128)} %bitcast.23.refs_0_, bf16[256,1152]{1,0:T(8,128)(2,1)S(1)} %copy-done.59, bf16[256,1152]{1,0:T(8,128)(2,1)S(1)} %copy-done.63, ...), custom_call_target="tpu_custom_call" | custom-call | flops 1000 | bytes 1000 | tf_op jit(solution)/shard_map/weight_grads/pallas_call | solution.py:58
  249.4 4.2 attn_backward.4
  266.3 18.5 %attn_backward.5 = (bf16[2,256,864]{2,1,0:T(8,128)(2,1)S(1)}, bf16[2,256,864]{2,1,0:T(8,128)(2,1)S(1)}, f32[8,128]{1,0:T(8,128)S(1)}) custom-call(f32[8,128]{1,0:T(8,128)S(1)} %get-tuple-element.559.token_ref, bf16[2,256,864]{2,1,0:T(8,128)(2,1)S(1)} %get-tuple-element.471.refs_0_.refs_1_, ...), custom_call_target="tpu_custom_call" | custom-call | flops 1000 | bytes 1000 | tf_op jit(solution)/shard_map/attn_backward/pallas_call | solution.py:58
  293.1 20.0 %collective-permute-done.57.refs_1_ = bf16[128,1152]{1,0:T(8,128)(2,1)S(1)} collective-permute-done((bf16[128,1152]{1,0:T(8,128)(2,1)S(1)}, bf16[128,1152]{1,0:T(8,128)(2,1)S(1)}, u32[]{:S(2)}, u32[]{:S(2)}) %collective-permute-start.57) | collective-permute-done | bytes 294944 | tf_op jit(solution)/shard_map/ppermute | solution.py:750
  316.5 9.6 %weight_grads.8 = (bf16[4,144,1152]{2,1,0:T(8,128)(2,1)S(1)}, bf16[4,144,1152]{2,1,0:T(8,128)(2,1)}, f32[8,1152]{1,0:T(8,128)S(1)}, f32[8,128]{1,0:T(8,128)S(1)}) custom-call(f32[8,128]{1,0:T(8,128)S(1)} %get-tuple-element.577.token_ref, s32[1]{0:T(128)} %bitcast.22.refs_0_, bf16[256,1152]{1,0:T(8,128)(2,1)S(1)} %get-tuple-element.562.refs_4_.refs_1_, ...), custom_call_target="tpu_custom_call" | custom-call | flops 1000 | bytes 1000 | tf_op jit(solution)/shard_map/weight_grads/pallas_call | solution.py:58
  344.8 4.8 collective-permute-done.66.refs_1_
  353.3 4.9 weight_grads.9
  360.9 4.9 weight_grads.10
  370.4 4.2 collective-permute-done.72.refs_1_
  377.4 7.5 %attn_backward.7 = (bf16[2,128,864]{2,1,0:T(8,128)(2,1)S(1)}, bf16[2,128,864]{2,1,0:T(8,128)(2,1)S(1)}, f32[8,128]{1,0:T(8,128)S(1)}) custom-call(f32[8,128]{1,0:T(8,128)S(1)} %get-tuple-element.636.token_ref, bf16[2,128,864]{2,1,0:T(8,128)(2,1)S(1)} %copy-done.15, bf16[2,128,864]{2,1,0:T(8,128)(2,1)S(1)} %copy-done.17, f32[4,2,1,128]{3,2,1,0:T(1,128)S(1)} %copy-done.246, ...), custom_call_target="tpu_custom_call" | custom-call | flops 1000 | bytes 1000 | tf_op jit(solution)/shard_map/attn_backward/pallas_call | solution.py:58
  392.2 7.5 %weight_grads.11 = (bf16[4,144,1152]{2,1,0:T(8,128)(2,1)S(1)}, bf16[4,144,1152]{2,1,0:T(8,128)(2,1)}, f32[8,1152]{1,0:T(8,128)S(1)}, f32[8,128]{1,0:T(8,128)S(1)}) custom-call(f32[8,128]{1,0:T(8,128)S(1)} %get-tuple-element.651.token_ref, s32[1]{0:T(128)} %bitcast.22.refs_0_, bf16[128,1152]{1,0:T(8,128)(2,1)S(1)} %get-tuple-element.639.refs_4_.refs_1_, ...), custom_call_target="tpu_custom_call" | custom-call | flops 1000 | bytes 1000 | tf_op jit(solution)/shard_map/weight_grads/pallas_call | solution.py:58
  399.8 6.3 collective-permute-done.77.refs_1_
  414.6 34.9 %collective-permute-done.96 = bf16[4,1,2,2,864]{4,3,2,0,1:T(2,128)(2,1)S(1)} collective-permute-done((bf16[4,1,2,2,864]{4,3,2,0,1:T(2,128)(2,1)S(1)}, bf16[4,1,2,2,864]{4,3,2,0,1:T(2,128)(2,1)S(1)}, u32[]{:S(2)}, u32[]{:S(2)}) %collective-permute-start.96) | collective-permute-done | bytes 27680 | tf_op jit(solution)/shard_map/ppermute | solution.py:753
  450.1 7.9 %collective-permute-done.97 = bf16[2,2,2,2,864]{4,3,2,0,1:T(2,128)(2,1)S(1)} collective-permute-done((bf16[2,2,2,2,864]{4,3,2,0,1:T(2,128)(2,1)S(1)}, bf16[2,2,2,2,864]{4,3,2,0,1:T(2,128)(2,1)S(1)}, u32[]{:S(2)}, u32[]{:S(2)}) %collective-permute-start.97) | collective-permute-done | bytes 27680 | tf_op jit(solution)/shard_map/ppermute | solution.py:753
  463.1 12.1 %collective-permute-done.105 = f32[9216]{0:T(1024)S(1)} collective-permute-done((f32[9216]{0:T(1024)S(1)}, f32[9216]{0:T(1024)S(1)}, u32[]{:S(2)}, u32[]{:S(2)}) %collective-permute-start.105) | collective-permute-done | bytes 36896 | tf_op jit(solution)/shard_map/ppermute | solution.py:753
  500.7 5.5 place_rows.4
  514.3 4.7 convolution_bitcast_fusion
  519.0 11.0 %collective-permute-done.100 = bf16[2,2,1152]{2,1,0:T(2,128)(2,1)S(1)} collective-permute-done((bf16[2,2,1152]{2,1,0:T(2,128)(2,1)S(1)}, bf16[2,2,1152]{2,1,0:T(2,128)(2,1)S(1)}, u32[]{:S(2)}, u32[]{:S(2)}) %collective-permute-start.100) | collective-permute-done | bytes 9248 | tf_op jit(solution)/shard_map/ppermute | solution.py:753
  531.0 3.8 collective-permute-done.107
  539.5 4.5 collective-permute-done.101
  545.8 15.2 %collective-permute-done.111 = bf16[1,144,1152]{2,1,0:T(8,128)(2,1)S(1)} collective-permute-done((bf16[1,144,1152]{2,1,0:T(8,128)(2,1)}, bf16[1,144,1152]{2,1,0:T(8,128)(2,1)S(1)}, u32[]{:S(2)}, u32[]{:S(2)}) %collective-permute-start.111) | collective-permute-done | bytes 331808 | tf_op jit(solution)/shard_map/ppermute | solution.py:753
  566.8 10.8 %collective-permute-done.109 = bf16[1,144,1152]{2,1,0:T(8,128)(2,1)S(1)} collective-permute-done((bf16[1,144,1152]{2,1,0:T(8,128)(2,1)}, bf16[1,144,1152]{2,1,0:T(8,128)(2,1)S(1)}, u32[]{:S(2)}, u32[]{:S(2)}) %collective-permute-start.109) | collective-permute-done | bytes 331808 | tf_op jit(solution)/shard_map/ppermute | solution.py:753
  583.7 2.9 place_rows.6
  587.9 20.4 %collective-permute-done.110 = bf16[1,144,1152]{2,1,0:T(8,128)(2,1)S(1)} collective-permute-done((bf16[1,144,1152]{2,1,0:T(8,128)(2,1)S(1)}, bf16[1,144,1152]{2,1,0:T(8,128)(2,1)S(1)}, u32[]{:S(2)}, u32[]{:S(2)}) %collective-permute-start.110) | collective-permute-done | bytes 331808 | tf_op jit(solution)/shard_map/ppermute | solution.py:753
  608.3 7.0 %collective-permute-done.108 = bf16[1,144,1152]{2,1,0:T(8,128)(2,1)S(1)} collective-permute-done((bf16[1,144,1152]{2,1,0:T(8,128)(2,1)S(1)}, bf16[1,144,1152]{2,1,0:T(8,128)(2,1)S(1)}, u32[]{:S(2)}, u32[]{:S(2)}) %collective-permute-start.108) | collective-permute-done | bytes 331808 | tf_op jit(solution)/shard_map/ppermute | solution.py:753
  617.4 5.0 collective-permute-done.104
  625.7 15.2 %collective-permute-done.103 = bf16[1,144,1152]{2,1,0:T(8,128)(2,1)} collective-permute-done((bf16[1,144,1152]{2,1,0:T(8,128)(2,1)S(1)}, bf16[1,144,1152]{2,1,0:T(8,128)(2,1)}, u32[]{:S(2)}, u32[]{:S(2)}) %collective-permute-start.103) | collective-permute-done | bytes 331808 | tf_op jit(solution)/shard_map/ppermute | solution.py:753
  (948 shorter events, 278.6 us)
Async XLA Ops:
  123.1 15.6 %collective-permute-start.30 = (bf16[256,1152]{1,0:T(8,128)(2,1)S(1)}, bf16[256,1152]{1,0:T(8,128)(2,1)S(1)}, u32[]{:S(2)}, u32[]{:S(2)}) collective-permute-start(bf16[256,1152]{1,0:T(8,128)(2,1)S(1)} %get-tuple-element.489.refs_1_.refs_6_), channel_id=1, source_target_pairs={{0,2},{1,3},{2,0},{3,1},{4,6},{5,7},{6,4},{7,5},{8,10},{9,11},{10,... | collective-permute-start | bytes 1769480 | tf_op jit(solution)/shard_map/ppermute | solution.py:750
  139.6 15.7 %collective-permute-start.32 = (bf16[256,1152]{1,0:T(8,128)(2,1)S(1)}, bf16[256,1152]{1,0:T(8,128)(2,1)S(1)}, u32[]{:S(2)}, u32[]{:S(2)}) collective-permute-start(bf16[256,1152]{1,0:T(8,128)(2,1)S(1)} %get-tuple-element.493.refs_1_.refs_6_), channel_id=1, source_target_pairs={{0,2},{1,3},{2,0},{3,1},{4,6},{5,7},{6,4},{7,5},{8,10},{9,11},{10,... | collective-permute-start | bytes 1769480 | tf_op jit(solution)/shard_map/ppermute | solution.py:750
  157.6 13.7 %collective-permute-start.36 = (bf16[256,1152]{1,0:T(8,128)(2,1)S(1)}, bf16[256,1152]{1,0:T(8,128)(2,1)S(1)}, u32[]{:S(2)}, u32[]{:S(2)}) collective-permute-start(bf16[256,1152]{1,0:T(8,128)(2,1)S(1)} %get-tuple-element.503.refs_0_.refs_1_), channel_id=1, source_target_pairs={{0,1},{1,0},{2,3},{3,2},{4,5},{5,4},{6,7},{7,6},{8,9},{9,8},{10,11... | collective-permute-start | bytes 1769480 | tf_op jit(solution)/shard_map/ppermute | solution.py:747
  183.7 31.7 %collective-permute-start.45 = (bf16[256,1152]{1,0:T(8,128)(2,1)}, bf16[256,1152]{1,0:T(8,128)(2,1)}, u32[]{:S(2)}, u32[]{:S(2)}) collective-permute-start(bf16[256,1152]{1,0:T(8,128)(2,1)} %get-tuple-element.534.refs_1_), channel_id=1, source_target_pairs={{0,2},{1,3},{2,0},{3,1},{4,6},{5,7},{6,4},{7,5},{8,10},{9,11},{10,... | collective-permute-start | bytes 1769480 | tf_op jit(solution)/shard_map/ppermute | solution.py:750
  185.2 32.9 %collective-permute-start.46 = (bf16[256,1152]{1,0:T(8,128)(2,1)}, bf16[256,1152]{1,0:T(8,128)(2,1)}, u32[]{:S(2)}, u32[]{:S(2)}) collective-permute-start(bf16[256,1152]{1,0:T(8,128)(2,1)} %get-tuple-element.537.refs_1_), channel_id=1, source_target_pairs={{0,2},{1,3},{2,0},{3,1},{4,6},{5,7},{6,4},{7,5},{8,10},{9,11},{10,... | collective-permute-start | bytes 1769480 | tf_op jit(solution)/shard_map/ppermute | solution.py:750
  190.2 30.6 %collective-permute-start.47 = (bf16[128,1152]{1,0:T(8,128)(2,1)}, bf16[128,1152]{1,0:T(8,128)(2,1)}, u32[]{:S(2)}, u32[]{:S(2)}) collective-permute-start(bf16[128,1152]{1,0:T(8,128)(2,1)} %get-tuple-element.540.refs_1_), channel_id=1, source_target_pairs={{0,2},{1,3},{2,0},{3,1},{4,6},{5,7},{6,4},{7,5},{8,10},{9,11},{10,... | collective-permute-start | bytes 884744 | tf_op jit(solution)/shard_map/ppermute | solution.py:750
  192.5 33.0 %collective-permute-start.48 = (bf16[128,1152]{1,0:T(8,128)(2,1)}, bf16[128,1152]{1,0:T(8,128)(2,1)}, u32[]{:S(2)}, u32[]{:S(2)}) collective-permute-start(bf16[128,1152]{1,0:T(8,128)(2,1)} %get-tuple-element.542.refs_0_), channel_id=1, source_target_pairs={{0,2},{1,3},{2,0},{3,1},{4,6},{5,7},{6,4},{7,5},{8,10},{9,11},{10,... | collective-permute-start | bytes 884744 | tf_op jit(solution)/shard_map/ppermute | solution.py:750
  195.4 58.2 %collective-permute-start.50 = (bf16[256,1152]{1,0:T(8,128)(2,1)}, bf16[256,1152]{1,0:T(8,128)(2,1)}, u32[]{:S(2)}, u32[]{:S(2)}) collective-permute-start(bf16[256,1152]{1,0:T(8,128)(2,1)} %get-tuple-element.551.refs_0_), channel_id=1, source_target_pairs={{0,2},{1,3},{2,0},{3,1},{4,6},{5,7},{6,4},{7,5},{8,10},{9,11},{10,... | collective-permute-start | bytes 1769480 | tf_op jit(solution)/shard_map/ppermute | solution.py:750
  230.0 19.4 %collective-permute-start.49 = (bf16[128,1152]{1,0:T(8,128)(2,1)}, bf16[128,1152]{1,0:T(8,128)(2,1)}, u32[]{:S(2)}, u32[]{:S(2)}) collective-permute-start(bf16[128,1152]{1,0:T(8,128)(2,1)} %get-tuple-element.549.refs_2_.refs_5_), channel_id=1, source_target_pairs={{0,1},{1,0},{2,3},{3,2},{4,5},{5,4},{6,7},{7,6},{8,9},{9,8},{10,11... | collective-permute-start | bytes 884744 | tf_op jit(solution)/shard_map/ppermute | solution.py:747
  230.0 30.0 %collective-permute-start.52 = (bf16[256,1152]{1,0:T(8,128)(2,1)}, bf16[256,1152]{1,0:T(8,128)(2,1)}, u32[]{:S(2)}, u32[]{:S(2)}) collective-permute-start(bf16[256,1152]{1,0:T(8,128)(2,1)} %get-tuple-element.558.refs_0_), channel_id=1, source_target_pairs={{0,2},{1,3},{2,0},{3,1},{4,6},{5,7},{6,4},{7,5},{8,10},{9,11},{10,... | collective-permute-start | bytes 1769480 | tf_op jit(solution)/shard_map/ppermute | solution.py:750
  264.6 61.5 %collective-permute-start.58 = (bf16[4,144,1152]{2,1,0:T(8,128)(2,1)}, bf16[4,144,1152]{2,1,0:T(8,128)(2,1)}, u32[]{:S(2)}, u32[]{:S(2)}) collective-permute-start(bf16[4,144,1152]{2,1,0:T(8,128)(2,1)} %get-tuple-element.583), channel_id=1, source_target_pairs={{0,4},{4,0},{8,12},{12,8},{16,20},{20,16},{24,28},{28,24},{1,5},{5... | collective-permute-start | bytes 3981320 | tf_op jit(solution)/shard_map/ppermute | solution.py:753
  286.6 64.0 %collective-permute-start.67 = (bf16[4,144,1152]{2,1,0:T(8,128)(2,1)}, bf16[4,144,1152]{2,1,0:T(8,128)(2,1)}, u32[]{:S(2)}, u32[]{:S(2)}) collective-permute-start(bf16[4,144,1152]{2,1,0:T(8,128)(2,1)} %get-tuple-element.610), channel_id=1, source_target_pairs={{0,8},{4,12},{8,0},{12,4},{16,24},{20,28},{24,16},{28,20},{1,9},{5... | collective-permute-start | bytes 3981320 | tf_op jit(solution)/shard_map/ppermute | solution.py:753
  290.9 37.6 %collective-permute-start.59 = (bf16[256,1152]{1,0:T(8,128)(2,1)}, bf16[256,1152]{1,0:T(8,128)(2,1)}, u32[]{:S(2)}, u32[]{:S(2)}) collective-permute-start(bf16[256,1152]{1,0:T(8,128)(2,1)} %get-tuple-element.585.refs_0_), channel_id=1, source_target_pairs={{0,2},{1,3},{2,0},{3,1},{4,6},{5,7},{6,4},{7,5},{8,10},{9,11},{10,... | collective-permute-start | bytes 1769480 | tf_op jit(solution)/shard_map/ppermute | solution.py:750
  291.5 21.7 %collective-permute-start.57 = (bf16[128,1152]{1,0:T(8,128)(2,1)S(1)}, bf16[128,1152]{1,0:T(8,128)(2,1)S(1)}, u32[]{:S(2)}, u32[]{:S(2)}) collective-permute-start(bf16[128,1152]{1,0:T(8,128)(2,1)S(1)} %get-tuple-element.575.refs_0_), channel_id=1, source_target_pairs={{0,2},{1,3},{2,0},{3,1},{4,6},{5,7},{6,4},{7,5},{8,10},{9,11},{10,... | collective-permute-start | bytes 884744 | tf_op jit(solution)/shard_map/ppermute | solution.py:750
  333.4 16.2 %collective-permute-start.66 = (bf16[256,1152]{1,0:T(8,128)(2,1)S(1)}, bf16[256,1152]{1,0:T(8,128)(2,1)S(1)}, u32[]{:S(2)}, u32[]{:S(2)}) collective-permute-start(bf16[256,1152]{1,0:T(8,128)(2,1)S(1)} %copy-done.181), channel_id=1, source_target_pairs={{0,2},{1,3},{2,0},{3,1},{4,6},{5,7},{6,4},{7,5},{8,10},{9,11},{10,... | collective-permute-start | bytes 1769480 | tf_op jit(solution)/shard_map/ppermute | solution.py:750
  343.1 15.1 %collective-permute-start.68 = (bf16[64,1152]{1,0:T(8,128)(2,1)S(1)}, bf16[64,1152]{1,0:T(8,128)(2,1)S(1)}, u32[]{:S(2)}, u32[]{:S(2)}) collective-permute-start(bf16[64,1152]{1,0:T(8,128)(2,1)S(1)} %get-tuple-element.616.refs_0_), channel_id=1, source_target_pairs={{0,2},{1,3},{2,0},{3,1},{4,6},{5,7},{6,4},{7,5},{8,10},{9,11},{10,... | collective-permute-start | bytes 442376 | tf_op jit(solution)/shard_map/ppermute | solution.py:750
  359.4 15.1 %collective-permute-start.72 = (bf16[128,1152]{1,0:T(8,128)(2,1)S(1)}, bf16[128,1152]{1,0:T(8,128)(2,1)S(1)}, u32[]{:S(2)}, u32[]{:S(2)}) collective-permute-start(bf16[128,1152]{1,0:T(8,128)(2,1)S(1)} %get-tuple-element.634.refs_0_), channel_id=1, source_target_pairs={{0,2},{1,3},{2,0},{3,1},{4,6},{5,7},{6,4},{7,5},{8,10},{9,11},{10,... | collective-permute-start | bytes 884744 | tf_op jit(solution)/shard_map/ppermute | solution.py:750
  387.5 18.9 %collective-permute-start.78 = (bf16[128,1152]{1,0:T(8,128)(2,1)S(1)}, bf16[128,1152]{1,0:T(8,128)(2,1)S(1)}, u32[]{:S(2)}, u32[]{:S(2)}) collective-permute-start(bf16[128,1152]{1,0:T(8,128)(2,1)S(1)} %get-tuple-element.659.refs_0_), channel_id=1, source_target_pairs={{0,2},{1,3},{2,0},{3,1},{4,6},{5,7},{6,4},{7,5},{8,10},{9,11},{10,... | collective-permute-start | bytes 884744 | tf_op jit(solution)/shard_map/ppermute | solution.py:750
  388.5 19.2 %collective-permute-start.79 = (bf16[128,1152]{1,0:T(8,128)(2,1)S(1)}, bf16[128,1152]{1,0:T(8,128)(2,1)S(1)}, u32[]{:S(2)}, u32[]{:S(2)}) collective-permute-start(bf16[128,1152]{1,0:T(8,128)(2,1)S(1)} %get-tuple-element.662.refs_0_), channel_id=1, source_target_pairs={{0,2},{1,3},{2,0},{3,1},{4,6},{5,7},{6,4},{7,5},{8,10},{9,11},{10,... | collective-permute-start | bytes 884744 | tf_op jit(solution)/shard_map/ppermute | solution.py:750
  389.7 70.8 %collective-permute-start.82 = (bf16[4,144,1152]{2,1,0:T(8,128)(2,1)}, bf16[4,144,1152]{2,1,0:T(8,128)(2,1)}, u32[]{:S(2)}, u32[]{:S(2)}) collective-permute-start(bf16[4,144,1152]{2,1,0:T(8,128)(2,1)} %get-tuple-element.690), channel_id=1, source_target_pairs={{0,4},{4,0},{8,12},{12,8},{16,20},{20,16},{24,28},{28,24},{1,5},{5... | collective-permute-start | bytes 3981320 | tf_op jit(solution)/shard_map/ppermute | solution.py:753
  391.2 14.8 %collective-permute-start.77 = (bf16[64,1152]{1,0:T(8,128)(2,1)S(1)}, bf16[64,1152]{1,0:T(8,128)(2,1)S(1)}, u32[]{:S(2)}, u32[]{:S(2)}) collective-permute-start(bf16[64,1152]{1,0:T(8,128)(2,1)S(1)} %get-tuple-element.656.refs_0_), channel_id=1, source_target_pairs={{0,2},{1,3},{2,0},{3,1},{4,6},{5,7},{6,4},{7,5},{8,10},{9,11},{10,... | collective-permute-start | bytes 442376 | tf_op jit(solution)/shard_map/ppermute | solution.py:750
  409.3 67.3 %collective-permute-start.81 = (bf16[4,144,1152]{2,1,0:T(8,128)(2,1)}, bf16[4,144,1152]{2,1,0:T(8,128)(2,1)}, u32[]{:S(2)}, u32[]{:S(2)}) collective-permute-start(bf16[4,144,1152]{2,1,0:T(8,128)(2,1)} %get-tuple-element.687), channel_id=1, source_target_pairs={{0,4},{4,0},{8,12},{12,8},{16,20},{20,16},{24,28},{28,24},{1,5},{5... | collective-permute-start | bytes 3981320 | tf_op jit(solution)/shard_map/ppermute | solution.py:753
  411.6 47.2 %collective-permute-start.84 = (bf16[2,144,1152]{2,1,0:T(8,128)(2,1)}, bf16[2,144,1152]{2,1,0:T(8,128)(2,1)}, u32[]{:S(2)}, u32[]{:S(2)}) collective-permute-start(bf16[2,144,1152]{2,1,0:T(8,128)(2,1)} %get-tuple-element.696), channel_id=1, source_target_pairs={{0,8},{4,12},{8,0},{12,4},{16,24},{20,28},{24,16},{28,20},{1,9},{5... | collective-permute-start | bytes 1990664 | tf_op jit(solution)/shard_map/ppermute | solution.py:753
  412.1 68.3 %collective-permute-start.83 = (bf16[4,144,1152]{2,1,0:T(8,128)(2,1)}, bf16[4,144,1152]{2,1,0:T(8,128)(2,1)}, u32[]{:S(2)}, u32[]{:S(2)}) collective-permute-start(bf16[4,144,1152]{2,1,0:T(8,128)(2,1)} %get-tuple-element.693), channel_id=1, source_target_pairs={{0,8},{4,12},{8,0},{12,4},{16,24},{20,28},{24,16},{28,20},{1,9},{5... | collective-permute-start | bytes 3981320 | tf_op jit(solution)/shard_map/ppermute | solution.py:753
  414.0 35.6 %collective-permute-start.96 = (bf16[4,1,2,2,864]{4,3,2,0,1:T(2,128)(2,1)S(1)}, bf16[4,1,2,2,864]{4,3,2,0,1:T(2,128)(2,1)S(1)}, u32[]{:S(2)}, u32[]{:S(2)}) collective-permute-start(bf16[4,1,2,2,864]{4,3,2,0,1:T(2,128)(2,1)S(1)} %get-tuple-element.775), channel_id=1, source_target_pairs={{0,4},{4,0},{8,12},{12,8},{16,20},{20,16},{24,28},{28,24},{1,5},{5... | collective-permute-start | bytes 82952 | tf_op jit(solution)/shard_map/ppermute | solution.py:753
  458.0 18.5 %collective-permute-start.85 = (bf16[2,144,1152]{2,1,0:T(8,128)(2,1)}, bf16[2,144,1152]{2,1,0:T(8,128)(2,1)}, u32[]{:S(2)}, u32[]{:S(2)}) collective-permute-start(bf16[2,144,1152]{2,1,0:T(8,128)(2,1)} %get-tuple-element.699), channel_id=1, source_target_pairs={{0,4},{4,0},{8,12},{12,8},{16,20},{20,16},{24,28},{28,24},{1,5},{5... | collective-permute-start | bytes 1990664 | tf_op jit(solution)/shard_map/ppermute | solution.py:753
  458.8 16.4 %collective-permute-start.105 = (f32[9216]{0:T(1024)S(1)}, f32[9216]{0:T(1024)S(1)}, u32[]{:S(2)}, u32[]{:S(2)}) collective-permute-start(f32[9216]{0:T(1024)S(1)} %concatenate.65), channel_id=1, source_target_pairs={{0,4},{4,0},{8,12},{12,8},{16,20},{20,16},{24,28},{28,24},{1,5},{5... | collective-permute-start | bytes 110600 | tf_op jit(solution)/shard_map/ppermute | solution.py:753
  460.5 14.8 %collective-permute-start.98 = (bf16[1,4,2,2,864]{4,2,1,3,0:T(2,128)(2,1)S(1)}, bf16[1,4,2,2,864]{4,2,1,3,0:T(2,128)(2,1)S(1)}, u32[]{:S(2)}, u32[]{:S(2)}) collective-permute-start(bf16[1,4,2,2,864]{4,2,1,3,0:T(2,128)(2,1)S(1)} %get-tuple-element.771), channel_id=1, source_target_pairs={{0,16},{4,20},{8,24},{12,28},{16,0},{20,4},{24,8},{28,12},{1,17},{... | collective-permute-start | bytes 82952 | tf_op jit(solution)/shard_map/ppermute | solution.py:753
  475.2 22.5 %collective-permute-start.87 = (bf16[256,1152]{1,0:T(8,128)(2,1)}, bf16[256,1152]{1,0:T(8,128)(2,1)}, u32[]{:S(2)}, u32[]{:S(2)}) collective-permute-start(bf16[256,1152]{1,0:T(8,128)(2,1)} %copy-done.174), channel_id=1, source_target_pairs={{0,1},{1,0},{2,3},{3,2},{4,5},{5,4},{6,7},{7,6},{8,9},{9,8},{10,11... | collective-permute-start | bytes 1769480 | tf_op jit(solution)/shard_map/ppermute | solution.py:747
  475.2 23.7 %collective-permute-start.86 = (bf16[256,1152]{1,0:T(8,128)(2,1)}, bf16[256,1152]{1,0:T(8,128)(2,1)}, u32[]{:S(2)}, u32[]{:S(2)}) collective-permute-start(bf16[256,1152]{1,0:T(8,128)(2,1)} %copy-done.172), channel_id=1, source_target_pairs={{0,1},{1,0},{2,3},{3,2},{4,5},{5,4},{6,7},{7,6},{8,9},{9,8},{10,11... | collective-permute-start | bytes 1769480 | tf_op jit(solution)/shard_map/ppermute | solution.py:747
  476.5 29.7 %collective-permute-start.88 = (bf16[128,1152]{1,0:T(8,128)(2,1)}, bf16[128,1152]{1,0:T(8,128)(2,1)}, u32[]{:S(2)}, u32[]{:S(2)}) collective-permute-start(bf16[128,1152]{1,0:T(8,128)(2,1)} %copy-done.209), channel_id=1, source_target_pairs={{0,1},{1,0},{2,3},{3,2},{4,5},{5,4},{6,7},{7,6},{8,9},{9,8},{10,11... | collective-permute-start | bytes 884744 | tf_op jit(solution)/shard_map/ppermute | solution.py:747
  476.6 32.2 %collective-permute-start.106 = (f32[9216]{0:T(1024)S(1)}, f32[9216]{0:T(1024)}, u32[]{:S(2)}, u32[]{:S(2)}) collective-permute-start(f32[9216]{0:T(1024)S(1)} %add.88), channel_id=1, source_target_pairs={{0,8},{4,12},{8,0},{12,4},{16,24},{20,28},{24,16},{28,20},{1,9},{5... | collective-permute-start | bytes 110600 | tf_op jit(solution)/shard_map/ppermute | solution.py:753
  480.4 31.3 %collective-permute-start.99 = (bf16[4,2,1152]{2,1,0:T(2,128)(2,1)}, bf16[4,2,1152]{2,1,0:T(2,128)(2,1)}, u32[]{:S(2)}, u32[]{:S(2)}) collective-permute-start(bf16[4,2,1152]{2,1,0:T(2,128)(2,1)} %convert_element_type.135), channel_id=1, source_target_pairs={{0,16},{4,20},{8,24},{12,28},{16,0},{20,4},{24,8},{28,12},{1,17},{... | collective-permute-start | bytes 55304 | tf_op jit(solution)/shard_map/ppermute | solution.py:753
  498.5 80.0 %collective-permute-start.92 = (bf16[4,144,1152]{2,1,0:T(8,128)(2,1)}, bf16[4,144,1152]{2,1,0:T(8,128)(2,1)S(1)}, u32[]{:S(2)}, u32[]{:S(2)}) collective-permute-start(bf16[4,144,1152]{2,1,0:T(8,128)(2,1)} %get-tuple-element.718), channel_id=1, source_target_pairs={{0,4},{4,0},{8,12},{12,8},{16,20},{20,16},{24,28},{28,24},{1,5},{5... | collective-permute-start | bytes 3981320 | tf_op jit(solution)/shard_map/ppermute | solution.py:753
  498.9 63.1 %collective-permute-start.89 = (bf16[2,144,1152]{2,1,0:T(8,128)(2,1)}, bf16[2,144,1152]{2,1,0:T(8,128)(2,1)}, u32[]{:S(2)}, u32[]{:S(2)}) collective-permute-start(bf16[2,144,1152]{2,1,0:T(8,128)(2,1)} %get-tuple-element.709), channel_id=1, source_target_pairs={{0,8},{4,12},{8,0},{12,4},{16,24},{20,28},{24,16},{28,20},{1,9},{5... | collective-permute-start | bytes 1990664 | tf_op jit(solution)/shard_map/ppermute | solution.py:753
  506.2 57.3 %collective-permute-start.90 = (bf16[2,144,1152]{2,1,0:T(8,128)(2,1)}, bf16[2,144,1152]{2,1,0:T(8,128)(2,1)}, u32[]{:S(2)}, u32[]{:S(2)}) collective-permute-start(bf16[2,144,1152]{2,1,0:T(8,128)(2,1)} %get-tuple-element.712), channel_id=1, source_target_pairs={{0,8},{4,12},{8,0},{12,4},{16,24},{20,28},{24,16},{28,20},{1,9},{5... | collective-permute-start | bytes 1990664 | tf_op jit(solution)/shard_map/ppermute | solution.py:753
  508.8 56.6 %collective-permute-start.91 = (bf16[2,144,1152]{2,1,0:T(8,128)(2,1)}, bf16[2,144,1152]{2,1,0:T(8,128)(2,1)}, u32[]{:S(2)}, u32[]{:S(2)}) collective-permute-start(bf16[2,144,1152]{2,1,0:T(8,128)(2,1)} %get-tuple-element.715), channel_id=1, source_target_pairs={{0,4},{4,0},{8,12},{12,8},{16,20},{20,16},{24,28},{28,24},{1,5},{5... | collective-permute-start | bytes 1990664 | tf_op jit(solution)/shard_map/ppermute | solution.py:753
  512.5 17.5 %collective-permute-start.100 = (bf16[2,2,1152]{2,1,0:T(2,128)(2,1)S(1)}, bf16[2,2,1152]{2,1,0:T(2,128)(2,1)S(1)}, u32[]{:S(2)}, u32[]{:S(2)}) collective-permute-start(bf16[2,2,1152]{2,1,0:T(2,128)(2,1)S(1)} %slice.292), channel_id=1, source_target_pairs={{0,8},{4,12},{8,0},{12,4},{16,24},{20,28},{24,16},{28,20},{1,9},{5... | collective-permute-start | bytes 27656 | tf_op jit(solution)/shard_map/ppermute | solution.py:753
  544.0 16.9 %collective-permute-start.111 = (bf16[1,144,1152]{2,1,0:T(8,128)(2,1)}, bf16[1,144,1152]{2,1,0:T(8,128)(2,1)S(1)}, u32[]{:S(2)}, u32[]{:S(2)}) collective-permute-start(bf16[1,144,1152]{2,1,0:T(8,128)(2,1)} %copy-done.259), channel_id=1, source_target_pairs={{0,16},{4,20},{8,24},{12,28},{16,0},{20,4},{24,8},{28,12},{1,17},{... | collective-permute-start | bytes 995336 | tf_op jit(solution)/shard_map/ppermute | solution.py:753
  560.9 16.6 %collective-permute-start.109 = (bf16[1,144,1152]{2,1,0:T(8,128)(2,1)}, bf16[1,144,1152]{2,1,0:T(8,128)(2,1)S(1)}, u32[]{:S(2)}, u32[]{:S(2)}) collective-permute-start(bf16[1,144,1152]{2,1,0:T(8,128)(2,1)} %copy-done.258), channel_id=1, source_target_pairs={{0,16},{4,20},{8,24},{12,28},{16,0},{20,4},{24,8},{28,12},{1,17},{... | collective-permute-start | bytes 995336 | tf_op jit(solution)/shard_map/ppermute | solution.py:753
  562.1 24.5 %collective-permute-start.95 = (bf16[64,1152]{1,0:T(8,128)(2,1)S(1)}, bf16[64,1152]{1,0:T(8,128)(2,1)S(1)}, u32[]{:S(2)}, u32[]{:S(2)}) collective-permute-start(bf16[64,1152]{1,0:T(8,128)(2,1)S(1)} %copy-done.225), channel_id=1, source_target_pairs={{0,1},{1,0},{2,3},{3,2},{4,5},{5,4},{6,7},{7,6},{8,9},{9,8},{10,11... | collective-permute-start | bytes 442376 | tf_op jit(solution)/shard_map/ppermute | solution.py:747
  563.5 18.2 %collective-permute-start.94 = (bf16[128,1152]{1,0:T(8,128)(2,1)S(1)}, bf16[128,1152]{1,0:T(8,128)(2,1)S(1)}, u32[]{:S(2)}, u32[]{:S(2)}) collective-permute-start(bf16[128,1152]{1,0:T(8,128)(2,1)S(1)} %copy-done.214), channel_id=1, source_target_pairs={{0,1},{1,0},{2,3},{3,2},{4,5},{5,4},{6,7},{7,6},{8,9},{9,8},{10,11... | collective-permute-start | bytes 884744 | tf_op jit(solution)/shard_map/ppermute | solution.py:747
  565.4 16.4 %collective-permute-start.93 = (bf16[128,1152]{1,0:T(8,128)(2,1)S(1)}, bf16[128,1152]{1,0:T(8,128)(2,1)S(1)}, u32[]{:S(2)}, u32[]{:S(2)}) collective-permute-start(bf16[128,1152]{1,0:T(8,128)(2,1)S(1)} %copy-done.212), channel_id=1, source_target_pairs={{0,1},{1,0},{2,3},{3,2},{4,5},{5,4},{6,7},{7,6},{8,9},{9,8},{10,11... | collective-permute-start | bytes 884744 | tf_op jit(solution)/shard_map/ppermute | solution.py:747
  577.5 30.7 %collective-permute-start.110 = (bf16[1,144,1152]{2,1,0:T(8,128)(2,1)S(1)}, bf16[1,144,1152]{2,1,0:T(8,128)(2,1)S(1)}, u32[]{:S(2)}, u32[]{:S(2)}) collective-permute-start(bf16[1,144,1152]{2,1,0:T(8,128)(2,1)S(1)} %get-tuple-element.744), channel_id=1, source_target_pairs={{0,16},{4,20},{8,24},{12,28},{16,0},{20,4},{24,8},{28,12},{1,17},{... | collective-permute-start | bytes 995336 | tf_op jit(solution)/shard_map/ppermute | solution.py:753
  578.5 36.9 %collective-permute-start.108 = (bf16[1,144,1152]{2,1,0:T(8,128)(2,1)S(1)}, bf16[1,144,1152]{2,1,0:T(8,128)(2,1)S(1)}, u32[]{:S(2)}, u32[]{:S(2)}) collective-permute-start(bf16[1,144,1152]{2,1,0:T(8,128)(2,1)S(1)} %get-tuple-element.740), channel_id=1, source_target_pairs={{0,16},{4,20},{8,24},{12,28},{16,0},{20,4},{24,8},{28,12},{1,17},{... | collective-permute-start | bytes 995336 | tf_op jit(solution)/shard_map/ppermute | solution.py:753
  581.7 40.7 %collective-permute-start.104 = (bf16[1,144,1152]{2,1,0:T(8,128)(2,1)S(1)}, bf16[1,144,1152]{2,1,0:T(8,128)(2,1)S(1)}, u32[]{:S(2)}, u32[]{:S(2)}) collective-permute-start(bf16[1,144,1152]{2,1,0:T(8,128)(2,1)S(1)} %get-tuple-element.733), channel_id=1, source_target_pairs={{0,16},{4,20},{8,24},{12,28},{16,0},{20,4},{24,8},{28,12},{1,17},{... | collective-permute-start | bytes 995336 | tf_op jit(solution)/shard_map/ppermute | solution.py:753
  581.8 40.7 %collective-permute-start.102 = (bf16[2,144,1152]{2,1,0:T(8,128)(2,1)S(1)}, bf16[2,144,1152]{2,1,0:T(8,128)(2,1)S(1)}, u32[]{:S(2)}, u32[]{:S(2)}) collective-permute-start(bf16[2,144,1152]{2,1,0:T(8,128)(2,1)S(1)} %get-tuple-element.729), channel_id=1, source_target_pairs={{0,8},{4,12},{8,0},{12,4},{16,24},{20,28},{24,16},{28,20},{1,9},{5... | collective-permute-start | bytes 1990664 | tf_op jit(solution)/shard_map/ppermute | solution.py:753
  623.1 17.7 %collective-permute-start.103 = (bf16[1,144,1152]{2,1,0:T(8,128)(2,1)S(1)}, bf16[1,144,1152]{2,1,0:T(8,128)(2,1)}, u32[]{:S(2)}, u32[]{:S(2)}) collective-permute-start(bf16[1,144,1152]{2,1,0:T(8,128)(2,1)S(1)} %get-tuple-element.731), channel_id=1, source_target_pairs={{0,16},{4,20},{8,24},{12,28},{16,0},{20,4},{24,8},{28,12},{1,17},{... | collective-permute-start | bytes 995336 | tf_op jit(solution)/shard_map/ppermute | solution.py:753
  (346 other events, 2836.7 us)

commit v4 on v3

--- a/solution.py
+++ b/solution.py
@@ -37,6 +37,14 @@
     return jax.ShapeDtypeStruct(shape, dtype)
 
 
+COSTS = {
+    "gather_rows": 0.8, "ln_open": 0.4, "near_sum": 0.4, "merge_attn": 0.6, "merge_mlp": 0.6,
+    "finish": 1.0, "first_grad": 0.5, "qkv_forward": 1.2, "qkv_backward": 1.2, "mlp_forward": 3.5,
+    "mlp_backward": 3.0, "ln_back": 1.2, "attn_forward": 4.0, "attn_backward": 9.0,
+    "weight_grads": 6.5, "halve": 1.5, "place_rows": 3.0, "table_rows": 1.0,
+}
+
+
 class Queue:
     def __init__(self):
         self.token = jnp.zeros((8, 128), F32)
@@ -45,32 +53,54 @@
         *values, self.token = lax.optimization_barrier((*values, self.token))
         return values[0] if len(values) == 1 else tuple(values)
 
-    def call(self, body, operands, outs, name, scalars=(), far=(), scratch=(), limit=16):
+    def call(
+        self, body, operands, outs, name, scalars=(), far=(), far_outs=(), scratch=(), copies=0, limit=10
+    ):
         fast = pl.BlockSpec(memory_space=pltpu.VMEM)
         small = pl.BlockSpec(memory_space=pltpu.SMEM)
-        anywhere = pl.BlockSpec(memory_space=pl.ANY)
-        inputs = len(scalars) + len(far) + len(operands)
+        slow = pl.BlockSpec(memory_space=pltpu.HBM)
+        last = len(scalars) + len(far) + len(operands) + len(outs) + len(far_outs)
 
         def whole(token_ref, *refs):
-            body(*refs[: inputs + len(outs)], *refs[inputs + len(outs) + 1 :])
-            refs[inputs + len(outs)][...] = token_ref[...]
+            body(*refs[:last], *refs[last + 1 :])
+            refs[last][...] = token_ref[...]
 
         *results, self.token = pl.pallas_call(
             whole,
-            in_specs=[fast] + [small] * len(scalars) + [anywhere] * len(far) + [fast] * len(operands),
-            out_specs=[fast] * (len(outs) + 1),
-            out_shape=[*outs, shaped((8, 128), F32)],
-            scratch_shapes=list(scratch),
-            cost_estimate=pl.CostEstimate(flops=1000, transcendentals=0, bytes_accessed=1000),
+            in_specs=[fast] + [small] * len(scalars) + [slow] * len(far) + [fast] * len(operands),
+            out_specs=[fast] * len(outs) + [slow] * len(far_outs) + [fast],
+            out_shape=[
+                *outs,
+                *[pltpu.HBM(out.shape, out.dtype) for out in far_outs],
+                shaped((8, 128), F32),
+            ],
+            scratch_shapes=list(scratch)
+            + ([pltpu.SemaphoreType.DMA((copies,))] if copies else []),
+            cost_estimate=pl.CostEstimate(
+                flops=int(COSTS.get(name, 1.0) * 1e9), transcendentals=0, bytes_accessed=1000
+            ),
             compiler_params=pltpu.CompilerParams(vmem_limit_bytes=limit * MIB),
             name=name,
         )(
             pltpu.with_memory_space_constraint(self.token, pltpu.VMEM),
             *scalars,
-            *far,
+            *[pltpu.with_memory_space_constraint(value, pltpu.HBM) for value in far],
             *[pltpu.with_memory_space_constraint(value, pltpu.VMEM) for value in operands],
         )
         return results
+
+
+def copy_rows(sources, target, semaphores, first=0):
+    found, row = [], 0
+    for index, source in enumerate(sources):
+        count = source.shape[0]
+        copy = pltpu.make_async_copy(
+            source, target.at[pl.ds(row, count)], semaphores.at[first + index]
+        )
+        copy.start()
+        found.append(copy)
+        row += count
+    return found
 
 
 def normed_of(values):
@@ -114,33 +144,34 @@
     return (index == places).astype(F32).astype(BF16)
 
 
-def gather_rows(queue, core, perm, source, rows):
+def gather_rows(queue, core, perm, source, rows, dtype):
     length, features = source.shape
 
     def body(core_ref, perm_ref, source_ref, out_ref):
         pick = pick_columns(rows.places(perm_ref, core_ref[0]), length)
-        out_ref[...] = tn(pick, source_ref[...])
-
-    outs = [shaped((rows.count, features), F32)]
+        out_ref[...] = tn(pick, source_ref[...]).astype(dtype)
+
+    outs = [shaped((rows.count, features), dtype)]
     return queue.call(body, [perm, source], outs, "gather_rows", scalars=[core])[0]
 
 
-def place_rows(queue, core, perm, pairs, rows):
+def place_rows(queue, core, perm, own, other, rows, first):
     length = perm.shape[1]
-    features = pairs[0][0].shape[1]
-
-    def body(core_ref, perm_ref, *refs):
-        out_ref = refs[-1]
+    features = own.shape[1]
+    last = first + sum(chunk.count for chunk in rows)
+
+    def body(core_ref, perm_ref, own_ref, other_ref, out_ref):
         places = [
-            chunk.places(perm_ref, core_ref[0], other) for chunk in rows for other in (False, True)
+            chunk.places(perm_ref, core_ref[0], other) for other in (False, True) for chunk in rows
         ]
-        values = jnp.concatenate([ref[...] for ref in refs[:-1]], axis=0)
+        values = jnp.concatenate([own_ref[first:last, :], other_ref[first:last, :]], axis=0)
         pick = pick_columns(jnp.concatenate(places, axis=1), length)
         out_ref[...] = nn(pick, values).astype(BF16)
 
-    operands = [perm] + [half for pair in pairs for half in pair]
     outs = [shaped((length, features))]
-    return queue.call(body, operands, outs, "place_rows", scalars=[core], limit=24)[0]
+    return queue.call(
+        body, [perm, own, other], outs, "place_rows", scalars=[core], limit=12
+    )[0]
 
 
 def table_rows(queue, core, perm, waves, rows, filler=None):
@@ -228,19 +259,27 @@
     return queue.call(body, operands, outs, "merge_mlp")
 
 
-def finish(queue, middle, near, far, d_out, small, mods, at):
-    features = middle.shape[1]
-    block, latent = at
-
-    def body(mid_ref, near_ref, far_ref, d_ref, small_ref, mods_ref, out_ref, sums_ref):
-        branch = branch_of(near_ref, far_ref, small_ref, DOWN_BIAS + block, features)
-        gate = mods_ref[block, latent, GATE_MLP : GATE_MLP + 1, :]
-        out_ref[...] = (mid_ref[...] + gate * branch).astype(BF16)
-        total = jnp.sum(d_ref[...] * branch, axis=0, keepdims=True)
-        sums_ref[...] = jnp.broadcast_to(total, (8, features))
-
-    outs = [shaped(middle.shape), shaped((8, features), F32)]
-    return queue.call(body, [middle, near, far, d_out, small, mods], outs, "finish")
+def finish(queue, parts, small, mods):
+    counts = [part[0].shape[0] for part in parts]
+    features = parts[0][0].shape[1]
+
+    def body(small_ref, mods_ref, *refs):
+        out_ref, sums_ref = refs[-2:]
+        sums_ref[...] = jnp.zeros_like(sums_ref)
+        first = 0
+        for index, count in enumerate(counts):
+            mid_ref, near_ref, far_ref, d_ref = refs[4 * index : 4 * index + 4]
+            block, latent = parts[index][4]
+            branch = branch_of(near_ref, far_ref, small_ref, DOWN_BIAS + block, features)
+            gate = mods_ref[block, latent, GATE_MLP : GATE_MLP + 1, :]
+            out_ref[first : first + count, :] = (mid_ref[...] + gate * branch).astype(BF16)
+            total = jnp.sum(d_ref[...].astype(F32) * branch, axis=0, keepdims=True)
+            sums_ref[latent : latent + 1, :] += total
+            first += count
+
+    outs = [shaped((sum(counts), features)), shaped((8, features), F32)]
+    operands = [small, mods] + [value for part in parts for value in part[:4]]
+    return queue.call(body, operands, outs, "finish")
 
 
 def first_grad(queue, d_out, mods, at):
@@ -249,7 +288,7 @@
 
     def body(d_ref, mods_ref, out_ref, sums_ref):
         gate = mods_ref[block, latent, GATE_MLP : GATE_MLP + 1, :]
-        grad = (gate * d_ref[...]).astype(BF16)
+        grad = (gate * d_ref[...].astype(F32)).astype(BF16)
         out_ref[...] = grad
         total = jnp.sum(grad.astype(F32), axis=0, keepdims=True)
         sums_ref[...] = jnp.broadcast_to(total, (8, features))
@@ -259,18 +298,27 @@
 
 
 def qkv_forward(queue, own, other, weight, small, block):
-    rows = own.shape[0]
+    rows, features = own.shape
     width = weight.shape[1]
 
-    def body(own_ref, other_ref, w_ref, small_ref, out_ref):
+    def body(own_ref, other_ref, w_ref, small_ref, out_ref, rows_ref, done):
+        copies = copy_rows([own_ref, other_ref], rows_ref, done)
         bias = small_ref[QKV_BIAS + block : QKV_BIAS + block + 1, :width]
         both = jnp.concatenate([own_ref[...], other_ref[...]], axis=0)
         out = (nt(both, w_ref[block]) + bias).astype(BF16)
         out_ref[0] = out[:rows]
         out_ref[1] = out[rows:]
-
-    outs = [shaped((2, rows, width))]
-    return queue.call(body, [own, other, weight, small], outs, "qkv_forward")[0]
+        for copy in copies:
+            copy.wait()
+
+    return queue.call(
+        body,
+        [own, other, weight, small],
+        [shaped((2, rows, width))],
+        "qkv_forward",
+        far_outs=[shaped((2 * rows, features))],
+        copies=2,
+    )
 
 
 def qkv_backward(queue, grads, weight, block):
@@ -291,44 +339,71 @@
     rows, features = own.shape
     wide = up_weight.shape[2]
 
-    def body(own_ref, other_ref, up_ref, down_ref, small_ref, own_out, other_out, act_ref, slope_ref):
+    def body(
+        own_ref, other_ref, up_ref, down_ref, small_ref,
+        own_out, other_out, slope_ref, rows_ref, act_ref, act_s, done,
+    ):
+        copies = copy_rows([own_ref, other_ref], rows_ref, done)
         bias = small_ref[UP_BIAS + block : UP_BIAS + block + 1, :wide]
         both = jnp.concatenate([own_ref[...], other_ref[...]], axis=0)
         hidden = nn(both, up_ref[block]) + bias
         squared = hidden * hidden
         bent = jnp.tanh(GELU_A * hidden * (1.0 + GELU_B * squared))
         half = 0.5 + 0.5 * bent
-        active = (hidden * half).astype(BF16)
+        act_s[...] = (hidden * half).astype(BF16)
         slope = half + 0.5 * hidden * (1.0 - bent * bent) * (
             GELU_A + 3.0 * GELU_A * GELU_B * squared
         )
-        act_ref[...] = active
         slope_ref[...] = slope.astype(BF16)
-        out = nn(active, down_ref[block]).astype(BF16)
+        copies += copy_rows([act_s], act_ref, done, 2)
+        out = nn(act_s[...], down_ref[block]).astype(BF16)
         own_out[...] = out[:rows]
         other_out[...] = out[rows:]
-
-    part, full = shaped((rows, features)), shaped((2 * rows, wide))
-    operands = [own, other, up_weight, down_weight, small]
-    return queue.call(body, operands, [part, part, full, full], "mlp_forward")
+        for copy in copies:
+            copy.wait()
+
+    full = shaped((2 * rows, wide))
+    return queue.call(
+        body,
+        [own, other, up_weight, down_weight, small],
+        [shaped((rows, features)), shaped((rows, features)), full],
+        "mlp_forward",
+        far_outs=[shaped((2 * rows, features)), full],
+        scratch=[pltpu.VMEM((2 * rows, wide), BF16)],
+        copies=3,
+        limit=12,
+    )
 
 
 def mlp_backward(queue, own, other, slope, up_weight, down_weight, block):
     rows, features = own.shape
     wide = up_weight.shape[2]
 
-    def body(own_ref, other_ref, slope_ref, up_ref, down_ref, own_out, other_out, hid_ref):
+    def body(
+        own_ref, other_ref, slope_ref, up_ref, down_ref,
+        own_out, other_out, rows_ref, hid_ref, hid_s, done,
+    ):
+        copies = copy_rows([own_ref, other_ref], rows_ref, done)
         both = jnp.concatenate([own_ref[...], other_ref[...]], axis=0)
         d_active = nt(both, down_ref[block])
-        d_hidden = (d_active * slope_ref[...].astype(F32)).astype(BF16)
-        hid_ref[...] = d_hidden
-        out = nt(d_hidden, up_ref[block]).astype(BF16)
+        hid_s[...] = (d_active * slope_ref[...].astype(F32)).astype(BF16)
+        copies += copy_rows([hid_s], hid_ref, done, 2)
+        out = nt(hid_s[...], up_ref[block]).astype(BF16)
         own_out[...] = out[:rows]
         other_out[...] = out[rows:]
-
-    part = shaped((rows, features))
-    operands = [own, other, slope, up_weight, down_weight]
-    return queue.call(body, operands, [part, part, shaped((2 * rows, wide))], "mlp_backward")
+        for copy in copies:
+            copy.wait()
+
+    return queue.call(
+        body,
+        [own, other, slope, up_weight, down_weight],
+        [shaped((rows, features)), shaped((rows, features))],
+        "mlp_backward",
+        far_outs=[shaped((2 * rows, features)), shaped((2 * rows, wide))],
+        scratch=[pltpu.VMEM((2 * rows, wide), BF16)],
+        copies=3,
+        limit=12,
+    )
 
 
 def ln_back(queue, near, far, stream, d_out, mods, at, scale_part, branch=None, narrow=False):
@@ -355,7 +430,7 @@
         normed, spread = normed_of(x_ref[...])
         product = d_normed * normed
         grad = d_normed * (1.0 + scale)
-        d_x = d_ref[...] + spread * (
+        d_x = d_ref[...].astype(F32) + spread * (
             grad
             - jnp.mean(grad, axis=-1, keepdims=True)
             - normed * jnp.mean(grad * normed, axis=-1, keepdims=True)
@@ -405,7 +480,7 @@
     def body(*refs):
         q_ref, refs = refs[0], refs[1:]
         kv_refs, refs = refs[: len(merged)], refs[len(merged) :]
-        proj_ref, att_ref, lse_ref, own_out, other_out, q_s, k_s, v_s, o_s, l_s = refs
+        proj_ref, lse_ref, own_out, other_out, att_far, q_s, k_s, v_s, o_s, l_s, att_ref, done = refs
         for head in range(heads):
             low = head * HEAD_DIM
             first = 0
@@ -448,25 +523,29 @@
             out_ref[...] = nn(
                 att_ref[side * rows : (side + 1) * rows, :], proj_ref[block]
             ).astype(BF16)
+        for copy in copy_rows([att_ref], att_far, done):
+            copy.wait()
 
     return queue.call(
         body,
         [query, *merged, proj_weight],
         [
-            shaped((2 * rows, local)),
             shaped((heads, 2, 1, rows), F32),
             shaped((rows, features)),
             shaped((rows, features)),
         ],
         "attn_forward",
+        far_outs=[shaped((2 * rows, local))],
         scratch=[
             pltpu.VMEM((heads, 2, rows, HEAD_DIM), BF16),
             pltpu.VMEM((heads, total, HEAD_DIM), BF16),
             pltpu.VMEM((heads, total, HEAD_DIM), BF16),
             pltpu.VMEM((heads, 2, rows, HEAD_DIM), BF16),
             pltpu.VMEM((heads, 2, 8 if by_keys else rows, 128), F32),
+            pltpu.VMEM((2 * rows, local), BF16),
         ],
-        limit=24,
+        copies=1,
+        limit=13,
     )
 
 
@@ -477,6 +556,7 @@
     heads = local // HEAD_DIM
     halves = [part.shape[1] for part in merged]
     total = 2 * sum(halves)
+    features = proj_weight.shape[2]
     step = min(halves)
     steps = total // step
     unroll = 4 if step * steps > 512 else steps * heads
@@ -487,7 +567,14 @@
         g_refs, refs = refs[: 2 * count], refs[2 * count :]
         proj_ref, refs = refs[0], refs[1:]
         out_refs, refs = refs[:count], refs[count:]
-        q_s, k_s, kt_s, v_s, g_s, dq_s, dk_s, dv_s, l_s = refs
+        row_refs, refs = refs[:count], refs[count:]
+        qkv_refs, refs = refs[:count], refs[count:]
+        q_s, k_s, kt_s, v_s, g_s, dq_s, dk_s, dv_s, l_s, done = refs
+        copies = []
+        for index in range(count):
+            copies += copy_rows(
+                g_refs[2 * index : 2 * index + 2], row_refs[index], done, 2 * index
+            )
         first = 0
         for index in range(count):
             rows = halves[index]
@@ -541,6 +628,14 @@
                         head, at, :
                     ].astype(BF16)
                 first += rows
+            copies += copy_rows(
+                [out_refs[index].at[0], out_refs[index].at[1]],
+                qkv_refs[index],
+                done,
+                2 * count + 2 * index,
+            )
+        for copy in copies:
+            copy.wait()
 
     def lanes(dtype=BF16):
         return pltpu.VMEM((heads, total, HEAD_DIM), dtype)
@@ -550,6 +645,9 @@
         [*merged, *normers, *[half for pair in grads for half in pair], proj_weight],
         [shaped(part.shape) for part in merged],
         "attn_backward",
+        far_outs=[shaped((2 * rows, features)) for rows in halves]
+        + [shaped((2 * rows, width)) for rows in halves],
+        copies=4 * count,
         scratch=[
             lanes(),
             lanes(),
@@ -561,7 +659,7 @@
             lanes(F32),
             pltpu.VMEM((heads, steps, 1, step), F32),
         ],
-        limit=28,
+        limit=16,
     )
 
 
@@ -571,7 +669,7 @@
     return [index for index in range(1 << len(bits)) if not index & stride], stride
 
 
-def weight_grads(queue, pairs, mine, bits, bit):
+def weight_grads(queue, pairs, bits, cuts):
     blocks = 1 << len(bits)
     features = pairs[0][0][0].shape[1]
     widths = [rights[0].shape[1] for _, rights in pairs]
@@ -588,13 +686,18 @@
             scratch.append(pltpu.VMEM((rows, parts[0].shape[1]), BF16))
     buffers = len(scratch)
     scratch.append(pltpu.VMEM((blocks, each, sum(widths)), BF16))
-    scratch.append(pltpu.SemaphoreType.DMA((len(plan),)))
-    out = shaped((blocks // 2, each, sum(widths)))
-    starts, stride = split_at(bits, bit)
-
-    def body(mine_ref, *refs):
+    outs, far_outs = [], []
+    for columns, _, _ in cuts:
+        outs += [shaped((blocks // 2, each, columns))] * 2
+    if not cuts:
+        far_outs.append(shaped((blocks, each, sum(widths))))
+
+    def body(*refs):
+        mine_refs, refs = refs[: len(cuts)], refs[len(cuts) :]
         sources, refs = refs[: len(far)], refs[len(far) :]
-        kept_ref, away_ref, sums_ref, *held = refs
+        out_refs, refs = refs[: len(outs)], refs[len(outs) :]
+        sums_ref, *held = refs
+        whole_ref = None if cuts else held.pop(0)
         full, done = held[buffers], held[buffers + 1]
         copies = [
             pltpu.make_async_copy(
@@ -617,21 +720,34 @@
                 full[block, :, columns] = total[block * each : (block + 1) * each]
             sums_ref[:, columns] = nn(ones, right)
             low += width
-        at = mine_ref[0] * stride
-        for index, start in enumerate(starts):
-            kept_ref[index] = full[start + at]
-            away_ref[index] = full[start + stride - at]
-
-    return queue.call(
+        low = 0
+        for index, (width, bit, _) in enumerate(cuts):
+            starts, stride = split_at(bits, bit)
+            at = mine_refs[index][0] * stride
+            for place, start in enumerate(starts):
+                out_refs[2 * index][place] = full[start + at, :, low : low + width]
+                out_refs[2 * index + 1][place] = full[start + stride - at, :, low : low + width]
+            low += width
+        if not cuts:
+            whole = pltpu.make_async_copy(full, whole_ref, done.at[len(plan)])
+            whole.start()
+            whole.wait()
+
+    found = queue.call(
         body,
         [],
-        [out, out, shaped((8, sum(widths)), F32)],
+        [*outs, shaped((8, sum(widths)), F32)],
         "weight_grads",
-        scalars=[mine],
+        scalars=[mine for _, _, mine in cuts],
         far=far,
+        far_outs=far_outs,
         scratch=scratch,
-        limit=32,
-    )
+        copies=len(plan) + 1,
+        limit=20 if len(pairs) == 1 else 28,
+    )
+    if not cuts:
+        return found[1], found[0]
+    return list(zip(found[:-1:2], found[1:-1:2])), found[-1]
 
 
 def halve(queue, kept, moved, mine, bits, bit):
@@ -673,12 +789,14 @@
     )[0]
 
 
-def collect_sums(queue, sources, recipe):
+def collect_sums(queue, sources, recipe, parts):
     features = sources[0].shape[1]
     count = -(-len(recipe) // 8) * 8
+    counts = [part.shape[0] for part in parts]
 
     def body(*refs):
-        out_ref = refs[-1]
+        part_refs, refs = refs[: len(parts)], refs[len(parts) :]
+        out_ref, joined_ref = refs[-2:]
         for index, terms in enumerate(recipe):
             total = None
             for source, row in terms:
@@ -687,8 +805,13 @@
             out_ref[index : index + 1, :] = total
         if count > len(recipe):
             out_ref[len(recipe) :, :] = jnp.zeros((count - len(recipe), features), F32)
-
-    return queue.call(body, sources, [shaped((count, features), F32)], "collect_sums")[0]
+        first = 0
+        for part_ref, rows in zip(part_refs, counts):
+            joined_ref[first : first + rows, :] = part_ref[...]
+            first += rows
+
+    outs = [shaped((count, features), F32), shaped((sum(counts), features))]
+    return queue.call(body, [*parts, *sources], outs, "collect_sums")
 
 
 def pack_mods(queue, me, own, moved, latents, blocks, size, features):
@@ -758,13 +881,20 @@
             held = jnp.concatenate([held, self.dp_move(held, bit)], axis=0)
         return held
 
-    def exchange_relative(self, value):
+    def exchange_relative(self, value, total=None):
         held = value
-        for bit in self.dp_bits:
+        for bit in reversed(self.dp_bits):
             split = held.reshape((self.dp_size // (2 * bit), 2, bit) + held.shape[1:])
-            moved = self.dp_move(split[:, 1], bit)
+            away = split[:, 1]
+            if total is None:
+                moved = self.dp_move(away, bit)
+            else:
+                sent = jnp.concatenate([away.astype(F32).reshape(-1), total])
+                came = self.dp_move(sent, bit)
+                moved = came[: away.size].reshape(away.shape).astype(held.dtype)
+                total = total + came[away.size :]
             held = jnp.stack([split[:, 0], moved], axis=1).reshape(held.shape)
-        return held
+        return held if total is None else (held, total)
 
     def sum_relative(self, value):
         held = value
@@ -773,22 +903,12 @@
             held = held[:bit].astype(F32) + moved.astype(F32)
         return held[0]
 
-    def sum_all(self, value):
-        held = value
-        for bit in self.dp_bits:
-            held = held + self.dp_move(held, bit)
-        return held
-
 
 class ScatterSum:
-    def __init__(self, queue, links, pairs, order):
-        self.queue, self.links = queue, links
+    def __init__(self, queue, links, kept, away, order):
+        self.queue, self.links, self.kept = queue, links, kept
         self.order = list(order)
         self.open = sorted(self.order, reverse=True)
-        bit = self.order[0]
-        self.kept, away, self.sums = weight_grads(
-            queue, pairs, links.mine[bit], self.open, bit
-        )
         self.send(away)
 
     def send(self, away):
@@ -810,6 +930,26 @@
         return self.kept[0].astype(F32) + self.moved[0].astype(F32)
 
 
+def reduced(queue, links, pairs, after=None):
+    whole, sums = weight_grads(queue, pairs, sorted(links.dp_bits, reverse=True), [])
+    flat = whole.reshape(-1, whole.shape[-1])
+    if after is not None:
+        flat, after = lax.optimization_barrier((flat, after))
+    return lax.psum_scatter(flat, "dp", scatter_dimension=0, tiled=True), sums, after
+
+
+def scatter_sums(queue, links, pairs, cuts):
+    bits = sorted(links.dp_bits, reverse=True)
+    found, sums = weight_grads(
+        queue, pairs, bits, [(columns, order[0], links.mine[order[0]]) for columns, order in cuts]
+    )
+    pieces = [
+        ScatterSum(queue, links, kept, away, order)
+        for (kept, away), (_, order) in zip(found, cuts)
+    ]
+    return pieces, sums
+
+
 class Weights:
     def __init__(self, qkv, proj, up, down, small, mods):
         self.qkv, self.proj, self.up, self.down = qkv, proj, up, down
@@ -829,11 +969,13 @@
 
     def qkv(self):
         w = self.weights
-        self.merged = qkv_forward(self.queue, *self.normed_attn, w.qkv, w.small, self.block)
+        self.merged, self.normed_attn_rows = qkv_forward(
+            self.queue, *self.normed_attn, w.qkv, w.small, self.block
+        )
 
     def attention(self):
         merged = [chunk.merged for chunk in self.family]
-        self.attended, self.normer, own, other = attn_forward(
+        self.normer, own, other, self.attended_rows = attn_forward(
             self.queue, self.merged, merged, self.weights.proj, self.block
         )
         self.part = (own, self.links.swap(other))
@@ -852,7 +994,7 @@
 
     def mlp(self):
         w = self.weights
-        own, other, self.active, self.slope = mlp_forward(
+        own, other, self.slope, self.normed_mlp_rows, self.active_rows = mlp_forward(
             self.queue, *self.normed_mlp, w.up, w.down, w.small, self.block
         )
         self.part = (own, self.links.swap(other))
@@ -863,7 +1005,7 @@
 
     def mlp_back(self):
         w = self.weights
-        own, other, self.d_hidden = mlp_backward(
+        own, other, self.d_branch_mlp_rows, self.d_hidden_rows = mlp_backward(
             self.queue, *self.d_branch_mlp, self.slope, w.up, w.down, self.block
         )
         self.part = (own, self.links.swap(other))
@@ -886,8 +1028,9 @@
             self.weights.proj,
             self.block,
         )
-        for chunk, grad in zip(family, grads):
-            chunk.d_qkv = grad
+        count = len(family)
+        for index, chunk in enumerate(family):
+            chunk.d_qkv, chunk.d_branch_attn_rows, chunk.d_qkv_rows = grads[index::count]
 
     def qkv_back(self):
         own, other = qkv_backward(self.queue, self.d_qkv, self.weights.qkv, self.block)
@@ -909,14 +1052,8 @@
         return rest
 
 
-def pair_rows(chunks, name):
-    return [half for chunk in chunks for half in getattr(chunk, name)]
-
-
-def flat_rows(chunks, name):
-    return [
-        getattr(chunk, name).reshape(-1, getattr(chunk, name).shape[-1]) for chunk in chunks
-    ]
+def rows_of(chunks, name):
+    return [getattr(chunk, name + "_rows") for chunk in chunks]
 
 
 def on_device(dp_size, tensor_size, *arguments):
@@ -991,7 +1128,7 @@
     enc_latents, dec_latents = (0, 0, 1), (0, 0, 1)
 
     streams = [
-        gather_rows(queue, core, perms[latent], tokens[latent], rows)
+        gather_rows(queue, core, perms[latent], tokens[latent], rows, F32)
         for latent, rows in zip(enc_latents, enc_rows)
     ]
     mods = spread_mods(queue, links.me, columns, features)
@@ -1051,7 +1188,7 @@
     table_short = table_rows(queue, core, perms_later[1], waves[1], table_places[1])
     masked_short = table_rows(queue, core, perms_later[1], waves[1], masked_places[1], filler)
     d_out = [
-        gather_rows(queue, core, perms_later[latent], cots_later[latent], rows)
+        gather_rows(queue, core, perms_later[latent], cots_later[latent], rows, BF16)
         for latent, rows in zip(dec_latents, dec_rows)
     ]
     first_sums = []
@@ -1076,100 +1213,103 @@
     dk.merge()
     dk.mlp()
     dm.merge()
+    forward = {dk: dk.part}
+    dk.mlp_back()
+    dm.mlp()
     dk.near()
+    forward[dm] = dm.part
+    dm.mlp_back()
     dt.merge()
-    forward_sums = [dk.sum]
-    dm.mlp()
-    dk.mlp_back()
     dm.near()
-    forward_sums.append(dm.sum)
     dt.mlp()
-    dm.mlp_back()
+    forward[dt] = dt.part
+    dt.mlp_back()
     dt.near()
-    forward_sums.append(dt.sum)
-    dt.mlp_back()
-
-    dt.near()
-    dk.near()
-    dm.near()
+
     y_first, z_first = list(links.dp_bits), list(links.dp_bits)
     if len(z_first) > 1:
         z_first[0], z_first[1] = z_first[1], z_first[0]
 
-    def wide_sum(chunks, left, right, order):
-        return ScatterSum(queue, links, [(pair_rows(chunks, left), flat_rows(chunks, right))], order)
-
-    dec_up = wide_sum(decoder, "normed_mlp", "d_hidden", y_first)
-    decoded, gate_sums = [], []
-    for chunk, grad, summed in zip(decoder, d_out, forward_sums):
-        own, sums = finish(queue, chunk.middle, *summed, grad, small, mods, chunk.at)
-        gate_sums.append(sums)
-        decoded.append((own, links.swap(own)))
+    def wide_pairs(chunks):
+        return [
+            (rows_of(chunks, "normed_mlp"), rows_of(chunks, "d_hidden")),
+            (rows_of(chunks, "d_branch_mlp"), rows_of(chunks, "active")),
+        ]
+
+    def attention_pairs(chunks):
+        return [
+            (rows_of(chunks, "d_branch_attn"), rows_of(chunks, "attended")),
+            (rows_of(chunks, "normed_attn"), rows_of(chunks, "d_qkv")),
+        ]
+
+    sums_there = {}
+
+    def forward_sum(chunk):
+        near = near_sum(queue, *forward[chunk])
+        sums_there[chunk] = (near, links.cross(near))
+
+    dk.merge_back()
+    dec_wide, dec_wide_sums, _ = reduced(queue, links, wide_pairs(decoder))
+    dm.merge_back()
+    forward_sum(dk)
+    forward_sum(dm)
+    dm.attention_back()
+    dk.qkv_back()
+    dk.near()
+    dm.qkv_back()
     dt.merge_back()
-    dec_down = wide_sum(decoder, "d_branch_mlp", "active", z_first)
+    dm.near()
     dt.attention_back()
-    dk.merge_back()
     dt.qkv_back()
     dt.near()
-    dm.merge_back()
-    dm.attention_back()
-    dk.qkv_back()
-    dm.qkv_back()
-    dk.near()
-    dm.near()
-
     enc_branch = (small, DOWN_BIAS, (0, 0), GATE_MLP)
     short_branch = (small, DOWN_BIAS, (0, 1), GATE_MLP)
-    d_short, grad_short = dt.leave_back(([es.branch_mlp], *short_branch))
-    es.start_back(d_short, grad_short)
-    dec_proj = ScatterSum(
-        queue,
-        links,
-        [
-            (pair_rows(decoder, "d_branch_attn"), flat_rows(decoder, "attended")),
-            (pair_rows(decoder, "normed_attn"), flat_rows(decoder, "d_qkv")),
-        ],
-        y_first,
-    )
-    dec_up.step()
     d_a, d_b, grad_a, grad_b = dk.leave_back(([ea.branch_mlp, eb.branch_mlp], *enc_branch))
     ea.start_back(d_a, grad_a)
     eb.start_back(d_b, grad_b)
 
-    es.mlp_back()
     ea.mlp_back()
     eb.mlp_back()
-    es.near()
     ea.near()
     eb.near()
+    (dec_attn,), dec_attn_sums = scatter_sums(
+        queue, links, attention_pairs(decoder), [(4 * local, y_first)]
+    )
     dm.leave_back()
-    dec_down.step()
-    enc_up = wide_sum(encoder, "normed_mlp", "d_hidden", y_first)
+    d_short, grad_short = dt.leave_back(([es.branch_mlp], *short_branch))
+    es.start_back(d_short, grad_short)
+    es.mlp_back()
+    es.near()
+    ea.merge_back()
+    enc_wide, enc_wide_sums, dec_wide = reduced(queue, links, wide_pairs(encoder), dec_wide)
+    eb.merge_back()
+    forward_sum(dt)
+    dec_attn.step()
+    ea.attention_back()
+    ea.qkv_back()
+    ea.near()
+    eb.qkv_back()
     es.merge_back()
-    enc_down = wide_sum(encoder, "d_branch_mlp", "active", z_first)
+    eb.near()
     es.attention_back()
     es.qkv_back()
-    ea.merge_back()
     es.near()
-    eb.merge_back()
-    ea.attention_back()
-    ea.qkv_back()
-    eb.qkv_back()
-    ea.near()
-    eb.near()
-    enc_proj = ScatterSum(
+    (enc_attn,), enc_attn_sums = scatter_sums(
+        queue, links, attention_pairs(encoder), [(4 * local, y_first)]
+    )
+    dec_attn.step()
+    own_tokens = []
+    for chunk in (ea, eb, es):
+        own_tokens += chunk.leave_back(narrow=True)
+    decoded, gate_sums = finish(
         queue,
-        links,
         [
-            (pair_rows(encoder, "d_branch_attn"), flat_rows(encoder, "attended")),
-            (pair_rows(encoder, "normed_attn"), flat_rows(encoder, "d_qkv")),
+            (chunk.middle, *sums_there[chunk], d_out[index], chunk.at)
+            for index, chunk in enumerate(decoder)
         ],
-        y_first,
-    )
-    own_tokens = []
-    for chunk in (es, ea, eb):
-        (own,) = chunk.leave_back(narrow=True)
-        own_tokens.append((own, links.swap(own)))
+        small,
+        mods,
+    )
 
     sources, recipe = [], []
 
@@ -1186,11 +1326,7 @@
             if block == 0:
                 gates = [row((dk, dt)[latent].attn_sums, 2)]
             else:
-                gates = [
-                    row(gate_sums[index], 0)
-                    for index, chunk in enumerate(decoder)
-                    if chunk.latent == latent
-                ]
+                gates = [row(gate_sums, latent)]
             recipe += [
                 [row(chunk.attn_sums, 1) for chunk in members],
                 [row(chunk.attn_sums, 0) for chunk in members],
@@ -1206,11 +1342,19 @@
         [row(sums, 0) for sums in first_sums],
         [row(chunk.attn_sums, 4) for chunk in (dm, dt)],
     ]
-    own_sums = collect_sums(queue, sources, recipe)
+    own_sums, joined = collect_sums(queue, sources, recipe, own_tokens)
     packed, all_sums = pack_mods(
         queue, links.me, own_sums, links.swap(own_sums), 2, 2, dp_size, features
     )
-    mine = links.exchange_relative(packed)
+    totals = jnp.concatenate(
+        [all_sums[24:29].reshape(-1), enc_wide_sums[0, :wide], dec_wide_sums[0, :wide]]
+        + [
+            sums[0, first : first + local]
+            for sums in (enc_attn_sums, dec_attn_sums)
+            for first in (local, 3 * local)
+        ]
+    )
+    mine, totals = links.exchange_relative(packed, totals)
     flat_mine = mine.reshape((-1,) + mine.shape[2:])
     grad_ada = jnp.einsum("nd,nlm->ldm", flat_acts, flat_mine, preferred_element_type=F32)
     grad_ada_bias = jnp.sum(flat_mine.astype(F32), axis=0)
@@ -1219,12 +1363,6 @@
     gate = jax.nn.sigmoid(cond)
     d_cond = (d_act * gate * (1.0 + cond * (1.0 - gate))).astype(BF16)
 
-    qkv_sums = [part.sums[0, local:] for part in (enc_proj, dec_proj)]
-    totals = jnp.concatenate(
-        [all_sums[24:29].reshape(-1), enc_up.sums[0], dec_up.sums[0]]
-        + [part for sums in qkv_sums for part in (sums[:local], sums[2 * local :])]
-    )
-    totals = links.sum_all(totals)
     proj_out = totals[: 2 * features].reshape(2, features)
     down_out = totals[2 * features : 4 * features].reshape(2, features)
     mask_out = totals[4 * features : 5 * features]
@@ -1233,21 +1371,23 @@
     first += 2 * wide
     qv_out = totals[first : first + 4 * local].reshape(2, 2, local)
 
-    for part in (enc_up, dec_proj, enc_down, dec_up, dec_down):
-        part.step()
+    enc_attn.step()
+    decoded_other = links.swap(decoded)
     results = (
-        place_rows(queue, core, perms_later[0], decoded[:2], dec_rows[:2]),
-        place_rows(queue, core, perms_later[1], decoded[2:], dec_rows[2:]),
-    )
-    for part in (enc_up, dec_proj, enc_down, enc_proj):
-        part.step()
+        place_rows(queue, core, perms_later[0], decoded, decoded_other, dec_rows[:2], 0),
+        place_rows(
+            queue, core, perms_later[1], decoded, decoded_other, dec_rows[2:], 2 * long_half
+        ),
+    )
+    enc_attn.step()
+    joined_other = links.swap(joined)
     d_tokens = (
-        place_rows(queue, core, perms_later[0], own_tokens[1:], enc_rows[:2]),
-        place_rows(queue, core, perms_later[1], own_tokens[:1], enc_rows[2:]),
-    )
-    enc_att, dec_att = enc_proj.result(), dec_proj.result()
-    up_grad = jnp.stack([enc_up.result(), dec_up.result()])
-    down_grad = jnp.stack([enc_down.result(), dec_down.result()])
+        place_rows(queue, core, perms_later[0], joined, joined_other, enc_rows[:2], 0),
+        place_rows(queue, core, perms_later[1], joined, joined_other, enc_rows[2:], long_half),
+    )
+    up_grad = jnp.stack([enc_wide[:, :wide], dec_wide[:, :wide]]).astype(F32)
+    down_grad = jnp.stack([enc_wide[:, wide:], dec_wide[:, wide:]]).astype(F32)
+    dec_att, enc_att = dec_attn.result(), enc_attn.result()
     proj_grad = jnp.stack([enc_att[:, :local], dec_att[:, :local]])
     qkv_grad = jnp.stack([enc_att[:, local:], dec_att[:, local:]]).reshape(2, -1, 3, local)
 

time: 656 us -> 558 us (0.85)
  waiting for transfers between devices: 254 us -> 174 us
  starting transfers between devices: 85.9 us -> 70.2 us
  between operations: 4.71 us -> 17 us
  local copies, waits for them, and re-layouts: 62.6 us -> 51.9 us
    ppermute x33 -> x18, waiting for transfers between devices: 156 us -> 76.8 us  [dp_move(): return lax.ppermute(value, 'dp', partners(self.dp_size, bit))]
    unnamed x564 -> x354, local copies, waits for them, and re-layouts: 54.1 us -> 36.2 us
    ppermute x33 -> x18, starting transfers between devices: 45.2 us -> 32.5 us  [dp_move(): return lax.ppermute(value, 'dp', partners(self.dp_size, bit))]
    pallas_call x123 -> x111, Pallas kernels: 214 us -> 213 us  [call(): pl.pallas_call(whole, in_specs=[fast] + [small] * len(scalars) + [slow] *...]
  transfers between devices with their start and end apart: 112 -> 95, of which waited for: 43 -> 42; matrix products, arithmetic and copies ran while one was open for 4% -> 5% of each run, Pallas kernels for 28% -> 35%
where the time goes in v4:
time: 558 us; the launch traced here: 547 us
  Pallas kernels  213 us (38%)
  waiting for transfers between devices  174 us (31%)
  starting transfers between devices  70.2 us (13%)
  local copies, waits for them, and re-layouts  51.9 us (9%)
  between operations  17 us (3%)
  matrix products  10.8 us (2%)
  other arithmetic  10.5 us (2%)
    pallas_call x111, Pallas kernels, call(): pl.pallas_call(whole, in_specs=[fast] + [small] * len(scalars) + [slow] *...  213 us
    ppermute x24, waiting for transfers between devices, cross(): return lax.ppermute(value, 'tensor', partners(self.tensor_size, 2))  85.6 us
    ppermute x18, waiting for transfers between devices, dp_move(): return lax.ppermute(value, 'dp', partners(self.dp_size, bit))  76.8 us
    unnamed x354, local copies, waits for them, and re-layouts  36.2 us
    ppermute x18, starting transfers between devices, dp_move(): return lax.ppermute(value, 'dp', partners(self.dp_size, bit))  32.5 us
    ppermute x24, starting transfers between devices, cross(): return lax.ppermute(value, 'tensor', partners(self.tensor_size, 2))  27 us
    ppermute x51, waiting for transfers between devices, swap(): return lax.ppermute(value, 'tensor', partners(self.tensor_size, 1))  11.6 us
  transfers between devices with their start and end apart: 95, of which 42 were waited for; matrix products, arithmetic and copies ran while one was open for 5% of the time, Pallas kernels for 35%

profile of v4, /device:TPU:0, one launch (start us, length us, event | category | flops | bytes accessed | tf_op | source)
XLA Modules:
  0.0 547.5 jit_solution(6804623265747602365)
XLA Ops:
  8.0 3.0 collective-permute-start
  16.4 3.1 collective-permute-start.2
  22.7 3.4 fusion
  28.0 3.1 collective-permute-done.3
  45.2 3.7 attn_forward.6
  49.0 3.7 attn_forward.7
  60.8 7.8 %collective-permute-done.12.refs_2_.refs_7_ = bf16[128,1152]{1,0:T(8,128)(2,1)S(1)} collective-permute-done((bf16[128,1152]{1,0:T(8,128)(2,1)S(1)}, bf16[128,1152]{1,0:T(8,128)(2,1)S(1)}, u32[]{:S(2)}, u32[]{:S(2)}) %collective-permute-start.12) | collective-permute-done | bytes 294944 | tf_op jit(solution)/shard_map/ppermute | solution.py:873
  75.4 3.5 collective-permute-done.15.refs_2_.refs_7_
  97.0 5.9 %collective-permute-done.23.refs_8_.refs_9_ = bf16[128,1152]{1,0:T(8,128)(2,1)S(1)} collective-permute-done((bf16[128,1152]{1,0:T(8,128)(2,1)S(1)}, bf16[128,1152]{1,0:T(8,128)(2,1)S(1)}, u32[]{:S(2)}, u32[]{:S(2)}) %collective-permute-start.23) | collective-permute-done | bytes 294944 | tf_op jit(solution)/shard_map/ppermute | solution.py:873
  105.2 4.7 collective-permute-done.24.refs_5_.refs_7_
  111.8 5.9 %attn_forward.9 = (f32[4,2,1,256]{3,2,1,0:T(1,128)S(1)}, bf16[256,1152]{1,0:T(8,128)(2,1)S(1)}, bf16[256,1152]{1,0:T(8,128)(2,1)S(1)}, bf16[512,288]{1,0:T(8,128)(2,1)}, f32[8,128]{1,0:T(8,128)S(1)}) custom-call(f32[8,128]{1,0:T(8,128)S(1)} %get-tuple-element.465.token_ref, bf16[2,256,864]{2,1,0:T(8,128)(2,1)S(1)} %get-tuple-element.466.refs_0_.refs_1_, ...), custom_call_target="tpu_custom_call" | custom-call | flops 4000000000 | bytes 1000 | tf_op jit(solution)/shard_map/attn_forward/pallas_call | solution.py:68
  121.2 6.1 %attn_forward.10 = (f32[4,2,1,256]{3,2,1,0:T(1,128)S(1)}, bf16[256,1152]{1,0:T(8,128)(2,1)S(1)}, bf16[256,1152]{1,0:T(8,128)(2,1)S(1)}, bf16[512,288]{1,0:T(8,128)(2,1)}, f32[8,128]{1,0:T(8,128)S(1)}) custom-call(f32[8,128]{1,0:T(8,128)S(1)} %get-tuple-element.473.token_ref, bf16[2,256,864]{2,1,0:T(8,128)(2,1)S(1)} %get-tuple-element.467.refs_2_.refs_0_.refs_1_, ...), custom_call_target="tpu_custom_call" | custom-call | flops 4000000000 | bytes 1000 | tf_op jit(solution)/shard_map/attn_forward/pallas_call | solution.py:68
  133.7 9.4 %collective-permute-done.30.refs_2_.refs_7_ = bf16[256,1152]{1,0:T(8,128)(2,1)S(1)} collective-permute-done((bf16[256,1152]{1,0:T(8,128)(2,1)S(1)}, bf16[256,1152]{1,0:T(8,128)(2,1)S(1)}, u32[]{:S(2)}, u32[]{:S(2)}) %collective-permute-start.30) | collective-permute-done | bytes 589856 | tf_op jit(solution)/shard_map/ppermute | solution.py:873
  145.8 6.3 %mlp_forward.9 = (bf16[256,1152]{1,0:T(8,128)(2,1)S(1)}, bf16[256,1152]{1,0:T(8,128)(2,1)}, bf16[512,1152]{1,0:T(8,128)(2,1)S(1)}, bf16[512,1152]{1,0:T(8,128)(2...) custom-call(f32[8,128]{1,0:T(8,128)S(1)} %get-tuple-element.485.token_ref, ...), custom_call_target="tpu_custom_call" | custom-call | flops 3500000000 | bytes 1000 | tf_op jit(solution)/shard_map/mlp_forward/pallas_call | solution.py:68
  152.9 6.7 %collective-permute-done.32.refs_2_.refs_7_ = bf16[256,1152]{1,0:T(8,128)(2,1)S(1)} collective-permute-done((bf16[256,1152]{1,0:T(8,128)(2,1)S(1)}, bf16[256,1152]{1,0:T(8,128)(2,1)S(1)}, u32[]{:S(2)}, u32[]{:S(2)}) %collective-permute-start.32) | collective-permute-done | bytes 589856 | tf_op jit(solution)/shard_map/ppermute | solution.py:873
  160.3 3.6 mlp_backward.6
  166.0 6.7 %mlp_forward.10 = (bf16[256,1152]{1,0:T(8,128)(2,1)S(1)}, bf16[256,1152]{1,0:T(8,128)(2,1)}, bf16[512,1152]{1,0:T(8,128)(2,1)S(1)}, bf16[512,1152]{1,0:T(8,128)(...) custom-call(f32[8,128]{1,0:T(8,128)S(1)} %get-tuple-element.492.token_ref, ...), custom_call_target="tpu_custom_call" | custom-call | flops 3500000000 | bytes 1000 | tf_op jit(solution)/shard_map/mlp_forward/pallas_call | solution.py:68
  173.7 3.6 mlp_backward.7
  180.3 3.4 mlp_forward.11
  187.7 7.6 %collective-permute-done.42.refs_1_ = bf16[256,1152]{1,0:T(8,128)(2,1)S(1)} collective-permute-done((bf16[256,1152]{1,0:T(8,128)(2,1)S(1)}, bf16[256,1152]{1,0:T(8,128)(2,1)S(1)}, u32[]{:S(2)}, u32[]{:S(2)}) %collective-permute-start.42) | collective-permute-done | bytes 589856 | tf_op jit(solution)/shard_map/ppermute | solution.py:873
  199.3 14.9 %weight_grads.4 = (f32[8,2304]{1,0:T(8,128)S(1)}, bf16[8,144,2304]{2,1,0:T(8,128)(2,1)}, f32[8,128]{1,0:T(8,128)S(1)}) custom-call(f32[8,128]{1,0:T(8,128)S(1)} %get-tuple-element.517.token_ref, bf16[512,1152]{1,0:T(8,128)(2,1)} %get-tuple-element.518.refs_0_, bf16[512,1152]{1,0:T(8,128)(2,1)} %get-tuple-element.519.refs_1_, ...), custom_call_target="tpu_custom_call" | custom-call | flops 6499999744 | bytes 1000 | tf_op jit(solution)/shard_map/weight_grads/pallas_call | solution.py:68
  226.5 21.6 %attn_backward.4 = (bf16[2,256,864]{2,1,0:T(8,128)(2,1)S(1)}, bf16[2,256,864]{2,1,0:T(8,128)(2,1)S(1)}, bf16[512,1152]{1,0:T(8,128)(2,1)}, bf16[512,1152]{1,0:T(...) custom-call(f32[8,128]{1,0:T(8,128)S(1)} %get-tuple-element.539.token_ref, ...), custom_call_target="tpu_custom_call" | custom-call | flops 8999999488 | bytes 1000 | tf_op jit(solution)/shard_map/attn_backward/pallas_call | solution.py:68
  253.5 5.5 %collective-permute-done.49.refs_1_ = bf16[128,1152]{1,0:T(8,128)(2,1)S(1)} collective-permute-done((bf16[128,1152]{1,0:T(8,128)(2,1)S(1)}, bf16[128,1152]{1,0:T(8,128)(2,1)S(1)}, u32[]{:S(2)}, u32[]{:S(2)}) %collective-permute-start.49) | collective-permute-done | bytes 294944 | tf_op jit(solution)/shard_map/ppermute | solution.py:873
  262.4 3.8 attn_backward.5
  269.5 7.0 %collective-permute-done.53.refs_1_ = bf16[256,1152]{1,0:T(8,128)(2,1)S(1)} collective-permute-done((bf16[256,1152]{1,0:T(8,128)(2,1)S(1)}, bf16[256,1152]{1,0:T(8,128)(2,1)S(1)}, u32[]{:S(2)}, u32[]{:S(2)}) %collective-permute-start.53) | collective-permute-done | bytes 589856 | tf_op jit(solution)/shard_map/ppermute | solution.py:873
  282.9 3.2 mlp_backward.10
  290.4 8.8 %weight_grads.5 = (bf16[4,144,1152]{2,1,0:T(8,128)(2,1)S(1)}, bf16[4,144,1152]{2,1,0:T(8,128)(2,1)}, f32[8,1152]{1,0:T(8,128)S(1)}, f32[8,128]{1,0:T(8,128)S(1)}) custom-call(f32[8,128]{1,0:T(8,128)S(1)} %get-tuple-element.580.token_ref, s32[1]{0:T(128)} %bitcast.23.refs_0_, bf16[512,1152]{1,0:T(8,128)(2,1)} %get-tuple-element.581.refs_1_, ...), custom_call_target="tpu_custom_call" | custom-call | flops 6499999744 | bytes 1000 | tf_op jit(solution)/shard_map/weight_grads/pallas_call | solution.py:68
  299.3 4.3 collective-permute-done.58.refs_1_
  304.6 4.5 collective-permute-done.59.refs_1_
  323.7 9.9 %weight_grads.6 = (f32[8,2304]{1,0:T(8,128)S(1)}, bf16[8,144,2304]{2,1,0:T(8,128)(2,1)}, f32[8,128]{1,0:T(8,128)S(1)}) custom-call(f32[8,128]{1,0:T(8,128)S(1)} %get-tuple-element.608.token_ref, bf16[256,1152]{1,0:T(8,128)(2,1)} %get-tuple-element.609.refs_0_, bf16[256,1152]{1,0:T(8,128)(2,1)} %get-tuple-element.610.refs_1_, ...), custom_call_target="tpu_custom_call" | custom-call | flops 6499999744 | bytes 1000 | tf_op jit(solution)/shard_map/weight_grads/pallas_call | solution.py:68
  337.6 6.2 %collective-permute-done.65.refs_2_ = bf16[4,144,1152]{2,1,0:T(8,128)(2,1)} collective-permute-done((bf16[4,144,1152]{2,1,0:T(8,128)(2,1)}, bf16[4,144,1152]{2,1,0:T(8,128)(2,1)}, u32[]{:S(2)}, u32[]{:S(2)}) %collective-permute-start.65) | collective-permute-done | bytes 1327136 | tf_op jit(solution)/shard_map/ppermute | solution.py:876
  347.2 8.1 %attn_backward.6 = (bf16[2,128,864]{2,1,0:T(8,128)(2,1)S(1)}, bf16[2,128,864]{2,1,0:T(8,128)(2,1)S(1)}, bf16[256,1152]{1,0:T(8,128)(2,1)}, bf16[256,1152]{1,0:T(...) custom-call(f32[8,128]{1,0:T(8,128)S(1)} %get-tuple-element.630.token_ref, ...), custom_call_target="tpu_custom_call" | custom-call | flops 8999999488 | bytes 1000 | tf_op jit(solution)/shard_map/attn_backward/pallas_call | solution.py:68
  359.0 3.8 collective-permute-done.69.refs_1_
  367.6 3.5 attn_backward.7
  378.6 6.1 %weight_grads.7 = (bf16[4,144,1152]{2,1,0:T(8,128)(2,1)S(1)}, bf16[4,144,1152]{2,1,0:T(8,128)(2,1)}, f32[8,1152]{1,0:T(8,128)S(1)}, f32[8,128]{1,0:T(8,128)S(1)}) custom-call(f32[8,128]{1,0:T(8,128)S(1)} %get-tuple-element.656.token_ref, s32[1]{0:T(128)} %bitcast.23.refs_0_, bf16[256,1152]{1,0:T(8,128)(2,1)} %get-tuple-element.657.refs_1_, ...), custom_call_target="tpu_custom_call" | custom-call | flops 6499999744 | bytes 1000 | tf_op jit(solution)/shard_map/weight_grads/pallas_call | solution.py:68
  384.8 17.2 %collective-permute-done.73.refs_2_ = bf16[2,144,1152]{2,1,0:T(8,128)(2,1)} collective-permute-done((bf16[2,144,1152]{2,1,0:T(8,128)(2,1)}, bf16[2,144,1152]{2,1,0:T(8,128)(2,1)}, u32[]{:S(2)}, u32[]{:S(2)}) %collective-permute-start.73) | collective-permute-done | bytes 663584 | tf_op jit(solution)/shard_map/ppermute | solution.py:876
  410.5 3.3 collective-permute-done.75.refs_1_
  415.4 7.0 %collective-permute-done.76.refs_1_ = bf16[64,1152]{1,0:T(8,128)(2,1)S(1)} collective-permute-done((bf16[64,1152]{1,0:T(8,128)(2,1)S(1)}, bf16[64,1152]{1,0:T(8,128)(2,1)S(1)}, u32[]{:S(2)}, u32[]{:S(2)}) %collective-permute-start.76) | collective-permute-done | bytes 147488 | tf_op jit(solution)/shard_map/ppermute | solution.py:873
  424.5 3.2 finish.1
  435.6 10.9 %collective-permute-done.85 = f32[23040]{0:T(1024)} collective-permute-done((f32[23040]{0:T(1024)S(1)}, f32[23040]{0:T(1024)}, u32[]{:S(2)}, u32[]{:S(2)}) %collective-permute-start.85) | collective-permute-done | bytes 92192 | tf_op jit(solution)/shard_map/ppermute | solution.py:876
  448.5 5.0 collective-permute-done.92
  464.3 12.6 %collective-permute-done.87 = f32[23040]{0:T(1024)S(1)} collective-permute-done((f32[23040]{0:T(1024)S(1)}, f32[23040]{0:T(1024)S(1)}, u32[]{:S(2)}, u32[]{:S(2)}) %collective-permute-start.87) | collective-permute-done | bytes 92192 | tf_op jit(solution)/shard_map/ppermute | solution.py:876
  481.3 3.3 collective-permute-start.88
  484.6 4.5 convolution_bitcast_fusion
  503.8 4.3 place_rows.4
  509.4 7.7 %collective-permute-done.83.refs_2_ = bf16[2,144,1152]{2,1,0:T(8,128)(2,1)S(1)} collective-permute-done((bf16[2,144,1152]{2,1,0:T(8,128)(2,1)S(1)}, bf16[2,144,1152]{2,1,0:T(8,128)(2,1)S(1)}, u32[]{:S(2)}, u32[]{:S(2)}) %collective-permute-start.83) | collective-permute-done | bytes 663584 | tf_op jit(solution)/shard_map/ppermute | solution.py:876
  519.0 4.1 place_rows.6
  525.4 7.4 %collective-permute-done.91 = bf16[1,144,1152]{2,1,0:T(8,128)(2,1)S(1)} collective-permute-done((bf16[1,144,1152]{2,1,0:T(8,128)(2,1)S(1)}, bf16[1,144,1152]{2,1,0:T(8,128)(2,1)S(1)}, u32[]{:S(2)}, u32[]{:S(2)}) %collective-permute-start.91) | collective-permute-done | bytes 331808 | tf_op jit(solution)/shard_map/ppermute | solution.py:876
  (704 shorter events, 227.7 us)
Async XLA Ops:
  7.2 371.4 %reduce-scatter.3.cloned.1.call-start = ((), (), s32[]{:S(2)}) async-start(), calls=%async_computation.2 | async-start | bytes 5971968 | tf_op jit(solution)/shard_map/reduce_scatter | solution.py:938
  59.0 11.5 %collective-permute-start.13 = (bf16[256,1152]{1,0:T(8,128)(2,1)S(1)}, bf16[256,1152]{1,0:T(8,128)(2,1)S(1)}, u32[]{:S(2)}, u32[]{:S(2)}) collective-permute-start(bf16[256,1152]{1,0:T(8,128)(2,1)S(1)} %get-tuple-element.417.refs_0_), channel_id=1, source_target_pairs={{0,1},{1,0},{2,3},{3,2},{4,5},{5,4},{6,7},{7,6},{8,9},{9,8},{10,11... | collective-permute-start | bytes 1769480 | tf_op jit(solution)/shard_map/ppermute | solution.py:870
  59.3 9.3 %collective-permute-start.12 = (bf16[128,1152]{1,0:T(8,128)(2,1)S(1)}, bf16[128,1152]{1,0:T(8,128)(2,1)S(1)}, u32[]{:S(2)}, u32[]{:S(2)}) collective-permute-start(bf16[128,1152]{1,0:T(8,128)(2,1)S(1)} %get-tuple-element.415.refs_1_.refs_6_), channel_id=1, source_target_pairs={{0,2},{1,3},{2,0},{3,1},{4,6},{5,7},{6,4},{7,5},{8,10},{9,11},{10,... | collective-permute-start | bytes 884744 | tf_op jit(solution)/shard_map/ppermute | solution.py:873
  69.0 9.9 %collective-permute-start.15 = (bf16[128,1152]{1,0:T(8,128)(2,1)S(1)}, bf16[128,1152]{1,0:T(8,128)(2,1)S(1)}, u32[]{:S(2)}, u32[]{:S(2)}) collective-permute-start(bf16[128,1152]{1,0:T(8,128)(2,1)S(1)} %get-tuple-element.421.refs_1_.refs_6_), channel_id=1, source_target_pairs={{0,2},{1,3},{2,0},{3,1},{4,6},{5,7},{6,4},{7,5},{8,10},{9,11},{10,... | collective-permute-start | bytes 884744 | tf_op jit(solution)/shard_map/ppermute | solution.py:873
  74.8 6.7 %collective-permute-start.17 = (bf16[64,1152]{1,0:T(8,128)(2,1)S(1)}, bf16[64,1152]{1,0:T(8,128)(2,1)S(1)}, u32[]{:S(2)}, u32[]{:S(2)}) collective-permute-start(bf16[64,1152]{1,0:T(8,128)(2,1)S(1)} %get-tuple-element.426.refs_1_.refs_6_), channel_id=1, source_target_pairs={{0,2},{1,3},{2,0},{3,1},{4,6},{5,7},{6,4},{7,5},{8,10},{9,11},{10,... | collective-permute-start | bytes 442376 | tf_op jit(solution)/shard_map/ppermute | solution.py:873
  87.2 9.8 %collective-permute-start.22 = (bf16[128,1152]{1,0:T(8,128)(2,1)S(1)}, bf16[128,1152]{1,0:T(8,128)(2,1)S(1)}, u32[]{:S(2)}, u32[]{:S(2)}) collective-permute-start(bf16[128,1152]{1,0:T(8,128)(2,1)S(1)} %get-tuple-element.455.refs_4_.refs_6_), channel_id=1, source_target_pairs={{0,2},{1,3},{2,0},{3,1},{4,6},{5,7},{6,4},{7,5},{8,10},{9,11},{10,... | collective-permute-start | bytes 884744 | tf_op jit(solution)/shard_map/ppermute | solution.py:873
  88.7 14.2 %collective-permute-start.23 = (bf16[128,1152]{1,0:T(8,128)(2,1)S(1)}, bf16[128,1152]{1,0:T(8,128)(2,1)S(1)}, u32[]{:S(2)}, u32[]{:S(2)}) collective-permute-start(bf16[128,1152]{1,0:T(8,128)(2,1)S(1)} %get-tuple-element.457.refs_7_.refs_8_), channel_id=1, source_target_pairs={{0,2},{1,3},{2,0},{3,1},{4,6},{5,7},{6,4},{7,5},{8,10},{9,11},{10,... | collective-permute-start | bytes 884744 | tf_op jit(solution)/shard_map/ppermute | solution.py:873
  127.5 15.6 %collective-permute-start.30 = (bf16[256,1152]{1,0:T(8,128)(2,1)S(1)}, bf16[256,1152]{1,0:T(8,128)(2,1)S(1)}, u32[]{:S(2)}, u32[]{:S(2)}) collective-permute-start(bf16[256,1152]{1,0:T(8,128)(2,1)S(1)} %get-tuple-element.484.refs_1_.refs_6_), channel_id=1, source_target_pairs={{0,2},{1,3},{2,0},{3,1},{4,6},{5,7},{6,4},{7,5},{8,10},{9,11},{10,... | collective-permute-start | bytes 1769480 | tf_op jit(solution)/shard_map/ppermute | solution.py:873
  143.8 15.7 %collective-permute-start.32 = (bf16[256,1152]{1,0:T(8,128)(2,1)S(1)}, bf16[256,1152]{1,0:T(8,128)(2,1)S(1)}, u32[]{:S(2)}, u32[]{:S(2)}) collective-permute-start(bf16[256,1152]{1,0:T(8,128)(2,1)S(1)} %get-tuple-element.488.refs_1_.refs_6_), channel_id=1, source_target_pairs={{0,2},{1,3},{2,0},{3,1},{4,6},{5,7},{6,4},{7,5},{8,10},{9,11},{10,... | collective-permute-start | bytes 1769480 | tf_op jit(solution)/shard_map/ppermute | solution.py:873
  145.4 14.9 %collective-permute-start.33 = (bf16[256,1152]{1,0:T(8,128)(2,1)S(1)}, bf16[256,1152]{1,0:T(8,128)(2,1)S(1)}, u32[]{:S(2)}, u32[]{:S(2)}) collective-permute-start(bf16[256,1152]{1,0:T(8,128)(2,1)S(1)} %get-tuple-element.490.refs_0_), channel_id=1, source_target_pairs={{0,1},{1,0},{2,3},{3,2},{4,5},{5,4},{6,7},{7,6},{8,9},{9,8},{10,11... | collective-permute-start | bytes 1769480 | tf_op jit(solution)/shard_map/ppermute | solution.py:870
  163.9 9.6 %collective-permute-start.35 = (bf16[256,1152]{1,0:T(8,128)(2,1)S(1)}, bf16[256,1152]{1,0:T(8,128)(2,1)S(1)}, u32[]{:S(2)}, u32[]{:S(2)}) collective-permute-start(bf16[256,1152]{1,0:T(8,128)(2,1)S(1)} %get-tuple-element.496), channel_id=1, source_target_pairs={{0,1},{1,0},{2,3},{3,2},{4,5},{5,4},{6,7},{7,6},{8,9},{9,8},{10,11... | collective-permute-start | bytes 1769480 | tf_op jit(solution)/shard_map/ppermute | solution.py:870
  164.4 9.2 %collective-permute-start.36 = (bf16[256,1152]{1,0:T(8,128)(2,1)S(1)}, bf16[256,1152]{1,0:T(8,128)(2,1)S(1)}, u32[]{:S(2)}, u32[]{:S(2)}) collective-permute-start(bf16[256,1152]{1,0:T(8,128)(2,1)S(1)} %get-tuple-element.498.refs_0_), channel_id=1, source_target_pairs={{0,1},{1,0},{2,3},{3,2},{4,5},{5,4},{6,7},{7,6},{8,9},{9,8},{10,11... | collective-permute-start | bytes 1769480 | tf_op jit(solution)/shard_map/ppermute | solution.py:870
  164.5 13.0 %collective-permute-start.37 = (bf16[128,1152]{1,0:T(8,128)(2,1)S(1)}, bf16[128,1152]{1,0:T(8,128)(2,1)S(1)}, u32[]{:S(2)}, u32[]{:S(2)}) collective-permute-start(bf16[128,1152]{1,0:T(8,128)(2,1)S(1)} %get-tuple-element.502.refs_1_.refs_6_), channel_id=1, source_target_pairs={{0,2},{1,3},{2,0},{3,1},{4,6},{5,7},{6,4},{7,5},{8,10},{9,11},{10,... | collective-permute-start | bytes 884744 | tf_op jit(solution)/shard_map/ppermute | solution.py:873
  179.2 16.1 %collective-permute-start.42 = (bf16[256,1152]{1,0:T(8,128)(2,1)S(1)}, bf16[256,1152]{1,0:T(8,128)(2,1)S(1)}, u32[]{:S(2)}, u32[]{:S(2)}) collective-permute-start(bf16[256,1152]{1,0:T(8,128)(2,1)S(1)} %get-tuple-element.515.refs_0_), channel_id=1, source_target_pairs={{0,2},{1,3},{2,0},{3,1},{4,6},{5,7},{6,4},{7,5},{8,10},{9,11},{10,... | collective-permute-start | bytes 1769480 | tf_op jit(solution)/shard_map/ppermute | solution.py:873
  186.3 32.5 %collective-permute-start.44 = (bf16[256,1152]{1,0:T(8,128)(2,1)}, bf16[256,1152]{1,0:T(8,128)(2,1)}, u32[]{:S(2)}, u32[]{:S(2)}) collective-permute-start(bf16[256,1152]{1,0:T(8,128)(2,1)} %get-tuple-element.535), channel_id=1, source_target_pairs={{0,1},{1,0},{2,3},{3,2},{4,5},{5,4},{6,7},{7,6},{8,9},{9,8},{10,11... | collective-permute-start | bytes 1769480 | tf_op jit(solution)/shard_map/ppermute | solution.py:870
  186.5 35.6 %collective-permute-start.45 = (bf16[256,1152]{1,0:T(8,128)(2,1)}, bf16[256,1152]{1,0:T(8,128)(2,1)}, u32[]{:S(2)}, u32[]{:S(2)}) collective-permute-start(bf16[256,1152]{1,0:T(8,128)(2,1)} %get-tuple-element.538), channel_id=1, source_target_pairs={{0,1},{1,0},{2,3},{3,2},{4,5},{5,4},{6,7},{7,6},{8,9},{9,8},{10,11... | collective-permute-start | bytes 1769480 | tf_op jit(solution)/shard_map/ppermute | solution.py:870
  186.8 27.5 %collective-permute-start.43 = (bf16[256,1152]{1,0:T(8,128)(2,1)S(1)}, bf16[256,1152]{1,0:T(8,128)(2,1)S(1)}, u32[]{:S(2)}, u32[]{:S(2)}) collective-permute-start(bf16[256,1152]{1,0:T(8,128)(2,1)S(1)} %get-tuple-element.531.refs_0_), channel_id=1, source_target_pairs={{0,2},{1,3},{2,0},{3,1},{4,6},{5,7},{6,4},{7,5},{8,10},{9,11},{10,... | collective-permute-start | bytes 1769480 | tf_op jit(solution)/shard_map/ppermute | solution.py:873
  199.3 25.8 %collective-permute-start.46 = (bf16[256,1152]{1,0:T(8,128)(2,1)}, bf16[256,1152]{1,0:T(8,128)(2,1)}, u32[]{:S(2)}, u32[]{:S(2)}) collective-permute-start(bf16[256,1152]{1,0:T(8,128)(2,1)} %get-tuple-element.542.refs_4_), channel_id=1, source_target_pairs={{0,1},{1,0},{2,3},{3,2},{4,5},{5,4},{6,7},{7,6},{8,9},{9,8},{10,11... | collective-permute-start | bytes 1769480 | tf_op jit(solution)/shard_map/ppermute | solution.py:870
  218.2 6.9 %collective-permute-start.47 = (bf16[256,1152]{1,0:T(8,128)(2,1)}, bf16[256,1152]{1,0:T(8,128)(2,1)}, u32[]{:S(2)}, u32[]{:S(2)}) collective-permute-start(bf16[256,1152]{1,0:T(8,128)(2,1)} %get-tuple-element.543.refs_6_), channel_id=1, source_target_pairs={{0,1},{1,0},{2,3},{3,2},{4,5},{5,4},{6,7},{7,6},{8,9},{9,8},{10,11... | collective-permute-start | bytes 1769480 | tf_op jit(solution)/shard_map/ppermute | solution.py:870
  218.7 318.3 %reduce-scatter.5.cloned.1.call-start = ((), (), s32[]{:S(2)}) async-start(), calls=%async_computation.3 | async-start | bytes 5971968 | tf_op jit(solution)/shard_map/reduce_scatter | solution.py:938
  249.8 9.3 %collective-permute-start.49 = (bf16[128,1152]{1,0:T(8,128)(2,1)S(1)}, bf16[128,1152]{1,0:T(8,128)(2,1)S(1)}, u32[]{:S(2)}, u32[]{:S(2)}) collective-permute-start(bf16[128,1152]{1,0:T(8,128)(2,1)S(1)} %copy-done.77), channel_id=1, source_target_pairs={{0,2},{1,3},{2,0},{3,1},{4,6},{5,7},{6,4},{7,5},{8,10},{9,11},{10,... | collective-permute-start | bytes 884744 | tf_op jit(solution)/shard_map/ppermute | solution.py:873
  253.3 8.0 %collective-permute-start.50 = (bf16[256,1152]{1,0:T(8,128)(2,1)S(1)}, bf16[256,1152]{1,0:T(8,128)(2,1)S(1)}, u32[]{:S(2)}, u32[]{:S(2)}) collective-permute-start(bf16[256,1152]{1,0:T(8,128)(2,1)S(1)} %get-tuple-element.556), channel_id=1, source_target_pairs={{0,1},{1,0},{2,3},{3,2},{4,5},{5,4},{6,7},{7,6},{8,9},{9,8},{10,11... | collective-permute-start | bytes 1769480 | tf_op jit(solution)/shard_map/ppermute | solution.py:870
  260.8 15.7 %collective-permute-start.53 = (bf16[256,1152]{1,0:T(8,128)(2,1)S(1)}, bf16[256,1152]{1,0:T(8,128)(2,1)S(1)}, u32[]{:S(2)}, u32[]{:S(2)}) collective-permute-start(bf16[256,1152]{1,0:T(8,128)(2,1)S(1)} %get-tuple-element.566.refs_0_), channel_id=1, source_target_pairs={{0,2},{1,3},{2,0},{3,1},{4,6},{5,7},{6,4},{7,5},{8,10},{9,11},{10,... | collective-permute-start | bytes 1769480 | tf_op jit(solution)/shard_map/ppermute | solution.py:873
  287.2 16.4 %collective-permute-start.58 = (bf16[256,1152]{1,0:T(8,128)(2,1)}, bf16[256,1152]{1,0:T(8,128)(2,1)S(1)}, u32[]{:S(2)}, u32[]{:S(2)}) collective-permute-start(bf16[256,1152]{1,0:T(8,128)(2,1)} %copy-done.56), channel_id=1, source_target_pairs={{0,2},{1,3},{2,0},{3,1},{4,6},{5,7},{6,4},{7,5},{8,10},{9,11},{10,... | collective-permute-start | bytes 1769480 | tf_op jit(solution)/shard_map/ppermute | solution.py:873
  287.8 21.3 %collective-permute-start.59 = (bf16[128,1152]{1,0:T(8,128)(2,1)}, bf16[128,1152]{1,0:T(8,128)(2,1)S(1)}, u32[]{:S(2)}, u32[]{:S(2)}) collective-permute-start(bf16[128,1152]{1,0:T(8,128)(2,1)} %get-tuple-element.597.refs_0_), channel_id=1, source_target_pairs={{0,2},{1,3},{2,0},{3,1},{4,6},{5,7},{6,4},{7,5},{8,10},{9,11},{10,... | collective-permute-start | bytes 884744 | tf_op jit(solution)/shard_map/ppermute | solution.py:873
  311.6 9.9 %collective-permute-start.62 = (bf16[128,1152]{1,0:T(8,128)(2,1)S(1)}, bf16[128,1152]{1,0:T(8,128)(2,1)S(1)}, u32[]{:S(2)}, u32[]{:S(2)}) collective-permute-start(bf16[128,1152]{1,0:T(8,128)(2,1)S(1)} %get-tuple-element.606.refs_0_), channel_id=1, source_target_pairs={{0,2},{1,3},{2,0},{3,1},{4,6},{5,7},{6,4},{7,5},{8,10},{9,11},{10,... | collective-permute-start | bytes 884744 | tf_op jit(solution)/shard_map/ppermute | solution.py:873
  312.2 31.6 %collective-permute-start.65 = (bf16[4,144,1152]{2,1,0:T(8,128)(2,1)}, bf16[4,144,1152]{2,1,0:T(8,128)(2,1)}, u32[]{:S(2)}, u32[]{:S(2)}) collective-permute-start(bf16[4,144,1152]{2,1,0:T(8,128)(2,1)} %get-tuple-element.629), channel_id=1, source_target_pairs={{0,4},{4,0},{8,12},{12,8},{16,20},{20,16},{24,28},{28,24},{1,5},{5... | collective-permute-start | bytes 3981320 | tf_op jit(solution)/shard_map/ppermute | solution.py:876
  318.6 17.2 %collective-permute-start.64 = (bf16[128,1152]{1,0:T(8,128)(2,1)}, bf16[128,1152]{1,0:T(8,128)(2,1)S(1)}, u32[]{:S(2)}, u32[]{:S(2)}) collective-permute-start(bf16[128,1152]{1,0:T(8,128)(2,1)} %get-tuple-element.626), channel_id=1, source_target_pairs={{0,1},{1,0},{2,3},{3,2},{4,5},{5,4},{6,7},{7,6},{8,9},{9,8},{10,11... | collective-permute-start | bytes 884744 | tf_op jit(solution)/shard_map/ppermute | solution.py:870
  319.1 14.5 %collective-permute-start.63 = (bf16[128,1152]{1,0:T(8,128)(2,1)S(1)}, bf16[128,1152]{1,0:T(8,128)(2,1)S(1)}, u32[]{:S(2)}, u32[]{:S(2)}) collective-permute-start(bf16[128,1152]{1,0:T(8,128)(2,1)S(1)} %get-tuple-element.622.refs_0_), channel_id=1, source_target_pairs={{0,2},{1,3},{2,0},{3,1},{4,6},{5,7},{6,4},{7,5},{8,10},{9,11},{10,... | collective-permute-start | bytes 884744 | tf_op jit(solution)/shard_map/ppermute | solution.py:873
  335.3 11.9 %collective-permute-start.67 = (bf16[128,1152]{1,0:T(8,128)(2,1)S(1)}, bf16[128,1152]{1,0:T(8,128)(2,1)S(1)}, u32[]{:S(2)}, u32[]{:S(2)}) collective-permute-start(bf16[128,1152]{1,0:T(8,128)(2,1)S(1)} %get-tuple-element.634.refs_6_), channel_id=1, source_target_pairs={{0,1},{1,0},{2,3},{3,2},{4,5},{5,4},{6,7},{7,6},{8,9},{9,8},{10,11... | collective-permute-start | bytes 884744 | tf_op jit(solution)/shard_map/ppermute | solution.py:870
  335.3 11.9 %collective-permute-start.66 = (bf16[128,1152]{1,0:T(8,128)(2,1)S(1)}, bf16[128,1152]{1,0:T(8,128)(2,1)S(1)}, u32[]{:S(2)}, u32[]{:S(2)}) collective-permute-start(bf16[128,1152]{1,0:T(8,128)(2,1)S(1)} %get-tuple-element.633.refs_4_), channel_id=1, source_target_pairs={{0,1},{1,0},{2,3},{3,2},{4,5},{5,4},{6,7},{7,6},{8,9},{9,8},{10,11... | collective-permute-start | bytes 884744 | tf_op jit(solution)/shard_map/ppermute | solution.py:870
  372.2 50.5 %collective-permute-start.78 = (bf16[256,1152]{1,0:T(8,128)(2,1)S(1)}, bf16[256,1152]{1,0:T(8,128)(2,1)S(1)}, u32[]{:S(2)}, u32[]{:S(2)}) collective-permute-start(bf16[256,1152]{1,0:T(8,128)(2,1)S(1)} %copy-done.21), channel_id=1, source_target_pairs={{0,2},{1,3},{2,0},{3,1},{4,6},{5,7},{6,4},{7,5},{8,10},{9,11},{10,... | collective-permute-start | bytes 1769480 | tf_op jit(solution)/shard_map/ppermute | solution.py:873
  373.6 49.1 %collective-permute-start.77 = (bf16[256,1152]{1,0:T(8,128)(2,1)S(1)}, bf16[256,1152]{1,0:T(8,128)(2,1)}, u32[]{:S(2)}, u32[]{:S(2)}) collective-permute-start(bf16[256,1152]{1,0:T(8,128)(2,1)S(1)} %copy-done.19), channel_id=1, source_target_pairs={{0,2},{1,3},{2,0},{3,1},{4,6},{5,7},{6,4},{7,5},{8,10},{9,11},{10,... | collective-permute-start | bytes 1769480 | tf_op jit(solution)/shard_map/ppermute | solution.py:873
  374.2 27.7 %collective-permute-start.73 = (bf16[2,144,1152]{2,1,0:T(8,128)(2,1)}, bf16[2,144,1152]{2,1,0:T(8,128)(2,1)}, u32[]{:S(2)}, u32[]{:S(2)}) collective-permute-start(bf16[2,144,1152]{2,1,0:T(8,128)(2,1)} %get-tuple-element.671), channel_id=1, source_target_pairs={{0,8},{4,12},{8,0},{12,4},{16,24},{20,28},{24,16},{28,20},{1,9},{5... | collective-permute-start | bytes 1990664 | tf_op jit(solution)/shard_map/ppermute | solution.py:876
  375.8 31.6 %collective-permute-start.74 = (bf16[128,1152]{1,0:T(8,128)(2,1)S(1)}, bf16[128,1152]{1,0:T(8,128)(2,1)}, u32[]{:S(2)}, u32[]{:S(2)}) collective-permute-start(bf16[128,1152]{1,0:T(8,128)(2,1)S(1)} %get-tuple-element.673.refs_0_), channel_id=1, source_target_pairs={{0,2},{1,3},{2,0},{3,1},{4,6},{5,7},{6,4},{7,5},{8,10},{9,11},{10,... | collective-permute-start | bytes 884744 | tf_op jit(solution)/shard_map/ppermute | solution.py:873
  377.5 36.2 %collective-permute-start.75 = (bf16[128,1152]{1,0:T(8,128)(2,1)S(1)}, bf16[128,1152]{1,0:T(8,128)(2,1)}, u32[]{:S(2)}, u32[]{:S(2)}) collective-permute-start(bf16[128,1152]{1,0:T(8,128)(2,1)S(1)} %get-tuple-element.676.refs_0_), channel_id=1, source_target_pairs={{0,2},{1,3},{2,0},{3,1},{4,6},{5,7},{6,4},{7,5},{8,10},{9,11},{10,... | collective-permute-start | bytes 884744 | tf_op jit(solution)/shard_map/ppermute | solution.py:873
  401.9 20.8 %collective-permute-start.79 = (bf16[128,1152]{1,0:T(8,128)(2,1)}, bf16[128,1152]{1,0:T(8,128)(2,1)S(1)}, u32[]{:S(2)}, u32[]{:S(2)}) collective-permute-start(bf16[128,1152]{1,0:T(8,128)(2,1)} %get-tuple-element.684.refs_11_), channel_id=1, source_target_pairs={{0,2},{1,3},{2,0},{3,1},{4,6},{5,7},{6,4},{7,5},{8,10},{9,11},{10,... | collective-permute-start | bytes 884744 | tf_op jit(solution)/shard_map/ppermute | solution.py:873
  407.4 14.9 %collective-permute-start.76 = (bf16[64,1152]{1,0:T(8,128)(2,1)S(1)}, bf16[64,1152]{1,0:T(8,128)(2,1)S(1)}, u32[]{:S(2)}, u32[]{:S(2)}) collective-permute-start(bf16[64,1152]{1,0:T(8,128)(2,1)S(1)} %copy-done.89), channel_id=1, source_target_pairs={{0,2},{1,3},{2,0},{3,1},{4,6},{5,7},{6,4},{7,5},{8,10},{9,11},{10,... | collective-permute-start | bytes 442376 | tf_op jit(solution)/shard_map/ppermute | solution.py:873
  430.6 15.9 %collective-permute-start.85 = (f32[23040]{0:T(1024)S(1)}, f32[23040]{0:T(1024)}, u32[]{:S(2)}, u32[]{:S(2)}) collective-permute-start(f32[23040]{0:T(1024)S(1)} %concatenate.74), channel_id=1, source_target_pairs={{0,16},{4,20},{8,24},{12,28},{16,0},{20,4},{24,8},{28,12},{1,17},{... | collective-permute-start | bytes 276488 | tf_op jit(solution)/shard_map/ppermute | solution.py:876
  432.7 65.8 %collective-permute-start.81 = (bf16[4,144,1152]{2,1,0:T(8,128)(2,1)}, bf16[4,144,1152]{2,1,0:T(8,128)(2,1)}, u32[]{:S(2)}, u32[]{:S(2)}) collective-permute-start(bf16[4,144,1152]{2,1,0:T(8,128)(2,1)} %get-tuple-element.709), channel_id=1, source_target_pairs={{0,4},{4,0},{8,12},{12,8},{16,20},{20,16},{24,28},{28,24},{1,5},{5... | collective-permute-start | bytes 3981320 | tf_op jit(solution)/shard_map/ppermute | solution.py:876
  434.2 19.3 %collective-permute-start.92 = (bf16[1,144,1152]{2,1,0:T(8,128)(2,1)}, bf16[1,144,1152]{2,1,0:T(8,128)(2,1)}, u32[]{:S(2)}, u32[]{:S(2)}) collective-permute-start(bf16[1,144,1152]{2,1,0:T(8,128)(2,1)} %get-tuple-element.732), channel_id=1, source_target_pairs={{0,16},{4,20},{8,24},{12,28},{16,0},{20,4},{24,8},{28,12},{1,17},{... | collective-permute-start | bytes 995336 | tf_op jit(solution)/shard_map/ppermute | solution.py:876
  435.0 68.8 %collective-permute-start.82 = (bf16[640,1152]{1,0:T(8,128)(2,1)S(1)}, bf16[640,1152]{1,0:T(8,128)(2,1)S(1)}, u32[]{:S(2)}, u32[]{:S(2)}) collective-permute-start(bf16[640,1152]{1,0:T(8,128)(2,1)S(1)} %copy-done.39), channel_id=1, source_target_pairs={{0,1},{1,0},{2,3},{3,2},{4,5},{5,4},{6,7},{7,6},{8,9},{9,8},{10,11... | collective-permute-start | bytes 4423688 | tf_op jit(solution)/shard_map/ppermute | solution.py:870
  435.0 84.0 %collective-permute-start.84 = (bf16[320,1152]{1,0:T(8,128)(2,1)}, bf16[320,1152]{1,0:T(8,128)(2,1)}, u32[]{:S(2)}, u32[]{:S(2)}) collective-permute-start(bf16[320,1152]{1,0:T(8,128)(2,1)} %copy-done.48), channel_id=1, source_target_pairs={{0,1},{1,0},{2,3},{3,2},{4,5},{5,4},{6,7},{7,6},{8,9},{9,8},{10,11... | collective-permute-start | bytes 2211848 | tf_op jit(solution)/shard_map/ppermute | solution.py:870
  448.4 6.9 %collective-permute-start.86 = (f32[23040]{0:T(1024)S(1)}, f32[23040]{0:T(1024)S(1)}, u32[]{:S(2)}, u32[]{:S(2)}) collective-permute-start(f32[23040]{0:T(1024)S(1)} %pad_maximum_fusion.1), channel_id=1, source_target_pairs={{0,8},{4,12},{8,0},{12,4},{16,24},{20,28},{24,16},{28,20},{1,9},{5... | collective-permute-start | bytes 276488 | tf_op jit(solution)/shard_map/ppermute | solution.py:876
  457.2 19.7 %collective-permute-start.87 = (f32[23040]{0:T(1024)S(1)}, f32[23040]{0:T(1024)S(1)}, u32[]{:S(2)}, u32[]{:S(2)}) collective-permute-start(f32[23040]{0:T(1024)S(1)} %pad_maximum_fusion.2), channel_id=1, source_target_pairs={{0,4},{4,0},{8,12},{12,8},{16,20},{20,16},{24,28},{28,24},{1,5},{5... | collective-permute-start | bytes 276488 | tf_op jit(solution)/shard_map/ppermute | solution.py:876
  481.3 7.9 %collective-permute-start.88 = (bf16[4,2,1152]{2,1,0:T(2,128)(2,1)}, bf16[4,2,1152]{2,1,0:T(2,128)(2,1)}, u32[]{:S(2)}, u32[]{:S(2)}) collective-permute-start(bf16[4,2,1152]{2,1,0:T(2,128)(2,1)} %convert_element_type.192), channel_id=1, source_target_pairs={{0,16},{4,20},{8,24},{12,28},{16,0},{20,4},{24,8},{28,12},{1,17},{... | collective-permute-start | bytes 55304 | tf_op jit(solution)/shard_map/ppermute | solution.py:876
  501.5 15.6 %collective-permute-start.83 = (bf16[2,144,1152]{2,1,0:T(8,128)(2,1)S(1)}, bf16[2,144,1152]{2,1,0:T(8,128)(2,1)S(1)}, u32[]{:S(2)}, u32[]{:S(2)}) collective-permute-start(bf16[2,144,1152]{2,1,0:T(8,128)(2,1)S(1)} %get-tuple-element.717), channel_id=1, source_target_pairs={{0,8},{4,12},{8,0},{12,4},{16,24},{20,28},{24,16},{28,20},{1,9},{5... | collective-permute-start | bytes 1990664 | tf_op jit(solution)/shard_map/ppermute | solution.py:876
  517.3 15.6 %collective-permute-start.91 = (bf16[1,144,1152]{2,1,0:T(8,128)(2,1)S(1)}, bf16[1,144,1152]{2,1,0:T(8,128)(2,1)S(1)}, u32[]{:S(2)}, u32[]{:S(2)}) collective-permute-start(bf16[1,144,1152]{2,1,0:T(8,128)(2,1)S(1)} %get-tuple-element.730), channel_id=1, source_target_pairs={{0,16},{4,20},{8,24},{12,28},{16,0},{20,4},{24,8},{28,12},{1,17},{... | collective-permute-start | bytes 995336 | tf_op jit(solution)/shard_map/ppermute | solution.py:876
  (223 other events, 1904.9 us)
Sparse Core Ops, SparseCore 0:
  218.8 103.7 reduce-scatter.2
  378.7 125.6 reduce-scatter.4

commit v5 on v4

--- a/solution.py
+++ b/solution.py
@@ -40,7 +40,7 @@
 COSTS = {
     "gather_rows": 0.8, "ln_open": 0.4, "near_sum": 0.4, "merge_attn": 0.6, "merge_mlp": 0.6,
     "finish": 1.0, "first_grad": 0.5, "qkv_forward": 1.2, "qkv_backward": 1.2, "mlp_forward": 3.5,
-    "mlp_backward": 3.0, "ln_back": 1.2, "attn_forward": 4.0, "attn_backward": 9.0,
+    "mlp_backward": 3.0, "ln_back": 1.2, "attn_forward": 0.0, "attn_backward": 0.0,
     "weight_grads": 6.5, "halve": 1.5, "place_rows": 3.0, "table_rows": 1.0,
 }
 
@@ -77,7 +77,7 @@
             scratch_shapes=list(scratch)
             + ([pltpu.SemaphoreType.DMA((copies,))] if copies else []),
             cost_estimate=pl.CostEstimate(
-                flops=int(COSTS.get(name, 1.0) * 1e9), transcendentals=0, bytes_accessed=1000
+                flops=int(COSTS.get(name, 1.0) * 1.15e9), transcendentals=0, bytes_accessed=1000
             ),
             compiler_params=pltpu.CompilerParams(vmem_limit_bytes=limit * MIB),
             name=name,
@@ -924,18 +924,52 @@
             )
             self.send(away)
 
-    def result(self):
-        while self.order:
-            self.step()
-        return self.kept[0].astype(F32) + self.moved[0].astype(F32)
-
-
-def reduced(queue, links, pairs, after=None):
+
+def last_sums(queue, parts):
+    shapes = [part.kept.shape[1:] for part in parts]
+
+    def body(*refs):
+        for index in range(len(parts)):
+            kept_ref, moved_ref = refs[2 * index : 2 * index + 2]
+            total = kept_ref[0].astype(F32) + moved_ref[0].astype(F32)
+            refs[2 * len(parts) + index][...] = total
+
+    operands = [value for part in parts for value in (part.kept, part.moved)]
+    return queue.call(body, operands, [shaped(shape, F32) for shape in shapes], "last_sums")
+
+
+def emit_wide(queue, parts, wide):
+    each = parts[0].shape[0]
+
+    def body(up_ref, down_ref, both_ref, up_out, down_out):
+        up_out[0] = up_ref[...]
+        down_out[0] = down_ref[...]
+        up_out[1] = both_ref[:, :wide].astype(F32)
+        down_out[1] = both_ref[:, wide:].astype(F32)
+
+    features = parts[1].shape[1]
+    outs = [shaped((2, each, wide), F32), shaped((2, each, features), F32)]
+    return queue.call(body, parts, outs, "emit_wide")
+
+
+def emit_attention(queue, encoder, decoder, local):
+    each = decoder.shape[0]
+
+    def body(kept_ref, moved_ref, dec_ref, proj_ref, qkv_ref):
+        total = kept_ref[0].astype(F32) + moved_ref[0].astype(F32)
+        for index, value in enumerate((total, dec_ref[...])):
+            proj_ref[index] = value[:, :local]
+            for part in range(3):
+                qkv_ref[index, part] = value[:, (part + 1) * local : (part + 2) * local]
+
+    outs = [shaped((2, each, local), F32), shaped((2, 3, each, local), F32)]
+    return queue.call(body, [encoder.kept, encoder.moved, decoder], outs, "emit_attention")
+
+
+def reduced(queue, links, pairs):
     whole, sums = weight_grads(queue, pairs, sorted(links.dp_bits, reverse=True), [])
     flat = whole.reshape(-1, whole.shape[-1])
-    if after is not None:
-        flat, after = lax.optimization_barrier((flat, after))
-    return lax.psum_scatter(flat, "dp", scatter_dimension=0, tiled=True), sums, after
+    return lax.psum_scatter(flat, "dp", scatter_dimension=0, tiled=True), sums
 
 
 def scatter_sums(queue, links, pairs, cuts):
@@ -1248,20 +1282,36 @@
         near = near_sum(queue, *forward[chunk])
         sums_there[chunk] = (near, links.cross(near))
 
+    def finished(*chunks):
+        return finish(
+            queue,
+            [
+                (chunk.middle, *sums_there[chunk], d_out[decoder.index(chunk)], chunk.at)
+                for chunk in chunks
+            ],
+            small,
+            mods,
+        )
+
     dk.merge_back()
-    dec_wide, dec_wide_sums, _ = reduced(queue, links, wide_pairs(decoder))
+    dec_wide, dec_wide_sums = reduced(queue, links, wide_pairs(decoder))
     dm.merge_back()
     forward_sum(dk)
     forward_sum(dm)
     dm.attention_back()
+    decoded_long, long_sums = finished(dk, dm)
+    decoded_other = links.swap(decoded_long)
     dk.qkv_back()
+    dm.qkv_back()
     dk.near()
-    dm.qkv_back()
+    dm.near()
     dt.merge_back()
-    dm.near()
     dt.attention_back()
     dt.qkv_back()
     dt.near()
+    result_long = place_rows(
+        queue, core, perms_later[0], decoded_long, decoded_other, dec_rows[:2], 0
+    )
     enc_branch = (small, DOWN_BIAS, (0, 0), GATE_MLP)
     short_branch = (small, DOWN_BIAS, (0, 1), GATE_MLP)
     d_a, d_b, grad_a, grad_b = dk.leave_back(([ea.branch_mlp, eb.branch_mlp], *enc_branch))
@@ -1281,35 +1331,34 @@
     es.mlp_back()
     es.near()
     ea.merge_back()
-    enc_wide, enc_wide_sums, dec_wide = reduced(queue, links, wide_pairs(encoder), dec_wide)
+    (enc_up, enc_down), enc_wide_sums = scatter_sums(
+        queue, links, wide_pairs(encoder), [(wide, y_first), (wide, z_first)]
+    )
+    dec_attn.step()
     eb.merge_back()
     forward_sum(dt)
-    dec_attn.step()
     ea.attention_back()
     ea.qkv_back()
+    eb.qkv_back()
     ea.near()
-    eb.qkv_back()
+    eb.near()
+    enc_up.step()
+    enc_down.step()
     es.merge_back()
-    eb.near()
     es.attention_back()
     es.qkv_back()
     es.near()
     (enc_attn,), enc_attn_sums = scatter_sums(
         queue, links, attention_pairs(encoder), [(4 * local, y_first)]
     )
-    dec_attn.step()
+    enc_up.step()
+    enc_down.step()
     own_tokens = []
     for chunk in (ea, eb, es):
         own_tokens += chunk.leave_back(narrow=True)
-    decoded, gate_sums = finish(
-        queue,
-        [
-            (chunk.middle, *sums_there[chunk], d_out[index], chunk.at)
-            for index, chunk in enumerate(decoder)
-        ],
-        small,
-        mods,
-    )
+    decoded_short, short_sums = finished(dt)
+    decoded_other = links.swap(decoded_short)
+    dec_attn.step()
 
     sources, recipe = [], []
 
@@ -1326,7 +1375,7 @@
             if block == 0:
                 gates = [row((dk, dt)[latent].attn_sums, 2)]
             else:
-                gates = [row(gate_sums, latent)]
+                gates = [row((long_sums, short_sums)[latent], latent)]
             recipe += [
                 [row(chunk.attn_sums, 1) for chunk in members],
                 [row(chunk.attn_sums, 0) for chunk in members],
@@ -1343,6 +1392,9 @@
         [row(chunk.attn_sums, 4) for chunk in (dm, dt)],
     ]
     own_sums, joined = collect_sums(queue, sources, recipe, own_tokens)
+    enc_attn.step()
+    enc_up, enc_down = last_sums(queue, [enc_up, enc_down])
+    up_grad, down_grad = emit_wide(queue, [enc_up, enc_down, dec_wide], wide)
     packed, all_sums = pack_mods(
         queue, links.me, own_sums, links.swap(own_sums), 2, 2, dp_size, features
     )
@@ -1355,6 +1407,12 @@
         ]
     )
     mine, totals = links.exchange_relative(packed, totals)
+    mine, totals, enc_attn.moved = lax.optimization_barrier((mine, totals, enc_attn.moved))
+    enc_attn.step()
+    mine = queue.tie(mine)
+    result_short = place_rows(
+        queue, core, perms_later[1], decoded_short, decoded_other, dec_rows[2:], 0
+    )
     flat_mine = mine.reshape((-1,) + mine.shape[2:])
     grad_ada = jnp.einsum("nd,nlm->ldm", flat_acts, flat_mine, preferred_element_type=F32)
     grad_ada_bias = jnp.sum(flat_mine.astype(F32), axis=0)
@@ -1371,36 +1429,24 @@
     first += 2 * wide
     qv_out = totals[first : first + 4 * local].reshape(2, 2, local)
 
-    enc_attn.step()
-    decoded_other = links.swap(decoded)
-    results = (
-        place_rows(queue, core, perms_later[0], decoded, decoded_other, dec_rows[:2], 0),
-        place_rows(
-            queue, core, perms_later[1], decoded, decoded_other, dec_rows[2:], 2 * long_half
-        ),
-    )
-    enc_attn.step()
     joined_other = links.swap(joined)
     d_tokens = (
         place_rows(queue, core, perms_later[0], joined, joined_other, enc_rows[:2], 0),
         place_rows(queue, core, perms_later[1], joined, joined_other, enc_rows[2:], long_half),
     )
-    up_grad = jnp.stack([enc_wide[:, :wide], dec_wide[:, :wide]]).astype(F32)
-    down_grad = jnp.stack([enc_wide[:, wide:], dec_wide[:, wide:]]).astype(F32)
-    dec_att, enc_att = dec_attn.result(), enc_attn.result()
-    proj_grad = jnp.stack([enc_att[:, :local], dec_att[:, :local]])
-    qkv_grad = jnp.stack([enc_att[:, local:], dec_att[:, local:]]).reshape(2, -1, 3, local)
+    (dec_attn,) = last_sums(queue, [dec_attn])
+    proj_grad, qkv_grad = emit_attention(queue, enc_attn, dec_attn, local)
 
     return (
-        results[0][None],
-        results[1][None],
+        result_long[None],
+        result_short[None],
         d_tokens[0][None],
         d_tokens[1][None],
         d_cond[:1],
         d_cond[1:],
         grad_ada,
         grad_ada_bias,
-        qkv_grad,
+        jnp.transpose(qkv_grad, (0, 2, 1, 3)),
         qv_out,
         jnp.transpose(proj_grad, (0, 2, 1)),
         proj_out,

time: 558 us -> 524 us (0.939)
  local copies, waits for them, and re-layouts: 51.9 us -> 42.2 us
  Pallas kernels: 213 us -> 205 us
  other arithmetic: 10.5 us -> 2.82 us
  waiting for transfers between devices: 174 us -> 168 us
    pallas_call x111 -> x120, Pallas kernels: 213 us -> 205 us  [call(): pl.pallas_call(whole, in_specs=[fast] + [small] * len(scalars) + [slow] *...]
    ppermute x18 -> x24, waiting for transfers between devices: 76.8 us -> 69.3 us  [dp_move(): return lax.ppermute(value, 'dp', partners(self.dp_size, bit))]
    ppermute x51 -> x52, waiting for transfers between devices: 11.6 us -> 13.9 us  [swap(): return lax.ppermute(value, 'tensor', partners(self.tensor_size, 1))]
    ppermute x18 -> x24, starting transfers between devices: 32.5 us -> 33.3 us  [dp_move(): return lax.ppermute(value, 'dp', partners(self.dp_size, bit))]
    unnamed x354 -> x395, local copies, waits for them, and re-layouts: 36.2 us -> 36.1 us
  transfers between devices with their start and end apart: 95 -> 101, of which waited for: 42 -> 48; matrix products, arithmetic and copies ran while one was open for 5% -> 2% of each run, Pallas kernels for 35% -> 35%
where the time goes in v5:
time: 524 us; the launch traced here: 514 us
  Pallas kernels  205 us (39%)
  waiting for transfers between devices  168 us (32%)
  starting transfers between devices  70.4 us (13%)
  local copies, waits for them, and re-layouts  42.2 us (8%)
  between operations  17.3 us (3%)
  matrix products  8.57 us (2%)
    pallas_call x120, Pallas kernels, call(): pl.pallas_call(whole, in_specs=[fast] + [small] * len(scalars) + [slow] *...  205 us
    ppermute x24, waiting for transfers between devices, cross(): return lax.ppermute(value, 'tensor', partners(self.tensor_size, 2))  85 us
    ppermute x24, waiting for transfers between devices, dp_move(): return lax.ppermute(value, 'dp', partners(self.dp_size, bit))  69.3 us
    unnamed x395, local copies, waits for them, and re-layouts  36.1 us
    ppermute x24, starting transfers between devices, dp_move(): return lax.ppermute(value, 'dp', partners(self.dp_size, bit))  33.3 us
    ppermute x24, starting transfers between devices, cross(): return lax.ppermute(value, 'tensor', partners(self.tensor_size, 2))  26.1 us
    ppermute x52, waiting for transfers between devices, swap(): return lax.ppermute(value, 'tensor', partners(self.tensor_size, 1))  13.9 us
    ppermute x52, starting transfers between devices, swap(): return lax.ppermute(value, 'tensor', partners(self.tensor_size, 1))  10.9 us
  transfers between devices with their start and end apart: 101, of which 48 were waited for; matrix products, arithmetic and copies ran while one was open for 2% of the time, Pallas kernels for 35%

profile of v5, /device:TPU:0, one launch (start us, length us, event | category | flops | bytes accessed | tf_op | source)
XLA Modules:
  0.0 514.2 jit_solution(1550079317885207982)
XLA Ops:
  8.0 3.0 collective-permute-start
  16.5 3.1 collective-permute-start.2
  22.8 3.4 fusion
  28.1 3.1 collective-permute-done.3
  45.2 3.7 attn_forward.6
  49.1 3.7 attn_forward.7
  61.1 7.8 %collective-permute-done.12.refs_2_.refs_7_ = bf16[128,1152]{1,0:T(8,128)(2,1)S(1)} collective-permute-done((bf16[128,1152]{1,0:T(8,128)(2,1)S(1)}, bf16[128,1152]{1,0:T(8,128)(2,1)S(1)}, u32[]{:S(2)}, u32[]{:S(2)}) %collective-permute-start.12) | collective-permute-done | bytes 294944 | tf_op jit(solution)/shard_map/ppermute | solution.py:873
  75.7 3.5 collective-permute-done.15.refs_2_.refs_7_
  97.5 5.6 %collective-permute-done.23.refs_8_.refs_9_ = bf16[128,1152]{1,0:T(8,128)(2,1)S(1)} collective-permute-done((bf16[128,1152]{1,0:T(8,128)(2,1)S(1)}, bf16[128,1152]{1,0:T(8,128)(2,1)S(1)}, u32[]{:S(2)}, u32[]{:S(2)}) %collective-permute-start.23) | collective-permute-done | bytes 294944 | tf_op jit(solution)/shard_map/ppermute | solution.py:873
  105.5 4.7 collective-permute-done.24.refs_5_.refs_7_
  112.0 5.9 %attn_forward.9 = (f32[4,2,1,256]{3,2,1,0:T(1,128)S(1)}, bf16[256,1152]{1,0:T(8,128)(2,1)S(1)}, bf16[256,1152]{1,0:T(8,128)(2,1)S(1)}, bf16[512,288]{1,0:T(8,128)(2,1)}, f32[8,128]{1,0:T(8,128)S(1)}) custom-call(f32[8,128]{1,0:T(8,128)S(1)} %get-tuple-element.497.token_ref, bf16[2,256,864]{2,1,0:T(8,128)(2,1)S(1)} %get-tuple-element.498.refs_0_.refs_1_, ...), custom_call_target="tpu_custom_call" | custom-call | bytes 1000 | tf_op jit(solution)/shard_map/attn_forward/pallas_call | solution.py:68
  121.5 6.1 %attn_forward.10 = (f32[4,2,1,256]{3,2,1,0:T(1,128)S(1)}, bf16[256,1152]{1,0:T(8,128)(2,1)S(1)}, bf16[256,1152]{1,0:T(8,128)(2,1)S(1)}, bf16[512,288]{1,0:T(8,128)(2,1)}, f32[8,128]{1,0:T(8,128)S(1)}) custom-call(f32[8,128]{1,0:T(8,128)S(1)} %get-tuple-element.505.token_ref, bf16[2,256,864]{2,1,0:T(8,128)(2,1)S(1)} %get-tuple-element.499.refs_2_.refs_0_.refs_1_, ...), custom_call_target="tpu_custom_call" | custom-call | bytes 1000 | tf_op jit(solution)/shard_map/attn_forward/pallas_call | solution.py:68
  129.3 2.9 attn_forward.11
  133.9 9.4 %collective-permute-done.30.refs_2_.refs_7_ = bf16[256,1152]{1,0:T(8,128)(2,1)S(1)} collective-permute-done((bf16[256,1152]{1,0:T(8,128)(2,1)S(1)}, bf16[256,1152]{1,0:T(8,128)(2,1)S(1)}, u32[]{:S(2)}, u32[]{:S(2)}) %collective-permute-start.30) | collective-permute-done | bytes 589856 | tf_op jit(solution)/shard_map/ppermute | solution.py:873
  146.0 4.5 mlp_forward.9
  150.5 9.3 %collective-permute-done.32.refs_2_.refs_7_ = bf16[256,1152]{1,0:T(8,128)(2,1)S(1)} collective-permute-done((bf16[256,1152]{1,0:T(8,128)(2,1)S(1)}, bf16[256,1152]{1,0:T(8,128)(2,1)S(1)}, u32[]{:S(2)}, u32[]{:S(2)}) %collective-permute-start.32) | collective-permute-done | bytes 589856 | tf_op jit(solution)/shard_map/ppermute | solution.py:873
  160.5 3.6 mlp_backward.6
  166.2 4.9 mlp_forward.10
  171.3 3.6 mlp_backward.7
  185.0 7.9 %collective-permute-done.42.refs_1_ = bf16[256,1152]{1,0:T(8,128)(2,1)S(1)} collective-permute-done((bf16[256,1152]{1,0:T(8,128)(2,1)S(1)}, bf16[256,1152]{1,0:T(8,128)(2,1)S(1)}, u32[]{:S(2)}, u32[]{:S(2)}) %collective-permute-start.42) | collective-permute-done | bytes 589856 | tf_op jit(solution)/shard_map/ppermute | solution.py:873
  196.8 14.9 %weight_grads.4 = (f32[8,2304]{1,0:T(8,128)S(1)}, bf16[8,144,2304]{2,1,0:T(8,128)(2,1)}, f32[8,128]{1,0:T(8,128)S(1)}) custom-call(f32[8,128]{1,0:T(8,128)S(1)} %get-tuple-element.549.token_ref, bf16[512,1152]{1,0:T(8,128)(2,1)} %get-tuple-element.550.refs_0_, bf16[512,1152]{1,0:T(8,128)(2,1)} %get-tuple-element.551.refs_1_, ...), custom_call_target="tpu_custom_call" | custom-call | flops 7474999808 | bytes 1000 | tf_op jit(solution)/shard_map/weight_grads/pallas_call | solution.py:68
  218.5 22.2 %attn_backward.4 = (bf16[2,256,864]{2,1,0:T(8,128)(2,1)S(1)}, bf16[2,256,864]{2,1,0:T(8,128)(2,1)S(1)}, bf16[512,1152]{1,0:T(8,128)(2,1)}, bf16[512,1152]{1,0:T(...) custom-call(f32[8,128]{1,0:T(8,128)S(1)} %get-tuple-element.571.token_ref, ...), custom_call_target="tpu_custom_call" | custom-call | bytes 1000 | tf_op jit(solution)/shard_map/attn_backward/pallas_call | solution.py:68
  240.7 4.0 collective-permute-done.48.refs_4_
  244.8 3.5 finish.2
  253.7 7.2 %collective-permute-done.52.refs_1_ = bf16[128,1152]{1,0:T(8,128)(2,1)S(1)} collective-permute-done((bf16[128,1152]{1,0:T(8,128)(2,1)S(1)}, bf16[128,1152]{1,0:T(8,128)(2,1)S(1)}, u32[]{:S(2)}, u32[]{:S(2)}) %collective-permute-start.52) | collective-permute-done | bytes 294944 | tf_op jit(solution)/shard_map/ppermute | solution.py:873
  263.4 3.8 attn_backward.5
  270.6 4.5 place_rows.4
  275.1 8.8 %collective-permute-done.56.refs_1_ = bf16[256,1152]{1,0:T(8,128)(2,1)S(1)} collective-permute-done((bf16[256,1152]{1,0:T(8,128)(2,1)S(1)}, bf16[256,1152]{1,0:T(8,128)(2,1)S(1)}, u32[]{:S(2)}, u32[]{:S(2)}) %collective-permute-start.56) | collective-permute-done | bytes 589856 | tf_op jit(solution)/shard_map/ppermute | solution.py:873
  287.2 2.9 mlp_backward.9
  301.0 8.8 %weight_grads.5 = (bf16[4,144,1152]{2,1,0:T(8,128)(2,1)S(1)}, bf16[4,144,1152]{2,1,0:T(8,128)(2,1)}, f32[8,1152]{1,0:T(8,128)S(1)}, f32[8,128]{1,0:T(8,128)S(1)}) custom-call(f32[8,128]{1,0:T(8,128)S(1)} %get-tuple-element.618.token_ref, s32[1]{0:T(128)} %bitcast.24.refs_0_, bf16[512,1152]{1,0:T(8,128)(2,1)} %get-tuple-element.619.refs_1_, ...), custom_call_target="tpu_custom_call" | custom-call | flops 7474999808 | bytes 1000 | tf_op jit(solution)/shard_map/weight_grads/pallas_call | solution.py:68
  311.6 4.4 collective-permute-done.62.refs_1_
  337.4 7.7 %weight_grads.6 = (bf16[4,144,1152]{2,1,0:T(8,128)(2,1)S(1)}, bf16[4,144,1152]{2,1,0:T(8,128)(2,1)S(1)}, bf16[4,144,1152]{2,1,0:T(8,128)(2,1)S(1)}, bf16[4,144,1...) custom-call(f32[8,128]{1,0:T(8,128)S(1)} %get-tuple-element.646.token_ref, s32[1]{0:T(128)} %bitcast.24.refs_0_, ...), custom_call_target="tpu_custom_call" | custom-call | flops 7474999808 | bytes 1000 | tf_op jit(solution)/shard_map/weight_grads/pallas_call | solution.py:68
  357.4 8.6 %attn_backward.6 = (bf16[2,128,864]{2,1,0:T(8,128)(2,1)S(1)}, bf16[2,128,864]{2,1,0:T(8,128)(2,1)S(1)}, bf16[256,1152]{1,0:T(8,128)(2,1)}, bf16[256,1152]{1,0:T(...) custom-call(f32[8,128]{1,0:T(8,128)S(1)} %get-tuple-element.668.token_ref, ...), custom_call_target="tpu_custom_call" | custom-call | bytes 1000 | tf_op jit(solution)/shard_map/attn_backward/pallas_call | solution.py:68
  371.2 6.7 %collective-permute-done.73.refs_2_ = bf16[4,144,1152]{2,1,0:T(8,128)(2,1)S(1)} collective-permute-done((bf16[4,144,1152]{2,1,0:T(8,128)(2,1)S(1)}, bf16[4,144,1152]{2,1,0:T(8,128)(2,1)S(1)}, u32[]{:S(2)}, u32[]{:S(2)}) %collective-permute-start.73) | collective-permute-done | bytes 1327136 | tf_op jit(solution)/shard_map/ppermute | solution.py:876
  383.1 3.2 attn_backward.7
  390.7 5.1 weight_grads.7
  398.5 6.6 %collective-permute-done.78.refs_2_ = bf16[2,144,1152]{2,1,0:T(8,128)(2,1)S(1)} collective-permute-done((bf16[2,144,1152]{2,1,0:T(8,128)(2,1)S(1)}, bf16[2,144,1152]{2,1,0:T(8,128)(2,1)S(1)}, u32[]{:S(2)}, u32[]{:S(2)}) %collective-permute-start.78) | collective-permute-done | bytes 663584 | tf_op jit(solution)/shard_map/ppermute | solution.py:876
  410.5 4.5 collective-permute-done.81.refs_1_
  417.7 4.4 collective-permute-done.82.refs_1_
  427.5 6.7 %collective-permute-done.85.refs_2_ = bf16[4,144,1152]{2,1,0:T(8,128)(2,1)S(1)} collective-permute-done((bf16[4,144,1152]{2,1,0:T(8,128)(2,1)S(1)}, bf16[4,144,1152]{2,1,0:T(8,128)(2,1)S(1)}, u32[]{:S(2)}, u32[]{:S(2)}) %collective-permute-start.85) | collective-permute-done | bytes 1327136 | tf_op jit(solution)/shard_map/ppermute | solution.py:876
  435.4 4.5 collective-permute-done.87.refs_3_
  439.9 4.3 collective-permute-done.86.refs_1_
  449.5 6.2 %collective-permute-done.89 = f32[23040]{0:T(1024)S(1)} collective-permute-done((f32[23040]{0:T(1024)S(1)}, f32[23040]{0:T(1024)S(1)}, u32[]{:S(2)}, u32[]{:S(2)}) %collective-permute-start.89) | collective-permute-done | bytes 92192 | tf_op jit(solution)/shard_map/ppermute | solution.py:876
  458.2 3.6 collective-permute-done.90
  467.1 8.4 %collective-permute-done.92.refs_2_ = bf16[2,144,1152]{2,1,0:T(8,128)(2,1)S(1)} collective-permute-done((bf16[2,144,1152]{2,1,0:T(8,128)(2,1)S(1)}, bf16[2,144,1152]{2,1,0:T(8,128)(2,1)S(1)}, u32[]{:S(2)}, u32[]{:S(2)}) %collective-permute-start.92) | collective-permute-done | bytes 663584 | tf_op jit(solution)/shard_map/ppermute | solution.py:876
  477.7 4.5 convolution_bitcast_fusion
  489.3 2.9 place_rows.6
  492.2 4.5 collective-permute-done.95
  (751 shorter events, 219.6 us)
Async XLA Ops:
  7.2 438.0 %reduce-scatter.2.cloned.1.call-start = ((), (), s32[]{:S(2)}) async-start(), calls=%async_computation.1 | async-start | bytes 5971968 | tf_op jit(solution)/shard_map/reduce_scatter | solution.py:972
  59.4 11.5 %collective-permute-start.13 = (bf16[256,1152]{1,0:T(8,128)(2,1)S(1)}, bf16[256,1152]{1,0:T(8,128)(2,1)S(1)}, u32[]{:S(2)}, u32[]{:S(2)}) collective-permute-start(bf16[256,1152]{1,0:T(8,128)(2,1)S(1)} %get-tuple-element.449.refs_0_), channel_id=1, source_target_pairs={{0,1},{1,0},{2,3},{3,2},{4,5},{5,4},{6,7},{7,6},{8,9},{9,8},{10,11... | collective-permute-start | bytes 1769480 | tf_op jit(solution)/shard_map/ppermute | solution.py:870
  59.6 9.3 %collective-permute-start.12 = (bf16[128,1152]{1,0:T(8,128)(2,1)S(1)}, bf16[128,1152]{1,0:T(8,128)(2,1)S(1)}, u32[]{:S(2)}, u32[]{:S(2)}) collective-permute-start(bf16[128,1152]{1,0:T(8,128)(2,1)S(1)} %get-tuple-element.447.refs_1_.refs_6_), channel_id=1, source_target_pairs={{0,2},{1,3},{2,0},{3,1},{4,6},{5,7},{6,4},{7,5},{8,10},{9,11},{10,... | collective-permute-start | bytes 884744 | tf_op jit(solution)/shard_map/ppermute | solution.py:873
  69.3 9.9 %collective-permute-start.15 = (bf16[128,1152]{1,0:T(8,128)(2,1)S(1)}, bf16[128,1152]{1,0:T(8,128)(2,1)S(1)}, u32[]{:S(2)}, u32[]{:S(2)}) collective-permute-start(bf16[128,1152]{1,0:T(8,128)(2,1)S(1)} %get-tuple-element.453.refs_1_.refs_6_), channel_id=1, source_target_pairs={{0,2},{1,3},{2,0},{3,1},{4,6},{5,7},{6,4},{7,5},{8,10},{9,11},{10,... | collective-permute-start | bytes 884744 | tf_op jit(solution)/shard_map/ppermute | solution.py:873
  87.7 9.8 %collective-permute-start.22 = (bf16[128,1152]{1,0:T(8,128)(2,1)S(1)}, bf16[128,1152]{1,0:T(8,128)(2,1)S(1)}, u32[]{:S(2)}, u32[]{:S(2)}) collective-permute-start(bf16[128,1152]{1,0:T(8,128)(2,1)S(1)} %get-tuple-element.487.refs_4_.refs_6_), channel_id=1, source_target_pairs={{0,2},{1,3},{2,0},{3,1},{4,6},{5,7},{6,4},{7,5},{8,10},{9,11},{10,... | collective-permute-start | bytes 884744 | tf_op jit(solution)/shard_map/ppermute | solution.py:873
  89.2 13.9 %collective-permute-start.23 = (bf16[128,1152]{1,0:T(8,128)(2,1)S(1)}, bf16[128,1152]{1,0:T(8,128)(2,1)S(1)}, u32[]{:S(2)}, u32[]{:S(2)}) collective-permute-start(bf16[128,1152]{1,0:T(8,128)(2,1)S(1)} %get-tuple-element.489.refs_7_.refs_8_), channel_id=1, source_target_pairs={{0,2},{1,3},{2,0},{3,1},{4,6},{5,7},{6,4},{7,5},{8,10},{9,11},{10,... | collective-permute-start | bytes 884744 | tf_op jit(solution)/shard_map/ppermute | solution.py:873
  127.8 15.6 %collective-permute-start.30 = (bf16[256,1152]{1,0:T(8,128)(2,1)S(1)}, bf16[256,1152]{1,0:T(8,128)(2,1)S(1)}, u32[]{:S(2)}, u32[]{:S(2)}) collective-permute-start(bf16[256,1152]{1,0:T(8,128)(2,1)S(1)} %get-tuple-element.516.refs_1_.refs_6_), channel_id=1, source_target_pairs={{0,2},{1,3},{2,0},{3,1},{4,6},{5,7},{6,4},{7,5},{8,10},{9,11},{10,... | collective-permute-start | bytes 1769480 | tf_op jit(solution)/shard_map/ppermute | solution.py:873
  144.0 15.7 %collective-permute-start.32 = (bf16[256,1152]{1,0:T(8,128)(2,1)S(1)}, bf16[256,1152]{1,0:T(8,128)(2,1)S(1)}, u32[]{:S(2)}, u32[]{:S(2)}) collective-permute-start(bf16[256,1152]{1,0:T(8,128)(2,1)S(1)} %get-tuple-element.520.refs_1_.refs_6_), channel_id=1, source_target_pairs={{0,2},{1,3},{2,0},{3,1},{4,6},{5,7},{6,4},{7,5},{8,10},{9,11},{10,... | collective-permute-start | bytes 1769480 | tf_op jit(solution)/shard_map/ppermute | solution.py:873
  145.6 14.9 %collective-permute-start.33 = (bf16[256,1152]{1,0:T(8,128)(2,1)S(1)}, bf16[256,1152]{1,0:T(8,128)(2,1)S(1)}, u32[]{:S(2)}, u32[]{:S(2)}) collective-permute-start(bf16[256,1152]{1,0:T(8,128)(2,1)S(1)} %get-tuple-element.522.refs_0_), channel_id=1, source_target_pairs={{0,1},{1,0},{2,3},{3,2},{4,5},{5,4},{6,7},{7,6},{8,9},{9,8},{10,11... | collective-permute-start | bytes 1769480 | tf_op jit(solution)/shard_map/ppermute | solution.py:870
  164.1 7.1 %collective-permute-start.35 = (bf16[256,1152]{1,0:T(8,128)(2,1)S(1)}, bf16[256,1152]{1,0:T(8,128)(2,1)S(1)}, u32[]{:S(2)}, u32[]{:S(2)}) collective-permute-start(bf16[256,1152]{1,0:T(8,128)(2,1)S(1)} %get-tuple-element.528), channel_id=1, source_target_pairs={{0,1},{1,0},{2,3},{3,2},{4,5},{5,4},{6,7},{7,6},{8,9},{9,8},{10,11... | collective-permute-start | bytes 1769480 | tf_op jit(solution)/shard_map/ppermute | solution.py:870
  164.7 10.4 %collective-permute-start.37 = (bf16[128,1152]{1,0:T(8,128)(2,1)S(1)}, bf16[128,1152]{1,0:T(8,128)(2,1)S(1)}, u32[]{:S(2)}, u32[]{:S(2)}) collective-permute-start(bf16[128,1152]{1,0:T(8,128)(2,1)S(1)} %get-tuple-element.534.refs_1_.refs_6_), channel_id=1, source_target_pairs={{0,2},{1,3},{2,0},{3,1},{4,6},{5,7},{6,4},{7,5},{8,10},{9,11},{10,... | collective-permute-start | bytes 884744 | tf_op jit(solution)/shard_map/ppermute | solution.py:873
  176.8 16.1 %collective-permute-start.42 = (bf16[256,1152]{1,0:T(8,128)(2,1)S(1)}, bf16[256,1152]{1,0:T(8,128)(2,1)S(1)}, u32[]{:S(2)}, u32[]{:S(2)}) collective-permute-start(bf16[256,1152]{1,0:T(8,128)(2,1)S(1)} %get-tuple-element.547.refs_0_), channel_id=1, source_target_pairs={{0,2},{1,3},{2,0},{3,1},{4,6},{5,7},{6,4},{7,5},{8,10},{9,11},{10,... | collective-permute-start | bytes 1769480 | tf_op jit(solution)/shard_map/ppermute | solution.py:873
  183.6 30.9 %collective-permute-start.44 = (bf16[256,1152]{1,0:T(8,128)(2,1)S(1)}, bf16[256,1152]{1,0:T(8,128)(2,1)S(1)}, u32[]{:S(2)}, u32[]{:S(2)}) collective-permute-start(bf16[256,1152]{1,0:T(8,128)(2,1)S(1)} %get-tuple-element.567), channel_id=1, source_target_pairs={{0,1},{1,0},{2,3},{3,2},{4,5},{5,4},{6,7},{7,6},{8,9},{9,8},{10,11... | collective-permute-start | bytes 1769480 | tf_op jit(solution)/shard_map/ppermute | solution.py:870
  183.7 31.7 %collective-permute-start.45 = (bf16[256,1152]{1,0:T(8,128)(2,1)S(1)}, bf16[256,1152]{1,0:T(8,128)(2,1)S(1)}, u32[]{:S(2)}, u32[]{:S(2)}) collective-permute-start(bf16[256,1152]{1,0:T(8,128)(2,1)S(1)} %get-tuple-element.570), channel_id=1, source_target_pairs={{0,1},{1,0},{2,3},{3,2},{4,5},{5,4},{6,7},{7,6},{8,9},{9,8},{10,11... | collective-permute-start | bytes 1769480 | tf_op jit(solution)/shard_map/ppermute | solution.py:870
  184.1 27.7 %collective-permute-start.43 = (bf16[256,1152]{1,0:T(8,128)(2,1)S(1)}, bf16[256,1152]{1,0:T(8,128)(2,1)S(1)}, u32[]{:S(2)}, u32[]{:S(2)}) collective-permute-start(bf16[256,1152]{1,0:T(8,128)(2,1)S(1)} %get-tuple-element.563.refs_0_), channel_id=1, source_target_pairs={{0,2},{1,3},{2,0},{3,1},{4,6},{5,7},{6,4},{7,5},{8,10},{9,11},{10,... | collective-permute-start | bytes 1769480 | tf_op jit(solution)/shard_map/ppermute | solution.py:873
  196.8 21.7 %collective-permute-start.46 = (bf16[256,1152]{1,0:T(8,128)(2,1)}, bf16[256,1152]{1,0:T(8,128)(2,1)}, u32[]{:S(2)}, u32[]{:S(2)}) collective-permute-start(bf16[256,1152]{1,0:T(8,128)(2,1)} %get-tuple-element.574.refs_4_), channel_id=1, source_target_pairs={{0,1},{1,0},{2,3},{3,2},{4,5},{5,4},{6,7},{7,6},{8,9},{9,8},{10,11... | collective-permute-start | bytes 1769480 | tf_op jit(solution)/shard_map/ppermute | solution.py:870
  216.4 24.3 %collective-permute-start.49 = (bf16[256,1152]{1,0:T(8,128)(2,1)}, bf16[256,1152]{1,0:T(8,128)(2,1)}, u32[]{:S(2)}, u32[]{:S(2)}) collective-permute-start(bf16[256,1152]{1,0:T(8,128)(2,1)} %get-tuple-element.578.refs_7_), channel_id=1, source_target_pairs={{0,2},{1,3},{2,0},{3,1},{4,6},{5,7},{6,4},{7,5},{8,10},{9,11},{10,... | collective-permute-start | bytes 1769480 | tf_op jit(solution)/shard_map/ppermute | solution.py:873
  216.9 27.8 %collective-permute-start.48 = (bf16[256,1152]{1,0:T(8,128)(2,1)}, bf16[256,1152]{1,0:T(8,128)(2,1)}, u32[]{:S(2)}, u32[]{:S(2)}) collective-permute-start(bf16[256,1152]{1,0:T(8,128)(2,1)} %get-tuple-element.577.refs_3_), channel_id=1, source_target_pairs={{0,2},{1,3},{2,0},{3,1},{4,6},{5,7},{6,4},{7,5},{8,10},{9,11},{10,... | collective-permute-start | bytes 1769480 | tf_op jit(solution)/shard_map/ppermute | solution.py:873
  251.9 9.0 %collective-permute-start.52 = (bf16[128,1152]{1,0:T(8,128)(2,1)S(1)}, bf16[128,1152]{1,0:T(8,128)(2,1)S(1)}, u32[]{:S(2)}, u32[]{:S(2)}) collective-permute-start(bf16[128,1152]{1,0:T(8,128)(2,1)S(1)} %copy-done.68), channel_id=1, source_target_pairs={{0,2},{1,3},{2,0},{3,1},{4,6},{5,7},{6,4},{7,5},{8,10},{9,11},{10,... | collective-permute-start | bytes 884744 | tf_op jit(solution)/shard_map/ppermute | solution.py:873
  252.3 18.2 %collective-permute-start.55 = (bf16[512,1152]{1,0:T(8,128)(2,1)S(1)}, bf16[512,1152]{1,0:T(8,128)(2,1)S(1)}, u32[]{:S(2)}, u32[]{:S(2)}) collective-permute-start(bf16[512,1152]{1,0:T(8,128)(2,1)S(1)} %get-tuple-element.601.refs_2_), channel_id=1, source_target_pairs={{0,1},{1,0},{2,3},{3,2},{4,5},{5,4},{6,7},{7,6},{8,9},{9,8},{10,11... | collective-permute-start | bytes 3538952 | tf_op jit(solution)/shard_map/ppermute | solution.py:870
  268.3 15.6 %collective-permute-start.56 = (bf16[256,1152]{1,0:T(8,128)(2,1)S(1)}, bf16[256,1152]{1,0:T(8,128)(2,1)S(1)}, u32[]{:S(2)}, u32[]{:S(2)}) collective-permute-start(bf16[256,1152]{1,0:T(8,128)(2,1)S(1)} %get-tuple-element.604.refs_0_), channel_id=1, source_target_pairs={{0,2},{1,3},{2,0},{3,1},{4,6},{5,7},{6,4},{7,5},{8,10},{9,11},{10,... | collective-permute-start | bytes 1769480 | tf_op jit(solution)/shard_map/ppermute | solution.py:873
  294.4 16.2 %collective-permute-start.61 = (bf16[256,1152]{1,0:T(8,128)(2,1)S(1)}, bf16[256,1152]{1,0:T(8,128)(2,1)S(1)}, u32[]{:S(2)}, u32[]{:S(2)}) collective-permute-start(bf16[256,1152]{1,0:T(8,128)(2,1)S(1)} %get-tuple-element.632.refs_0_), channel_id=1, source_target_pairs={{0,2},{1,3},{2,0},{3,1},{4,6},{5,7},{6,4},{7,5},{8,10},{9,11},{10,... | collective-permute-start | bytes 1769480 | tf_op jit(solution)/shard_map/ppermute | solution.py:873
  294.8 21.2 %collective-permute-start.62 = (bf16[128,1152]{1,0:T(8,128)(2,1)S(1)}, bf16[128,1152]{1,0:T(8,128)(2,1)S(1)}, u32[]{:S(2)}, u32[]{:S(2)}) collective-permute-start(bf16[128,1152]{1,0:T(8,128)(2,1)S(1)} %copy-done.70), channel_id=1, source_target_pairs={{0,2},{1,3},{2,0},{3,1},{4,6},{5,7},{6,4},{7,5},{8,10},{9,11},{10,... | collective-permute-start | bytes 884744 | tf_op jit(solution)/shard_map/ppermute | solution.py:873
  317.5 13.9 %collective-permute-start.65 = (bf16[128,1152]{1,0:T(8,128)(2,1)}, bf16[128,1152]{1,0:T(8,128)(2,1)S(1)}, u32[]{:S(2)}, u32[]{:S(2)}) collective-permute-start(bf16[128,1152]{1,0:T(8,128)(2,1)} %get-tuple-element.644.refs_0_), channel_id=1, source_target_pairs={{0,2},{1,3},{2,0},{3,1},{4,6},{5,7},{6,4},{7,5},{8,10},{9,11},{10,... | collective-permute-start | bytes 884744 | tf_op jit(solution)/shard_map/ppermute | solution.py:873
  317.9 32.3 %collective-permute-start.66 = (bf16[4,144,1152]{2,1,0:T(8,128)(2,1)}, bf16[4,144,1152]{2,1,0:T(8,128)(2,1)}, u32[]{:S(2)}, u32[]{:S(2)}) collective-permute-start(bf16[4,144,1152]{2,1,0:T(8,128)(2,1)} %get-tuple-element.661), channel_id=1, source_target_pairs={{0,4},{4,0},{8,12},{12,8},{16,20},{20,16},{24,28},{28,24},{1,5},{5... | collective-permute-start | bytes 3981320 | tf_op jit(solution)/shard_map/ppermute | solution.py:876
  345.1 32.8 %collective-permute-start.73 = (bf16[4,144,1152]{2,1,0:T(8,128)(2,1)S(1)}, bf16[4,144,1152]{2,1,0:T(8,128)(2,1)S(1)}, u32[]{:S(2)}, u32[]{:S(2)}) collective-permute-start(bf16[4,144,1152]{2,1,0:T(8,128)(2,1)S(1)} %get-tuple-element.685), channel_id=1, source_target_pairs={{0,4},{4,0},{8,12},{12,8},{16,20},{20,16},{24,28},{28,24},{1,5},{5... | collective-permute-start | bytes 3981320 | tf_op jit(solution)/shard_map/ppermute | solution.py:876
  346.2 8.8 %collective-permute-start.67 = (bf16[128,1152]{1,0:T(8,128)(2,1)S(1)}, bf16[128,1152]{1,0:T(8,128)(2,1)S(1)}, u32[]{:S(2)}, u32[]{:S(2)}) collective-permute-start(bf16[128,1152]{1,0:T(8,128)(2,1)S(1)} %copy-done.66), channel_id=1, source_target_pairs={{0,2},{1,3},{2,0},{3,1},{4,6},{5,7},{6,4},{7,5},{8,10},{9,11},{10,... | collective-permute-start | bytes 884744 | tf_op jit(solution)/shard_map/ppermute | solution.py:873
  347.3 8.5 %collective-permute-start.68 = (bf16[128,1152]{1,0:T(8,128)(2,1)S(1)}, bf16[128,1152]{1,0:T(8,128)(2,1)S(1)}, u32[]{:S(2)}, u32[]{:S(2)}) collective-permute-start(bf16[128,1152]{1,0:T(8,128)(2,1)S(1)} %copy-done.54), channel_id=1, source_target_pairs={{0,1},{1,0},{2,3},{3,2},{4,5},{5,4},{6,7},{7,6},{8,9},{9,8},{10,11... | collective-permute-start | bytes 884744 | tf_op jit(solution)/shard_map/ppermute | solution.py:870
  347.3 9.4 %collective-permute-start.69 = (bf16[128,1152]{1,0:T(8,128)(2,1)S(1)}, bf16[128,1152]{1,0:T(8,128)(2,1)S(1)}, u32[]{:S(2)}, u32[]{:S(2)}) collective-permute-start(bf16[128,1152]{1,0:T(8,128)(2,1)S(1)} %get-tuple-element.671.refs_4_), channel_id=1, source_target_pairs={{0,1},{1,0},{2,3},{3,2},{4,5},{5,4},{6,7},{7,6},{8,9},{9,8},{10,11... | collective-permute-start | bytes 884744 | tf_op jit(solution)/shard_map/ppermute | solution.py:870
  350.2 29.7 %collective-permute-start.74 = (bf16[4,144,1152]{2,1,0:T(8,128)(2,1)S(1)}, bf16[4,144,1152]{2,1,0:T(8,128)(2,1)S(1)}, u32[]{:S(2)}, u32[]{:S(2)}) collective-permute-start(bf16[4,144,1152]{2,1,0:T(8,128)(2,1)S(1)} %get-tuple-element.688), channel_id=1, source_target_pairs={{0,8},{4,12},{8,0},{12,4},{16,24},{20,28},{24,16},{28,20},{1,9},{5... | collective-permute-start | bytes 3981320 | tf_op jit(solution)/shard_map/ppermute | solution.py:876
  368.4 11.9 %collective-permute-start.75 = (bf16[64,1152]{1,0:T(8,128)(2,1)S(1)}, bf16[64,1152]{1,0:T(8,128)(2,1)S(1)}, u32[]{:S(2)}, u32[]{:S(2)}) collective-permute-start(bf16[64,1152]{1,0:T(8,128)(2,1)S(1)} %get-tuple-element.690.refs_0_), channel_id=1, source_target_pairs={{0,2},{1,3},{2,0},{3,1},{4,6},{5,7},{6,4},{7,5},{8,10},{9,11},{10,... | collective-permute-start | bytes 442376 | tf_op jit(solution)/shard_map/ppermute | solution.py:873
  387.3 17.8 %collective-permute-start.78 = (bf16[2,144,1152]{2,1,0:T(8,128)(2,1)S(1)}, bf16[2,144,1152]{2,1,0:T(8,128)(2,1)S(1)}, u32[]{:S(2)}, u32[]{:S(2)}) collective-permute-start(bf16[2,144,1152]{2,1,0:T(8,128)(2,1)S(1)} %copy-done.42), channel_id=1, source_target_pairs={{0,8},{4,12},{8,0},{12,4},{16,24},{20,28},{24,16},{28,20},{1,9},{5... | collective-permute-start | bytes 1990664 | tf_op jit(solution)/shard_map/ppermute | solution.py:876
  389.0 17.8 %collective-permute-start.79 = (bf16[2,144,1152]{2,1,0:T(8,128)(2,1)S(1)}, bf16[2,144,1152]{2,1,0:T(8,128)(2,1)S(1)}, u32[]{:S(2)}, u32[]{:S(2)}) collective-permute-start(bf16[2,144,1152]{2,1,0:T(8,128)(2,1)S(1)} %get-tuple-element.718), channel_id=1, source_target_pairs={{0,4},{4,0},{8,12},{12,8},{16,20},{20,16},{24,28},{28,24},{1,5},{5... | collective-permute-start | bytes 1990664 | tf_op jit(solution)/shard_map/ppermute | solution.py:876
  395.8 38.4 %collective-permute-start.85 = (bf16[4,144,1152]{2,1,0:T(8,128)(2,1)S(1)}, bf16[4,144,1152]{2,1,0:T(8,128)(2,1)S(1)}, u32[]{:S(2)}, u32[]{:S(2)}) collective-permute-start(bf16[4,144,1152]{2,1,0:T(8,128)(2,1)S(1)} %get-tuple-element.756), channel_id=1, source_target_pairs={{0,4},{4,0},{8,12},{12,8},{16,20},{20,16},{24,28},{28,24},{1,5},{5... | collective-permute-start | bytes 3981320 | tf_op jit(solution)/shard_map/ppermute | solution.py:876
  396.4 29.6 %collective-permute-start.84 = (bf16[2,144,1152]{2,1,0:T(8,128)(2,1)S(1)}, bf16[2,144,1152]{2,1,0:T(8,128)(2,1)S(1)}, u32[]{:S(2)}, u32[]{:S(2)}) collective-permute-start(bf16[2,144,1152]{2,1,0:T(8,128)(2,1)S(1)} %get-tuple-element.732), channel_id=1, source_target_pairs={{0,8},{4,12},{8,0},{12,4},{16,24},{20,28},{24,16},{28,20},{1,9},{5... | collective-permute-start | bytes 1990664 | tf_op jit(solution)/shard_map/ppermute | solution.py:876
  396.9 11.5 %collective-permute-start.80 = (bf16[128,1152]{1,0:T(8,128)(2,1)S(1)}, bf16[128,1152]{1,0:T(8,128)(2,1)S(1)}, u32[]{:S(2)}, u32[]{:S(2)}) collective-permute-start(bf16[128,1152]{1,0:T(8,128)(2,1)S(1)} %copy-done.64), channel_id=1, source_target_pairs={{0,2},{1,3},{2,0},{3,1},{4,6},{5,7},{6,4},{7,5},{8,10},{9,11},{10,... | collective-permute-start | bytes 884744 | tf_op jit(solution)/shard_map/ppermute | solution.py:873
  405.1 9.9 %collective-permute-start.81 = (bf16[128,1152]{1,0:T(8,128)(2,1)S(1)}, bf16[128,1152]{1,0:T(8,128)(2,1)S(1)}, u32[]{:S(2)}, u32[]{:S(2)}) collective-permute-start(bf16[128,1152]{1,0:T(8,128)(2,1)S(1)} %copy-done.62), channel_id=1, source_target_pairs={{0,2},{1,3},{2,0},{3,1},{4,6},{5,7},{6,4},{7,5},{8,10},{9,11},{10,... | collective-permute-start | bytes 884744 | tf_op jit(solution)/shard_map/ppermute | solution.py:873
  407.7 16.6 %collective-permute-start.83 = (bf16[128,1152]{1,0:T(8,128)(2,1)S(1)}, bf16[128,1152]{1,0:T(8,128)(2,1)S(1)}, u32[]{:S(2)}, u32[]{:S(2)}) collective-permute-start(bf16[128,1152]{1,0:T(8,128)(2,1)S(1)} %copy-done.58), channel_id=1, source_target_pairs={{0,2},{1,3},{2,0},{3,1},{4,6},{5,7},{6,4},{7,5},{8,10},{9,11},{10,... | collective-permute-start | bytes 884744 | tf_op jit(solution)/shard_map/ppermute | solution.py:873
  408.4 13.6 %collective-permute-start.82 = (bf16[64,1152]{1,0:T(8,128)(2,1)S(1)}, bf16[64,1152]{1,0:T(8,128)(2,1)S(1)}, u32[]{:S(2)}, u32[]{:S(2)}) collective-permute-start(bf16[64,1152]{1,0:T(8,128)(2,1)S(1)} %get-tuple-element.726.refs_0_), channel_id=1, source_target_pairs={{0,2},{1,3},{2,0},{3,1},{4,6},{5,7},{6,4},{7,5},{8,10},{9,11},{10,... | collective-permute-start | bytes 442376 | tf_op jit(solution)/shard_map/ppermute | solution.py:873
  415.0 24.8 %collective-permute-start.87 = (bf16[1,144,1152]{2,1,0:T(8,128)(2,1)S(1)}, bf16[1,144,1152]{2,1,0:T(8,128)(2,1)S(1)}, u32[]{:S(2)}, u32[]{:S(2)}) collective-permute-start(bf16[1,144,1152]{2,1,0:T(8,128)(2,1)S(1)} %get-tuple-element.761), channel_id=1, source_target_pairs={{0,16},{4,20},{8,24},{12,28},{16,0},{20,4},{24,8},{28,12},{1,17},{... | collective-permute-start | bytes 995336 | tf_op jit(solution)/shard_map/ppermute | solution.py:876
  422.0 22.1 %collective-permute-start.86 = (bf16[1,144,1152]{2,1,0:T(8,128)(2,1)S(1)}, bf16[1,144,1152]{2,1,0:T(8,128)(2,1)S(1)}, u32[]{:S(2)}, u32[]{:S(2)}) collective-permute-start(bf16[1,144,1152]{2,1,0:T(8,128)(2,1)S(1)} %get-tuple-element.759), channel_id=1, source_target_pairs={{0,16},{4,20},{8,24},{12,28},{16,0},{20,4},{24,8},{28,12},{1,17},{... | collective-permute-start | bytes 995336 | tf_op jit(solution)/shard_map/ppermute | solution.py:876
  427.4 21.6 %collective-permute-start.88 = (f32[32,1152]{1,0:T(8,128)S(1)}, f32[32,1152]{1,0:T(8,128)S(1)}, u32[]{:S(2)}, u32[]{:S(2)}) collective-permute-start(f32[32,1152]{1,0:T(8,128)S(1)} %get-tuple-element.767.refs_1_), channel_id=1, source_target_pairs={{0,1},{1,0},{2,3},{3,2},{4,5},{5,4},{6,7},{7,6},{8,9},{9,8},{10,11... | collective-permute-start | bytes 442376 | tf_op jit(solution)/shard_map/ppermute | solution.py:870
  456.1 19.4 %collective-permute-start.92 = (bf16[2,144,1152]{2,1,0:T(8,128)(2,1)S(1)}, bf16[2,144,1152]{2,1,0:T(8,128)(2,1)S(1)}, u32[]{:S(2)}, u32[]{:S(2)}) collective-permute-start(bf16[2,144,1152]{2,1,0:T(8,128)(2,1)S(1)} %get-tuple-element.774), channel_id=1, source_target_pairs={{0,8},{4,12},{8,0},{12,4},{16,24},{20,28},{24,16},{28,20},{1,9},{5... | collective-permute-start | bytes 1990664 | tf_op jit(solution)/shard_map/ppermute | solution.py:876
  463.8 23.1 %collective-permute-start.93 = (bf16[128,1152]{1,0:T(8,128)(2,1)}, bf16[128,1152]{1,0:T(8,128)(2,1)}, u32[]{:S(2)}, u32[]{:S(2)}) collective-permute-start(bf16[128,1152]{1,0:T(8,128)(2,1)} %get-tuple-element.781.refs_2_), channel_id=1, source_target_pairs={{0,1},{1,0},{2,3},{3,2},{4,5},{5,4},{6,7},{7,6},{8,9},{9,8},{10,11... | collective-permute-start | bytes 884744 | tf_op jit(solution)/shard_map/ppermute | solution.py:870
  463.8 25.5 %collective-permute-start.94 = (bf16[320,1152]{1,0:T(8,128)(2,1)S(1)}, bf16[320,1152]{1,0:T(8,128)(2,1)S(1)}, u32[]{:S(2)}, u32[]{:S(2)}) collective-permute-start(bf16[320,1152]{1,0:T(8,128)(2,1)S(1)} %get-tuple-element.784.refs_2_), channel_id=1, source_target_pairs={{0,1},{1,0},{2,3},{3,2},{4,5},{5,4},{6,7},{7,6},{8,9},{9,8},{10,11... | collective-permute-start | bytes 2211848 | tf_op jit(solution)/shard_map/ppermute | solution.py:870
  464.3 37.0 %collective-permute-start.98 = (bf16[1,144,1152]{2,1,0:T(8,128)(2,1)S(1)}, bf16[1,144,1152]{2,1,0:T(8,128)(2,1)}, u32[]{:S(2)}, u32[]{:S(2)}) collective-permute-start(bf16[1,144,1152]{2,1,0:T(8,128)(2,1)S(1)} %get-tuple-element.791), channel_id=1, source_target_pairs={{0,16},{4,20},{8,24},{12,28},{16,0},{20,4},{24,8},{28,12},{1,17},{... | collective-permute-start | bytes 995336 | tf_op jit(solution)/shard_map/ppermute | solution.py:876
  477.5 28.1 %collective-permute-start.99 = (bf16[1,144,1152]{2,1,0:T(8,128)(2,1)S(1)}, bf16[1,144,1152]{2,1,0:T(8,128)(2,1)S(1)}, u32[]{:S(2)}, u32[]{:S(2)}) collective-permute-start(bf16[1,144,1152]{2,1,0:T(8,128)(2,1)S(1)} %get-tuple-element.794), channel_id=1, source_target_pairs={{0,16},{4,20},{8,24},{12,28},{16,0},{20,4},{24,8},{28,12},{1,17},{... | collective-permute-start | bytes 995336 | tf_op jit(solution)/shard_map/ppermute | solution.py:876
  482.9 13.9 %collective-permute-start.95 = (bf16[4,2,1152]{2,1,0:T(2,128)(2,1)S(1)}, bf16[4,2,1152]{2,1,0:T(2,128)(2,1)S(1)}, u32[]{:S(2)}, u32[]{:S(2)}) collective-permute-start(bf16[4,2,1152]{2,1,0:T(2,128)(2,1)S(1)} %convert_element_type.153), channel_id=1, source_target_pairs={{0,16},{4,20},{8,24},{12,28},{16,0},{20,4},{24,8},{28,12},{1,17},{... | collective-permute-start | bytes 55304 | tf_op jit(solution)/shard_map/ppermute | solution.py:876
  (250 other events, 2033.0 us)
Sparse Core Ops, SparseCore 0:
  218.6 103.8 reduce-scatter.1

commit v6 on v5

--- a/solution.py
+++ b/solution.py
@@ -39,7 +39,7 @@
 
 COSTS = {
     "gather_rows": 0.8, "ln_open": 0.4, "near_sum": 0.4, "merge_attn": 0.6, "merge_mlp": 0.6,
-    "finish": 1.0, "first_grad": 0.5, "qkv_forward": 1.2, "qkv_backward": 1.2, "mlp_forward": 3.5,
+    "finish": 1.0, "first_grad": 0.5, "qkv_forward": 1.2, "qkv_backward": 0.0, "mlp_forward": 3.5,
     "mlp_backward": 3.0, "ln_back": 1.2, "attn_forward": 0.0, "attn_backward": 0.0,
     "weight_grads": 6.5, "halve": 1.5, "place_rows": 3.0, "table_rows": 1.0,
 }

time: 524 us -> 534 us (1.019)
  waiting for transfers between devices: 168 us -> 179 us
    ppermute x24, waiting for transfers between devices: 69.3 us -> 80.4 us  [dp_move(): return lax.ppermute(value, 'dp', partners(self.dp_size, bit))]
  transfers between devices with their start and end apart: 101 -> 101, of which waited for: 48 -> 47; matrix products, arithmetic and copies ran while one was open for 2% -> 2% of each run, Pallas kernels for 35% -> 35%
where the time goes in v6:
time: 534 us; the launch traced here: 524 us
  Pallas kernels  205 us (38%)
  waiting for transfers between devices  179 us (34%)
  starting transfers between devices  68.3 us (13%)
  local copies, waits for them, and re-layouts  43 us (8%)
  between operations  17.2 us (3%)
  matrix products  8.57 us (2%)
    pallas_call x120, Pallas kernels, call(): pl.pallas_call(whole, in_specs=[fast] + [small] * len(scalars) + [slow] *...  205 us
    ppermute x24, waiting for transfers between devices, cross(): return lax.ppermute(value, 'tensor', partners(self.tensor_size, 2))  85.5 us
    ppermute x24, waiting for transfers between devices, dp_move(): return lax.ppermute(value, 'dp', partners(self.dp_size, bit))  80.4 us
    unnamed x395, local copies, waits for them, and re-layouts  36.9 us
    ppermute x24, starting transfers between devices, dp_move(): return lax.ppermute(value, 'dp', partners(self.dp_size, bit))  33.8 us
    ppermute x24, starting transfers between devices, cross(): return lax.ppermute(value, 'tensor', partners(self.tensor_size, 2))  23.4 us
    ppermute x52, waiting for transfers between devices, swap(): return lax.ppermute(value, 'tensor', partners(self.tensor_size, 1))  13.5 us
    ppermute x52, starting transfers between devices, swap(): return lax.ppermute(value, 'tensor', partners(self.tensor_size, 1))  11.1 us
  transfers between devices with their start and end apart: 101, of which 47 were waited for; matrix products, arithmetic and copies ran while one was open for 2% of the time, Pallas kernels for 35%

profile of v6, /device:TPU:0, one launch (start us, length us, event | category | flops | bytes accessed | tf_op | source)
XLA Modules:
  0.0 524.0 jit_solution(15037925432864626874)
XLA Ops:
  8.0 3.0 collective-permute-start
  16.5 3.1 collective-permute-start.2
  22.8 3.4 fusion
  28.1 3.1 collective-permute-done.3
  45.2 3.7 attn_forward.6
  49.1 3.7 attn_forward.7
  61.1 7.8 %collective-permute-done.12.refs_2_.refs_7_ = bf16[128,1152]{1,0:T(8,128)(2,1)S(1)} collective-permute-done((bf16[128,1152]{1,0:T(8,128)(2,1)S(1)}, bf16[128,1152]{1,0:T(8,128)(2,1)S(1)}, u32[]{:S(2)}, u32[]{:S(2)}) %collective-permute-start.12) | collective-permute-done | bytes 294944 | tf_op jit(solution)/shard_map/ppermute | solution.py:873
  75.7 3.5 collective-permute-done.15.refs_2_.refs_7_
  97.5 5.6 %collective-permute-done.23.refs_8_.refs_9_ = bf16[128,1152]{1,0:T(8,128)(2,1)S(1)} collective-permute-done((bf16[128,1152]{1,0:T(8,128)(2,1)S(1)}, bf16[128,1152]{1,0:T(8,128)(2,1)S(1)}, u32[]{:S(2)}, u32[]{:S(2)}) %collective-permute-start.23) | collective-permute-done | bytes 294944 | tf_op jit(solution)/shard_map/ppermute | solution.py:873
  105.5 4.7 collective-permute-done.24.refs_5_.refs_7_
  112.0 5.9 %attn_forward.9 = (f32[4,2,1,256]{3,2,1,0:T(1,128)S(1)}, bf16[256,1152]{1,0:T(8,128)(2,1)S(1)}, bf16[256,1152]{1,0:T(8,128)(2,1)S(1)}, bf16[512,288]{1,0:T(8,128)(2,1)}, f32[8,128]{1,0:T(8,128)S(1)}) custom-call(f32[8,128]{1,0:T(8,128)S(1)} %get-tuple-element.497.token_ref, bf16[2,256,864]{2,1,0:T(8,128)(2,1)S(1)} %get-tuple-element.498.refs_0_.refs_1_, ...), custom_call_target="tpu_custom_call" | custom-call | bytes 1000 | tf_op jit(solution)/shard_map/attn_forward/pallas_call | solution.py:68
  121.5 6.1 %attn_forward.10 = (f32[4,2,1,256]{3,2,1,0:T(1,128)S(1)}, bf16[256,1152]{1,0:T(8,128)(2,1)S(1)}, bf16[256,1152]{1,0:T(8,128)(2,1)S(1)}, bf16[512,288]{1,0:T(8,128)(2,1)}, f32[8,128]{1,0:T(8,128)S(1)}) custom-call(f32[8,128]{1,0:T(8,128)S(1)} %get-tuple-element.505.token_ref, bf16[2,256,864]{2,1,0:T(8,128)(2,1)S(1)} %get-tuple-element.499.refs_2_.refs_0_.refs_1_, ...), custom_call_target="tpu_custom_call" | custom-call | bytes 1000 | tf_op jit(solution)/shard_map/attn_forward/pallas_call | solution.py:68
  133.9 9.4 %collective-permute-done.30.refs_2_.refs_7_ = bf16[256,1152]{1,0:T(8,128)(2,1)S(1)} collective-permute-done((bf16[256,1152]{1,0:T(8,128)(2,1)S(1)}, bf16[256,1152]{1,0:T(8,128)(2,1)S(1)}, u32[]{:S(2)}, u32[]{:S(2)}) %collective-permute-start.30) | collective-permute-done | bytes 589856 | tf_op jit(solution)/shard_map/ppermute | solution.py:873
  146.0 4.5 mlp_forward.9
  150.5 9.3 %collective-permute-done.32.refs_2_.refs_7_ = bf16[256,1152]{1,0:T(8,128)(2,1)S(1)} collective-permute-done((bf16[256,1152]{1,0:T(8,128)(2,1)S(1)}, bf16[256,1152]{1,0:T(8,128)(2,1)S(1)}, u32[]{:S(2)}, u32[]{:S(2)}) %collective-permute-start.32) | collective-permute-done | bytes 589856 | tf_op jit(solution)/shard_map/ppermute | solution.py:873
  160.5 3.6 mlp_backward.6
  166.2 4.9 mlp_forward.10
  171.3 3.6 mlp_backward.7
  185.0 7.9 %collective-permute-done.42.refs_1_ = bf16[256,1152]{1,0:T(8,128)(2,1)S(1)} collective-permute-done((bf16[256,1152]{1,0:T(8,128)(2,1)S(1)}, bf16[256,1152]{1,0:T(8,128)(2,1)S(1)}, u32[]{:S(2)}, u32[]{:S(2)}) %collective-permute-start.42) | collective-permute-done | bytes 589856 | tf_op jit(solution)/shard_map/ppermute | solution.py:873
  196.8 14.9 %weight_grads.4 = (f32[8,2304]{1,0:T(8,128)S(1)}, bf16[8,144,2304]{2,1,0:T(8,128)(2,1)}, f32[8,128]{1,0:T(8,128)S(1)}) custom-call(f32[8,128]{1,0:T(8,128)S(1)} %get-tuple-element.549.token_ref, bf16[512,1152]{1,0:T(8,128)(2,1)} %get-tuple-element.550.refs_0_, bf16[512,1152]{1,0:T(8,128)(2,1)} %get-tuple-element.551.refs_1_, ...), custom_call_target="tpu_custom_call" | custom-call | flops 7474999808 | bytes 1000 | tf_op jit(solution)/shard_map/weight_grads/pallas_call | solution.py:68
  218.5 22.2 %attn_backward.4 = (bf16[2,256,864]{2,1,0:T(8,128)(2,1)S(1)}, bf16[2,256,864]{2,1,0:T(8,128)(2,1)S(1)}, bf16[512,1152]{1,0:T(8,128)(2,1)}, bf16[512,1152]{1,0:T(...) custom-call(f32[8,128]{1,0:T(8,128)S(1)} %get-tuple-element.571.token_ref, ...), custom_call_target="tpu_custom_call" | custom-call | bytes 1000 | tf_op jit(solution)/shard_map/attn_backward/pallas_call | solution.py:68
  240.7 4.0 collective-permute-done.48.refs_4_
  244.8 3.5 finish.2
  253.7 7.7 %collective-permute-done.52.refs_1_ = bf16[128,1152]{1,0:T(8,128)(2,1)S(1)} collective-permute-done((bf16[128,1152]{1,0:T(8,128)(2,1)S(1)}, bf16[128,1152]{1,0:T(8,128)(2,1)S(1)}, u32[]{:S(2)}, u32[]{:S(2)}) %collective-permute-start.52) | collective-permute-done | bytes 294944 | tf_op jit(solution)/shard_map/ppermute | solution.py:873
  263.8 3.8 attn_backward.5
  271.0 4.5 place_rows.4
  275.5 8.8 %collective-permute-done.56.refs_1_ = bf16[256,1152]{1,0:T(8,128)(2,1)S(1)} collective-permute-done((bf16[256,1152]{1,0:T(8,128)(2,1)S(1)}, bf16[256,1152]{1,0:T(8,128)(2,1)S(1)}, u32[]{:S(2)}, u32[]{:S(2)}) %collective-permute-start.56) | collective-permute-done | bytes 589856 | tf_op jit(solution)/shard_map/ppermute | solution.py:873
  287.6 2.9 mlp_backward.9
  301.5 8.8 %weight_grads.5 = (bf16[4,144,1152]{2,1,0:T(8,128)(2,1)S(1)}, bf16[4,144,1152]{2,1,0:T(8,128)(2,1)}, f32[8,1152]{1,0:T(8,128)S(1)}, f32[8,128]{1,0:T(8,128)S(1)}) custom-call(f32[8,128]{1,0:T(8,128)S(1)} %get-tuple-element.618.token_ref, s32[1]{0:T(128)} %bitcast.24.refs_0_, bf16[512,1152]{1,0:T(8,128)(2,1)} %get-tuple-element.619.refs_1_, ...), custom_call_target="tpu_custom_call" | custom-call | flops 7474999808 | bytes 1000 | tf_op jit(solution)/shard_map/weight_grads/pallas_call | solution.py:68
  312.0 4.4 collective-permute-done.62.refs_1_
  337.2 7.7 %weight_grads.6 = (bf16[4,144,1152]{2,1,0:T(8,128)(2,1)S(1)}, bf16[4,144,1152]{2,1,0:T(8,128)(2,1)S(1)}, bf16[4,144,1152]{2,1,0:T(8,128)(2,1)S(1)}, bf16[4,144,1...) custom-call(f32[8,128]{1,0:T(8,128)S(1)} %get-tuple-element.646.token_ref, s32[1]{0:T(128)} %bitcast.24.refs_0_, ...), custom_call_target="tpu_custom_call" | custom-call | flops 7474999808 | bytes 1000 | tf_op jit(solution)/shard_map/weight_grads/pallas_call | solution.py:68
  348.7 11.4 %collective-permute-done.66.refs_2_ = bf16[4,144,1152]{2,1,0:T(8,128)(2,1)} collective-permute-done((bf16[4,144,1152]{2,1,0:T(8,128)(2,1)}, bf16[4,144,1152]{2,1,0:T(8,128)(2,1)}, u32[]{:S(2)}, u32[]{:S(2)}) %collective-permute-start.66) | collective-permute-done | bytes 1327136 | tf_op jit(solution)/shard_map/ppermute | solution.py:876
  365.4 8.6 %attn_backward.6 = (bf16[2,128,864]{2,1,0:T(8,128)(2,1)S(1)}, bf16[2,128,864]{2,1,0:T(8,128)(2,1)S(1)}, bf16[256,1152]{1,0:T(8,128)(2,1)}, bf16[256,1152]{1,0:T(...) custom-call(f32[8,128]{1,0:T(8,128)S(1)} %get-tuple-element.668.token_ref, ...), custom_call_target="tpu_custom_call" | custom-call | bytes 1000 | tf_op jit(solution)/shard_map/attn_backward/pallas_call | solution.py:68
  378.7 9.2 %collective-permute-done.73.refs_2_ = bf16[4,144,1152]{2,1,0:T(8,128)(2,1)S(1)} collective-permute-done((bf16[4,144,1152]{2,1,0:T(8,128)(2,1)S(1)}, bf16[4,144,1152]{2,1,0:T(8,128)(2,1)S(1)}, u32[]{:S(2)}, u32[]{:S(2)}) %collective-permute-start.73) | collective-permute-done | bytes 1327136 | tf_op jit(solution)/shard_map/ppermute | solution.py:876
  393.0 3.2 attn_backward.7
  400.4 5.1 weight_grads.7
  407.6 7.5 %collective-permute-done.78.refs_2_ = bf16[2,144,1152]{2,1,0:T(8,128)(2,1)S(1)} collective-permute-done((bf16[2,144,1152]{2,1,0:T(8,128)(2,1)S(1)}, bf16[2,144,1152]{2,1,0:T(8,128)(2,1)S(1)}, u32[]{:S(2)}, u32[]{:S(2)}) %collective-permute-start.78) | collective-permute-done | bytes 663584 | tf_op jit(solution)/shard_map/ppermute | solution.py:876
  419.9 5.2 collective-permute-done.81.refs_1_
  427.6 4.3 collective-permute-done.82.refs_1_
  437.4 6.5 %collective-permute-done.85.refs_2_ = bf16[4,144,1152]{2,1,0:T(8,128)(2,1)S(1)} collective-permute-done((bf16[4,144,1152]{2,1,0:T(8,128)(2,1)S(1)}, bf16[4,144,1152]{2,1,0:T(8,128)(2,1)S(1)}, u32[]{:S(2)}, u32[]{:S(2)}) %collective-permute-start.85) | collective-permute-done | bytes 1327136 | tf_op jit(solution)/shard_map/ppermute | solution.py:876
  445.1 4.7 collective-permute-done.87.refs_3_
  449.8 4.3 collective-permute-done.86.refs_1_
  459.5 5.9 %collective-permute-done.89 = f32[23040]{0:T(1024)S(1)} collective-permute-done((f32[23040]{0:T(1024)S(1)}, f32[23040]{0:T(1024)S(1)}, u32[]{:S(2)}, u32[]{:S(2)}) %collective-permute-start.89) | collective-permute-done | bytes 92192 | tf_op jit(solution)/shard_map/ppermute | solution.py:876
  467.9 3.6 collective-permute-done.90
  476.9 8.6 %collective-permute-done.92.refs_2_ = bf16[2,144,1152]{2,1,0:T(8,128)(2,1)S(1)} collective-permute-done((bf16[2,144,1152]{2,1,0:T(8,128)(2,1)S(1)}, bf16[2,144,1152]{2,1,0:T(8,128)(2,1)S(1)}, u32[]{:S(2)}, u32[]{:S(2)}) %collective-permute-start.92) | collective-permute-done | bytes 663584 | tf_op jit(solution)/shard_map/ppermute | solution.py:876
  487.9 4.5 convolution_bitcast_fusion
  499.2 2.9 place_rows.6
  502.1 4.4 collective-permute-done.95
  (751 shorter events, 216.8 us)
Async XLA Ops:
  7.2 447.9 %reduce-scatter.2.cloned.1.call-start = ((), (), s32[]{:S(2)}) async-start(), calls=%async_computation.1 | async-start | bytes 5971968 | tf_op jit(solution)/shard_map/reduce_scatter | solution.py:972
  59.4 11.5 %collective-permute-start.13 = (bf16[256,1152]{1,0:T(8,128)(2,1)S(1)}, bf16[256,1152]{1,0:T(8,128)(2,1)S(1)}, u32[]{:S(2)}, u32[]{:S(2)}) collective-permute-start(bf16[256,1152]{1,0:T(8,128)(2,1)S(1)} %get-tuple-element.449.refs_0_), channel_id=1, source_target_pairs={{0,1},{1,0},{2,3},{3,2},{4,5},{5,4},{6,7},{7,6},{8,9},{9,8},{10,11... | collective-permute-start | bytes 1769480 | tf_op jit(solution)/shard_map/ppermute | solution.py:870
  59.6 9.3 %collective-permute-start.12 = (bf16[128,1152]{1,0:T(8,128)(2,1)S(1)}, bf16[128,1152]{1,0:T(8,128)(2,1)S(1)}, u32[]{:S(2)}, u32[]{:S(2)}) collective-permute-start(bf16[128,1152]{1,0:T(8,128)(2,1)S(1)} %get-tuple-element.447.refs_1_.refs_6_), channel_id=1, source_target_pairs={{0,2},{1,3},{2,0},{3,1},{4,6},{5,7},{6,4},{7,5},{8,10},{9,11},{10,... | collective-permute-start | bytes 884744 | tf_op jit(solution)/shard_map/ppermute | solution.py:873
  69.3 9.9 %collective-permute-start.15 = (bf16[128,1152]{1,0:T(8,128)(2,1)S(1)}, bf16[128,1152]{1,0:T(8,128)(2,1)S(1)}, u32[]{:S(2)}, u32[]{:S(2)}) collective-permute-start(bf16[128,1152]{1,0:T(8,128)(2,1)S(1)} %get-tuple-element.453.refs_1_.refs_6_), channel_id=1, source_target_pairs={{0,2},{1,3},{2,0},{3,1},{4,6},{5,7},{6,4},{7,5},{8,10},{9,11},{10,... | collective-permute-start | bytes 884744 | tf_op jit(solution)/shard_map/ppermute | solution.py:873
  75.2 6.7 %collective-permute-start.17 = (bf16[64,1152]{1,0:T(8,128)(2,1)S(1)}, bf16[64,1152]{1,0:T(8,128)(2,1)S(1)}, u32[]{:S(2)}, u32[]{:S(2)}) collective-permute-start(bf16[64,1152]{1,0:T(8,128)(2,1)S(1)} %get-tuple-element.458.refs_1_.refs_6_), channel_id=1, source_target_pairs={{0,2},{1,3},{2,0},{3,1},{4,6},{5,7},{6,4},{7,5},{8,10},{9,11},{10,... | collective-permute-start | bytes 442376 | tf_op jit(solution)/shard_map/ppermute | solution.py:873
  87.7 9.8 %collective-permute-start.22 = (bf16[128,1152]{1,0:T(8,128)(2,1)S(1)}, bf16[128,1152]{1,0:T(8,128)(2,1)S(1)}, u32[]{:S(2)}, u32[]{:S(2)}) collective-permute-start(bf16[128,1152]{1,0:T(8,128)(2,1)S(1)} %get-tuple-element.487.refs_4_.refs_6_), channel_id=1, source_target_pairs={{0,2},{1,3},{2,0},{3,1},{4,6},{5,7},{6,4},{7,5},{8,10},{9,11},{10,... | collective-permute-start | bytes 884744 | tf_op jit(solution)/shard_map/ppermute | solution.py:873
  89.2 13.9 %collective-permute-start.23 = (bf16[128,1152]{1,0:T(8,128)(2,1)S(1)}, bf16[128,1152]{1,0:T(8,128)(2,1)S(1)}, u32[]{:S(2)}, u32[]{:S(2)}) collective-permute-start(bf16[128,1152]{1,0:T(8,128)(2,1)S(1)} %get-tuple-element.489.refs_7_.refs_8_), channel_id=1, source_target_pairs={{0,2},{1,3},{2,0},{3,1},{4,6},{5,7},{6,4},{7,5},{8,10},{9,11},{10,... | collective-permute-start | bytes 884744 | tf_op jit(solution)/shard_map/ppermute | solution.py:873
  127.8 15.6 %collective-permute-start.30 = (bf16[256,1152]{1,0:T(8,128)(2,1)S(1)}, bf16[256,1152]{1,0:T(8,128)(2,1)S(1)}, u32[]{:S(2)}, u32[]{:S(2)}) collective-permute-start(bf16[256,1152]{1,0:T(8,128)(2,1)S(1)} %get-tuple-element.516.refs_1_.refs_6_), channel_id=1, source_target_pairs={{0,2},{1,3},{2,0},{3,1},{4,6},{5,7},{6,4},{7,5},{8,10},{9,11},{10,... | collective-permute-start | bytes 1769480 | tf_op jit(solution)/shard_map/ppermute | solution.py:873
  144.0 15.7 %collective-permute-start.32 = (bf16[256,1152]{1,0:T(8,128)(2,1)S(1)}, bf16[256,1152]{1,0:T(8,128)(2,1)S(1)}, u32[]{:S(2)}, u32[]{:S(2)}) collective-permute-start(bf16[256,1152]{1,0:T(8,128)(2,1)S(1)} %get-tuple-element.520.refs_1_.refs_6_), channel_id=1, source_target_pairs={{0,2},{1,3},{2,0},{3,1},{4,6},{5,7},{6,4},{7,5},{8,10},{9,11},{10,... | collective-permute-start | bytes 1769480 | tf_op jit(solution)/shard_map/ppermute | solution.py:873
  145.6 14.9 %collective-permute-start.33 = (bf16[256,1152]{1,0:T(8,128)(2,1)S(1)}, bf16[256,1152]{1,0:T(8,128)(2,1)S(1)}, u32[]{:S(2)}, u32[]{:S(2)}) collective-permute-start(bf16[256,1152]{1,0:T(8,128)(2,1)S(1)} %get-tuple-element.522.refs_0_), channel_id=1, source_target_pairs={{0,1},{1,0},{2,3},{3,2},{4,5},{5,4},{6,7},{7,6},{8,9},{9,8},{10,11... | collective-permute-start | bytes 1769480 | tf_op jit(solution)/shard_map/ppermute | solution.py:870
  164.1 7.1 %collective-permute-start.35 = (bf16[256,1152]{1,0:T(8,128)(2,1)S(1)}, bf16[256,1152]{1,0:T(8,128)(2,1)S(1)}, u32[]{:S(2)}, u32[]{:S(2)}) collective-permute-start(bf16[256,1152]{1,0:T(8,128)(2,1)S(1)} %get-tuple-element.528), channel_id=1, source_target_pairs={{0,1},{1,0},{2,3},{3,2},{4,5},{5,4},{6,7},{7,6},{8,9},{9,8},{10,11... | collective-permute-start | bytes 1769480 | tf_op jit(solution)/shard_map/ppermute | solution.py:870
  164.7 10.4 %collective-permute-start.37 = (bf16[128,1152]{1,0:T(8,128)(2,1)S(1)}, bf16[128,1152]{1,0:T(8,128)(2,1)S(1)}, u32[]{:S(2)}, u32[]{:S(2)}) collective-permute-start(bf16[128,1152]{1,0:T(8,128)(2,1)S(1)} %get-tuple-element.534.refs_1_.refs_6_), channel_id=1, source_target_pairs={{0,2},{1,3},{2,0},{3,1},{4,6},{5,7},{6,4},{7,5},{8,10},{9,11},{10,... | collective-permute-start | bytes 884744 | tf_op jit(solution)/shard_map/ppermute | solution.py:873
  176.8 16.1 %collective-permute-start.42 = (bf16[256,1152]{1,0:T(8,128)(2,1)S(1)}, bf16[256,1152]{1,0:T(8,128)(2,1)S(1)}, u32[]{:S(2)}, u32[]{:S(2)}) collective-permute-start(bf16[256,1152]{1,0:T(8,128)(2,1)S(1)} %get-tuple-element.547.refs_0_), channel_id=1, source_target_pairs={{0,2},{1,3},{2,0},{3,1},{4,6},{5,7},{6,4},{7,5},{8,10},{9,11},{10,... | collective-permute-start | bytes 1769480 | tf_op jit(solution)/shard_map/ppermute | solution.py:873
  183.6 30.9 %collective-permute-start.44 = (bf16[256,1152]{1,0:T(8,128)(2,1)S(1)}, bf16[256,1152]{1,0:T(8,128)(2,1)S(1)}, u32[]{:S(2)}, u32[]{:S(2)}) collective-permute-start(bf16[256,1152]{1,0:T(8,128)(2,1)S(1)} %get-tuple-element.567), channel_id=1, source_target_pairs={{0,1},{1,0},{2,3},{3,2},{4,5},{5,4},{6,7},{7,6},{8,9},{9,8},{10,11... | collective-permute-start | bytes 1769480 | tf_op jit(solution)/shard_map/ppermute | solution.py:870
  183.7 31.7 %collective-permute-start.45 = (bf16[256,1152]{1,0:T(8,128)(2,1)S(1)}, bf16[256,1152]{1,0:T(8,128)(2,1)S(1)}, u32[]{:S(2)}, u32[]{:S(2)}) collective-permute-start(bf16[256,1152]{1,0:T(8,128)(2,1)S(1)} %get-tuple-element.570), channel_id=1, source_target_pairs={{0,1},{1,0},{2,3},{3,2},{4,5},{5,4},{6,7},{7,6},{8,9},{9,8},{10,11... | collective-permute-start | bytes 1769480 | tf_op jit(solution)/shard_map/ppermute | solution.py:870
  184.1 27.7 %collective-permute-start.43 = (bf16[256,1152]{1,0:T(8,128)(2,1)S(1)}, bf16[256,1152]{1,0:T(8,128)(2,1)S(1)}, u32[]{:S(2)}, u32[]{:S(2)}) collective-permute-start(bf16[256,1152]{1,0:T(8,128)(2,1)S(1)} %get-tuple-element.563.refs_0_), channel_id=1, source_target_pairs={{0,2},{1,3},{2,0},{3,1},{4,6},{5,7},{6,4},{7,5},{8,10},{9,11},{10,... | collective-permute-start | bytes 1769480 | tf_op jit(solution)/shard_map/ppermute | solution.py:873
  196.8 21.7 %collective-permute-start.46 = (bf16[256,1152]{1,0:T(8,128)(2,1)}, bf16[256,1152]{1,0:T(8,128)(2,1)}, u32[]{:S(2)}, u32[]{:S(2)}) collective-permute-start(bf16[256,1152]{1,0:T(8,128)(2,1)} %get-tuple-element.574.refs_4_), channel_id=1, source_target_pairs={{0,1},{1,0},{2,3},{3,2},{4,5},{5,4},{6,7},{7,6},{8,9},{9,8},{10,11... | collective-permute-start | bytes 1769480 | tf_op jit(solution)/shard_map/ppermute | solution.py:870
  216.4 24.3 %collective-permute-start.49 = (bf16[256,1152]{1,0:T(8,128)(2,1)}, bf16[256,1152]{1,0:T(8,128)(2,1)}, u32[]{:S(2)}, u32[]{:S(2)}) collective-permute-start(bf16[256,1152]{1,0:T(8,128)(2,1)} %get-tuple-element.578.refs_7_), channel_id=1, source_target_pairs={{0,2},{1,3},{2,0},{3,1},{4,6},{5,7},{6,4},{7,5},{8,10},{9,11},{10,... | collective-permute-start | bytes 1769480 | tf_op jit(solution)/shard_map/ppermute | solution.py:873
  216.9 27.8 %collective-permute-start.48 = (bf16[256,1152]{1,0:T(8,128)(2,1)}, bf16[256,1152]{1,0:T(8,128)(2,1)}, u32[]{:S(2)}, u32[]{:S(2)}) collective-permute-start(bf16[256,1152]{1,0:T(8,128)(2,1)} %get-tuple-element.577.refs_3_), channel_id=1, source_target_pairs={{0,2},{1,3},{2,0},{3,1},{4,6},{5,7},{6,4},{7,5},{8,10},{9,11},{10,... | collective-permute-start | bytes 1769480 | tf_op jit(solution)/shard_map/ppermute | solution.py:873
  251.9 19.1 %collective-permute-start.55 = (bf16[512,1152]{1,0:T(8,128)(2,1)S(1)}, bf16[512,1152]{1,0:T(8,128)(2,1)S(1)}, u32[]{:S(2)}, u32[]{:S(2)}) collective-permute-start(bf16[512,1152]{1,0:T(8,128)(2,1)S(1)} %get-tuple-element.601.refs_2_), channel_id=1, source_target_pairs={{0,1},{1,0},{2,3},{3,2},{4,5},{5,4},{6,7},{7,6},{8,9},{9,8},{10,11... | collective-permute-start | bytes 3538952 | tf_op jit(solution)/shard_map/ppermute | solution.py:870
  252.0 9.4 %collective-permute-start.52 = (bf16[128,1152]{1,0:T(8,128)(2,1)S(1)}, bf16[128,1152]{1,0:T(8,128)(2,1)S(1)}, u32[]{:S(2)}, u32[]{:S(2)}) collective-permute-start(bf16[128,1152]{1,0:T(8,128)(2,1)S(1)} %copy-done.68), channel_id=1, source_target_pairs={{0,2},{1,3},{2,0},{3,1},{4,6},{5,7},{6,4},{7,5},{8,10},{9,11},{10,... | collective-permute-start | bytes 884744 | tf_op jit(solution)/shard_map/ppermute | solution.py:873
  268.7 15.6 %collective-permute-start.56 = (bf16[256,1152]{1,0:T(8,128)(2,1)S(1)}, bf16[256,1152]{1,0:T(8,128)(2,1)S(1)}, u32[]{:S(2)}, u32[]{:S(2)}) collective-permute-start(bf16[256,1152]{1,0:T(8,128)(2,1)S(1)} %get-tuple-element.604.refs_0_), channel_id=1, source_target_pairs={{0,2},{1,3},{2,0},{3,1},{4,6},{5,7},{6,4},{7,5},{8,10},{9,11},{10,... | collective-permute-start | bytes 1769480 | tf_op jit(solution)/shard_map/ppermute | solution.py:873
  294.8 16.2 %collective-permute-start.61 = (bf16[256,1152]{1,0:T(8,128)(2,1)S(1)}, bf16[256,1152]{1,0:T(8,128)(2,1)S(1)}, u32[]{:S(2)}, u32[]{:S(2)}) collective-permute-start(bf16[256,1152]{1,0:T(8,128)(2,1)S(1)} %get-tuple-element.632.refs_0_), channel_id=1, source_target_pairs={{0,2},{1,3},{2,0},{3,1},{4,6},{5,7},{6,4},{7,5},{8,10},{9,11},{10,... | collective-permute-start | bytes 1769480 | tf_op jit(solution)/shard_map/ppermute | solution.py:873
  295.2 21.2 %collective-permute-start.62 = (bf16[128,1152]{1,0:T(8,128)(2,1)S(1)}, bf16[128,1152]{1,0:T(8,128)(2,1)S(1)}, u32[]{:S(2)}, u32[]{:S(2)}) collective-permute-start(bf16[128,1152]{1,0:T(8,128)(2,1)S(1)} %copy-done.70), channel_id=1, source_target_pairs={{0,2},{1,3},{2,0},{3,1},{4,6},{5,7},{6,4},{7,5},{8,10},{9,11},{10,... | collective-permute-start | bytes 884744 | tf_op jit(solution)/shard_map/ppermute | solution.py:873
  318.0 13.3 %collective-permute-start.65 = (bf16[128,1152]{1,0:T(8,128)(2,1)}, bf16[128,1152]{1,0:T(8,128)(2,1)S(1)}, u32[]{:S(2)}, u32[]{:S(2)}) collective-permute-start(bf16[128,1152]{1,0:T(8,128)(2,1)} %get-tuple-element.644.refs_0_), channel_id=1, source_target_pairs={{0,2},{1,3},{2,0},{3,1},{4,6},{5,7},{6,4},{7,5},{8,10},{9,11},{10,... | collective-permute-start | bytes 884744 | tf_op jit(solution)/shard_map/ppermute | solution.py:873
  327.8 32.3 %collective-permute-start.66 = (bf16[4,144,1152]{2,1,0:T(8,128)(2,1)}, bf16[4,144,1152]{2,1,0:T(8,128)(2,1)}, u32[]{:S(2)}, u32[]{:S(2)}) collective-permute-start(bf16[4,144,1152]{2,1,0:T(8,128)(2,1)} %get-tuple-element.661), channel_id=1, source_target_pairs={{0,4},{4,0},{8,12},{12,8},{16,20},{20,16},{24,28},{28,24},{1,5},{5... | collective-permute-start | bytes 3981320 | tf_op jit(solution)/shard_map/ppermute | solution.py:876
  345.0 43.0 %collective-permute-start.73 = (bf16[4,144,1152]{2,1,0:T(8,128)(2,1)S(1)}, bf16[4,144,1152]{2,1,0:T(8,128)(2,1)S(1)}, u32[]{:S(2)}, u32[]{:S(2)}) collective-permute-start(bf16[4,144,1152]{2,1,0:T(8,128)(2,1)S(1)} %get-tuple-element.685), channel_id=1, source_target_pairs={{0,4},{4,0},{8,12},{12,8},{16,20},{20,16},{24,28},{28,24},{1,5},{5... | collective-permute-start | bytes 3981320 | tf_op jit(solution)/shard_map/ppermute | solution.py:876
  346.5 42.5 %collective-permute-start.74 = (bf16[4,144,1152]{2,1,0:T(8,128)(2,1)S(1)}, bf16[4,144,1152]{2,1,0:T(8,128)(2,1)S(1)}, u32[]{:S(2)}, u32[]{:S(2)}) collective-permute-start(bf16[4,144,1152]{2,1,0:T(8,128)(2,1)S(1)} %get-tuple-element.688), channel_id=1, source_target_pairs={{0,8},{4,12},{8,0},{12,4},{16,24},{20,28},{24,16},{28,20},{1,9},{5... | collective-permute-start | bytes 3981320 | tf_op jit(solution)/shard_map/ppermute | solution.py:876
  348.0 14.8 %collective-permute-start.67 = (bf16[128,1152]{1,0:T(8,128)(2,1)S(1)}, bf16[128,1152]{1,0:T(8,128)(2,1)S(1)}, u32[]{:S(2)}, u32[]{:S(2)}) collective-permute-start(bf16[128,1152]{1,0:T(8,128)(2,1)S(1)} %copy-done.66), channel_id=1, source_target_pairs={{0,2},{1,3},{2,0},{3,1},{4,6},{5,7},{6,4},{7,5},{8,10},{9,11},{10,... | collective-permute-start | bytes 884744 | tf_op jit(solution)/shard_map/ppermute | solution.py:873
  348.7 15.5 %collective-permute-start.68 = (bf16[128,1152]{1,0:T(8,128)(2,1)S(1)}, bf16[128,1152]{1,0:T(8,128)(2,1)S(1)}, u32[]{:S(2)}, u32[]{:S(2)}) collective-permute-start(bf16[128,1152]{1,0:T(8,128)(2,1)S(1)} %copy-done.54), channel_id=1, source_target_pairs={{0,1},{1,0},{2,3},{3,2},{4,5},{5,4},{6,7},{7,6},{8,9},{9,8},{10,11... | collective-permute-start | bytes 884744 | tf_op jit(solution)/shard_map/ppermute | solution.py:870
  376.4 13.5 %collective-permute-start.75 = (bf16[64,1152]{1,0:T(8,128)(2,1)S(1)}, bf16[64,1152]{1,0:T(8,128)(2,1)S(1)}, u32[]{:S(2)}, u32[]{:S(2)}) collective-permute-start(bf16[64,1152]{1,0:T(8,128)(2,1)S(1)} %get-tuple-element.690.refs_0_), channel_id=1, source_target_pairs={{0,2},{1,3},{2,0},{3,1},{4,6},{5,7},{6,4},{7,5},{8,10},{9,11},{10,... | collective-permute-start | bytes 442376 | tf_op jit(solution)/shard_map/ppermute | solution.py:873
  397.3 17.8 %collective-permute-start.78 = (bf16[2,144,1152]{2,1,0:T(8,128)(2,1)S(1)}, bf16[2,144,1152]{2,1,0:T(8,128)(2,1)S(1)}, u32[]{:S(2)}, u32[]{:S(2)}) collective-permute-start(bf16[2,144,1152]{2,1,0:T(8,128)(2,1)S(1)} %copy-done.42), channel_id=1, source_target_pairs={{0,8},{4,12},{8,0},{12,4},{16,24},{20,28},{24,16},{28,20},{1,9},{5... | collective-permute-start | bytes 1990664 | tf_op jit(solution)/shard_map/ppermute | solution.py:876
  398.8 17.8 %collective-permute-start.79 = (bf16[2,144,1152]{2,1,0:T(8,128)(2,1)S(1)}, bf16[2,144,1152]{2,1,0:T(8,128)(2,1)S(1)}, u32[]{:S(2)}, u32[]{:S(2)}) collective-permute-start(bf16[2,144,1152]{2,1,0:T(8,128)(2,1)S(1)} %get-tuple-element.718), channel_id=1, source_target_pairs={{0,4},{4,0},{8,12},{12,8},{16,20},{20,16},{24,28},{28,24},{1,5},{5... | collective-permute-start | bytes 1990664 | tf_op jit(solution)/shard_map/ppermute | solution.py:876
  405.5 38.4 %collective-permute-start.85 = (bf16[4,144,1152]{2,1,0:T(8,128)(2,1)S(1)}, bf16[4,144,1152]{2,1,0:T(8,128)(2,1)S(1)}, u32[]{:S(2)}, u32[]{:S(2)}) collective-permute-start(bf16[4,144,1152]{2,1,0:T(8,128)(2,1)S(1)} %get-tuple-element.756), channel_id=1, source_target_pairs={{0,4},{4,0},{8,12},{12,8},{16,20},{20,16},{24,28},{28,24},{1,5},{5... | collective-permute-start | bytes 3981320 | tf_op jit(solution)/shard_map/ppermute | solution.py:876
  406.2 29.8 %collective-permute-start.84 = (bf16[2,144,1152]{2,1,0:T(8,128)(2,1)S(1)}, bf16[2,144,1152]{2,1,0:T(8,128)(2,1)S(1)}, u32[]{:S(2)}, u32[]{:S(2)}) collective-permute-start(bf16[2,144,1152]{2,1,0:T(8,128)(2,1)S(1)} %get-tuple-element.732), channel_id=1, source_target_pairs={{0,8},{4,12},{8,0},{12,4},{16,24},{20,28},{24,16},{28,20},{1,9},{5... | collective-permute-start | bytes 1990664 | tf_op jit(solution)/shard_map/ppermute | solution.py:876
  406.8 11.4 %collective-permute-start.80 = (bf16[128,1152]{1,0:T(8,128)(2,1)S(1)}, bf16[128,1152]{1,0:T(8,128)(2,1)S(1)}, u32[]{:S(2)}, u32[]{:S(2)}) collective-permute-start(bf16[128,1152]{1,0:T(8,128)(2,1)S(1)} %copy-done.64), channel_id=1, source_target_pairs={{0,2},{1,3},{2,0},{3,1},{4,6},{5,7},{6,4},{7,5},{8,10},{9,11},{10,... | collective-permute-start | bytes 884744 | tf_op jit(solution)/shard_map/ppermute | solution.py:873
  415.1 9.9 %collective-permute-start.81 = (bf16[128,1152]{1,0:T(8,128)(2,1)S(1)}, bf16[128,1152]{1,0:T(8,128)(2,1)S(1)}, u32[]{:S(2)}, u32[]{:S(2)}) collective-permute-start(bf16[128,1152]{1,0:T(8,128)(2,1)S(1)} %copy-done.62), channel_id=1, source_target_pairs={{0,2},{1,3},{2,0},{3,1},{4,6},{5,7},{6,4},{7,5},{8,10},{9,11},{10,... | collective-permute-start | bytes 884744 | tf_op jit(solution)/shard_map/ppermute | solution.py:873
  416.7 17.5 %collective-permute-start.83 = (bf16[128,1152]{1,0:T(8,128)(2,1)S(1)}, bf16[128,1152]{1,0:T(8,128)(2,1)S(1)}, u32[]{:S(2)}, u32[]{:S(2)}) collective-permute-start(bf16[128,1152]{1,0:T(8,128)(2,1)S(1)} %copy-done.58), channel_id=1, source_target_pairs={{0,2},{1,3},{2,0},{3,1},{4,6},{5,7},{6,4},{7,5},{8,10},{9,11},{10,... | collective-permute-start | bytes 884744 | tf_op jit(solution)/shard_map/ppermute | solution.py:873
  418.3 13.7 %collective-permute-start.82 = (bf16[64,1152]{1,0:T(8,128)(2,1)S(1)}, bf16[64,1152]{1,0:T(8,128)(2,1)S(1)}, u32[]{:S(2)}, u32[]{:S(2)}) collective-permute-start(bf16[64,1152]{1,0:T(8,128)(2,1)S(1)} %get-tuple-element.726.refs_0_), channel_id=1, source_target_pairs={{0,2},{1,3},{2,0},{3,1},{4,6},{5,7},{6,4},{7,5},{8,10},{9,11},{10,... | collective-permute-start | bytes 442376 | tf_op jit(solution)/shard_map/ppermute | solution.py:873
  425.0 24.8 %collective-permute-start.87 = (bf16[1,144,1152]{2,1,0:T(8,128)(2,1)S(1)}, bf16[1,144,1152]{2,1,0:T(8,128)(2,1)S(1)}, u32[]{:S(2)}, u32[]{:S(2)}) collective-permute-start(bf16[1,144,1152]{2,1,0:T(8,128)(2,1)S(1)} %get-tuple-element.761), channel_id=1, source_target_pairs={{0,16},{4,20},{8,24},{12,28},{16,0},{20,4},{24,8},{28,12},{1,17},{... | collective-permute-start | bytes 995336 | tf_op jit(solution)/shard_map/ppermute | solution.py:876
  432.0 22.2 %collective-permute-start.86 = (bf16[1,144,1152]{2,1,0:T(8,128)(2,1)S(1)}, bf16[1,144,1152]{2,1,0:T(8,128)(2,1)S(1)}, u32[]{:S(2)}, u32[]{:S(2)}) collective-permute-start(bf16[1,144,1152]{2,1,0:T(8,128)(2,1)S(1)} %get-tuple-element.759), channel_id=1, source_target_pairs={{0,16},{4,20},{8,24},{12,28},{16,0},{20,4},{24,8},{28,12},{1,17},{... | collective-permute-start | bytes 995336 | tf_op jit(solution)/shard_map/ppermute | solution.py:876
  437.4 21.6 %collective-permute-start.88 = (f32[32,1152]{1,0:T(8,128)S(1)}, f32[32,1152]{1,0:T(8,128)S(1)}, u32[]{:S(2)}, u32[]{:S(2)}) collective-permute-start(f32[32,1152]{1,0:T(8,128)S(1)} %get-tuple-element.767.refs_1_), channel_id=1, source_target_pairs={{0,1},{1,0},{2,3},{3,2},{4,5},{5,4},{6,7},{7,6},{8,9},{9,8},{10,11... | collective-permute-start | bytes 442376 | tf_op jit(solution)/shard_map/ppermute | solution.py:870
  465.9 19.5 %collective-permute-start.92 = (bf16[2,144,1152]{2,1,0:T(8,128)(2,1)S(1)}, bf16[2,144,1152]{2,1,0:T(8,128)(2,1)S(1)}, u32[]{:S(2)}, u32[]{:S(2)}) collective-permute-start(bf16[2,144,1152]{2,1,0:T(8,128)(2,1)S(1)} %get-tuple-element.774), channel_id=1, source_target_pairs={{0,8},{4,12},{8,0},{12,4},{16,24},{20,28},{24,16},{28,20},{1,9},{5... | collective-permute-start | bytes 1990664 | tf_op jit(solution)/shard_map/ppermute | solution.py:876
  473.5 23.3 %collective-permute-start.93 = (bf16[128,1152]{1,0:T(8,128)(2,1)}, bf16[128,1152]{1,0:T(8,128)(2,1)}, u32[]{:S(2)}, u32[]{:S(2)}) collective-permute-start(bf16[128,1152]{1,0:T(8,128)(2,1)} %get-tuple-element.781.refs_2_), channel_id=1, source_target_pairs={{0,1},{1,0},{2,3},{3,2},{4,5},{5,4},{6,7},{7,6},{8,9},{9,8},{10,11... | collective-permute-start | bytes 884744 | tf_op jit(solution)/shard_map/ppermute | solution.py:870
  473.5 25.6 %collective-permute-start.94 = (bf16[320,1152]{1,0:T(8,128)(2,1)S(1)}, bf16[320,1152]{1,0:T(8,128)(2,1)S(1)}, u32[]{:S(2)}, u32[]{:S(2)}) collective-permute-start(bf16[320,1152]{1,0:T(8,128)(2,1)S(1)} %get-tuple-element.784.refs_2_), channel_id=1, source_target_pairs={{0,1},{1,0},{2,3},{3,2},{4,5},{5,4},{6,7},{7,6},{8,9},{9,8},{10,11... | collective-permute-start | bytes 2211848 | tf_op jit(solution)/shard_map/ppermute | solution.py:870
  474.0 37.1 %collective-permute-start.98 = (bf16[1,144,1152]{2,1,0:T(8,128)(2,1)S(1)}, bf16[1,144,1152]{2,1,0:T(8,128)(2,1)}, u32[]{:S(2)}, u32[]{:S(2)}) collective-permute-start(bf16[1,144,1152]{2,1,0:T(8,128)(2,1)S(1)} %get-tuple-element.791), channel_id=1, source_target_pairs={{0,16},{4,20},{8,24},{12,28},{16,0},{20,4},{24,8},{28,12},{1,17},{... | collective-permute-start | bytes 995336 | tf_op jit(solution)/shard_map/ppermute | solution.py:876
  487.4 28.0 %collective-permute-start.99 = (bf16[1,144,1152]{2,1,0:T(8,128)(2,1)S(1)}, bf16[1,144,1152]{2,1,0:T(8,128)(2,1)S(1)}, u32[]{:S(2)}, u32[]{:S(2)}) collective-permute-start(bf16[1,144,1152]{2,1,0:T(8,128)(2,1)S(1)} %get-tuple-element.794), channel_id=1, source_target_pairs={{0,16},{4,20},{8,24},{12,28},{16,0},{20,4},{24,8},{28,12},{1,17},{... | collective-permute-start | bytes 995336 | tf_op jit(solution)/shard_map/ppermute | solution.py:876
  493.1 13.4 %collective-permute-start.95 = (bf16[4,2,1152]{2,1,0:T(2,128)(2,1)S(1)}, bf16[4,2,1152]{2,1,0:T(2,128)(2,1)S(1)}, u32[]{:S(2)}, u32[]{:S(2)}) collective-permute-start(bf16[4,2,1152]{2,1,0:T(2,128)(2,1)S(1)} %convert_element_type.153), channel_id=1, source_target_pairs={{0,16},{4,20},{8,24},{12,28},{16,0},{20,4},{24,8},{28,12},{1,17},{... | collective-permute-start | bytes 55304 | tf_op jit(solution)/shard_map/ppermute | solution.py:876
  (250 other events, 2043.7 us)
Sparse Core Ops, SparseCore 0:
  218.6 103.8 reduce-scatter.1
